TPU v7x, 32 devices: a whole 2x2x4 slice. The times are simulated.
32 devices in a mesh: dp: 2 (over x), row: 4 (over z), col: 4 (over y, core).
Axes of the slice: x: 2, y: 2, z: 4, core: 2. Of those that a mesh axis runs over, the one named last changes fastest.
Arguments:
- tokens: bfloat16 [4, 1024, 2048], P('dp', 'col', 'row'), may hold values from -6 to 6
- query_weight: bfloat16 [2048, 2048], P('row', 'col'), may hold values from -0.1875 to 0.1875
- key_weight: bfloat16 [2048, 2048], P('row', 'col'), may hold values from -0.1875 to 0.1875
- value_weight: bfloat16 [2048, 2048], P('row', 'col'), may hold values from -0.23201941 to 0.23201941
- out_weight: bfloat16 [2048, 2048], P('col', 'row'), may hold values from -0.75 to 0.75
- gate_weight: bfloat16 [2048, 8192], P('row', 'col'), may hold values from -0.23201941 to 0.23201941
- up_weight: bfloat16 [2048, 8192], P('row', 'col'), may hold values from -0.125 to 0.125
- down_weight: bfloat16 [8192, 2048], P('col', 'row'), may hold values from -0.0625 to 0.0625
- cotangent: bfloat16 [4, 1024, 2048], P('dp', 'col', 'row'), may hold values from -6 to 6
Outputs:
- layer_out: bfloat16 [4, 1024, 2048], P('dp', 'col', 'row')
- input_grad: float32 [4, 1024, 2048], P('dp', 'col', 'row')
- query_grad: float32 [2048, 2048], P('row', 'col')
- key_grad: float32 [2048, 2048], P('row', 'col')
- value_grad: float32 [2048, 2048], P('row', 'col')
- output_grad: float32 [2048, 2048], P('col', 'row')
- gate_grad: float32 [2048, 8192], P('row', 'col')
- up_grad: float32 [2048, 8192], P('row', 'col')
- down_grad: float32 [8192, 2048], P('col', 'row')
All inputs are finite; a program needn't handle non-finite values.
Results may differ from a plain program's by a relative error of at most 0.03.
Values may be sent and summed in bfloat16 or wider, within the bound.
No kernel may reach another device: no remote copies, remote signals or barrier semaphores. Data moves between devices by JAX's collectives and lax.ppermute only.
A program may use at most 192 MiB of HBM per device.

v0:
```python
import jax
import jax.numpy as jnp
from jax import lax
from jax.sharding import PartitionSpec as P

HEAD_DIM = 128
SEQ = 1024
BLOCK = 512


epsilon = 1e-05
rope_base = 10000.0
masked_score = -1e30


def rope_tables(length, head_depth):
    halfway = head_depth // 2
    position = jnp.arange(length).astype(jnp.float32)[:, None]
    frequency = rope_base ** (-(2.0 * jnp.arange(halfway).astype(jnp.float32)) / head_depth)
    angles = position * frequency[None, :]
    cosine = jnp.concatenate([jnp.cos(angles), jnp.cos(angles)], axis=1)
    sine_table = jnp.concatenate([jnp.sin(angles), jnp.sin(angles)], axis=1)
    return (cosine, sine_table)


def rope_apply(vector, cosine, sine_table):
    halfway = vector.shape[-1] // 2
    turned = jnp.concatenate([-vector[..., halfway:], vector[..., :halfway]], axis=-1)
    return vector * cosine + turned * sine_table


def rope_undo(gradient, cosine, sine_table):
    halfway = gradient.shape[-1] // 2
    scaled = gradient * sine_table
    turned = jnp.concatenate([scaled[..., halfway:], -scaled[..., :halfway]], axis=-1)
    return gradient * cosine + turned


def norm_forward(stream):
    totals = jnp.sum(stream, axis=1)
    squares = jnp.sum(stream * stream, axis=1)
    totals, squares = lax.psum((totals, squares), "row")
    features = stream.shape[1] * lax.axis_size("row")
    average = totals / features
    spread = squares / features - average * average
    inverse = lax.rsqrt(spread + epsilon)
    return ((stream - average[:, None]) * inverse[:, None], inverse)


def norm_backward(normed, inverse, gradient):
    totals = jnp.sum(gradient, axis=1)
    crossed = jnp.sum(gradient * normed, axis=1)
    totals, crossed = lax.psum((totals, crossed), "row")
    features = normed.shape[1] * lax.axis_size("row")
    return inverse[:, None] * (
        gradient - totals[:, None] / features - normed * (crossed[:, None] / features)
    )


def gather_normed(normed_low):
    return lax.all_gather(normed_low, "col", axis=0, tiled=True)


def gather_grads(grad_low):
    return lax.all_gather(grad_low, "col", axis=0, tiled=True)


def gather_heads(head_low):
    return lax.all_gather(head_low, "row", axis=1, tiled=True)


def gather_hidden(hidden_low):
    return lax.all_gather(hidden_low, "row", axis=0, tiled=True)


def branch_sum(producer, row_count):
    return lax.psum_scatter(
        producer(jnp.int32(0), row_count * lax.axis_size("col")).astype(jnp.bfloat16),
        "col",
        scatter_dimension=0,
        tiled=True,
    ).astype(jnp.float32)


def causal_mask(number, block_rows, finish):
    query_place = number * block_rows + jnp.arange(block_rows)
    key_place = jnp.arange(finish)
    return query_place[:, None] >= key_place[None, :]


def attend_forward(queries, key_rows, values, block_rows):
    scaling = queries.shape[1] ** (-0.5)
    outputs = []
    logsums = []
    for number in range(queries.shape[0] // block_rows):
        opening = number * block_rows
        finish = opening + block_rows
        scores = (
            jnp.einsum(
                "qd,kd->qk",
                queries[opening:finish],
                key_rows[:finish],
                preferred_element_type=jnp.float32,
            )
            * scaling
        )
        scores = jnp.where(causal_mask(number, block_rows, finish), scores, masked_score)
        highest = jnp.max(scores, axis=1, keepdims=True)
        shifted = jnp.exp(scores - highest)
        totals = jnp.sum(shifted, axis=1, keepdims=True)
        logsums.append(highest + jnp.log(totals))
        weights = (shifted / totals).astype(jnp.bfloat16)
        outputs.append(jnp.dot(weights, values[:finish], preferred_element_type=jnp.float32))
    return (jnp.concatenate(outputs, axis=0), jnp.concatenate(logsums, axis=0))


def attend_backward(queries, key_rows, values, logsums, grad_low, block_rows):
    scaling = queries.shape[1] ** (-0.5)
    query_parts = []
    key_grad = jnp.zeros(key_rows.shape, jnp.float32)
    value_grad = jnp.zeros(values.shape, jnp.float32)
    for number in range(queries.shape[0] // block_rows):
        opening = number * block_rows
        finish = opening + block_rows
        query_block = queries[opening:finish]
        grad_block = grad_low[opening:finish]
        scores = (
            jnp.einsum(
                "qd,kd->qk", query_block, key_rows[:finish], preferred_element_type=jnp.float32
            )
            * scaling
        )
        scores = jnp.where(causal_mask(number, block_rows, finish), scores, masked_score)
        probable = jnp.exp(scores - logsums[opening:finish])
        weights = probable.astype(jnp.bfloat16)
        product = jnp.einsum(
            "qd,kd->qk", grad_block, values[:finish], preferred_element_type=jnp.float32
        )
        slopes = probable * (product - jnp.sum(probable * product, axis=1, keepdims=True))
        slopes_low = slopes.astype(jnp.bfloat16)
        query_parts.append(
            jnp.dot(slopes_low, key_rows[:finish], preferred_element_type=jnp.float32) * scaling
        )
        key_grad = key_grad.at[:finish].add(
            jnp.einsum("qk,qd->kd", slopes_low, query_block, preferred_element_type=jnp.float32)
            * scaling
        )
        value_grad = value_grad.at[:finish].add(
            jnp.einsum("qk,qd->kd", weights, grad_block, preferred_element_type=jnp.float32)
        )
    return (jnp.concatenate(query_parts, axis=0), key_grad, value_grad)


def on_device(
    tokens,
    query_weight,
    key_weight,
    value_weight,
    out_weight,
    gate_weight,
    up_weight,
    down_weight,
    cotangent,
):
    cosine, sine_table = rope_tables(SEQ, HEAD_DIM)
    hidden_width = gate_weight.shape[1]

    def micro_step(totals, sequence_pair):
        stream_in, slope_in = sequence_pair
        stream = stream_in.astype(jnp.float32)
        row_count = stream.shape[0]
        normed_one, inverse_one = norm_forward(stream)
        normed_low_one = normed_one.astype(jnp.bfloat16)
        rows_one = gather_normed(normed_low_one)
        query_sum, key_sum, value_sum = (
            lax.psum_scatter(
                jnp.dot(rows_one, query_weight, preferred_element_type=jnp.float32),
                "row",
                scatter_dimension=1,
                tiled=True,
            ),
            lax.psum_scatter(
                jnp.dot(rows_one, key_weight, preferred_element_type=jnp.float32),
                "row",
                scatter_dimension=1,
                tiled=True,
            ),
            lax.psum_scatter(
                jnp.dot(rows_one, value_weight, preferred_element_type=jnp.float32),
                "row",
                scatter_dimension=1,
                tiled=True,
            ),
        )
        queries = rope_apply(query_sum, cosine, sine_table).astype(jnp.bfloat16)
        key_rows = rope_apply(key_sum, cosine, sine_table).astype(jnp.bfloat16)
        values = value_sum.astype(jnp.bfloat16)
        attended, logsums = attend_forward(queries, key_rows, values, BLOCK)
        head_low = attended.astype(jnp.bfloat16)
        heads_all = gather_heads(head_low)

        def attention_term(offset, amount):
            return jnp.dot(
                lax.dynamic_slice_in_dim(heads_all, offset, amount, 0),
                out_weight,
                preferred_element_type=jnp.float32,
            )

        middle = stream + branch_sum(attention_term, row_count)
        normed_two, inverse_two = norm_forward(middle)
        normed_low_two = normed_two.astype(jnp.bfloat16)
        rows_two = gather_normed(normed_low_two)
        hidden_rows_count = rows_two.shape[0] // lax.axis_size("row")
        picked = lax.slice_in_dim(rows_two, 0, hidden_rows_count * lax.axis_size("row"), axis=0)
        gate_up = lax.psum_scatter(
            jnp.concatenate(
                [
                    jnp.dot(picked, gate_weight, preferred_element_type=jnp.float32),
                    jnp.dot(picked, up_weight, preferred_element_type=jnp.float32),
                ],
                axis=1,
            ).astype(jnp.bfloat16),
            "row",
            scatter_dimension=0,
            tiled=True,
        ).astype(jnp.float32)
        gate_sum = gate_up[:, :hidden_width]
        up_sum = gate_up[:, hidden_width:]
        sigmoid = jax.nn.sigmoid(gate_sum)
        activated = gate_sum * sigmoid
        hidden_low = (activated * up_sum).astype(jnp.bfloat16)
        hidden_all = gather_hidden(hidden_low)

        def down_term(offset, amount):
            return jnp.dot(
                lax.dynamic_slice_in_dim(hidden_all, offset, amount, 0),
                down_weight,
                preferred_element_type=jnp.float32,
            )

        output = middle + branch_sum(down_term, row_count)
        slope_all = gather_grads(slope_in)
        hidden_back = gather_hidden(hidden_low)
        down_grad = jnp.einsum(
            "tf,td->fd", hidden_back, slope_all, preferred_element_type=jnp.float32
        )
        hidden_grad = lax.psum_scatter(
            jnp.einsum(
                "td,fd->tf",
                lax.slice_in_dim(slope_all, 0, hidden_rows_count * lax.axis_size("row"), axis=0),
                down_weight,
                preferred_element_type=jnp.float32,
            ).astype(jnp.bfloat16),
            "row",
            scatter_dimension=0,
            tiled=True,
        ).astype(jnp.float32)
        up_slope = (hidden_grad * activated).astype(jnp.bfloat16)
        gate_slope = (hidden_grad * up_sum * sigmoid * (1.0 + gate_sum * (1.0 - sigmoid))).astype(
            jnp.bfloat16
        )
        gate_all, up_all = (
            lax.all_gather(gate_slope, "row", axis=0, tiled=True),
            lax.all_gather(up_slope, "row", axis=0, tiled=True),
        )
        rows_two_back = gather_normed(normed_low_two)
        gate_grad = jnp.einsum(
            "td,tf->df", rows_two_back, gate_all, preferred_element_type=jnp.float32
        )
        up_grad = jnp.einsum("td,tf->df", rows_two_back, up_all, preferred_element_type=jnp.float32)

        def normed_two_term(offset, amount):
            gate_piece = lax.dynamic_slice_in_dim(gate_all, offset, amount, 0)
            up_piece = lax.dynamic_slice_in_dim(up_all, offset, amount, 0)
            return jnp.einsum(
                "tf,df->td", gate_piece, gate_weight, preferred_element_type=jnp.float32
            ) + jnp.einsum("tf,df->td", up_piece, up_weight, preferred_element_type=jnp.float32)

        middle_grad = slope_in.astype(jnp.float32) + norm_backward(
            normed_two, inverse_two, branch_sum(normed_two_term, row_count)
        )
        middle_all = gather_grads(middle_grad.astype(jnp.bfloat16))
        heads_back = gather_heads(head_low)
        out_grad = jnp.einsum(
            "tc,tr->cr", heads_back, middle_all, preferred_element_type=jnp.float32
        )
        head_grad = lax.psum_scatter(
            jnp.einsum(
                "tr,cr->tc", middle_all, out_weight, preferred_element_type=jnp.float32
            ).astype(jnp.bfloat16),
            "row",
            scatter_dimension=1,
            tiled=True,
        )
        query_rot, key_rot, value_slope = attend_backward(
            queries, key_rows, values, logsums, head_grad, BLOCK
        )
        query_low = rope_undo(query_rot, cosine, sine_table).astype(jnp.bfloat16)
        key_low = rope_undo(key_rot, cosine, sine_table).astype(jnp.bfloat16)
        value_low = value_slope.astype(jnp.bfloat16)
        query_all, key_all, value_all = (
            lax.all_gather(query_low, "row", axis=1, tiled=True),
            lax.all_gather(key_low, "row", axis=1, tiled=True),
            lax.all_gather(value_low, "row", axis=1, tiled=True),
        )
        rows_one_back = gather_normed(normed_low_one)
        query_grad = jnp.einsum(
            "tr,tc->rc", rows_one_back, query_all, preferred_element_type=jnp.float32
        )
        key_grad = jnp.einsum(
            "tr,tc->rc", rows_one_back, key_all, preferred_element_type=jnp.float32
        )
        value_grad = jnp.einsum(
            "tr,tc->rc", rows_one_back, value_all, preferred_element_type=jnp.float32
        )

        def normed_one_term(offset, amount):
            query_piece = lax.dynamic_slice_in_dim(query_all, offset, amount, 0)
            summed = jnp.einsum(
                "tc,rc->tr", query_piece, query_weight, preferred_element_type=jnp.float32
            )
            summed = summed + jnp.einsum(
                "tc,rc->tr", key_all, key_weight, preferred_element_type=jnp.float32
            )
            return summed + jnp.einsum(
                "tc,rc->tr", value_all, value_weight, preferred_element_type=jnp.float32
            )

        input_grad = middle_grad + norm_backward(
            normed_one, inverse_one, branch_sum(normed_one_term, row_count)
        )
        fresh_grads = (query_grad, key_grad, value_grad, out_grad, gate_grad, up_grad, down_grad)
        totals = tuple((summed + fresh for summed, fresh in zip(totals, fresh_grads)))
        return (totals, (output.astype(jnp.bfloat16), input_grad))

    starting = (
        jnp.zeros(query_weight.shape, jnp.float32),
        jnp.zeros(key_weight.shape, jnp.float32),
        jnp.zeros(value_weight.shape, jnp.float32),
        jnp.zeros(out_weight.shape, jnp.float32),
        jnp.zeros(gate_weight.shape, jnp.float32),
        jnp.zeros(up_weight.shape, jnp.float32),
        jnp.zeros(down_weight.shape, jnp.float32),
    )
    totals, (layer_out, input_grad) = lax.scan(micro_step, starting, (tokens, cotangent))
    query_total, key_total, value_total, out_total, gate_total, up_total, down_total = totals
    summed_grads = (
        lax.psum(query_total.astype(jnp.bfloat16), "dp").astype(jnp.float32),
        lax.psum(key_total.astype(jnp.bfloat16), "dp").astype(jnp.float32),
        lax.psum(value_total.astype(jnp.bfloat16), "dp").astype(jnp.float32),
        lax.psum(out_total.astype(jnp.bfloat16), "dp").astype(jnp.float32),
        lax.psum(gate_total.astype(jnp.bfloat16), "dp").astype(jnp.float32),
        lax.psum(up_total.astype(jnp.bfloat16), "dp").astype(jnp.float32),
        lax.psum(down_total.astype(jnp.bfloat16), "dp").astype(jnp.float32),
    )
    return (
        layer_out,
        input_grad,
        summed_grads[0],
        summed_grads[1],
        summed_grads[2],
        summed_grads[3],
        summed_grads[4],
        summed_grads[5],
        summed_grads[6],
    )


def solution(mesh):
    return jax.shard_map(
        on_device,
        mesh=mesh,
        in_specs=(
            P("dp", "col", "row"),
            P("row", "col"),
            P("row", "col"),
            P("row", "col"),
            P("col", "row"),
            P("row", "col"),
            P("row", "col"),
            P("col", "row"),
            P("dp", "col", "row"),
        ),
        out_specs=(
            P("dp", "col", "row"),
            P("dp", "col", "row"),
            P("row", "col"),
            P("row", "col"),
            P("row", "col"),
            P("col", "row"),
            P("row", "col"),
            P("row", "col"),
            P("col", "row"),
        ),
        check_vma=False,
    )
```

profile of v0, /device:TPU:0, one launch (start us, length us, event | category | flops | bytes accessed | tf_op | source)
XLA Modules:
  0.0 2251.0 jit_solution(1278516431725611672)
XLA Ops:
  10.4 2006.7 %while.36 = (s32[]{:T(128)}, f32[512,512]{1,0:T(8,128)}, f32[512,512]{1,0:T(8,128)}, f32[512,512]{1,0:T(8,128)}, f32[512,512]{1,0:T(8,128)}, /*index=5*/f32[512,...) while((s32[]{:T(128)}, f32[512,512]{1,0:T(8,128)}, ...), condition=%wide.region_33.34_spmd.clone, body=%wide.region_0.33_spmd.clone.sunk | while | flops 26914390016 | bytes 517847232 | solution.py:345
  50.0 37.8 %reduce-scatter.15.cloned.1.call-done = f32[1024,128]{1,0:T(8,128)} async-done(((f32[1024,512]{1,0:T(8,128)}), f32[1024,128]{1,0:T(8,128)}) %reduce-scatter.15.cloned.1.call-update) | async-done | bytes 524304 | tf_op jit(solution)/shard_map/while/body/eval_jaxpr/reduce_scatter | solution.py:176
  89.3 44.1 %reduce-scatter.17.cloned.1.call-done = f32[1024,128]{1,0:T(8,128)} async-done(((f32[1024,512]{1,0:T(8,128)}), f32[1024,128]{1,0:T(8,128)}) %reduce-scatter.17.cloned.1.call-update) | async-done | bytes 524304 | tf_op jit(solution)/shard_map/while/body/eval_jaxpr/reduce_scatter | solution.py:182
  138.0 40.8 %reduce-scatter.19.cloned.1.call-done = f32[1024,128]{1,0:T(8,128)} async-done(((f32[1024,512]{1,0:T(8,128)}), f32[1024,128]{1,0:T(8,128)}) %reduce-scatter.19.cloned.1.call-update) | async-done | bytes 524304 | tf_op jit(solution)/shard_map/while/body/eval_jaxpr/reduce_scatter | solution.py:188
  184.8 29.6 %all-gather.20.cloned.1.call-done = bf16[1024,512]{1,0:T(8,128)(2,1)} async-done(((bf16[1024,128]{1,0:T(8,128)(2,1)}), bf16[1024,512]{1,0:T(8,128)(2,1)}) %all-gather.20.cloned.1.call-update) | async-done | bytes 1048592 | tf_op jit(solution)/shard_map/while/body/eval_jaxpr/all_gather | solution.py:69
  295.4 139.4 %reduce-scatter.25.cloned.1.call-done = bf16[256,4096]{1,0:T(8,128)(2,1)} async-done(((bf16[1024,4096]{1,0:T(8,128)(2,1)}), bf16[256,4096]{1,0:T(8,128)(2,1)}) %reduce-scatter.25.cloned.1.call-update) | async-done | bytes 2097168 | tf_op jit(solution)/shard_map/while/body/eval_jaxpr/reduce_scatter | solution.py:215
  439.0 75.6 %reduce-scatter.21.cloned.1.call-done = bf16[256,2048]{1,0:T(8,128)(2,1)} async-done(((bf16[1024,2048]{1,0:T(8,128)(2,1)}), bf16[256,2048]{1,0:T(8,128)(2,1)}) %reduce-scatter.21.cloned.1.call-update) | async-done | bytes 1048592 | tf_op jit(solution)/shard_map/while/body/eval_jaxpr/reduce_scatter | solution.py:247
  520.9 80.8 %all-gather.24.cloned.1.call-done = bf16[1024,2048]{1,0:T(8,128)(2,1)} async-done(((bf16[256,2048]{1,0:T(8,128)(2,1)}), bf16[1024,2048]{1,0:T(8,128)(2,1)}) %all-gather.24.cloned.1.call-update) | async-done | bytes 4194320 | tf_op jit(solution)/shard_map/while/body/eval_jaxpr/all_gather | solution.py:263
  608.3 74.3 %all-gather.26.cloned.1.call-done = bf16[1024,2048]{1,0:T(8,128)(2,1)} async-done(((bf16[256,2048]{1,0:T(8,128)(2,1)}), bf16[1024,2048]{1,0:T(8,128)(2,1)}) %all-gather.26.cloned.1.call-update) | async-done | bytes 4194320 | tf_op jit(solution)/shard_map/while/body/eval_jaxpr/all_gather | solution.py:264
  787.7 68.2 %all-gather.36.cloned.1.call-done = bf16[1024,2048]{1,0:T(8,128)(2,1)} async-done(((bf16[256,2048]{1,0:T(8,128)(2,1)}), bf16[1024,2048]{1,0:T(8,128)(2,1)}) %all-gather.36.cloned.1.call-update) | async-done | bytes 4194320 | tf_op jit(solution)/shard_map/while/body/eval_jaxpr/all_gather | solution.py:73
  888.1 28.1 %all-gather.32.cloned.1.call-done = bf16[1024,512]{1,0:T(8,128)(2,1)} async-done(((bf16[1024,128]{1,0:T(8,128)(2,1)}), bf16[1024,512]{1,0:T(8,128)(2,1)}) %all-gather.32.cloned.1.call-update) | async-done | bytes 1048592 | tf_op jit(solution)/shard_map/while/body/eval_jaxpr/all_gather | solution.py:303
  919.4 26.9 %all-gather.34.cloned.1.call-done = bf16[1024,512]{1,0:T(8,128)(2,1)} async-done(((bf16[1024,128]{1,0:T(8,128)(2,1)}), bf16[1024,512]{1,0:T(8,128)(2,1)}) %all-gather.34.cloned.1.call-update) | async-done | bytes 1048592 | tf_op jit(solution)/shard_map/while/body/eval_jaxpr/all_gather | solution.py:304
  1049.6 37.8 %reduce-scatter.15.cloned.1.call-done = f32[1024,128]{1,0:T(8,128)} async-done(((f32[1024,512]{1,0:T(8,128)}), f32[1024,128]{1,0:T(8,128)}) %reduce-scatter.15.cloned.1.call-update) | async-done | bytes 524304 | tf_op jit(solution)/shard_map/while/body/eval_jaxpr/reduce_scatter | solution.py:176
  1088.9 44.0 %reduce-scatter.17.cloned.1.call-done = f32[1024,128]{1,0:T(8,128)} async-done(((f32[1024,512]{1,0:T(8,128)}), f32[1024,128]{1,0:T(8,128)}) %reduce-scatter.17.cloned.1.call-update) | async-done | bytes 524304 | tf_op jit(solution)/shard_map/while/body/eval_jaxpr/reduce_scatter | solution.py:182
  1137.5 40.9 %reduce-scatter.19.cloned.1.call-done = f32[1024,128]{1,0:T(8,128)} async-done(((f32[1024,512]{1,0:T(8,128)}), f32[1024,128]{1,0:T(8,128)}) %reduce-scatter.19.cloned.1.call-update) | async-done | bytes 524304 | tf_op jit(solution)/shard_map/while/body/eval_jaxpr/reduce_scatter | solution.py:188
  1184.5 29.6 %all-gather.20.cloned.1.call-done = bf16[1024,512]{1,0:T(8,128)(2,1)} async-done(((bf16[1024,128]{1,0:T(8,128)(2,1)}), bf16[1024,512]{1,0:T(8,128)(2,1)}) %all-gather.20.cloned.1.call-update) | async-done | bytes 1048592 | tf_op jit(solution)/shard_map/while/body/eval_jaxpr/all_gather | solution.py:69
  1294.7 139.7 %reduce-scatter.25.cloned.1.call-done = bf16[256,4096]{1,0:T(8,128)(2,1)} async-done(((bf16[1024,4096]{1,0:T(8,128)(2,1)}), bf16[256,4096]{1,0:T(8,128)(2,1)}) %reduce-scatter.25.cloned.1.call-update) | async-done | bytes 2097168 | tf_op jit(solution)/shard_map/while/body/eval_jaxpr/reduce_scatter | solution.py:215
  1438.5 75.7 %reduce-scatter.21.cloned.1.call-done = bf16[256,2048]{1,0:T(8,128)(2,1)} async-done(((bf16[1024,2048]{1,0:T(8,128)(2,1)}), bf16[256,2048]{1,0:T(8,128)(2,1)}) %reduce-scatter.21.cloned.1.call-update) | async-done | bytes 1048592 | tf_op jit(solution)/shard_map/while/body/eval_jaxpr/reduce_scatter | solution.py:247
  1520.6 80.8 %all-gather.24.cloned.1.call-done = bf16[1024,2048]{1,0:T(8,128)(2,1)} async-done(((bf16[256,2048]{1,0:T(8,128)(2,1)}), bf16[1024,2048]{1,0:T(8,128)(2,1)}) %all-gather.24.cloned.1.call-update) | async-done | bytes 4194320 | tf_op jit(solution)/shard_map/while/body/eval_jaxpr/all_gather | solution.py:263
  1608.0 74.3 %all-gather.26.cloned.1.call-done = bf16[1024,2048]{1,0:T(8,128)(2,1)} async-done(((bf16[256,2048]{1,0:T(8,128)(2,1)}), bf16[1024,2048]{1,0:T(8,128)(2,1)}) %all-gather.26.cloned.1.call-update) | async-done | bytes 4194320 | tf_op jit(solution)/shard_map/while/body/eval_jaxpr/all_gather | solution.py:264
  1787.4 68.2 %all-gather.36.cloned.1.call-done = bf16[1024,2048]{1,0:T(8,128)(2,1)} async-done(((bf16[256,2048]{1,0:T(8,128)(2,1)}), bf16[1024,2048]{1,0:T(8,128)(2,1)}) %all-gather.36.cloned.1.call-update) | async-done | bytes 4194320 | tf_op jit(solution)/shard_map/while/body/eval_jaxpr/all_gather | solution.py:73
  1887.9 28.1 %all-gather.32.cloned.1.call-done = bf16[1024,512]{1,0:T(8,128)(2,1)} async-done(((bf16[1024,128]{1,0:T(8,128)(2,1)}), bf16[1024,512]{1,0:T(8,128)(2,1)}) %all-gather.32.cloned.1.call-update) | async-done | bytes 1048592 | tf_op jit(solution)/shard_map/while/body/eval_jaxpr/all_gather | solution.py:303
  1919.3 26.9 %all-gather.34.cloned.1.call-done = bf16[1024,512]{1,0:T(8,128)(2,1)} async-done(((bf16[1024,128]{1,0:T(8,128)(2,1)}), bf16[1024,512]{1,0:T(8,128)(2,1)}) %all-gather.34.cloned.1.call-update) | async-done | bytes 1048592 | tf_op jit(solution)/shard_map/while/body/eval_jaxpr/all_gather | solution.py:304
  2031.4 198.3 %all-reduce.17.cloned.1.call-done = (bf16[512,512]{1,0:T(8,128)(2,1)}, bf16[512,512]{1,0:T(8,128)(2,1)}, bf16[512,512]{1,0:T(8,128)(2,1)}, bf16[512,512]{1,0:T(8...) async-done(((bf16[512,512]{1,0:T(8,128)(2,1)}, bf16[512,512]{1,0:T(8,128)(2,1)}, bf16[512,512]{1,0:T(8,128)(2,1)}, ...) | async-done | bytes 8388624 | tf_op jit(solution)/shard_map/psum | solution.py:348
  (459 shorter events, 741.0 us)
Async XLA Ops:
  50.0 164.4 %all-gather.20.cloned.1.call-start = ((), (), s32[]{:S(2)}) async-start(), calls=%async_computation.17 | async-start | bytes 1310720 | tf_op jit(solution)/shard_map/while/body/eval_jaxpr/all_gather | solution.py:69
  256.4 178.4 %reduce-scatter.25.cloned.1.call-start = ((), (), s32[]{:S(2)}) async-start(), calls=%async_computation.20 | async-start | bytes 10485760 | tf_op jit(solution)/shard_map/while/body/eval_jaxpr/reduce_scatter | solution.py:215
  288.3 226.2 %reduce-scatter.21.cloned.1.call-start = ((), (), s32[]{:S(2)}) async-start(), calls=%async_computation.16 | async-start | bytes 5242880 | tf_op jit(solution)/shard_map/while/body/eval_jaxpr/reduce_scatter | solution.py:247
  294.8 306.9 %all-gather.24.cloned.1.call-start = ((), (), s32[]{:S(2)}) async-start(), calls=%async_computation.21 | async-start | bytes 5242880 | tf_op jit(solution)/shard_map/while/body/eval_jaxpr/all_gather | solution.py:263
  520.3 162.2 %all-gather.26.cloned.1.call-start = ((), (), s32[]{:S(2)}) async-start(), calls=%async_computation.22 | async-start | bytes 5242880 | tf_op jit(solution)/shard_map/while/body/eval_jaxpr/all_gather | solution.py:264
  520.9 192.1 %reduce-scatter.27.cloned.1.call-start = ((), (), s32[]{:S(2)}) async-start(), calls=%async_computation.23 | async-start | bytes 1310720 | tf_op jit(solution)/shard_map/while/body/eval_jaxpr/reduce_scatter | solution.py:77
  748.2 137.9 %all-gather.30.cloned.1.call-start = ((), (), s32[]{:S(2)}) async-start(), calls=%async_computation.26 | async-start | bytes 1310720 | tf_op jit(solution)/shard_map/while/body/eval_jaxpr/all_gather | solution.py:302
  783.4 132.7 %all-gather.32.cloned.1.call-start = ((), (), s32[]{:S(2)}) async-start(), calls=%async_computation.27 | async-start | bytes 1310720 | tf_op jit(solution)/shard_map/while/body/eval_jaxpr/all_gather | solution.py:303
  784.0 162.3 %all-gather.34.cloned.1.call-start = ((), (), s32[]{:S(2)}) async-start(), calls=%async_computation.28 | async-start | bytes 1310720 | tf_op jit(solution)/shard_map/while/body/eval_jaxpr/all_gather | solution.py:304
  787.6 184.5 %reduce-scatter.31.cloned.1.call-start = ((), (), s32[]{:S(2)}) async-start(), calls=%async_computation.30 | async-start | bytes 1310720 | tf_op jit(solution)/shard_map/while/body/eval_jaxpr/reduce_scatter | solution.py:77
  862.0 137.5 %reduce-scatter.33.cloned.1.call-start = ((), (), s32[]{:S(2)}) async-start(), calls=%async_computation.31 | async-start | bytes 1310720 | tf_op jit(solution)/shard_map/while/body/eval_jaxpr/reduce_scatter | solution.py:77
  1046.5 131.9 %reduce-scatter.19.cloned.1.call-start = ((), (), s32[]{:S(2)}) async-start(), calls=%async_computation.14 | async-start | bytes 2621440 | tf_op jit(solution)/shard_map/while/body/eval_jaxpr/reduce_scatter | solution.py:188
  1049.6 164.5 %all-gather.20.cloned.1.call-start = ((), (), s32[]{:S(2)}) async-start(), calls=%async_computation.17 | async-start | bytes 1310720 | tf_op jit(solution)/shard_map/while/body/eval_jaxpr/all_gather | solution.py:69
  1256.1 178.3 %reduce-scatter.25.cloned.1.call-start = ((), (), s32[]{:S(2)}) async-start(), calls=%async_computation.20 | async-start | bytes 10485760 | tf_op jit(solution)/shard_map/while/body/eval_jaxpr/reduce_scatter | solution.py:215
  1288.0 226.2 %reduce-scatter.21.cloned.1.call-start = ((), (), s32[]{:S(2)}) async-start(), calls=%async_computation.16 | async-start | bytes 5242880 | tf_op jit(solution)/shard_map/while/body/eval_jaxpr/reduce_scatter | solution.py:247
  1294.5 306.9 %all-gather.24.cloned.1.call-start = ((), (), s32[]{:S(2)}) async-start(), calls=%async_computation.21 | async-start | bytes 5242880 | tf_op jit(solution)/shard_map/while/body/eval_jaxpr/all_gather | solution.py:263
  1520.0 162.3 %all-gather.26.cloned.1.call-start = ((), (), s32[]{:S(2)}) async-start(), calls=%async_computation.22 | async-start | bytes 5242880 | tf_op jit(solution)/shard_map/while/body/eval_jaxpr/all_gather | solution.py:264
  1520.6 192.1 %reduce-scatter.27.cloned.1.call-start = ((), (), s32[]{:S(2)}) async-start(), calls=%async_computation.23 | async-start | bytes 1310720 | tf_op jit(solution)/shard_map/while/body/eval_jaxpr/reduce_scatter | solution.py:77
  1747.9 138.1 %all-gather.30.cloned.1.call-start = ((), (), s32[]{:S(2)}) async-start(), calls=%async_computation.26 | async-start | bytes 1310720 | tf_op jit(solution)/shard_map/while/body/eval_jaxpr/all_gather | solution.py:302
  1783.1 132.8 %all-gather.32.cloned.1.call-start = ((), (), s32[]{:S(2)}) async-start(), calls=%async_computation.27 | async-start | bytes 1310720 | tf_op jit(solution)/shard_map/while/body/eval_jaxpr/all_gather | solution.py:303
  1783.7 162.4 %all-gather.34.cloned.1.call-start = ((), (), s32[]{:S(2)}) async-start(), calls=%async_computation.28 | async-start | bytes 1310720 | tf_op jit(solution)/shard_map/while/body/eval_jaxpr/all_gather | solution.py:304
  1787.3 184.8 %reduce-scatter.31.cloned.1.call-start = ((), (), s32[]{:S(2)}) async-start(), calls=%async_computation.30 | async-start | bytes 1310720 | tf_op jit(solution)/shard_map/while/body/eval_jaxpr/reduce_scatter | solution.py:77
  1861.7 137.8 %reduce-scatter.33.cloned.1.call-start = ((), (), s32[]{:S(2)}) async-start(), calls=%async_computation.31 | async-start | bytes 1310720 | tf_op jit(solution)/shard_map/while/body/eval_jaxpr/reduce_scatter | solution.py:77
  2017.1 212.6 %all-reduce.17.cloned.1.call-start = ((), (), s32[]{:S(2)}) async-start(), calls=%async_computation.10 | async-start | bytes 16777216 | tf_op jit(solution)/shard_map/psum | solution.py:348
  (109 other events, 2865.6 us)
Sparse Core Ops, SparseCore 0:
  43.9 43.8 reduce-scatter.14
  90.2 43.1 reduce-scatter.16
  135.5 43.1 reduce-scatter.18
  184.8 29.4 all-gather.19
  290.4 144.4 reduce-scatter.24
  437.0 77.4 reduce-scatter.20
  520.4 81.2 all-gather.23
  603.2 79.2 all-gather.25
  776.4 79.3 all-gather.35
  857.3 28.7 all-gather.29
  887.6 28.4 all-gather.31
  917.8 28.4 all-gather.33
  1043.5 43.8 reduce-scatter.14
  1089.7 43.1 reduce-scatter.16
  1135.2 43.1 reduce-scatter.18
  1184.5 29.4 all-gather.19
  1289.9 144.4 reduce-scatter.24
  1436.7 77.4 reduce-scatter.20
  1520.1 81.2 all-gather.23
  1602.9 79.2 all-gather.25
  1776.1 79.3 all-gather.35
  1857.2 28.7 all-gather.29
  1887.4 28.4 all-gather.31
  1917.6 28.4 all-gather.33
  (18 shorter events, 362.3 us)
Sparse Core Ops, SparseCore 1:
  2031.5 198.1 all-reduce.16
where the time goes:
time: 2260 us; the launch traced here: 2250 us
  waiting for transfers between devices  1810 us (80%)
  matrix products  197 us (9%)
  other arithmetic  107 us (5%)
  blocking collectives  91.9 us (4%)
    reduce_scatter x2, waiting for transfers between devices, micro_step(): lax.psum_scatter(jnp.concatenate([jnp.dot(picked, gate_weight, preferred_...  279 us
    psum x1, waiting for transfers between devices, on_device(): lax.psum(query_total.astype(jnp.bfloat16), 'dp').astype(jnp.float32)  198 us
    all_gather x2, waiting for transfers between devices, micro_step(): lax.all_gather(gate_slope, 'row', axis=0, tiled=True)  162 us
    reduce_scatter x8, waiting for transfers between devices, branch_sum(): lax.psum_scatter(producer(jnp.int32(0), row_count * lax.axis_size('col'))...  154 us
    reduce_scatter x2, waiting for transfers between devices, micro_step(): lax.psum_scatter(jnp.einsum('td,fd->tf', lax.slice_in_dim(slope_all, 0, h...  151 us
    all_gather x2, waiting for transfers between devices, micro_step(): lax.all_gather(up_slope, 'row', axis=0, tiled=True)  149 us
    all_gather x2, waiting for transfers between devices, gather_hidden(): return lax.all_gather(hidden_low, 'row', axis=0, tiled=True)  136 us
    reduce_scatter x2, waiting for transfers between devices, micro_step(): lax.psum_scatter(jnp.dot(rows_one, key_weight, preferred_element_type=jnp...  88 us
  transfers between devices with their start and end apart: 43, of which 41 were waited for; matrix products, arithmetic and copies ran while one was open for 9% of the time, Pallas kernels for 0%

commit v1 on v0

v1 whole, which is shorter than its diff:
```python
import jax
import jax.numpy as jnp
from jax import lax
from jax.sharding import Mesh
from jax.sharding import PartitionSpec as P

HEAD_DIM = 128
BLOCK = 512
CORES = 2

epsilon = 1e-05
rope_base = 10000.0
masked_score = -1e30
low = jnp.bfloat16
wide = jnp.float32


def rope_tables(length, head_depth):
    halfway = head_depth // 2
    position = jnp.arange(length).astype(jnp.float32)[:, None]
    frequency = rope_base ** (-(2.0 * jnp.arange(halfway).astype(jnp.float32)) / head_depth)
    angles = position * frequency[None, :]
    cosine = jnp.concatenate([jnp.cos(angles), jnp.cos(angles)], axis=1)
    sine_table = jnp.concatenate([jnp.sin(angles), jnp.sin(angles)], axis=1)
    return (cosine, sine_table)


def rope_apply(vector, cosine, sine_table):
    halfway = vector.shape[-1] // 2
    turned = jnp.concatenate([-vector[..., halfway:], vector[..., :halfway]], axis=-1)
    return vector * cosine + turned * sine_table


def rope_undo(gradient, cosine, sine_table):
    halfway = gradient.shape[-1] // 2
    scaled = gradient * sine_table
    turned = jnp.concatenate([scaled[..., halfway:], -scaled[..., :halfway]], axis=-1)
    return gradient * cosine + turned


def dot(left, right):
    return jnp.dot(left, right, preferred_element_type=wide)


def dot_nt(left, right):
    return jnp.einsum("mk,nk->mn", left, right, preferred_element_type=wide)


def dot_tn(left, right):
    return jnp.einsum("km,kn->mn", left, right, preferred_element_type=wide)


def layer_norm(stream):
    average = jnp.mean(stream, axis=1, keepdims=True)
    centered = stream - average
    inverse = lax.rsqrt(jnp.mean(centered * centered, axis=1, keepdims=True) + epsilon)
    return centered * inverse, inverse


def norm_backward(normed, inverse, gradient):
    average = jnp.mean(gradient, axis=1, keepdims=True)
    crossed = jnp.mean(gradient * normed, axis=1, keepdims=True)
    return inverse * (gradient - average - normed * crossed)


def causal_mask(number, block_rows, finish):
    query_place = number * block_rows + jnp.arange(block_rows)
    key_place = jnp.arange(finish)
    return query_place[:, None] >= key_place[None, :]


def attend_forward(queries, key_rows, values, block_rows):
    scaling = queries.shape[1] ** (-0.5)
    outputs = []
    logsums = []
    for number in range(queries.shape[0] // block_rows):
        opening = number * block_rows
        finish = opening + block_rows
        scores = dot_nt(queries[opening:finish], key_rows[:finish]) * scaling
        scores = jnp.where(causal_mask(number, block_rows, finish), scores, masked_score)
        highest = jnp.max(scores, axis=1, keepdims=True)
        shifted = jnp.exp(scores - highest)
        totals = jnp.sum(shifted, axis=1, keepdims=True)
        logsums.append(highest + jnp.log(totals))
        weights = (shifted / totals).astype(low)
        outputs.append(dot(weights, values[:finish]))
    return (jnp.concatenate(outputs, axis=0), jnp.concatenate(logsums, axis=0))


def attend_backward(queries, key_rows, values, logsums, grad_low, block_rows):
    scaling = queries.shape[1] ** (-0.5)
    query_parts = []
    key_grad = jnp.zeros(key_rows.shape, wide)
    value_grad = jnp.zeros(values.shape, wide)
    for number in range(queries.shape[0] // block_rows):
        opening = number * block_rows
        finish = opening + block_rows
        query_block = queries[opening:finish]
        grad_block = grad_low[opening:finish]
        scores = dot_nt(query_block, key_rows[:finish]) * scaling
        scores = jnp.where(causal_mask(number, block_rows, finish), scores, masked_score)
        probable = jnp.exp(scores - logsums[opening:finish])
        weights = probable.astype(low)
        product = dot_nt(grad_block, values[:finish])
        slopes = probable * (product - jnp.sum(probable * product, axis=1, keepdims=True))
        slopes_low = slopes.astype(low)
        query_parts.append(dot(slopes_low, key_rows[:finish]) * scaling)
        key_grad = key_grad.at[:finish].add(dot_tn(slopes_low, query_block) * scaling)
        value_grad = value_grad.at[:finish].add(dot_tn(weights, grad_block))
    return (jnp.concatenate(query_parts, axis=0), key_grad, value_grad)


class Layout:
    def __init__(self, dp, rows):
        self.dp = dp
        self.rows = rows
        self.ring = 2 * rows
        place = lambda number: (number, 0) if number < rows else (2 * rows - 1 - number, 1)
        flat = [place(number)[0] * 2 + place(number)[1] for number in range(self.ring)]
        self.flat = flat
        self.onward = [(flat[i], flat[(i + 1) % self.ring]) for i in range(self.ring)]
        self.backward = [(b, a) for a, b in self.onward]

    def locate(self):
        self.d = lax.axis_index("dp")
        self.r = lax.axis_index("row")
        self.y = lax.axis_index("y")
        self.c = lax.axis_index("core")
        self.place = jnp.where(self.y == 0, self.r, self.ring - 1 - self.r)

    def swap_core(self, array):
        return lax.ppermute(array, "core", [(0, 1), (1, 0)])

    def ordered(self, mine, theirs):
        first = jnp.where(self.c == 0, mine, theirs)
        second = jnp.where(self.c == 0, theirs, mine)
        return jnp.stack([first, second])

    def exchange_rows(self, array):
        return lax.all_to_all(array, "row", 0, 0, tiled=True)

    def exchange_ring(self, array):
        by_flat = [0] * self.ring
        for place, flat in enumerate(self.flat):
            by_flat[flat] = place
        sent = jnp.stack([array[place] for place in by_flat])
        got = lax.all_to_all(sent, ("row", "y"), 0, 0, tiled=True)
        return jnp.stack([got[flat] for flat in self.flat])

    def flip(self, array):
        return jnp.where(self.y == 0, array, array[::-1])

    def to_shard(self, array):
        mine = lax.dynamic_index_in_dim(array, self.c, 0, keepdims=False)
        other = lax.dynamic_index_in_dim(array, 1 - self.c, 0, keepdims=False)
        both = self.ordered(mine, self.swap_core(other))
        tokens, width = 2 * array.shape[1], array.shape[2]
        pieces = self.flip(both.reshape(self.rows, tokens // self.rows, width))
        got = self.exchange_rows(pieces)
        return jnp.transpose(got, (1, 0, 2)).reshape(tokens // self.rows, self.rows * width)

    def from_shard(self, array):
        tokens, width = array.shape[0], array.shape[1] // self.rows
        pieces = jnp.transpose(array.reshape(tokens, self.rows, width), (1, 0, 2))
        got = self.flip(self.exchange_rows(pieces))
        both = got.reshape(CORES, self.rows * tokens // CORES, width)
        mine = lax.dynamic_index_in_dim(both, self.c, 0, keepdims=False)
        other = lax.dynamic_index_in_dim(both, 1 - self.c, 0, keepdims=False)
        return self.ordered(mine, self.swap_core(other))

    def gather_ring(self, shard):
        half = self.ring // 2
        slots = [None] * self.ring
        slots[half] = shard
        up = down = shard
        for step in range(1, half + 1):
            up = lax.ppermute(up, ("row", "y"), self.onward)
            slots[half - step] = up
            if step < half:
                down = lax.ppermute(down, ("row", "y"), self.backward)
                slots[half + step] = down
        return jnp.concatenate(slots, axis=0)

    def scatter_ring(self, partial):
        half = self.ring // 2
        rows = partial.shape[0] // self.ring
        part = lambda slot: partial[slot * rows : (slot + 1) * rows]
        up, down = part(self.ring - 1), part(0)
        for step in range(1, half + 1):
            down = lax.ppermute(down, ("row", "y"), self.backward)
            if step < half:
                down = (down.astype(wide) + part(step).astype(wide)).astype(low)
                up = lax.ppermute(up, ("row", "y"), self.onward)
                if step < half - 1:
                    up = (up.astype(wide) + part(self.ring - 1 - step).astype(wide)).astype(low)
        return part(half).astype(wide) + up.astype(wide) + down.astype(wide)

    def roll_to_order(self, array):
        rows = array.shape[0] // self.ring
        start = ((self.ring + self.ring // 2 - self.place) % self.ring) * rows
        return lax.dynamic_slice_in_dim(
            jnp.concatenate([array, array], axis=0), start, array.shape[0], 0
        )

    def roll_to_ring(self, array):
        rows = array.shape[0] // self.ring
        start = ((self.ring + self.place - self.ring // 2) % self.ring) * rows
        return lax.dynamic_slice_in_dim(
            jnp.concatenate([array, array], axis=0), start, array.shape[0], 0
        )

    def dp_turn(self, array, step):
        return lax.ppermute(
            array, "dp", [(i, (i + step) % self.dp) for i in range(self.dp)]
        )

    def dp_gather(self, array):
        shape = (array.shape[0], self.dp) + array.shape[1:]
        whole = jnp.zeros(shape, array.dtype)
        for step in range(self.dp):
            got = array if step == 0 else self.dp_turn(array, step)
            source = (self.d + self.dp - step) % self.dp
            whole = lax.dynamic_update_slice_in_dim(whole, got[:, None], source, 1)
        return whole

    def dp_scatter(self, array):
        total = lax.dynamic_index_in_dim(array, self.d, 1, keepdims=False).astype(wide)
        for step in range(1, self.dp):
            target = (self.d + step) % self.dp
            sent = lax.dynamic_index_in_dim(array, target, 1, keepdims=False)
            total = total + self.dp_turn(sent, step).astype(wide)
        return total.astype(low)

    def spread_weight(self, pieces):
        rows, n, m = pieces.shape
        parts = pieces.reshape(rows, self.dp, n // self.dp, m)
        mine = lax.dynamic_index_in_dim(parts, self.d, 1, keepdims=False)
        got = self.exchange_rows(mine)
        return self.dp_gather(got).reshape(rows, n, m)

    def collect_grad(self, own, other):
        rows, n, m = own.shape
        total = own + self.swap_core(other.astype(low)).astype(wide)
        parts = total.astype(low).reshape(rows, self.dp, n // self.dp, m)
        summed = self.dp_scatter(parts)
        got = self.exchange_rows(summed)
        return self.dp_gather(got).reshape(rows, n, m)


def on_device(
    layout,
    tokens,
    query_weight,
    key_weight,
    value_weight,
    out_weight,
    gate_weight,
    up_weight,
    down_weight,
    cotangent,
):
    layout.locate()
    rows, ring = layout.rows, layout.ring
    depth = HEAD_DIM

    stream = layout.to_shard(tokens).astype(wide)
    slope_low = layout.to_shard(cotangent)
    shard, width = stream.shape
    length = shard * ring
    normed_one, inverse_one = layer_norm(stream)
    rows_one = layout.gather_ring(normed_one.astype(low))

    block = query_weight.shape[0]
    heads_of = lambda weight: jnp.transpose(weight.reshape(block, rows, depth), (1, 0, 2))
    qkv_own = layout.spread_weight(
        jnp.concatenate([heads_of(query_weight), heads_of(key_weight), heads_of(value_weight)], axis=2)
    ).reshape(width, 3 * depth)
    qkv_other = layout.swap_core(qkv_own)

    hidden = gate_weight.shape[1] // rows
    units_of = lambda weight: jnp.transpose(weight.reshape(block, rows, hidden), (1, 0, 2))
    gu_own = layout.spread_weight(
        jnp.concatenate([units_of(gate_weight), units_of(up_weight)], axis=2)
    ).reshape(width, 2 * hidden)
    gu_other = layout.swap_core(gu_own)
    down_own = jnp.transpose(
        layout.spread_weight(down_weight.reshape(rows, hidden, block)), (1, 0, 2)
    ).reshape(hidden, width)
    down_other = layout.swap_core(down_own)

    out_mine = jnp.transpose(
        layout.exchange_rows(out_weight.reshape(rows, depth, block)), (1, 0, 2)
    ).reshape(depth, width)
    out_half = lax.all_gather(out_mine, ("row", "y"), axis=0, tiled=False)
    out_all = jnp.stack([out_half, layout.swap_core(out_half)], axis=1)
    flat = jnp.array(layout.flat)
    out_all = out_all[flat].reshape(ring * 2 * depth, width)

    cosine, sine_table = rope_tables(length, depth)
    qkv = layout.roll_to_order(
        jnp.concatenate([dot(rows_one, qkv_own), dot(rows_one, qkv_other)], axis=1)
    )
    head_parts = []
    for head in range(2):
        at = 3 * depth * head
        queries = rope_apply(qkv[:, at : at + depth], cosine, sine_table).astype(low)
        key_rows = rope_apply(qkv[:, at + depth : at + 2 * depth], cosine, sine_table).astype(low)
        values = qkv[:, at + 2 * depth : at + 3 * depth].astype(low)
        attended, logsums = attend_forward(queries, key_rows, values, BLOCK)
        head_parts.append((queries, key_rows, values, logsums, attended.astype(low)))
    heads = jnp.concatenate([part[4] for part in head_parts], axis=1)

    heads_shard = jnp.transpose(
        layout.exchange_ring(heads.reshape(ring, shard, 2 * depth)), (1, 0, 2)
    ).reshape(shard, ring * 2 * depth)
    middle = stream + dot(heads_shard, out_all)
    normed_two, inverse_two = layer_norm(middle)
    rows_two = layout.gather_ring(normed_two.astype(low))
    slope_all = layout.gather_ring(slope_low)

    def feed_forward(gu_weight, down_part):
        gate_up = dot(rows_two, gu_weight)
        gate_sum, up_sum = gate_up[:, :hidden], gate_up[:, hidden:]
        sigmoid = jax.nn.sigmoid(gate_sum)
        activated = gate_sum * sigmoid
        hidden_low = (activated * up_sum).astype(low)
        hidden_grad = dot_nt(slope_all, down_part)
        up_slope = (hidden_grad * activated).astype(low)
        gate_slope = (hidden_grad * up_sum * sigmoid * (1.0 + gate_sum * (1.0 - sigmoid))).astype(low)
        return hidden_low, jnp.concatenate([gate_slope, up_slope], axis=1)

    hidden_own, gu_slope_own = feed_forward(gu_own, down_own)
    hidden_other, gu_slope_other = feed_forward(gu_other, down_other)
    grad_two = layout.scatter_ring(
        (dot_nt(gu_slope_own, gu_own) + dot_nt(gu_slope_other, gu_other)).astype(low)
    )
    middle_grad = slope_low.astype(wide) + norm_backward(normed_two, inverse_two, grad_two)
    middle_low = middle_grad.astype(low)
    head_slope = dot_nt(middle_low, out_all).astype(low)
    head_grad = layout.exchange_ring(
        jnp.transpose(head_slope.reshape(shard, ring, 2 * depth), (1, 0, 2))
    ).reshape(length, 2 * depth)

    slopes = []
    for head in range(2):
        queries, key_rows, values, logsums, _ = head_parts[head]
        query_rot, key_rot, value_slope = attend_backward(
            queries, key_rows, values, logsums, head_grad[:, head * depth : (head + 1) * depth], BLOCK
        )
        slopes += [
            rope_undo(query_rot, cosine, sine_table).astype(low),
            rope_undo(key_rot, cosine, sine_table).astype(low),
            value_slope.astype(low),
        ]
    qkv_slope = layout.roll_to_ring(jnp.concatenate(slopes, axis=1))
    slope_own, slope_other = qkv_slope[:, : 3 * depth], qkv_slope[:, 3 * depth :]
    grad_one = layout.scatter_ring(
        (dot_nt(slope_own, qkv_own) + dot_nt(slope_other, qkv_other)).astype(low)
    )
    input_grad = layout.from_shard(
        middle_grad + norm_backward(normed_one, inverse_one, grad_one)
    )

    branch = layout.scatter_ring(
        (dot(hidden_own, down_own) + dot(hidden_other, down_other)).astype(low)
    )
    layer_out = layout.from_shard((middle + branch).astype(low))

    gu_grad = layout.collect_grad(
        dot_tn(rows_two, gu_slope_own).reshape(rows, block, 2 * hidden),
        dot_tn(rows_two, gu_slope_other).reshape(rows, block, 2 * hidden),
    )
    units_back = lambda grad: jnp.transpose(grad, (1, 0, 2)).reshape(block, rows * hidden).astype(wide)
    gate_grad = units_back(gu_grad[:, :, :hidden])
    up_grad = units_back(gu_grad[:, :, hidden:])
    by_block = lambda grad: jnp.transpose(grad.reshape(-1, rows, block), (1, 0, 2))
    down_grad = layout.collect_grad(
        by_block(dot_tn(hidden_own, slope_all)), by_block(dot_tn(hidden_other, slope_all))
    ).reshape(rows * hidden, block).astype(wide)
    middle_all = layout.gather_ring(middle_low)
    out_sum = by_block(dot_tn(layout.roll_to_ring(heads), middle_all))
    out_grad = layout.collect_grad(out_sum[:, :depth], out_sum[:, depth:])
    out_grad = out_grad.reshape(rows * depth, block).astype(wide)
    qkv_grad = layout.collect_grad(
        dot_tn(rows_one, slope_own).reshape(rows, block, 3 * depth),
        dot_tn(rows_one, slope_other).reshape(rows, block, 3 * depth),
    )
    heads_back = lambda grad: jnp.transpose(grad, (1, 0, 2)).reshape(block, rows * depth).astype(wide)
    query_grad = heads_back(qkv_grad[:, :, :depth])
    key_grad = heads_back(qkv_grad[:, :, depth : 2 * depth])
    value_grad = heads_back(qkv_grad[:, :, 2 * depth :])
    return (
        layer_out,
        input_grad,
        query_grad,
        key_grad,
        value_grad,
        out_grad,
        gate_grad,
        up_grad,
        down_grad,
    )


def solution(mesh):
    dp, rows, cols = (mesh.shape[name] for name in ("dp", "row", "col"))
    fine = Mesh(
        mesh.devices.reshape(dp, rows, cols // CORES, CORES), ("dp", "row", "y", "core")
    )
    layout = Layout(dp, rows)
    split = P("dp", ("y", "core"), "row")
    inward = P("row", ("y", "core"))
    outward = P(("y", "core"), "row")

    def program(*arrays):
        return on_device(layout, *arrays)

    return jax.shard_map(
        program,
        mesh=fine,
        in_specs=(split, inward, inward, inward, outward, inward, inward, outward, split),
        out_specs=(split, split, inward, inward, inward, outward, inward, inward, outward),
        check_vma=False,
    )
```

time: 2260 us -> 1030 us (0.46)
  waiting for transfers between devices: 1810 us -> 389 us
  starting transfers between devices: 3.19 us -> 231 us
  local copies, waits for them, and re-layouts: 18.3 us -> 187 us
  blocking collectives: 91.9 us -> 0 us
  matrix products: 197 us -> 116 us
  other arithmetic: 107 us -> 74.2 us
    reduce_scatter x18 -> x0, waiting for transfers between devices: 830 us -> none  [the longest x2 279 us: micro_step(): lax.psum_scatter(jnp.concatenate([jnp.dot(picked, gate_weight, preferred_...]
    all_gather x22 -> x1, waiting for transfers between devices: 722 us -> 0.02 us  [on_device(): out_half = lax.all_gather(out_mine, ('row', 'y'), axis=0, tiled=False)]
    ppermute x0 -> x72, waiting for transfers between devices: none -> 339 us  [the longest x11 124 us: dp_turn(): lax.ppermute(array, 'dp', [(i, (i + step) % self.dp) for i in range(self....]
    psum x1 -> x0, waiting for transfers between devices: 198 us -> none  [on_device(): lax.psum(query_total.astype(jnp.bfloat16), 'dp').astype(jnp.float32)]
    ppermute x0 -> x72, starting transfers between devices: none -> 144 us  [the longest x16 65.6 us: gather_ring(): up = lax.ppermute(up, ('row', 'y'), self.onward)]
    psum x8 -> x0, blocking collectives: 91.9 us -> none  [the longest x4 46.7 us: norm_backward(): totals, crossed = lax.psum((totals, crossed), 'row')]
    all_to_all x0 -> x14, starting transfers between devices: none -> 86.8 us  [the longest x12 56.6 us: exchange_rows(): return lax.all_to_all(array, 'row', 0, 0, tiled=True)]
    dot_general x64 -> x45, matrix products: 197 us -> 116 us  [the longest x15 46.1 us: dot_nt(): return jnp.einsum('mk,nk->mn', left, right, preferred_element_type=wide)]
  transfers between devices with their start and end apart: 43 -> 87, of which waited for: 41 -> 38; matrix products, arithmetic and copies ran while one was open for 9% -> 33% of each run, Pallas kernels for 0% -> 0%
where the time goes in v1:
time: 1030 us; the launch traced here: 1010 us
  waiting for transfers between devices  389 us (38%)
  starting transfers between devices  231 us (22%)
  local copies, waits for them, and re-layouts  187 us (18%)
  matrix products  116 us (11%)
  other arithmetic  74.2 us (7%)
  between operations  16.2 us (2%)
    ppermute x11, waiting for transfers between devices, dp_turn(): lax.ppermute(array, 'dp', [(i, (i + step) % self.dp) for i in range(self....  124 us
    ppermute x12, waiting for transfers between devices, gather_ring(): down = lax.ppermute(down, ('row', 'y'), self.backward)  98.2 us
    ppermute x16, starting transfers between devices, gather_ring(): up = lax.ppermute(up, ('row', 'y'), self.onward)  65.6 us
    dynamic_update_slice x15, local copies, waits for them, and re-layouts, dp_gather(): whole = lax.dynamic_update_slice_in_dim(whole, got[:, None], source, 1)  59.7 us
    unnamed x188, local copies, waits for them, and re-layouts  56.8 us
    all_to_all x12, starting transfers between devices, exchange_rows(): return lax.all_to_all(array, 'row', 0, 0, tiled=True)  56.6 us
    ppermute x12, waiting for transfers between devices, scatter_ring(): down = lax.ppermute(down, ('row', 'y'), self.backward)  52.9 us
    all_to_all x12, waiting for transfers between devices, exchange_rows(): return lax.all_to_all(array, 'row', 0, 0, tiled=True)  50.4 us
  transfers between devices with their start and end apart: 87, of which 38 were waited for; matrix products, arithmetic and copies ran while one was open for 33% of the time, Pallas kernels for 0%

profile of v1, /device:TPU:0, one launch (start us, length us, event | category | flops | bytes accessed | tf_op | source)
XLA Modules:
  0.0 1012.9 jit_solution(3010352724332289135)
XLA Ops:
  18.5 11.3 %all-to-all-done.3 = bf16[4,128,512]{2,1,0:T(8,128)(2,1)S(1)} async-done(((bf16[4,128,512]{2,1,0:T(8,128)(2,1)}), bf16[4,128,512]{2,1,0:T(8,128)(2,1)S(1)}, u32[]{:S(2)}, u32[]{:S(2)}) %all-to-all-start.3) | async-done | bytes 524320 | tf_op jit(solution)/shard_map/all_to_all | solution.py:140
  76.1 14.3 %all-to-all-done.1 = bf16[4,256,384]{2,1,0:T(8,128)(2,1)} async-done(((bf16[4,256,384]{2,1,0:T(8,128)(2,1)}), bf16[4,256,384]{2,1,0:T(8,128)(2,1)}, u32[]{:S(2)}, u32[]{:S(2)}) %all-to-all-start.1) | async-done | bytes 786464 | tf_op jit(solution)/shard_map/all_to_all | solution.py:140
  99.1 12.5 %collective-permute-start.2 = (bf16[128,2048]{1,0:T(8,128)(2,1)}, bf16[128,2048]{1,0:T(8,128)(2,1)}, u32[]{:S(2)}, u32[]{:S(2)}) collective-permute-start(bf16[128,2048]{1,0:T(8,128)(2,1)} %collective-permute-done.1), channel_id=1, source_target_pairs={{0,4},{4,8},{8,12},{12,14},{14,10},{10,6},{6,2},{2,0},{1,5},{5,9},... | collective-permute-start | bytes 1572872 | tf_op jit(solution)/shard_map/ppermute | solution.py:177
  124.8 11.3 %collective-permute-start.32 = (bf16[128,2048]{1,0:T(8,128)(2,1)}, bf16[128,2048]{1,0:T(8,128)(2,1)}, u32[]{:S(2)}, u32[]{:S(2)}) collective-permute-start(bf16[128,2048]{1,0:T(8,128)(2,1)} %collective-permute-done.31), channel_id=1, source_target_pairs={{0,4},{4,8},{8,12},{12,14},{14,10},{10,6},{6,2},{2,0},{1,5},{5,9},... | collective-permute-start | bytes 1572872 | tf_op jit(solution)/shard_map/ppermute | solution.py:177
  136.1 11.2 %collective-permute-start.3 = (bf16[128,2048]{1,0:T(8,128)(2,1)}, bf16[128,2048]{1,0:T(8,128)(2,1)}, u32[]{:S(2)}, u32[]{:S(2)}) collective-permute-start(bf16[128,2048]{1,0:T(8,128)(2,1)} %collective-permute-done.2), channel_id=1, source_target_pairs={{0,4},{4,8},{8,12},{12,14},{14,10},{10,6},{6,2},{2,0},{1,5},{5,9},... | collective-permute-start | bytes 1572872 | tf_op jit(solution)/shard_map/ppermute | solution.py:177
  182.4 18.5 %collective-permute-done.6 = bf16[128,2048]{1,0:T(8,128)(2,1)} collective-permute-done((bf16[128,2048]{1,0:T(8,128)(2,1)}, bf16[128,2048]{1,0:T(8,128)(2,1)}, u32[]{:S(2)}, u32[]{:S(2)}) %collective-permute-start.6) | collective-permute-done | bytes 524320 | tf_op jit(solution)/shard_map/ppermute | solution.py:180
  216.3 61.3 %collective-permute-done.7 = bf16[128,2048]{1,0:T(8,128)(2,1)S(1)} collective-permute-done((bf16[128,2048]{1,0:T(8,128)(2,1)}, bf16[128,2048]{1,0:T(8,128)(2,1)S(1)}, u32[]{:S(2)}, u32[]{:S(2)}) %collective-permute-start.7) | collective-permute-done | bytes 524320 | tf_op jit(solution)/shard_map/ppermute | solution.py:180
  296.6 24.9 %all-to-all-start.2 = ((bf16[8,128,256]{2,1,0:T(8,128)(2,1)}), bf16[8,128,256]{2,1,0:T(8,128)(2,1)}, u32[]{:S(2)}, u32[]{:S(2)}) async-start(bf16[8,128,256]{2,1,0:T(8,128)(2,1)} %constant_dynamic-update-slice_fusion.8), calls=%async_computation.2 | async-start | bytes 1048576 | tf_op jit(solution)/shard_map/all_to_all | solution.py:147
  338.2 38.5 %dynamic_update_slice.47 = bf16[4,2,256,512]{2,1,3,0:T(2,128)(2,1)S(1)} dynamic-update-slice(bf16[4,2,256,512]{2,1,3,0:T(2,128)(2,1)S(1)} %copy.149, bf16[4,1,256,512]{2,1,3,0:T(2,128)(2,1)} %copy.150, s32[]{:T(128)} %constant.387.clone.1, s32[]{:T(128)S(6)} %select_n.204, s32[]{:T(128)} %constant.387.clone.1, s32[]{:T(128)} %constant.387.clone.1) | dynamic-update-slice | bytes 2097156 | tf_op jit(solution)/shard_map/dynamic_update_slice | solution.py:223
  400.3 8.2 gather_fusion
  419.4 8.4 collective-permute-done.11
  524.7 9.9 collective-permute-done.25
  548.3 8.8 collective-permute-done.26
  570.7 8.8 collective-permute-done.27
  591.2 8.8 collective-permute-done.28
  725.3 46.3 %collective-permute-done.64 = bf16[4,64,512]{2,1,0:T(8,128)(2,1)S(1)} collective-permute-done((bf16[4,64,512]{2,1,0:T(8,128)(2,1)S(1)}, bf16[4,64,512]{2,1,0:T(8,128)(2,1)S(1)}, u32[]{:S(2)}, u32[]{:S(2)}) %collective-permute-start.64) | collective-permute-done | bytes 262176 | tf_op jit(solution)/shard_map/ppermute | solution.py:213
  802.7 12.7 %all-to-all-done.10 = bf16[4,256,384]{2,1,0:T(8,128)(2,1)} async-done(((bf16[4,256,384]{2,1,0:T(8,128)(2,1)}), bf16[4,256,384]{2,1,0:T(8,128)(2,1)}, u32[]{:S(2)}, u32[]{:S(2)}) %all-to-all-start.10) | async-done | bytes 786464 | tf_op jit(solution)/shard_map/all_to_all | solution.py:140
  822.0 18.0 %collective-permute-start.46 = (bf16[128,2048]{1,0:T(8,128)(2,1)S(1)}, bf16[128,2048]{1,0:T(8,128)(2,1)S(1)}, u32[]{:S(2)}, u32[]{:S(2)}) collective-permute-start(bf16[128,2048]{1,0:T(8,128)(2,1)S(1)} %get-tuple-element.153), channel_id=1, source_target_pairs={{0,4},{4,8},{8,12},{12,14},{14,10},{10,6},{6,2},{2,0},{1,5},{5,9},... | collective-permute-start | bytes 1572872 | tf_op jit(solution)/shard_map/ppermute | solution.py:193
  840.0 23.4 %collective-permute-done.46 = bf16[128,2048]{1,0:T(8,128)(2,1)S(1)} collective-permute-done((bf16[128,2048]{1,0:T(8,128)(2,1)S(1)}, bf16[128,2048]{1,0:T(8,128)(2,1)S(1)}, u32[]{:S(2)}, u32[]{:S(2)}) %collective-permute-start.46) | collective-permute-done | bytes 524320 | tf_op jit(solution)/shard_map/ppermute | solution.py:193
  865.6 18.3 %collective-permute-start.47 = (bf16[128,2048]{1,0:T(8,128)(2,1)S(1)}, bf16[128,2048]{1,0:T(8,128)(2,1)S(1)}, u32[]{:S(2)}, u32[]{:S(2)}) collective-permute-start(bf16[128,2048]{1,0:T(8,128)(2,1)S(1)} %get-tuple-element.151), channel_id=1, source_target_pairs={{0,4},{4,8},{8,12},{12,14},{14,10},{10,6},{6,2},{2,0},{1,5},{5,9},... | collective-permute-start | bytes 1572872 | tf_op jit(solution)/shard_map/ppermute | solution.py:193
  885.5 9.5 collective-permute-done.51
  908.2 26.4 %collective-permute-done.65 = bf16[4,64,512]{2,1,0:T(8,128)(2,1)S(1)} collective-permute-done((bf16[4,64,512]{2,1,0:T(8,128)(2,1)S(1)}, bf16[4,64,512]{2,1,0:T(8,128)(2,1)S(1)}, u32[]{:S(2)}, u32[]{:S(2)}) %collective-permute-start.65) | collective-permute-done | bytes 262176 | tf_op jit(solution)/shard_map/ppermute | solution.py:213
  946.4 10.2 %collective-permute-done.55 = bf16[4,256,384]{2,1,0:T(8,128)(2,1)} collective-permute-done((bf16[4,256,384]{2,1,0:T(8,128)(2,1)}, bf16[4,256,384]{2,1,0:T(8,128)(2,1)}, u32[]{:S(2)}, u32[]{:S(2)}) %collective-permute-start.55) | collective-permute-done | bytes 786464 | tf_op jit(solution)/shard_map/ppermute | solution.py:213
  963.9 33.9 %collective-permute-done.68 = bf16[4,256,1024]{2,1,0:T(8,128)(2,1)} collective-permute-done((bf16[4,256,1024]{2,1,0:T(8,128)(2,1)}, bf16[4,256,1024]{2,1,0:T(8,128)(2,1)}, u32[]{:S(2)}, u32[]{:S(2)}) %collective-permute-start.68) | collective-permute-done | bytes 2097184 | tf_op jit(solution)/shard_map/ppermute | solution.py:213
  (537 shorter events, 541.4 us)
Async XLA Ops:
  90.5 83.6 %all-to-all-start.5 = ((bf16[4,256,512]{2,1,0:T(8,128)(2,1)}), bf16[4,256,512]{2,1,0:T(8,128)(2,1)}, u32[]{:S(2)}, u32[]{:S(2)}) async-start(bf16[4,256,512]{2,1,0:T(8,128)(2,1)} %dynamic-slice_bitcast_fusion.3), calls=%async_computation.5 | async-start | bytes 2097152 | tf_op jit(solution)/shard_map/all_to_all | solution.py:140
  95.2 196.2 %all-gather.2.cloned.1.call-start = ((), (), s32[]{:S(2)}) async-start(), calls=%async_computation.14 | async-start | bytes 4718592 | tf_op jit(solution)/shard_map/all_gather | solution.py:294
  122.3 57.2 %collective-permute-start.8 = (bf16[4,256,384]{2,1,0:T(8,128)(2,1)}, bf16[4,256,384]{2,1,0:T(8,128)(2,1)}, u32[]{:S(2)}, u32[]{:S(2)}) collective-permute-start(bf16[4,256,384]{2,1,0:T(8,128)(2,1)} %all-to-all-done.1), channel_id=1, source_target_pairs={{0,16},{16,0},{1,17},{17,1},{2,18},{18,2},{3,19},{19,3},{4,20},{20... | collective-permute-start | bytes 2359304 | tf_op jit(solution)/shard_map/ppermute | solution.py:213
  174.1 156.0 %collective-permute-start.36 = (bf16[128,2048]{1,0:T(8,128)(2,1)}, bf16[128,2048]{1,0:T(8,128)(2,1)}, u32[]{:S(2)}, u32[]{:S(2)}) collective-permute-start(bf16[128,2048]{1,0:T(8,128)(2,1)} %collective-permute-done.35), channel_id=1, source_target_pairs={{4,0},{8,4},{12,8},{14,12},{10,14},{6,10},{2,6},{0,2},{5,1},{9,5},... | collective-permute-start | bytes 1572872 | tf_op jit(solution)/shard_map/ppermute | solution.py:180
  174.1 122.5 %all-to-all-start.4 = ((bf16[4,256,1024]{2,1,0:T(8,128)(2,1)}), bf16[4,256,1024]{2,1,0:T(8,128)(2,1)}, u32[]{:S(2)}, u32[]{:S(2)}) async-start(bf16[4,256,1024]{2,1,0:T(8,128)(2,1)} %dynamic-slice_bitcast_fusion.1), calls=%async_computation.4 | async-start | bytes 4194304 | tf_op jit(solution)/shard_map/all_to_all | solution.py:140
  179.5 152.7 %collective-permute-start.19 = (bf16[4,256,512]{2,1,0:T(8,128)(2,1)}, bf16[4,256,512]{2,1,0:T(8,128)(2,1)}, u32[]{:S(2)}, u32[]{:S(2)}) collective-permute-start(bf16[4,256,512]{2,1,0:T(8,128)(2,1)} %all-to-all-done.5), channel_id=1, source_target_pairs={{0,16},{16,0},{1,17},{17,1},{2,18},{18,2},{3,19},{19,3},{4,20},{20... | collective-permute-start | bytes 3145736 | tf_op jit(solution)/shard_map/ppermute | solution.py:213
  200.9 78.6 %collective-permute-start.9 = (bf16[2048,384]{1,0:T(8,128)(2,1)S(1)}, bf16[2048,384]{1,0:T(8,128)(2,1)S(1)}, u32[]{:S(2)}, u32[]{:S(2)}) collective-permute-start(bf16[2048,384]{1,0:T(8,128)(2,1)S(1)} %bitcast.351), channel_id=1, source_target_pairs={{0,1},{1,0},{2,3},{3,2},{4,5},{5,4},{6,7},{7,6},{8,9},{9,8},{10,11... | collective-permute-start | bytes 4718600 | tf_op jit(solution)/shard_map/ppermute | solution.py:132
  200.9 76.7 %collective-permute-start.7 = (bf16[128,2048]{1,0:T(8,128)(2,1)}, bf16[128,2048]{1,0:T(8,128)(2,1)S(1)}, u32[]{:S(2)}, u32[]{:S(2)}) collective-permute-start(bf16[128,2048]{1,0:T(8,128)(2,1)} %collective-permute-done.6), channel_id=1, source_target_pairs={{4,0},{8,4},{12,8},{14,12},{10,14},{6,10},{2,6},{0,2},{5,1},{9,5},... | collective-permute-start | bytes 1572872 | tf_op jit(solution)/shard_map/ppermute | solution.py:180
  202.3 178.5 %collective-permute-start.34 = (bf16[128,2048]{1,0:T(8,128)(2,1)}, bf16[128,2048]{1,0:T(8,128)(2,1)}, u32[]{:S(2)}, u32[]{:S(2)}) collective-permute-start(bf16[128,2048]{1,0:T(8,128)(2,1)} %collective-permute-done.33), channel_id=1, source_target_pairs={{0,4},{4,8},{8,12},{12,14},{14,10},{10,6},{6,2},{2,0},{1,5},{5,9},... | collective-permute-start | bytes 1572872 | tf_op jit(solution)/shard_map/ppermute | solution.py:177
  291.4 101.3 %collective-permute-start.10 = (bf16[8,128,2048]{2,1,0:T(8,128)(2,1)}, bf16[8,128,2048]{2,1,0:T(8,128)(2,1)}, u32[]{:S(2)}, u32[]{:S(2)}) collective-permute-start(bf16[8,128,2048]{2,1,0:T(8,128)(2,1)} %all-gather.2.cloned.1.call-done), channel_id=1, source_target_pairs={{0,1},{1,0},{2,3},{3,2},{4,5},{5,4},{6,7},{7,6},{8,9},{9,8},{10,11... | collective-permute-start | bytes 12582920 | tf_op jit(solution)/shard_map/ppermute | solution.py:132
  296.6 89.9 %all-to-all-start.2 = ((bf16[8,128,256]{2,1,0:T(8,128)(2,1)}), bf16[8,128,256]{2,1,0:T(8,128)(2,1)}, u32[]{:S(2)}, u32[]{:S(2)}) async-start(bf16[8,128,256]{2,1,0:T(8,128)(2,1)} %constant_dynamic-update-slice_fusion.8), calls=%async_computation.2 | async-start | bytes 1048576 | tf_op jit(solution)/shard_map/all_to_all | solution.py:147
  330.2 111.5 %collective-permute-start.37 = (bf16[128,2048]{1,0:T(8,128)(2,1)}, bf16[128,2048]{1,0:T(8,128)(2,1)}, u32[]{:S(2)}, u32[]{:S(2)}) collective-permute-start(bf16[128,2048]{1,0:T(8,128)(2,1)} %collective-permute-done.36), channel_id=1, source_target_pairs={{4,0},{8,4},{12,8},{14,12},{10,14},{6,10},{2,6},{0,2},{5,1},{9,5},... | collective-permute-start | bytes 1572872 | tf_op jit(solution)/shard_map/ppermute | solution.py:180
  379.3 108.5 %collective-permute-start.21 = (bf16[512,2048]{0,1:T(8,128)(2,1)}, bf16[512,2048]{0,1:T(8,128)(2,1)}, u32[]{:S(2)}, u32[]{:S(2)}) collective-permute-start(bf16[512,2048]{0,1:T(8,128)(2,1)} %bitcast.386), channel_id=1, source_target_pairs={{0,1},{1,0},{2,3},{3,2},{4,5},{5,4},{6,7},{7,6},{8,9},{9,8},{10,11... | collective-permute-start | bytes 6291464 | tf_op jit(solution)/shard_map/ppermute | solution.py:132
  379.3 75.0 %collective-permute-start.18 = (bf16[4,256,1024]{2,1,0:T(8,128)(2,1)}, bf16[4,256,1024]{2,1,0:T(8,128)(2,1)}, u32[]{:S(2)}, u32[]{:S(2)}) collective-permute-start(bf16[4,256,1024]{2,1,0:T(8,128)(2,1)} %all-to-all-done.4), channel_id=1, source_target_pairs={{0,16},{16,0},{1,17},{17,1},{2,18},{18,2},{3,19},{19,3},{4,20},{20... | collective-permute-start | bytes 6291464 | tf_op jit(solution)/shard_map/ppermute | solution.py:213
  586.9 122.3 %collective-permute-start.66 = (bf16[4,512,1024]{2,1,0:T(8,128)(2,1)}, bf16[4,512,1024]{2,1,0:T(8,128)(2,1)}, u32[]{:S(2)}, u32[]{:S(2)}) collective-permute-start(bf16[4,512,1024]{2,1,0:T(8,128)(2,1)} %bitcast.92), channel_id=1, source_target_pairs={{0,1},{1,0},{2,3},{3,2},{4,5},{5,4},{6,7},{7,6},{8,9},{9,8},{10,11... | collective-permute-start | bytes 12582920 | tf_op jit(solution)/shard_map/ppermute | solution.py:132
  627.5 50.3 %collective-permute-start.70 = (bf16[4,256,512]{2,1,0:T(8,128)(2,1)}, bf16[4,256,512]{2,1,0:T(8,128)(2,1)}, u32[]{:S(2)}, u32[]{:S(2)}) collective-permute-start(bf16[4,256,512]{2,1,0:T(8,128)(2,1)} %dynamic-slice_bitcast_fusion.2), channel_id=1, source_target_pairs={{0,16},{16,0},{1,17},{17,1},{2,18},{18,2},{3,19},{19,3},{4,20},{20... | collective-permute-start | bytes 3145736 | tf_op jit(solution)/shard_map/ppermute | solution.py:213
  637.9 65.2 %all-to-all-start.6 = ((bf16[4,128,512]{2,1,0:T(8,128)(2,1)}), bf16[4,128,512]{2,1,0:T(8,128)(2,1)S(1)}, u32[]{:S(2)}, u32[]{:S(2)}) async-start(bf16[4,128,512]{2,1,0:T(8,128)(2,1)} %bitcast.391), calls=%async_computation.6 | async-start | bytes 1048576 | tf_op jit(solution)/shard_map/all_to_all | solution.py:140
  677.8 43.3 %collective-permute-start.53 = (bf16[4,512,384]{2,1,0:T(8,128)(2,1)}, bf16[4,512,384]{2,1,0:T(8,128)(2,1)}, u32[]{:S(2)}, u32[]{:S(2)}) collective-permute-start(bf16[4,512,384]{2,1,0:T(8,128)(2,1)} %bitcast.72), channel_id=1, source_target_pairs={{0,1},{1,0},{2,3},{3,2},{4,5},{5,4},{6,7},{7,6},{8,9},{9,8},{10,11... | collective-permute-start | bytes 4718600 | tf_op jit(solution)/shard_map/ppermute | solution.py:132
  703.8 68.5 %all-to-all-start.13 = ((bf16[4,256,512]{2,1,0:T(8,128)(2,1)}), bf16[4,256,512]{2,1,0:T(8,128)(2,1)S(1)}, u32[]{:S(2)}, u32[]{:S(2)}) async-start(bf16[4,256,512]{2,1,0:T(8,128)(2,1)} %fusion.6), calls=%async_computation.13 | async-start | bytes 2097152 | tf_op jit(solution)/shard_map/all_to_all | solution.py:140
  717.3 80.8 %collective-permute-start.67 = (bf16[4,256,1024]{2,1,0:T(8,128)(2,1)}, bf16[4,256,1024]{2,1,0:T(8,128)(2,1)}, u32[]{:S(2)}, u32[]{:S(2)}) collective-permute-start(bf16[4,256,1024]{2,1,0:T(8,128)(2,1)} %dynamic-slice_bitcast_fusion), channel_id=1, source_target_pairs={{0,16},{16,0},{1,17},{17,1},{2,18},{18,2},{3,19},{19,3},{4,20},{20... | collective-permute-start | bytes 6291464 | tf_op jit(solution)/shard_map/ppermute | solution.py:213
  720.5 51.1 %collective-permute-start.64 = (bf16[4,64,512]{2,1,0:T(8,128)(2,1)S(1)}, bf16[4,64,512]{2,1,0:T(8,128)(2,1)S(1)}, u32[]{:S(2)}, u32[]{:S(2)}) collective-permute-start(bf16[4,64,512]{2,1,0:T(8,128)(2,1)S(1)} %bitcast.406), channel_id=1, source_target_pairs={{0,16},{16,0},{1,17},{17,1},{2,18},{18,2},{3,19},{19,3},{4,20},{20... | collective-permute-start | bytes 786440 | tf_op jit(solution)/shard_map/ppermute | solution.py:213
  723.8 64.0 %collective-permute-start.54 = (bf16[4,256,384]{2,1,0:T(8,128)(2,1)}, bf16[4,256,384]{2,1,0:T(8,128)(2,1)}, u32[]{:S(2)}, u32[]{:S(2)}) collective-permute-start(bf16[4,256,384]{2,1,0:T(8,128)(2,1)} %dynamic-slice_bitcast_fusion.4), channel_id=1, source_target_pairs={{0,16},{16,0},{1,17},{17,1},{2,18},{18,2},{3,19},{19,3},{4,20},{20... | collective-permute-start | bytes 2359304 | tf_op jit(solution)/shard_map/ppermute | solution.py:213
  815.4 84.1 %all-to-all-start.12 = ((bf16[4,256,1024]{2,1,0:T(8,128)(2,1)}), bf16[4,256,1024]{2,1,0:T(8,128)(2,1)}, u32[]{:S(2)}, u32[]{:S(2)}) async-start(bf16[4,256,1024]{2,1,0:T(8,128)(2,1)} %fusion.2), calls=%async_computation.12 | async-start | bytes 4194304 | tf_op jit(solution)/shard_map/all_to_all | solution.py:140
  936.3 61.5 %collective-permute-start.68 = (bf16[4,256,1024]{2,1,0:T(8,128)(2,1)}, bf16[4,256,1024]{2,1,0:T(8,128)(2,1)}, u32[]{:S(2)}, u32[]{:S(2)}) collective-permute-start(bf16[4,256,1024]{2,1,0:T(8,128)(2,1)} %all-to-all-done.12), channel_id=1, source_target_pairs={{0,16},{16,0},{1,17},{17,1},{2,18},{18,2},{3,19},{19,3},{4,20},{20... | collective-permute-start | bytes 6291464 | tf_op jit(solution)/shard_map/ppermute | solution.py:213
  (129 other events, 3183.9 us)
Sparse Core Ops, SparseCore 0:
  159.2 121.9 all-gather.1

commit v2 on v1

v2 whole, which is shorter than its diff:
```python
import jax
import jax.numpy as jnp
from jax import lax
from jax.sharding import Mesh
from jax.sharding import PartitionSpec as P

HEAD_DIM = 128
BLOCK = 512
HALF = 2

epsilon = 1e-05
rope_base = 10000.0
masked_score = -1e30
low = jnp.bfloat16
wide = jnp.float32


def rope_tables(places, head_depth):
    halfway = head_depth // 2
    position = places.astype(jnp.float32)[:, None]
    frequency = rope_base ** (-(2.0 * jnp.arange(halfway).astype(jnp.float32)) / head_depth)
    angles = position * frequency[None, :]
    cosine = jnp.concatenate([jnp.cos(angles), jnp.cos(angles)], axis=1)
    sine_table = jnp.concatenate([jnp.sin(angles), jnp.sin(angles)], axis=1)
    return (cosine, sine_table)


def rope_apply(vector, cosine, sine_table):
    halfway = vector.shape[-1] // 2
    turned = jnp.concatenate([-vector[..., halfway:], vector[..., :halfway]], axis=-1)
    return vector * cosine + turned * sine_table


def rope_undo(gradient, cosine, sine_table):
    halfway = gradient.shape[-1] // 2
    scaled = gradient * sine_table
    turned = jnp.concatenate([scaled[..., halfway:], -scaled[..., :halfway]], axis=-1)
    return gradient * cosine + turned


def dot(left, right):
    return jnp.dot(left, right, preferred_element_type=wide)


def dot_nt(left, right):
    return jnp.einsum("mk,nk->mn", left, right, preferred_element_type=wide)


def dot_tn(left, right):
    return jnp.einsum("km,kn->mn", left, right, preferred_element_type=wide)


def layer_norm(stream):
    average = jnp.mean(stream, axis=1, keepdims=True)
    centered = stream - average
    inverse = lax.rsqrt(jnp.mean(centered * centered, axis=1, keepdims=True) + epsilon)
    return centered * inverse, inverse


def norm_backward(normed, inverse, gradient):
    average = jnp.mean(gradient, axis=1, keepdims=True)
    crossed = jnp.mean(gradient * normed, axis=1, keepdims=True)
    return inverse * (gradient - average - normed * crossed)


def attend_forward(queries, key_rows, values, places, block_rows):
    scaling = queries.shape[1] ** (-0.5)
    outputs = []
    logsums = []
    for opening in range(0, queries.shape[0], block_rows):
        finish = opening + block_rows
        scores = dot_nt(queries[opening:finish], key_rows) * scaling
        seen = places[opening:finish, None] >= places[None, :]
        scores = jnp.where(seen, scores, masked_score)
        highest = jnp.max(scores, axis=1, keepdims=True)
        shifted = jnp.exp(scores - highest)
        totals = jnp.sum(shifted, axis=1, keepdims=True)
        logsums.append(highest + jnp.log(totals))
        weights = (shifted / totals).astype(low)
        outputs.append(dot(weights, values))
    return (jnp.concatenate(outputs, axis=0), jnp.concatenate(logsums, axis=0))


def attend_backward(queries, key_rows, values, places, logsums, grad_low, block_rows):
    scaling = queries.shape[1] ** (-0.5)
    query_parts = []
    key_grad = jnp.zeros(key_rows.shape, wide)
    value_grad = jnp.zeros(values.shape, wide)
    for opening in range(0, queries.shape[0], block_rows):
        finish = opening + block_rows
        query_block = queries[opening:finish]
        grad_block = grad_low[opening:finish]
        scores = dot_nt(query_block, key_rows) * scaling
        seen = places[opening:finish, None] >= places[None, :]
        scores = jnp.where(seen, scores, masked_score)
        probable = jnp.exp(scores - logsums[opening:finish])
        weights = probable.astype(low)
        product = dot_nt(grad_block, values)
        slopes = probable * (product - jnp.sum(probable * product, axis=1, keepdims=True))
        slopes_low = slopes.astype(low)
        query_parts.append(dot(slopes_low, key_rows) * scaling)
        key_grad = key_grad + dot_tn(slopes_low, query_block) * scaling
        value_grad = value_grad + dot_tn(weights, grad_block)
    return (jnp.concatenate(query_parts, axis=0), key_grad, value_grad)


def swap(array, axis):
    return lax.ppermute(array, axis, [(0, 1), (1, 0)])


class Ring:
    def __init__(self, axes, line):
        self.axes = axes
        self.size = 2 * line
        self.half = line
        flat = [2 * n if n < line else 2 * (2 * line - 1 - n) + 1 for n in range(self.size)]
        self.upward = [(flat[i], flat[(i + 1) % self.size]) for i in range(self.size)]
        self.downward = [(b, a) for a, b in self.upward]

    def up(self, array):
        return lax.ppermute(array, self.axes, self.upward)

    def down(self, array):
        return lax.ppermute(array, self.axes, self.downward)

    def gather(self, shard):
        half, cut = self.half, shard.shape[0] // 2
        slots = [None] * self.size
        slots[half] = rising = falling = shard
        for step in range(1, half):
            slots[half - step] = rising = self.up(rising)
            slots[half + step] = falling = self.down(falling)
        slots[0] = jnp.concatenate([self.up(rising[:cut]), self.down(falling[cut:])], axis=0)
        return slots

    def scatter(self, parts):
        half, cut = self.half, parts[0].shape[0] // 2
        rising, falling = self.up(parts[0][:cut]), self.down(parts[0][cut:])
        for step in range(1, half):
            over, under = parts[self.size - step], parts[step]
            if step == 1:
                over = jnp.concatenate([add_low(over[:cut], rising), over[cut:]], axis=0)
                under = jnp.concatenate([under[:cut], add_low(under[cut:], falling)], axis=0)
            else:
                over, under = add_low(over, rising), add_low(under, falling)
            rising, falling = self.up(over), self.down(under)
        return parts[half].astype(wide) + rising.astype(wide) + falling.astype(wide)


def add_low(left, right):
    return (left.astype(wide) + right.astype(wide)).astype(low)


def split_rows(array, count):
    rows = array.shape[0] // count
    return [array[i * rows : (i + 1) * rows] for i in range(count)]


def gather_group(ring, shard):
    slots = ring.gather(shard)
    return jnp.concatenate(slots + [swap(slot, "core") for slot in slots], axis=0)


def scatter_group(ring, partial):
    own, other = split_rows(partial, HALF)
    return ring.scatter(split_rows(add_low(own, swap(other, "core")), ring.size))


def exchange_rows(array):
    return lax.all_to_all(array, ROW, 0, 0, tiled=True)


ROW = ("zhi", "zlo")


def to_shard(array):
    rows = lax.axis_size(ROW)
    seqs, tokens, width = array.shape
    pieces = array.reshape(rows, seqs * tokens // rows, width)
    got = exchange_rows(pieces)
    return jnp.transpose(got, (1, 0, 2)).reshape(pieces.shape[1], rows * width)


def from_shard(array, seqs):
    rows = lax.axis_size(ROW)
    tokens, width = array.shape[0], array.shape[1] // rows
    pieces = jnp.transpose(array.reshape(tokens, rows, width), (1, 0, 2))
    return exchange_rows(pieces).reshape(seqs, rows * tokens // seqs, width)


def pick(array, index, axis):
    return lax.dynamic_index_in_dim(array, index, axis, keepdims=False)


def in_order(mine, theirs, axis):
    at_first = lax.axis_index("x") == 0
    return jnp.stack(
        [jnp.where(at_first, mine, theirs), jnp.where(at_first, theirs, mine)], axis=axis
    )


def sum_grad(mine, theirs):
    total = add_low(mine, swap(theirs, "x"))
    if lax.axis_size("pair") > 1:
        total = lax.psum(total, "pair")
    rows = lax.axis_size(ROW)
    return exchange_rows(total.reshape(rows, total.shape[0] // rows, total.shape[1]))


def on_device(
    tokens,
    query_weight,
    key_weight,
    value_weight,
    out_weight,
    gate_weight,
    up_weight,
    down_weight,
    cotangent,
):
    depth = HEAD_DIM
    rows, line = lax.axis_size(ROW), lax.axis_size("zlo")
    x_index = lax.axis_index("x")
    small_ring = Ring(("zlo", "y"), line)
    large_ring = Ring(("zhi", "zlo", "y"), rows)
    seqs, width = tokens.shape[0], tokens.shape[2] * rows
    block = width // rows

    stream = to_shard(tokens).astype(wide)
    slope_low = to_shard(cotangent)
    shard = stream.shape[0]

    def heads_of(weight):
        return pick(weight.reshape(block, line, HALF, depth), x_index, 2)

    head_mats = [query_weight, key_weight, value_weight, out_weight.T]
    head_pieces = jnp.transpose(
        jnp.concatenate([heads_of(weight) for weight in head_mats], axis=2), (1, 0, 2)
    )
    head_pieces = jnp.concatenate([head_pieces] * (rows // line), axis=0)
    head_mine = exchange_rows(head_pieces).reshape(width, 4 * depth)
    head_weights = [head_mine, swap(head_mine, "x")]

    units = gate_weight.shape[1] // rows // HALF

    def units_of(weight):
        return jnp.transpose(pick(weight.reshape(block, rows, HALF, units), x_index, 2), (1, 0, 2))

    def spread(pieces):
        mine = exchange_rows(pieces).reshape(width, pieces.shape[2])
        theirs = swap(mine, "x")
        return jnp.concatenate([mine, theirs, swap(mine, "core"), swap(theirs, "core")], axis=1)

    gu_weight = spread(jnp.concatenate([units_of(gate_weight), units_of(up_weight)], axis=2))
    down_turned = spread(units_of(down_weight.T))

    place = jnp.arange(2 * small_ring.size)
    core = (lax.axis_index("core") + place // small_ring.size) % 2
    side, level = lax.axis_index("y"), lax.axis_index("zlo")
    here = jnp.where(side == 0, level, small_ring.size - 1 - level)
    spot = (here + place % small_ring.size + small_ring.half) % small_ring.size
    slot_side = spot // line
    slot_level = jnp.where(slot_side == 0, spot, small_ring.size - 1 - spot)
    first = ((2 * slot_side + core) * line + slot_level) * shard
    places = (first[:, None] + jnp.arange(shard)[None, :]).reshape(-1)
    cosine, sine_table = rope_tables(places, depth)

    normed_one, inverse_one = layer_norm(stream)
    rows_one = gather_group(small_ring, normed_one.astype(low))
    kept = []
    for weight in head_weights:
        qkv = dot(rows_one, weight[:, : 3 * depth])
        queries = rope_apply(qkv[:, :depth], cosine, sine_table).astype(low)
        key_rows = rope_apply(qkv[:, depth : 2 * depth], cosine, sine_table).astype(low)
        values = qkv[:, 2 * depth :].astype(low)
        attended, logsums = attend_forward(queries, key_rows, values, places, BLOCK)
        kept.append((queries, key_rows, values, logsums, attended.astype(low)))
    heads = jnp.concatenate([part[4] for part in kept], axis=1)
    out_turned = jnp.concatenate([weight[:, 3 * depth :] for weight in head_weights], axis=1)
    middle = stream + scatter_group(small_ring, dot_nt(heads, out_turned).astype(low))
    normed_two, inverse_two = layer_norm(middle)
    rows_two = jnp.concatenate(large_ring.gather(normed_two.astype(low)), axis=0)
    slope_all = jnp.concatenate(large_ring.gather(slope_low), axis=0)

    blocks = 2 * HALF
    gate_up = dot(rows_two, gu_weight).reshape(-1, blocks, 2, units)
    gate_sum, up_sum = (gate_up[:, :, i].reshape(-1, blocks * units) for i in range(2))
    sigmoid = jax.nn.sigmoid(gate_sum)
    activated = gate_sum * sigmoid
    hidden_low = (activated * up_sum).astype(low)
    hidden_grad = dot(slope_all, down_turned)
    up_slope = (hidden_grad * activated).astype(low)
    gate_slope = (hidden_grad * up_sum * sigmoid * (1.0 + gate_sum * (1.0 - sigmoid))).astype(low)
    gu_slope = jnp.stack(
        [part.reshape(-1, blocks, units) for part in (gate_slope, up_slope)], axis=2
    ).reshape(-1, 2 * blocks * units)
    grad_two = large_ring.scatter(
        split_rows(dot_nt(gu_slope, gu_weight).astype(low), large_ring.size)
    )
    middle_grad = slope_low.astype(wide) + norm_backward(normed_two, inverse_two, grad_two)
    middle_all = gather_group(small_ring, middle_grad.astype(low))

    head_grad = dot(middle_all, out_turned).astype(low)
    head_slopes = []
    for head in range(HALF):
        queries, key_rows, values, logsums, _ = kept[head]
        query_rot, key_rot, value_slope = attend_backward(
            queries, key_rows, values, places, logsums, head_grad[:, head * depth : (head + 1) * depth], BLOCK
        )
        parts = [
            rope_undo(query_rot, cosine, sine_table),
            rope_undo(key_rot, cosine, sine_table),
            value_slope,
        ]
        head_slopes.append(jnp.concatenate([part.astype(low) for part in parts], axis=1))
    grad_one = scatter_group(
        small_ring,
        sum(
            dot_nt(slope, weight[:, : 3 * depth])
            for slope, weight in zip(head_slopes, head_weights)
        ).astype(low),
    )
    input_grad = from_shard(middle_grad + norm_backward(normed_one, inverse_one, grad_one), seqs)

    branch = large_ring.scatter(
        split_rows(dot_nt(hidden_low, down_turned).astype(low), large_ring.size)
    )
    layer_out = from_shard((middle + branch).astype(low), seqs)

    def unit_grad(left, right, size):
        own = dot_tn(left, right[:, : 2 * size])
        other = dot_tn(left, right[:, 2 * size :]).astype(low)
        total = add_low(own, swap(other, "core"))
        mine = sum_grad(total[:, :size], total[:, size:])
        return in_order(mine, swap(mine, "x"), 2).astype(wide)

    def unit_columns(grad):
        return jnp.transpose(grad, (1, 0, 2, 3)).reshape(block, -1)

    gu_grad = unit_grad(rows_two, gu_slope, 2 * units)
    gate_grad = unit_columns(gu_grad[:, :, :, :units])
    up_grad = unit_columns(gu_grad[:, :, :, units:])
    down_grad = unit_columns(unit_grad(slope_all, hidden_low, units)).T

    head_sums = []
    for head in range(HALF):
        qkv_sum = dot_tn(rows_one, head_slopes[head])
        out_sum = dot_tn(middle_all, kept[head][4])
        head_sums.append(jnp.concatenate([qkv_sum, out_sum], axis=1).astype(low))
    head_all = sum_grad(head_sums[0], head_sums[1]).reshape(rows // line, line, block, 4 * depth)
    head_total = jnp.sum(head_all.astype(wide), axis=0).astype(low)
    head_total = in_order(head_total, swap(head_total, "x"), 2).astype(wide)
    head_total = jnp.transpose(head_total, (1, 0, 2, 3))
    head_grads = [
        head_total[..., i * depth : (i + 1) * depth].reshape(block, -1) for i in range(4)
    ]
    return (
        layer_out,
        input_grad,
        head_grads[0],
        head_grads[1],
        head_grads[2],
        head_grads[3].T,
        gate_grad,
        up_grad,
        down_grad,
    )


def solution(mesh):
    dp, rows, cols = (mesh.shape[name] for name in ("dp", "row", "col"))
    sizes = (dp // HALF, HALF, HALF, rows // HALF, cols // HALF, HALF)
    fine = Mesh(mesh.devices.reshape(sizes), ("pair", "x", "zhi", "zlo", "y", "core"))
    across, inner, tall = ("pair", "x"), ("y", "core"), ROW
    split = P(across, inner, tall)
    inward = P(tall, inner)
    outward = P(inner, tall)
    return jax.shard_map(
        on_device,
        mesh=fine,
        in_specs=(split, inward, inward, inward, outward, inward, inward, outward, split),
        out_specs=(split, split, inward, inward, inward, outward, inward, inward, outward),
        check_vma=False,
    )
```

time: 1030 us -> 888 us (0.86); the launches traced: 1010 us -> 882 us
  starting transfers between devices: 231 us -> 116 us
  local copies, waits for them, and re-layouts: 187 us -> 161 us
  waiting for transfers between devices: 389 us -> 410 us
  blocking collectives: 0 us -> 19.3 us
  other arithmetic: 74.2 us -> 56.3 us
  between operations: 16.2 us -> 2.85 us
    ppermute x72 -> x73, starting transfers between devices: 144 us -> 75.3 us  [the longest x24 33.6 us: down(): return lax.ppermute(array, self.axes, self.downward)]
    dynamic_update_slice x15 -> x0, local copies, waits for them, and re-layouts: 59.7 us -> none  [dp_gather(): whole = lax.dynamic_update_slice_in_dim(whole, got[:, None], source, 1)]
    ppermute x72 -> x73, waiting for transfers between devices: 339 us -> 388 us  [the longest x24 192 us: up(): return lax.ppermute(array, self.axes, self.upward)]
    all_to_all x14 -> x9, starting transfers between devices: 86.8 us -> 41 us  [exchange_rows(): return lax.all_to_all(array, ROW, 0, 0, tiled=True)]
    slice x4 -> x26, local copies, waits for them, and re-layouts: 3.42 us -> 47.7 us  [the longest x3 33.3 us: on_device(): gate_up[:, :, i].reshape(-1, blocks * units)]
    all_to_all x14 -> x9, waiting for transfers between devices: 50.4 us -> 21.3 us  [exchange_rows(): return lax.all_to_all(array, ROW, 0, 0, tiled=True)]
    transpose x2 -> x4, local copies, waits for them, and re-layouts: 0.54 us -> 20.5 us  [the longest x3 15.3 us: unit_columns(): return jnp.transpose(grad, (1, 0, 2, 3)).reshape(block, -1)]
    all_to_all x0 -> x1, blocking collectives: none -> 19.3 us  [exchange_rows(): return lax.all_to_all(array, ROW, 0, 0, tiled=True)]
  transfers between devices with their start and end apart: 87 -> 82, of which waited for: 38 -> 35; matrix products, arithmetic and copies ran while one was open for 33% -> 28% of each run, Pallas kernels for 0% -> 0%
where the time goes in v2:
time: 888 us; the launch traced here: 882 us
  waiting for transfers between devices  410 us (46%)
  local copies, waits for them, and re-layouts  161 us (18%)
  matrix products  117 us (13%)
  starting transfers between devices  116 us (13%)
  other arithmetic  56.3 us (6%)
  blocking collectives  19.3 us (2%)
    ppermute x24, waiting for transfers between devices, up(): return lax.ppermute(array, self.axes, self.upward)  192 us
    ppermute x25, waiting for transfers between devices, swap(): return lax.ppermute(array, axis, [(0, 1), (1, 0)])  144 us
    unnamed x209, local copies, waits for them, and re-layouts  57 us
    ppermute x24, waiting for transfers between devices, down(): return lax.ppermute(array, self.axes, self.downward)  52.8 us
    all_to_all x9, starting transfers between devices, exchange_rows(): return lax.all_to_all(array, ROW, 0, 0, tiled=True)  41 us
    dot_general x13, matrix products, dot(): return jnp.dot(left, right, preferred_element_type=wide)  40.1 us
    dot_general x13, matrix products, dot_nt(): return jnp.einsum('mk,nk->mn', left, right, preferred_element_type=wide)  38.8 us
    dot_general x16, matrix products, dot_tn(): return jnp.einsum('km,kn->mn', left, right, preferred_element_type=wide)  37.6 us
  transfers between devices with their start and end apart: 82, of which 35 were waited for; matrix products, arithmetic and copies ran while one was open for 28% of the time, Pallas kernels for 0%

profile of v2, /device:TPU:0, one launch (start us, length us, event | category | flops | bytes accessed | tf_op | source)
XLA Modules:
  0.0 882.2 jit_solution(5596266952702854640)
XLA Ops:
  11.4 10.3 %all-to-all-done = bf16[4,128,512]{2,1,0:T(8,128)(2,1)S(1)} async-done(((bf16[4,128,512]{2,1,0:T(8,128)(2,1)}), bf16[4,128,512]{2,1,0:T(8,128)(2,1)S(1)}, u32[]{:S(2)}, u32[]{:S(2)}) %all-to-all-start) | async-done | bytes 524320 | tf_op jit(solution)/shard_map/all_to_all | solution.py:170
  29.2 41.5 %collective-permute-done = bf16[128,2048]{1,0:T(8,128)(2,1)S(1)} collective-permute-done((bf16[128,2048]{1,0:T(8,128)(2,1)S(1)}, bf16[128,2048]{1,0:T(8,128)(2,1)S(1)}, u32[]{:S(2)}, u32[]{:S(2)}) %collective-permute-start) | collective-permute-done | bytes 524320 | tf_op jit(solution)/shard_map/ppermute | solution.py:121
  99.4 36.7 %collective-permute-done.8 = bf16[2048,512]{1,0:T(8,128)(2,1)S(1)} collective-permute-done((bf16[2048,512]{1,0:T(8,128)(2,1)}, bf16[2048,512]{1,0:T(8,128)(2,1)S(1)}, u32[]{:S(2)}, u32[]{:S(2)}) %collective-permute-start.8) | collective-permute-done | bytes 2097184 | tf_op jit(solution)/shard_map/ppermute | solution.py:108
  149.6 19.3 %all_to_all.50 = bf16[4,128,512]{2,1,0:T(8,128)(2,1)S(1)} all-to-all(bf16[4,128,512]{2,1,0:T(8,128)(2,1)S(1)} %bitcast.211), channel_id=1, replica_groups=mesh['pair'=1,'x'=2,'zhi'=2,'zlo'=2,'y'=2,'core'=2] {'zhi','zlo'}, dimensions={0} | all-to-all | bytes 1048576 | tf_op jit(solution)/shard_map/all_to_all | solution.py:170
  203.3 10.5 %collective-permute-done.37 = bf16[128,2048]{1,0:T(8,128)(2,1)} collective-permute-done((bf16[128,2048]{1,0:T(8,128)(2,1)}, bf16[128,2048]{1,0:T(8,128)(2,1)}, u32[]{:S(2)}, u32[]{:S(2)}) %collective-permute-start.37) | collective-permute-done | bytes 524320 | tf_op jit(solution)/shard_map/ppermute | solution.py:121
  236.2 9.1 %collective-permute-done.42 = bf16[128,2048]{1,0:T(8,128)(2,1)S(1)} collective-permute-done((bf16[128,2048]{1,0:T(8,128)(2,1)}, bf16[128,2048]{1,0:T(8,128)(2,1)S(1)}, u32[]{:S(2)}, u32[]{:S(2)}) %collective-permute-start.42) | collective-permute-done | bytes 524320 | tf_op jit(solution)/shard_map/ppermute | solution.py:124
  245.3 34.5 %collective-permute-done.39 = bf16[64,2048]{1,0:T(8,128)(2,1)S(1)} collective-permute-done((bf16[64,2048]{1,0:T(8,128)(2,1)S(1)}, bf16[64,2048]{1,0:T(8,128)(2,1)S(1)}, u32[]{:S(2)}, u32[]{:S(2)}) %collective-permute-start.39) | collective-permute-done | bytes 262176 | tf_op jit(solution)/shard_map/ppermute | solution.py:121
  328.9 9.2 %collective-permute-done.22 = bf16[2048,512]{1,0:T(8,128)(2,1)S(1)} collective-permute-done((bf16[2048,512]{1,0:T(8,128)(2,1)}, bf16[2048,512]{1,0:T(8,128)(2,1)S(1)}, u32[]{:S(2)}, u32[]{:S(2)}) %collective-permute-start.22) | collective-permute-done | bytes 2097184 | tf_op jit(solution)/shard_map/ppermute | solution.py:108
  346.1 13.1 %fusion.18 = f32[1024,2048]{1,0:T(8,128)} fusion(bf16[1024,2048]{1,0:T(8,128)(2,1)S(1)} %constant_dynamic-update-slice_fusion.9, bf16[2048,512]{1,0:T(8,128)(2,1)} %collective-permute-done.24, bf16[2048,512]{1,0:T(8,128)(2,1)S(1)} %collective-permute-done.23, bf16[2048,512]{1,0:T(8,128)(2,1)S(1)} %collective-permute-done.22, bf16[2048,512]{1,0:T(8,128)(2,1)} %bitcast.22), kind=kOutput, calls=%fused_computation.84 | convolution fusion | flops 8623489024 | bytes 20971520 | tf_op jit(solution)/shard_map/dot_general | solution.py:42
  359.1 11.7 %reshape.319 = f32[1024,4,2,256]{3,2,1,0:T(2,128)} reshape(f32[1024,2048]{1,0:T(8,128)} %fusion.18) | data formatting | bytes 16777216 | tf_op jit(solution)/shard_map/reshape | solution.py:286
  370.9 11.4 %fusion.137 = (f32[1024,4,1,256]{3,2,1,0:T(1,128)}, f32[1024,4,1,256]{3,2,1,0:T(1,128)}) fusion(f32[1024,4,2,256]{3,2,1,0:T(2,128)} %reshape.319), kind=kLoop, calls=%fused_computation.352 | loop fusion | bytes 16777216 | tf_op jit(solution)/shard_map/slice | solution.py:287
  382.3 11.0 %copy.129 = f32[1024,4,1,256]{0,3,1,2:T(8,128)} copy(f32[1024,4,1,256]{3,2,1,0:T(1,128)} %get-tuple-element.32) | data formatting | bytes 8388608 | tf_op jit(solution)/shard_map/slice | solution.py:287
  393.2 10.9 %copy.128 = f32[1024,4,1,256]{0,3,1,2:T(8,128)} copy(f32[1024,4,1,256]{3,2,1,0:T(1,128)} %get-tuple-element.31) | data formatting | bytes 8388608 | tf_op jit(solution)/shard_map/slice | solution.py:287
  404.1 12.3 %fusion.3 = (bf16[1024,1024]{0,1:T(8,128)(2,1)}, bf16[1024,1024]{0,1:T(8,128)(2,1)}, bf16[1024,1024]{0,1:T(8,128)(2,1)}) fusion(f32[1024,4,1,256]{0,3,1,2:T(8,128)} %copy.129, f32[1024,4,1,256]{0,3,1,2:T(8,128)} %copy.128, bf16[1024,2048]{1,0:T(8,128)(2,1)} %constant_dynamic-update-slice_fusion.18, bf16[2048,256]{1,0:T(8,128)(2,1)} %collective-permute-done.27, ...), kind=kOutput, calls=%fused_computation.13 | convolution fusion | flops 4327473152 | bytes 23068672 | tf_op jit(solution)/shard_map/dot_general | solution.py:42
  419.1 12.8 %convolution_convert_fusion = bf16[1024,2048]{1,0:T(8,128)(2,1)S(1)} fusion(bf16[1024,2048]{0,1:T(8,128)(2,1)S(1)} %bitcast.183, bf16[2048,512]{1,0:T(8,128)(2,1)} %collective-permute-done.24, bf16[2048,512]{1,0:T(8,128)(2,1)} %copy-done.73, bf16[2048,512]{1,0:T(8,128)(2,1)} %copy-done.72, bf16[2048,512]{1,0:T(8,128)(2,1)} %bitcast.22), kind=kOutput, calls=%fused_computation.29 | convolution fusion | flops 8625586176 | bytes 16777216 | tf_op jit(solution)/shard_map/mk,nk->mn/dot_general | solution.py:46
  452.6 8.8 collective-permute-done.45
  461.7 11.0 %collective-permute-done.29 = bf16[128,2048]{1,0:T(8,128)(2,1)S(1)} collective-permute-done((bf16[128,2048]{1,0:T(8,128)(2,1)S(1)}, bf16[128,2048]{1,0:T(8,128)(2,1)S(1)}, u32[]{:S(2)}, u32[]{:S(2)}) %collective-permute-start.29) | collective-permute-done | bytes 524320 | tf_op jit(solution)/shard_map/ppermute | solution.py:121
  498.4 10.6 %collective-permute-done.34 = bf16[128,2048]{1,0:T(8,128)(2,1)S(1)} collective-permute-done((bf16[128,2048]{1,0:T(8,128)(2,1)S(1)}, bf16[128,2048]{1,0:T(8,128)(2,1)S(1)}, u32[]{:S(2)}, u32[]{:S(2)}) %collective-permute-start.34) | collective-permute-done | bytes 524320 | tf_op jit(solution)/shard_map/ppermute | solution.py:124
  619.9 18.1 %collective-permute-done.65 = bf16[2048,512]{0,1:T(8,128)(2,1)} collective-permute-done((bf16[2048,512]{0,1:T(8,128)(2,1)}, bf16[2048,512]{0,1:T(8,128)(2,1)}, u32[]{:S(2)}, u32[]{:S(2)}) %collective-permute-start.65) | collective-permute-done | bytes 2097184 | tf_op jit(solution)/shard_map/ppermute | solution.py:108
  659.8 43.0 %collective-permute-done.68 = bf16[2048,512]{1,0:T(8,128)(2,1)S(1)} collective-permute-done((bf16[2048,512]{1,0:T(8,128)(2,1)S(1)}, bf16[2048,512]{1,0:T(8,128)(2,1)S(1)}, u32[]{:S(2)}, u32[]{:S(2)}) %collective-permute-start.68) | collective-permute-done | bytes 2097184 | tf_op jit(solution)/shard_map/ppermute | solution.py:108
  712.0 36.3 %collective-permute-done.61 = bf16[64,2048]{1,0:T(8,128)(2,1)S(1)} collective-permute-done((bf16[64,2048]{1,0:T(8,128)(2,1)S(1)}, bf16[64,2048]{1,0:T(8,128)(2,1)S(1)}, u32[]{:S(2)}, u32[]{:S(2)}) %collective-permute-start.61) | collective-permute-done | bytes 262176 | tf_op jit(solution)/shard_map/ppermute | solution.py:121
  753.6 14.5 %collective-permute-done.64 = bf16[128,2048]{1,0:T(8,128)(2,1)S(1)} collective-permute-done((bf16[128,2048]{1,0:T(8,128)(2,1)S(1)}, bf16[128,2048]{1,0:T(8,128)(2,1)S(1)}, u32[]{:S(2)}, u32[]{:S(2)}) %collective-permute-start.64) | collective-permute-done | bytes 524320 | tf_op jit(solution)/shard_map/ppermute | solution.py:124
  789.1 11.0 %all-to-all-done.6 = f32[4,128,512]{2,1,0:T(8,128)S(1)} async-done(((f32[4,128,512]{2,1,0:T(8,128)}), f32[4,128,512]{2,1,0:T(8,128)S(1)}, u32[]{:S(2)}, u32[]{:S(2)}) %all-to-all-start.6) | async-done | bytes 1048608 | tf_op jit(solution)/shard_map/all_to_all | solution.py:170
  820.3 28.3 %collective-permute-done.69 = bf16[4,512,512]{2,1,0:T(8,128)(2,1)} collective-permute-done((bf16[4,512,512]{2,1,0:T(8,128)(2,1)}, bf16[4,512,512]{2,1,0:T(8,128)(2,1)}, u32[]{:S(2)}, u32[]{:S(2)}) %collective-permute-start.69) | collective-permute-done | bytes 2097184 | tf_op jit(solution)/shard_map/ppermute | solution.py:108
  (528 shorter events, 443.5 us)
Async XLA Ops:
  21.6 66.2 %all-to-all-start.1 = ((bf16[4,512,512]{2,1,0:T(8,128)(2,1)}), bf16[4,512,512]{2,1,0:T(8,128)(2,1)}, u32[]{:S(2)}, u32[]{:S(2)}) async-start(bf16[4,512,512]{2,1,0:T(8,128)(2,1)} %pad_maximum_fusion.3), calls=%async_computation.1 | async-start | bytes 4194304 | tf_op jit(solution)/shard_map/all_to_all | solution.py:170
  27.0 43.7 %collective-permute-start = (bf16[128,2048]{1,0:T(8,128)(2,1)S(1)}, bf16[128,2048]{1,0:T(8,128)(2,1)S(1)}, u32[]{:S(2)}, u32[]{:S(2)}) collective-permute-start(bf16[128,2048]{1,0:T(8,128)(2,1)S(1)} %fusion.47), channel_id=1, source_target_pairs={{0,4},{4,6},{6,2},{2,0},{1,5},{5,7},{7,3},{3,1},{8,12},{12,14},{14... | collective-permute-start | bytes 1572872 | tf_op jit(solution)/shard_map/ppermute | solution.py:121
  29.0 44.3 %collective-permute-start.2 = (bf16[128,2048]{1,0:T(8,128)(2,1)S(1)}, bf16[128,2048]{1,0:T(8,128)(2,1)S(1)}, u32[]{:S(2)}, u32[]{:S(2)}) collective-permute-start(bf16[128,2048]{1,0:T(8,128)(2,1)S(1)} %fusion.47), channel_id=1, source_target_pairs={{4,0},{6,4},{2,6},{0,2},{5,1},{7,5},{3,7},{1,3},{12,8},{14,12},{10... | collective-permute-start | bytes 1572872 | tf_op jit(solution)/shard_map/ppermute | solution.py:124
  87.8 48.2 %collective-permute-start.8 = (bf16[2048,512]{1,0:T(8,128)(2,1)}, bf16[2048,512]{1,0:T(8,128)(2,1)S(1)}, u32[]{:S(2)}, u32[]{:S(2)}) collective-permute-start(bf16[2048,512]{1,0:T(8,128)(2,1)} %bitcast.14), channel_id=1, source_target_pairs={{0,16},{16,0},{1,17},{17,1},{2,18},{18,2},{3,19},{19,3},{4,20},{20... | collective-permute-start | bytes 6291464 | tf_op jit(solution)/shard_map/ppermute | solution.py:108
  149.6 41.9 %collective-permute-start.9 = (bf16[512,2048]{1,0:T(8,128)(2,1)}, bf16[512,2048]{1,0:T(8,128)(2,1)}, u32[]{:S(2)}, u32[]{:S(2)}) collective-permute-start(bf16[512,2048]{1,0:T(8,128)(2,1)} %slice.491), channel_id=1, source_target_pairs={{0,1},{1,0},{2,3},{3,2},{4,5},{5,4},{6,7},{7,6},{8,9},{9,8},{10,11... | collective-permute-start | bytes 6291464 | tf_op jit(solution)/shard_map/ppermute | solution.py:108
  179.9 39.6 %all-to-all-start.3 = ((bf16[4,512,256]{2,1,0:T(8,128)(2,1)}), bf16[4,512,256]{2,1,0:T(8,128)(2,1)}, u32[]{:S(2)}, u32[]{:S(2)}) async-start(bf16[4,512,256]{2,1,0:T(8,128)(2,1)} %bitcast.188), calls=%async_computation.3 | async-start | bytes 2097152 | tf_op jit(solution)/shard_map/all_to_all | solution.py:170
  219.5 73.7 %all-to-all-start.2 = ((bf16[4,512,512]{2,1,0:T(8,128)(2,1)}), bf16[4,512,512]{2,1,0:T(8,128)(2,1)}, u32[]{:S(2)}, u32[]{:S(2)}) async-start(bf16[4,512,512]{2,1,0:T(8,128)(2,1)} %pad_maximum_fusion.4), calls=%async_computation.2 | async-start | bytes 4194304 | tf_op jit(solution)/shard_map/all_to_all | solution.py:170
  227.0 58.7 %collective-permute-start.13 = (bf16[128,2048]{1,0:T(8,128)(2,1)S(1)}, bf16[128,2048]{1,0:T(8,128)(2,1)S(1)}, u32[]{:S(2)}, u32[]{:S(2)}) collective-permute-start(bf16[128,2048]{1,0:T(8,128)(2,1)S(1)} %pad_maximum_fusion.19), channel_id=1, source_target_pairs={{4,0},{6,4},{2,6},{0,2},{5,1},{7,5},{3,7},{1,3},{12,8},{14,12},{10... | collective-permute-start | bytes 1572872 | tf_op jit(solution)/shard_map/ppermute | solution.py:124
  230.0 55.7 %collective-permute-start.11 = (bf16[128,2048]{1,0:T(8,128)(2,1)S(1)}, bf16[128,2048]{1,0:T(8,128)(2,1)S(1)}, u32[]{:S(2)}, u32[]{:S(2)}) collective-permute-start(bf16[128,2048]{1,0:T(8,128)(2,1)S(1)} %pad_maximum_fusion.18), channel_id=1, source_target_pairs={{0,4},{4,6},{6,2},{2,0},{1,5},{5,7},{7,3},{3,1},{8,12},{12,14},{14... | collective-permute-start | bytes 1572872 | tf_op jit(solution)/shard_map/ppermute | solution.py:121
  232.2 47.7 %collective-permute-start.39 = (bf16[64,2048]{1,0:T(8,128)(2,1)S(1)}, bf16[64,2048]{1,0:T(8,128)(2,1)S(1)}, u32[]{:S(2)}, u32[]{:S(2)}) collective-permute-start(bf16[64,2048]{1,0:T(8,128)(2,1)S(1)} %slice.514), channel_id=1, source_target_pairs={{0,4},{4,8},{8,12},{12,14},{14,10},{10,6},{6,2},{2,0},{1,5},{5,9},... | collective-permute-start | bytes 786440 | tf_op jit(solution)/shard_map/ppermute | solution.py:121
  234.7 83.0 %collective-permute-start.25 = (bf16[2048,256]{1,0:T(8,128)(2,1)}, bf16[2048,256]{1,0:T(8,128)(2,1)}, u32[]{:S(2)}, u32[]{:S(2)}) collective-permute-start(bf16[2048,256]{1,0:T(8,128)(2,1)} %bitcast.29), channel_id=1, source_target_pairs={{0,16},{16,0},{1,17},{17,1},{2,18},{18,2},{3,19},{19,3},{4,20},{20... | collective-permute-start | bytes 3145736 | tf_op jit(solution)/shard_map/ppermute | solution.py:108
  245.3 158.9 %collective-permute-start.26 = (bf16[2048,256]{1,0:T(8,128)(2,1)}, bf16[2048,256]{1,0:T(8,128)(2,1)}, u32[]{:S(2)}, u32[]{:S(2)}) collective-permute-start(bf16[2048,256]{1,0:T(8,128)(2,1)} %bitcast.29), channel_id=1, source_target_pairs={{0,1},{1,0},{2,3},{3,2},{4,5},{5,4},{6,7},{7,6},{8,9},{9,8},{10,11... | collective-permute-start | bytes 3145736 | tf_op jit(solution)/shard_map/ppermute | solution.py:108
  293.2 44.9 %collective-permute-start.22 = (bf16[2048,512]{1,0:T(8,128)(2,1)}, bf16[2048,512]{1,0:T(8,128)(2,1)S(1)}, u32[]{:S(2)}, u32[]{:S(2)}) collective-permute-start(bf16[2048,512]{1,0:T(8,128)(2,1)} %bitcast.22), channel_id=1, source_target_pairs={{0,16},{16,0},{1,17},{17,1},{2,18},{18,2},{3,19},{19,3},{4,20},{20... | collective-permute-start | bytes 6291464 | tf_op jit(solution)/shard_map/ppermute | solution.py:108
  317.7 86.4 %collective-permute-start.27 = (bf16[2048,256]{1,0:T(8,128)(2,1)}, bf16[2048,256]{1,0:T(8,128)(2,1)}, u32[]{:S(2)}, u32[]{:S(2)}) collective-permute-start(bf16[2048,256]{1,0:T(8,128)(2,1)} %collective-permute-done.25), channel_id=1, source_target_pairs={{0,1},{1,0},{2,3},{3,2},{4,5},{5,4},{6,7},{7,6},{8,9},{9,8},{10,11... | collective-permute-start | bytes 3145736 | tf_op jit(solution)/shard_map/ppermute | solution.py:108
  539.3 107.3 %collective-permute-start.67 = (bf16[2048,1024]{1,0:T(8,128)(2,1)}, bf16[2048,1024]{1,0:T(8,128)(2,1)}, u32[]{:S(2)}, u32[]{:S(2)}) collective-permute-start(bf16[2048,1024]{1,0:T(8,128)(2,1)} %convolution_convert_fusion.2), channel_id=1, source_target_pairs={{0,1},{1,0},{2,3},{3,2},{4,5},{5,4},{6,7},{7,6},{8,9},{9,8},{10,11... | collective-permute-start | bytes 12582920 | tf_op jit(solution)/shard_map/ppermute | solution.py:108
  540.6 59.0 %all-to-all-start.4 = ((bf16[4,128,512]{2,1,0:T(8,128)(2,1)}), bf16[4,128,512]{2,1,0:T(8,128)(2,1)S(1)}, u32[]{:S(2)}, u32[]{:S(2)}) async-start(bf16[4,128,512]{2,1,0:T(8,128)(2,1)} %bitcast.197), calls=%async_computation.4 | async-start | bytes 1048576 | tf_op jit(solution)/shard_map/all_to_all | solution.py:170
  589.7 48.4 %collective-permute-start.65 = (bf16[2048,512]{0,1:T(8,128)(2,1)}, bf16[2048,512]{0,1:T(8,128)(2,1)}, u32[]{:S(2)}, u32[]{:S(2)}) collective-permute-start(bf16[2048,512]{0,1:T(8,128)(2,1)} %pad_maximum_fusion.5), channel_id=1, source_target_pairs={{0,16},{16,0},{1,17},{17,1},{2,18},{18,2},{3,19},{19,3},{4,20},{20... | collective-permute-start | bytes 6291464 | tf_op jit(solution)/shard_map/ppermute | solution.py:108
  600.4 41.5 %all-to-all-start.9 = ((bf16[4,512,256]{2,1,0:T(8,128)(2,1)}), bf16[4,512,256]{2,1,0:T(8,128)(2,1)S(1)}, u32[]{:S(2)}, u32[]{:S(2)}) async-start(bf16[4,512,256]{2,1,0:T(8,128)(2,1)} %bitcast.55), calls=%async_computation.9 | async-start | bytes 2097152 | tf_op jit(solution)/shard_map/all_to_all | solution.py:170
  613.8 43.3 %collective-permute-start.60 = (bf16[512,2048]{1,0:T(8,128)(2,1)}, bf16[512,2048]{1,0:T(8,128)(2,1)}, u32[]{:S(2)}, u32[]{:S(2)}) collective-permute-start(bf16[512,2048]{1,0:T(8,128)(2,1)} %slice.542), channel_id=1, source_target_pairs={{0,1},{1,0},{2,3},{3,2},{4,5},{5,4},{6,7},{7,6},{8,9},{9,8},{10,11... | collective-permute-start | bytes 6291464 | tf_op jit(solution)/shard_map/ppermute | solution.py:108
  641.9 63.1 %all-to-all-start.7 = ((bf16[4,512,512]{1,2,0:T(8,128)(2,1)}), bf16[4,512,512]{1,2,0:T(8,128)(2,1)}, u32[]{:S(2)}, u32[]{:S(2)}) async-start(bf16[4,512,512]{1,2,0:T(8,128)(2,1)} %bitcast.176), calls=%async_computation.7 | async-start | bytes 4194304 | tf_op jit(solution)/shard_map/all_to_all | solution.py:170
  655.5 47.3 %collective-permute-start.68 = (bf16[2048,512]{1,0:T(8,128)(2,1)S(1)}, bf16[2048,512]{1,0:T(8,128)(2,1)S(1)}, u32[]{:S(2)}, u32[]{:S(2)}) collective-permute-start(bf16[2048,512]{1,0:T(8,128)(2,1)S(1)} %slice.557), channel_id=1, source_target_pairs={{0,16},{16,0},{1,17},{17,1},{2,18},{18,2},{3,19},{19,3},{4,20},{20... | collective-permute-start | bytes 6291464 | tf_op jit(solution)/shard_map/ppermute | solution.py:108
  705.0 65.3 %all-to-all-start.8 = ((bf16[4,512,512]{2,1,0:T(8,128)(2,1)}), bf16[4,512,512]{2,1,0:T(8,128)(2,1)}, u32[]{:S(2)}, u32[]{:S(2)}) async-start(bf16[4,512,512]{2,1,0:T(8,128)(2,1)} %bitcast.174), calls=%async_computation.8 | async-start | bytes 4194304 | tf_op jit(solution)/shard_map/all_to_all | solution.py:170
  709.9 38.3 %collective-permute-start.61 = (bf16[64,2048]{1,0:T(8,128)(2,1)S(1)}, bf16[64,2048]{1,0:T(8,128)(2,1)S(1)}, u32[]{:S(2)}, u32[]{:S(2)}) collective-permute-start(bf16[64,2048]{1,0:T(8,128)(2,1)S(1)} %get-tuple-element.61), channel_id=1, source_target_pairs={{0,4},{4,6},{6,2},{2,0},{1,5},{5,7},{7,3},{3,1},{8,12},{12,14},{14... | collective-permute-start | bytes 786440 | tf_op jit(solution)/shard_map/ppermute | solution.py:121
  779.7 68.9 %collective-permute-start.69 = (bf16[4,512,512]{2,1,0:T(8,128)(2,1)}, bf16[4,512,512]{2,1,0:T(8,128)(2,1)}, u32[]{:S(2)}, u32[]{:S(2)}) collective-permute-start(bf16[4,512,512]{2,1,0:T(8,128)(2,1)} %all-to-all-done.8), channel_id=1, source_target_pairs={{0,16},{16,0},{1,17},{17,1},{2,18},{18,2},{3,19},{19,3},{4,20},{20... | collective-permute-start | bytes 6291464 | tf_op jit(solution)/shard_map/ppermute | solution.py:108
  (141 other events, 2296.9 us)

commit v3 on v2

v3 whole, which is shorter than its diff:
```python
import functools

import jax
import jax.numpy as jnp
from jax import lax
from jax.experimental import pallas as pl
from jax.experimental.pallas import tpu as pltpu
from jax.sharding import Mesh
from jax.sharding import PartitionSpec as P

HEAD_DIM = 128
BLOCK = 512
HALF = 2

epsilon = 1e-05
rope_base = 10000.0
masked_score = -1e30
low = jnp.bfloat16
wide = jnp.float32


def rope_tables(places, head_depth):
    halfway = head_depth // 2
    position = places.astype(jnp.float32)[:, None]
    frequency = rope_base ** (-(2.0 * jnp.arange(halfway).astype(jnp.float32)) / head_depth)
    angles = position * frequency[None, :]
    cosine = jnp.concatenate([jnp.cos(angles), jnp.cos(angles)], axis=1)
    sine_table = jnp.concatenate([jnp.sin(angles), jnp.sin(angles)], axis=1)
    return (cosine, sine_table)


def dot(left, right):
    return jnp.dot(left, right, preferred_element_type=wide)


def dot_nt(left, right):
    return jnp.einsum("mk,nk->mn", left, right, preferred_element_type=wide)


def dot_tn(left, right):
    return jnp.einsum("km,kn->mn", left, right, preferred_element_type=wide)


def layer_norm(stream):
    average = jnp.mean(stream, axis=1, keepdims=True)
    centered = stream - average
    inverse = lax.rsqrt(jnp.mean(centered * centered, axis=1, keepdims=True) + epsilon)
    return centered * inverse, inverse


def norm_backward(normed, inverse, gradient):
    average = jnp.mean(gradient, axis=1, keepdims=True)
    crossed = jnp.mean(gradient * normed, axis=1, keepdims=True)
    return inverse * (gradient - average - normed * crossed)


def turn(array):
    return pltpu.roll(array, array.shape[1] // 2, 1)


def rope_sign(depth):
    return jnp.where(lax.broadcasted_iota(jnp.int32, (1, depth), 1) < depth // 2, -1.0, 1.0)


def attend_kernel(rows_ref, weight_ref, cosine_ref, sine_ref, column_ref, line_ref, qkv_ref, heads_ref, logsum_ref):
    depth = heads_ref.shape[1]
    qkv = dot(rows_ref[...], weight_ref[:, : 3 * depth])
    cosine, sine = cosine_ref[...], sine_ref[...] * rope_sign(depth)
    rope = lambda w: (w * cosine + turn(w) * sine).astype(low)
    queries, key_rows = rope(qkv[:, :depth]), rope(qkv[:, depth : 2 * depth])
    values = qkv[:, 2 * depth :].astype(low)
    qkv_ref[...] = jnp.concatenate([queries, key_rows, values], axis=1)
    for at in range(0, queries.shape[0], BLOCK):
        part = slice(at, at + BLOCK)
        scores = dot_last(queries[part], key_rows) * depth**-0.5
        scores = jnp.where(column_ref[part] >= line_ref[...], scores, masked_score)
        highest = jnp.max(scores, axis=1, keepdims=True)
        shifted = jnp.exp(scores - highest)
        totals = jnp.sum(shifted, axis=1, keepdims=True)
        logsum_ref[part] = highest + jnp.log(totals)
        weights = (shifted * (1.0 / totals)).astype(low)
        heads_ref[part] = dot(weights, values).astype(low)


def attend_back_kernel(
    middle_ref, weight_ref, cosine_ref, sine_ref, column_ref, line_ref, qkv_ref, logsum_ref, slope_ref
):
    depth = cosine_ref.shape[1]
    scaling = depth**-0.5
    queries, key_rows, values = (qkv_ref[:, i * depth : (i + 1) * depth] for i in range(3))
    head_grad = dot(middle_ref[...], weight_ref[:, 3 * depth :]).astype(low)
    query_parts = []
    key_grad = value_grad = None
    for at in range(0, queries.shape[0], BLOCK):
        part = slice(at, at + BLOCK)
        scores = dot_last(queries[part], key_rows) * scaling
        scores = jnp.where(column_ref[part] >= line_ref[...], scores, masked_score)
        probable = jnp.exp(scores - logsum_ref[part])
        product = dot_last(head_grad[part], values)
        slopes = probable * (product - jnp.sum(probable * product, axis=1, keepdims=True))
        slopes = slopes.astype(low)
        query_parts.append(dot(slopes, key_rows) * scaling)
        key_part = dot_first(slopes, queries[part]) * scaling
        value_part = dot_first(probable.astype(low), head_grad[part])
        key_grad = key_part if at == 0 else key_grad + key_part
        value_grad = value_part if at == 0 else value_grad + value_part
    cosine, sine = cosine_ref[...], sine_ref[...]
    undo = lambda g: (g * cosine - turn(g * sine) * rope_sign(depth)).astype(low)
    slope_ref[:, :depth] = undo(jnp.concatenate(query_parts, axis=0))
    slope_ref[:, depth : 2 * depth] = undo(key_grad)
    slope_ref[:, 2 * depth :] = value_grad.astype(low)


def project_kernel(columns, *refs):
    lefts, weights, out_ref = refs[: len(refs) // 2], refs[len(refs) // 2 : -1], refs[-1]
    out_ref[...] = sum(
        dot_last(left[...], weight[:, columns]) for left, weight in zip(lefts, weights)
    ).astype(low)


def assemble_kernel(x_ref, mine_ref, theirs_ref, query_ref, key_ref, value_ref, out_ref):
    line, block, depth = mine_ref.shape[0], mine_ref.shape[1], HEAD_DIM
    for i in range(line):
        for source, turned in ((mine_ref, x_ref[0]), (theirs_ref, 1 - x_ref[0])):
            place = pl.ds(pl.multiple_of((HALF * i + turned) * depth, depth), depth)
            for n, target in enumerate((query_ref, key_ref, value_ref)):
                target[:, place] = source[i, :, n * depth : (n + 1) * depth].astype(wide)
            out_ref[place, :] = source[i, :, 3 * depth :].astype(wide).T


def assemble(mine, theirs):
    line, block, _ = mine.shape
    shape = jax.ShapeDtypeStruct((block, block), wide)
    whole = pl.BlockSpec(memory_space=pltpu.VMEM)
    return pl.pallas_call(
        assemble_kernel,
        in_specs=[pl.BlockSpec(memory_space=pltpu.SMEM), whole, whole],
        out_specs=[whole] * 4,
        out_shape=[shape] * 4,
        name="assemble",
    )(lax.axis_index("x")[None].astype(jnp.int32), mine, theirs)


def call_whole(kernel, name, shapes, *arrays):
    whole = pl.BlockSpec(memory_space=pltpu.VMEM)
    return pl.pallas_call(
        kernel,
        in_specs=[whole] * len(arrays),
        out_specs=[whole] * len(shapes),
        out_shape=shapes,
        compiler_params=pltpu.CompilerParams(vmem_limit_bytes=48 * 1024 * 1024),
        cost_estimate=pl.CostEstimate(flops=1, transcendentals=0, bytes_accessed=1),
        name=name,
    )(*arrays)


def dot_last(left, right):
    return lax.dot_general(left, right, (((1,), (1,)), ((), ())), preferred_element_type=wide)


def dot_first(left, right):
    return lax.dot_general(left, right, (((0,), (0,)), ((), ())), preferred_element_type=wide)


def swap(array, axis):
    return lax.ppermute(array, axis, [(0, 1), (1, 0)])


class Ring:
    def __init__(self, axes, line):
        self.axes = axes
        self.size = 2 * line
        self.half = line
        flat = [2 * n if n < line else 2 * (2 * line - 1 - n) + 1 for n in range(self.size)]
        self.upward = [(flat[i], flat[(i + 1) % self.size]) for i in range(self.size)]
        self.downward = [(b, a) for a, b in self.upward]

    def up(self, array):
        return lax.ppermute(array, self.axes, self.upward)

    def down(self, array):
        return lax.ppermute(array, self.axes, self.downward)

    def place(self):
        level, side = lax.axis_index(self.axes[:-1]), lax.axis_index(self.axes[-1])
        return jnp.where(side == 0, level, self.size - 1 - level)

    def gather(self, shard, waits={}):
        half, cut = self.half, shard.shape[0] // 2
        slots = [None] * self.size
        slots[half] = rising = falling = shard
        for step in range(1, half + 1):
            rising, falling = after((rising, falling), waits.get(step))
            if step == half:
                break
            slots[half - step] = rising = self.up(rising)
            slots[half + step] = falling = self.down(falling)
        slots[0] = jnp.concatenate([self.up(rising[:cut]), self.down(falling[cut:])], axis=0)
        return slots

    def scatter(self, parts, waits={}):
        half, cut = self.half, parts[0].shape[0] // 2
        rising, falling = self.up(parts[0][:cut]), self.down(parts[0][cut:])
        for step in range(1, half):
            over, under = parts[self.size - step], parts[step]
            if step == 1:
                over = jnp.concatenate([add_low(over[:cut], rising), over[cut:]], axis=0)
                under = jnp.concatenate([under[:cut], add_low(under[cut:], falling)], axis=0)
            else:
                over, under = add_low(over, rising), add_low(under, falling)
            over, under = after((over, under), waits.get(step))
            rising, falling = self.up(over), self.down(under)
        return parts[half].astype(wide) + rising.astype(wide) + falling.astype(wide)


def add_low(left, right):
    return (left.astype(wide) + right.astype(wide)).astype(low)


def split_rows(array, count):
    rows = array.shape[0] // count
    return [array[i * rows : (i + 1) * rows] for i in range(count)]


def gather_group(ring, shard, waits={}):
    slots = ring.gather(shard, waits)
    return jnp.concatenate(slots + [swap(slot, "core") for slot in slots], axis=0)


def scatter_group(ring, partial, waits={}):
    own, other = split_rows(partial, HALF)
    return ring.scatter(split_rows(add_low(own, swap(other, "core")), ring.size), waits)


def exchange_rows(array):
    return lax.all_to_all(array, ROW, 0, 0, tiled=True)


ROW = ("zhi", "zlo")


def to_shards(*arrays):
    rows = lax.axis_size(ROW)
    seqs, tokens, width = arrays[0].shape
    pieces = [array.reshape(rows, seqs * tokens // rows, width) for array in arrays]
    got = jnp.transpose(exchange_rows(jnp.concatenate(pieces, axis=1)), (1, 0, 2))
    return split_rows(got.reshape(-1, rows * width), len(arrays))


def from_shards(arrays, seqs):
    rows, count = lax.axis_size(ROW), len(arrays)
    tokens, width = arrays[0].shape[0], arrays[0].shape[1] // rows
    stacked = jnp.concatenate(arrays, axis=0).reshape(count * tokens, rows, width)
    got = exchange_rows(jnp.transpose(stacked, (1, 0, 2)))
    return [
        got[:, i * tokens : (i + 1) * tokens].reshape(seqs, rows * tokens // seqs, width)
        for i in range(count)
    ]


def after(arrays, others):
    if others is None:
        return arrays
    return lax.optimization_barrier((arrays, others))[0]


def choose(first, second):
    return jnp.where(lax.axis_index("x") == 0, first, second)


def spread(pieces):
    mine = exchange_rows(pieces)
    return [mine, swap(mine, "x")]


def sum_pair(mine, theirs):
    total = add_low(mine, swap(theirs, "x"))
    if lax.axis_size("pair") > 1:
        total = lax.psum(total, "pair")
    return total


def in_order(mine):
    theirs = swap(mine, "x")
    return choose(mine, theirs), choose(theirs, mine)


def by_block(array, count):
    return jnp.transpose(array.reshape(array.shape[0], count, -1), (1, 0, 2))


def from_block(array):
    return jnp.transpose(array, (1, 0, 2)).reshape(array.shape[1], -1)


def pack_kernel(x_ref, query, key, value, out, gate, up, down, head, gu, down_out):
    head[0] = jnp.concatenate([query[...], key[...], value[...], out[...].T], axis=1)
    gu[0] = jnp.concatenate([gate[...], up[...]], axis=1)
    down_out[0] = down[...]


def pack(query, key, value, out, gate, up, down, rows, line):
    depth, block = HEAD_DIM, query.shape[0]
    units = gate.shape[1] // rows // HALF
    head_at = lambda r, x: HALF * (r % line) + x[0]
    head_in = pl.BlockSpec((block, depth), lambda r, x: (0, head_at(r, x)))
    out_in = pl.BlockSpec((depth, block), lambda r, x: (head_at(r, x), 0))
    unit_in = pl.BlockSpec((block, units), lambda r, x: (0, HALF * r + x[0]))
    down_in = pl.BlockSpec((units, block), lambda r, x: (HALF * r + x[0], 0))
    shapes = [(block, 4 * depth), (block, 2 * units), (units, block)]
    return pl.pallas_call(
        pack_kernel,
        grid_spec=pltpu.PrefetchScalarGridSpec(
            num_scalar_prefetch=1,
            grid=(rows,),
            in_specs=[head_in, head_in, head_in, out_in, unit_in, unit_in, down_in],
            out_specs=[pl.BlockSpec((1,) + shape, lambda r, x: (r, 0, 0)) for shape in shapes],
        ),
        out_shape=[jax.ShapeDtypeStruct((rows,) + shape, low) for shape in shapes],
        name="pack_weights",
    )(lax.axis_index("x")[None].astype(jnp.int32), query, key, value, out, gate, up, down)


def mlp_kernel(blocks, rows_ref, slope_ref, *refs):
    weights, downs = refs[:blocks], refs[blocks : 2 * blocks]
    hidden_ref, gu_slope_ref, grad_ref = refs[2 * blocks :]
    parts, units, span = downs[0].shape
    rows = rows_ref[...]
    total = None
    for i in range(blocks):
        weight = weights[i][...]
        gate_up = dot(rows, weight)
        gate, up = gate_up[:, :units], gate_up[:, units:]
        sigmoid = 1.0 / (1.0 + jnp.exp(-gate))
        activated = gate * sigmoid
        hidden_ref[:, i * units : (i + 1) * units] = (activated * up).astype(low)
        hidden_grad = sum(
            dot_last(slope_ref[:, k * span : (k + 1) * span], downs[i][k]) for k in range(parts)
        )
        gate_slope = hidden_grad * up * sigmoid * (1.0 + gate * (1.0 - sigmoid))
        gu_slope = jnp.concatenate([gate_slope, hidden_grad * activated], axis=1).astype(low)
        gu_slope_ref[:, 2 * i * units : 2 * (i + 1) * units] = gu_slope
        part = dot_last(gu_slope, weight)
        total = part if total is None else total + part
    grad_ref[...] = total.astype(low)


def down_kernel(place_ref, hidden_ref, *refs):
    downs, out_ref = refs[:-1], refs[-1]
    parts, units, span = downs[0].shape
    for k in range(parts):
        out_ref[0, 0, :, k * span : (k + 1) * span] = sum(
            dot(hidden_ref[:, i * units : (i + 1) * units], down[k]) for i, down in enumerate(downs)
        ).astype(low)


def down_project(ring, hidden, downs, width):
    tile = hidden.shape[0] // ring.size

    def target(i, place):
        spot = (place[0] + i + ring.half) % ring.size
        side = spot // ring.half
        row = jnp.where(side == 0, spot, ring.size - 1 - spot)
        return (jnp.where(side == place[0] // ring.half, 0, 1), row, 0, 0)

    whole = lambda array: pl.BlockSpec(
        array.shape, lambda i, place: (0, 0, 0), pipeline_mode=pl.Buffered(buffer_count=1)
    )
    return pl.pallas_call(
        down_kernel,
        grid_spec=pltpu.PrefetchScalarGridSpec(
            num_scalar_prefetch=1,
            grid=(ring.size,),
            in_specs=[pl.BlockSpec((tile, hidden.shape[1]), lambda i, place: (i, 0))]
            + [whole(down) for down in downs],
            out_specs=pl.BlockSpec((1, 1, tile, width), target),
        ),
        out_shape=jax.ShapeDtypeStruct((HALF, ring.half, tile, width), low),
        compiler_params=pltpu.CompilerParams(vmem_limit_bytes=48 * 1024 * 1024),
        name="down_project",
    )(ring.place()[None].astype(jnp.int32), hidden, *downs)


def call_rows(kernel, name, arrays, held, sizes, tile=256):
    count = arrays[0].shape[0]
    row_block = lambda columns: pl.BlockSpec((tile, columns), lambda i: (i, 0))
    whole = lambda array: pl.BlockSpec(
        array.shape, lambda i: (0,) * array.ndim, pipeline_mode=pl.Buffered(buffer_count=1)
    )
    return pl.pallas_call(
        kernel,
        grid=(count // tile,),
        in_specs=[row_block(array.shape[1]) for array in arrays] + [whole(array) for array in held],
        out_specs=[row_block(size) for size in sizes],
        out_shape=[jax.ShapeDtypeStruct((count, size), low) for size in sizes],
        compiler_params=pltpu.CompilerParams(vmem_limit_bytes=48 * 1024 * 1024),
        name=name,
    )(*arrays, *held)


def on_device(
    tokens,
    query_weight,
    key_weight,
    value_weight,
    out_weight,
    gate_weight,
    up_weight,
    down_weight,
    cotangent,
):
    depth = HEAD_DIM
    rows, line = lax.axis_size(ROW), lax.axis_size("zlo")
    small_ring = Ring(("zlo", "y"), line)
    large_ring = Ring(("zhi", "zlo", "y"), rows)
    seqs, width = tokens.shape[0], tokens.shape[2] * rows
    block = width // rows
    units = gate_weight.shape[1] // rows // HALF
    flat = lambda got: got.reshape(width, got.shape[2])

    heads_weight, gu_pieces, down_pieces = pack(
        query_weight, key_weight, value_weight, out_weight, gate_weight, up_weight, down_weight, rows, line
    )
    stream_low, slope_low = to_shards(tokens, cotangent)
    stream = stream_low.astype(wide)
    shard = stream.shape[0]
    heads_weight = [flat(got) for got in spread(after(heads_weight, stream_low))]

    place = jnp.arange(2 * small_ring.size)
    core = (lax.axis_index("core") + place // small_ring.size) % 2
    spot = (small_ring.place() + place % small_ring.size + small_ring.half) % small_ring.size
    slot_side = spot // line
    slot_level = jnp.where(slot_side == 0, spot, small_ring.size - 1 - spot)
    first = ((2 * slot_side + core) * line + slot_level) * shard
    places = (first[:, None] + jnp.arange(shard)[None, :]).reshape(-1)
    cosine, sine_table = rope_tables(places, depth)

    normed_one, inverse_one = layer_norm(stream)
    rows_one = gather_group(small_ring, normed_one.astype(low))
    slope_slots = large_ring.gather(after(slope_low, (heads_weight[0], rows_one)), {4: heads_weight[1]})
    slope_all = jnp.concatenate(slope_slots, axis=0)

    gu_weight = [flat(got) for got in spread(after(gu_pieces, heads_weight[0]))]
    down = spread(after(down_pieces, gu_weight[0]))

    rows_one = after(rows_one, slope_slots[2:7])
    length = rows_one.shape[0]
    seen = (cosine, sine_table, places[:, None], places[None, :])
    qkv_shape = jax.ShapeDtypeStruct((length, 3 * depth), low)
    kept = []
    for weight in heads_weight:
        shapes = [qkv_shape, jax.ShapeDtypeStruct((length, depth), low), jax.ShapeDtypeStruct((length, 1), wide)]
        kept.append(call_whole(attend_kernel, "attend", shapes, rows_one, weight, *seen))
    heads = after([part[1] for part in kept], (slope_slots[1], slope_slots[7]))
    project = functools.partial(project_kernel, slice(3 * depth, 4 * depth))
    (out_part,) = call_rows(project, "out_project", heads, heads_weight, (width,))
    middle = stream + scatter_group(small_ring, out_part)
    normed_two, inverse_two = layer_norm(after(middle, (slope_slots[0], gu_weight[0])))
    waits = {2: down[0], 3: gu_weight[1]}
    rows_two = jnp.concatenate(large_ring.gather(normed_two.astype(low), waits), axis=0)
    gu_weight += [swap(part, "core") for part in gu_weight]
    down += [swap(part, "core") for part in down]

    sizes = (4 * units, 8 * units, width)
    hidden_low, gu_slope, grad_part = call_rows(
        functools.partial(mlp_kernel, len(down)), "feed_forward", [rows_two, slope_all], gu_weight + down, sizes
    )
    gu_own = dot_tn(rows_two, gu_slope[:, : 4 * units])
    gu_other = dot_tn(rows_two, gu_slope[:, 4 * units :]).astype(low)
    gu_total = add_low(gu_own, swap(gu_other, "core"))
    gu_sum = sum_pair(gu_total[:, : 2 * units], gu_total[:, 2 * units :])

    grad_two = large_ring.scatter(split_rows(grad_part, large_ring.size), {2: gu_total})
    middle_grad = slope_low.astype(wide) + norm_backward(normed_two, inverse_two, grad_two)
    middle_all = gather_group(small_ring, middle_grad.astype(low), {2: gu_sum})

    late_hidden, late_slope = after((hidden_low, slope_all), grad_two)
    down_own = dot_tn(late_hidden[:, : 2 * units], late_slope)
    down_other = dot_tn(late_hidden[:, 2 * units :], late_slope).astype(low)
    down_total = add_low(down_own, swap(down_other, "core"))
    down_sum = sum_pair(down_total[:units], down_total[units:])
    branch_part = down_project(large_ring, late_hidden, down, width)
    branch_half = add_low(branch_part[0], swap(branch_part[1], "y"))
    gu_got = exchange_rows(gu_sum.reshape(rows, block, 2 * units))
    down_got = exchange_rows(by_block(after(down_sum, gu_got), rows))
    branch_got = exchange_rows(after(branch_half, down_got))

    head_slopes, head_sums = [None] * HALF, [None] * HALF
    for head in reversed(range(HALF)):
        qkv, attended, logsums = kept[head]
        (slope,) = call_whole(
            attend_back_kernel, "attend_back", [qkv_shape], middle_all, heads_weight[head], *seen, qkv, logsums
        )
        sums = [dot_tn(rows_one, slope), dot_tn(middle_all, attended)]
        head_slopes[head] = slope
        head_sums[head] = jnp.concatenate(sums, axis=1).astype(low)
    project = functools.partial(project_kernel, slice(0, 3 * depth))
    (grad_part,) = call_rows(project, "qkv_back", head_slopes, heads_weight, (width,))
    grad_one = scatter_group(small_ring, grad_part, {1: branch_half})
    input_low = (middle_grad + norm_backward(normed_one, inverse_one, grad_one)).astype(low)
    head_total = sum_pair(*head_sums).reshape(rows, block, 4 * depth)
    head_got = exchange_rows(after(head_total, branch_got)).reshape(rows // line, line, block, 4 * depth)
    head_mine = jnp.sum(head_got.astype(wide), axis=0).astype(low)
    query_grad, key_grad, value_grad, out_grad = assemble(head_mine, swap(head_mine, "x"))
    branch = jnp.sum(branch_got.astype(wide), axis=0)
    output_low = (middle + branch).astype(low)
    layer_out, input_grad = from_shards(after((output_low, input_low), head_got), seqs)
    input_grad = input_grad.astype(wide)

    def unit_columns(first, second):
        parts = [part[i] for i in range(rows) for part in (first, second)]
        return jnp.concatenate(parts, axis=1).astype(wide)

    gu_grads = in_order(gu_got)
    gate_grad = unit_columns(*(part[:, :, :units] for part in gu_grads))
    up_grad = unit_columns(*(part[:, :, units:] for part in gu_grads))
    down_grad = jnp.stack(in_order(down_got), axis=1).reshape(-1, block).astype(wide)

    return (
        layer_out,
        input_grad,
        query_grad,
        key_grad,
        value_grad,
        out_grad,
        gate_grad,
        up_grad,
        down_grad,
    )


def solution(mesh):
    dp, rows, cols = (mesh.shape[name] for name in ("dp", "row", "col"))
    sizes = (dp // HALF, HALF, HALF, rows // HALF, cols // HALF, HALF)
    fine = Mesh(mesh.devices.reshape(sizes), ("pair", "x", "zhi", "zlo", "y", "core"))
    across, inner, tall = ("pair", "x"), ("y", "core"), ROW
    split = P(across, inner, tall)
    inward = P(tall, inner)
    outward = P(inner, tall)
    return jax.shard_map(
        on_device,
        mesh=fine,
        in_specs=(split, inward, inward, inward, outward, inward, inward, outward, split),
        out_specs=(split, split, inward, inward, inward, outward, inward, inward, outward),
        check_vma=False,
    )
```

time: 888 us -> 735 us (0.83)
  Pallas kernels: 0 us -> 96.6 us
  local copies, waits for them, and re-layouts: 161 us -> 77.5 us
  matrix products: 117 us -> 35.2 us
  waiting for transfers between devices: 410 us -> 339 us
  other arithmetic: 56.3 us -> 75.7 us
  blocking collectives: 19.3 us -> 0 us
  starting transfers between devices: 116 us -> 98.4 us
    ppermute x25 -> x26, waiting for transfers between devices: 144 us -> 40.3 us  [swap(): return lax.ppermute(array, axis, [(0, 1), (1, 0)])]
    pallas_call x0 -> x10, Pallas kernels: none -> 96.6 us  [the longest x3 45 us: call_rows(): pl.pallas_call(kernel, grid=(count // tile,), in_specs=[row_block(array.s...]
    dot_general x26 -> x0, matrix products: 78.9 us -> none  [the longest x13 40.1 us: dot(): return jnp.dot(left, right, preferred_element_type=wide)]
    all_to_all x9, waiting for transfers between devices: 21.3 us -> 70.7 us  [exchange_rows(): return lax.all_to_all(array, ROW, 0, 0, tiled=True)]
    slice x12 -> x5, local copies, waits for them, and re-layouts: 41.6 us -> 4.91 us  [the longest x1 2.06 us: from_shards(): got[:, i * tokens:(i + 1) * tokens]]
    ppermute x24 -> x20, waiting for transfers between devices: 52.8 us -> 29.9 us  [down(): return lax.ppermute(array, self.axes, self.downward)]
    reshape x7 -> x3, local copies, waits for them, and re-layouts: 28.3 us -> 6.78 us  [the longest x1 4.67 us: on_device(): head_total = sum_pair(*head_sums).reshape(rows, block, 4 * depth)]
    transpose x4 -> x0, local copies, waits for them, and re-layouts: 20.5 us -> none  [the longest x3 15.3 us: unit_columns(): return jnp.transpose(grad, (1, 0, 2, 3)).reshape(block, -1)]
  transfers between devices with their start and end apart: 82 -> 75, of which waited for: 35 -> 37; matrix products, arithmetic and copies ran while one was open for 28% -> 22% of each run, Pallas kernels for 0% -> 8%
where the time goes in v3:
time: 735 us; the launch traced here: 725 us
  waiting for transfers between devices  339 us (46%)
  starting transfers between devices  98.4 us (13%)
  Pallas kernels  96.6 us (13%)
  local copies, waits for them, and re-layouts  77.5 us (11%)
  other arithmetic  75.7 us (10%)
  matrix products  35.2 us (5%)
    ppermute x20, waiting for transfers between devices, up(): return lax.ppermute(array, self.axes, self.upward)  198 us
    all_to_all x9, waiting for transfers between devices, exchange_rows(): return lax.all_to_all(array, ROW, 0, 0, tiled=True)  70.7 us
    pallas_call x3, Pallas kernels, call_rows(): pl.pallas_call(kernel, grid=(count // tile,), in_specs=[row_block(array.s...  45 us
    unnamed x146, local copies, waits for them, and re-layouts  42.9 us
    ppermute x26, waiting for transfers between devices, swap(): return lax.ppermute(array, axis, [(0, 1), (1, 0)])  40.3 us
    all_to_all x9, starting transfers between devices, exchange_rows(): return lax.all_to_all(array, ROW, 0, 0, tiled=True)  40.3 us
    dot_general x8, matrix products, dot_tn(): return jnp.einsum('km,kn->mn', left, right, preferred_element_type=wide)  35.2 us
    pallas_call x4, Pallas kernels, call_whole(): pl.pallas_call(kernel, in_specs=[whole] * len(arrays), out_specs=[whole]...  32.8 us
  transfers between devices with their start and end apart: 75, of which 37 were waited for; matrix products, arithmetic and copies ran while one was open for 22% of the time, Pallas kernels for 8%

profile of v3, /device:TPU:0, one launch (start us, length us, event | category | flops | bytes accessed | tf_op | source)
XLA Modules:
  0.0 724.6 jit_solution(8086708929445442658)
XLA Ops:
  14.5 20.5 %all-to-all-done = bf16[4,256,512]{2,1,0:T(8,128)(2,1)S(1)} async-done(((bf16[4,256,512]{2,1,0:T(8,128)(2,1)}), bf16[4,256,512]{2,1,0:T(8,128)(2,1)S(1)}, u32[]{:S(2)}, u32[]{:S(2)}) %all-to-all-start) | async-done | bytes 1048608 | tf_op jit(solution)/shard_map/all_to_all | solution.py:236
  43.1 41.6 %collective-permute-done = bf16[128,2048]{1,0:T(8,128)(2,1)S(1)} collective-permute-done((bf16[128,2048]{1,0:T(8,128)(2,1)}, bf16[128,2048]{1,0:T(8,128)(2,1)S(1)}, u32[]{:S(2)}, u32[]{:S(2)}) %collective-permute-start) | collective-permute-done | bytes 524320 | tf_op jit(solution)/shard_map/ppermute | solution.py:179
  108.9 12.1 %collective-permute-done.8 = bf16[128,2048]{1,0:T(8,128)(2,1)} collective-permute-done((bf16[128,2048]{1,0:T(8,128)(2,1)S(1)}, bf16[128,2048]{1,0:T(8,128)(2,1)}, u32[]{:S(2)}, u32[]{:S(2)}) %collective-permute-start.8) | collective-permute-done | bytes 524320 | tf_op jit(solution)/shard_map/ppermute | solution.py:179
  123.1 11.5 %collective-permute-done.9 = bf16[128,2048]{1,0:T(8,128)(2,1)} collective-permute-done((bf16[128,2048]{1,0:T(8,128)(2,1)}, bf16[128,2048]{1,0:T(8,128)(2,1)}, u32[]{:S(2)}, u32[]{:S(2)}) %collective-permute-start.9) | collective-permute-done | bytes 524320 | tf_op jit(solution)/shard_map/ppermute | solution.py:179
  139.7 7.3 %attend.2 = (bf16[1024,384]{1,0:T(8,128)(2,1)S(1)}, bf16[1024,128]{1,0:T(8,128)(2,1)S(1)}, f32[1024,1]{1,0:T(8,128)S(1)}) custom-call(bf16[1024,2048]{1,0:T(8,128)(2,1)} %constant_dynamic-update-slice_fusion.rows_ref, bf16[2048,512]{1,0:T(8,128)(2,1)S(1)} %bitcast.134, f32[1024,128]{1,0:T(8,128)S(1)} %get-tuple-element.152.cosine_ref, ...), custom_call_target="tpu_custom_call" | custom-call | flops 1 | bytes 1 | tf_op jit(solution)/shard_map/attend/pallas_call | solution.py:146
  149.8 7.8 %attend.3 = (bf16[1024,384]{1,0:T(8,128)(2,1)S(1)}, bf16[1024,128]{1,0:T(8,128)(2,1)S(1)}, f32[1024,1]{1,0:T(8,128)S(1)}) custom-call(bf16[1024,2048]{1,0:T(8,128)(2,1)} %constant_dynamic-update-slice_fusion.rows_ref, bf16[2048,512]{1,0:T(8,128)(2,1)} %bitcast.8.weight_ref.refs_3_, f32[1024,128]{1,0:T(8,128)S(1)} %get-tuple-element.152.cosine_ref, ...), custom_call_target="tpu_custom_call" | custom-call | flops 1 | bytes 1 | tf_op jit(solution)/shard_map/attend/pallas_call | solution.py:146
  177.5 35.3 %collective-permute-done.16 = bf16[64,2048]{1,0:T(8,128)(2,1)S(1)} collective-permute-done((bf16[64,2048]{1,0:T(8,128)(2,1)S(1)}, bf16[64,2048]{1,0:T(8,128)(2,1)S(1)}, u32[]{:S(2)}, u32[]{:S(2)}) %collective-permute-start.16) | collective-permute-done | bytes 262176 | tf_op jit(solution)/shard_map/ppermute | solution.py:179
  228.8 8.7 %collective-permute-done.19 = bf16[128,2048]{1,0:T(8,128)(2,1)} collective-permute-done((bf16[128,2048]{1,0:T(8,128)(2,1)}, bf16[128,2048]{1,0:T(8,128)(2,1)}, u32[]{:S(2)}, u32[]{:S(2)}) %collective-permute-start.19) | collective-permute-done | bytes 524320 | tf_op jit(solution)/shard_map/ppermute | solution.py:182
  252.7 13.1 %collective-permute-done.29 = bf16[64,2048]{1,0:T(8,128)(2,1)S(1)} collective-permute-done((bf16[64,2048]{1,0:T(8,128)(2,1)S(1)}, bf16[64,2048]{1,0:T(8,128)(2,1)S(1)}, u32[]{:S(2)}, u32[]{:S(2)}) %collective-permute-start.29) | collective-permute-done | bytes 262176 | tf_op jit(solution)/shard_map/ppermute | solution.py:179
  313.4 31.3 %feed_forward.1 = (bf16[1024,1024]{1,0:T(8,128)(2,1)}, bf16[1024,2048]{1,0:T(8,128)(2,1)}, bf16[1024,2048]{1,0:T(8,128)(2,1)}) custom-call(bf16[1024,2048]{1,0:T(8,128)(2,1)} %copy-done.36, bf16[1024,2048]{1,0:T(8,128)(2,1)} %constant_dynamic-update-slice_fusion.18.slope_ref, bf16[2048,512]{1,0:T(8,128)(2,1)} %bitcast.10.refs_0_, ...), custom_call_target="tpu_custom_call" | custom-call | tf_op jit(solution)/shard_map/feed_forward/pallas_call | solution.py:390
  344.6 7.6 %convolution_convert_fusion = bf16[2048,1024]{1,0:T(8,128)(2,1)S(1)} fusion(bf16[1024,2048]{1,0:T(8,128)(2,1)} %copy-done.36, bf16[1024,2048]{1,0:T(8,128)(2,1)} %get-tuple-element.73), kind=kOutput, calls=%fused_computation.9 | convolution fusion | flops 4297064448 | bytes 10485760 | tf_op jit(solution)/shard_map/km,kn->mn/dot_general | solution.py:41
  363.8 11.0 %collective-permute-done.37 = bf16[128,2048]{1,0:T(8,128)(2,1)S(1)} collective-permute-done((bf16[128,2048]{1,0:T(8,128)(2,1)S(1)}, bf16[128,2048]{1,0:T(8,128)(2,1)S(1)}, u32[]{:S(2)}, u32[]{:S(2)}) %collective-permute-start.37) | collective-permute-done | bytes 524320 | tf_op jit(solution)/shard_map/ppermute | solution.py:179
  382.7 10.2 %collective-permute-done.41 = bf16[128,2048]{1,0:T(8,128)(2,1)S(1)} collective-permute-done((bf16[128,2048]{1,0:T(8,128)(2,1)S(1)}, bf16[128,2048]{1,0:T(8,128)(2,1)S(1)}, u32[]{:S(2)}, u32[]{:S(2)}) %collective-permute-start.41) | collective-permute-done | bytes 524320 | tf_op jit(solution)/shard_map/ppermute | solution.py:179
  400.4 6.7 collective-permute-done.42
  419.5 9.7 %down_project.1 = bf16[2,4,128,2048]{3,2,1,0:T(8,128)(2,1)} custom-call(s32[1]{0:T(128)} %bitcast.9.place_ref, bf16[1024,1024]{1,0:T(8,128)(2,1)} %get-tuple-element.76.hidden_ref, bf16[4,256,512]{2,1,0:T(8,128)(2,1)} %all-to-all-done.3.refs_4_.refs_0_, bf16[4,256,512]{2,1,0:T(8,128)(2,1)S(1)} %copy-done.3, bf16[4,256,512]{2,1,0:T(8,128)(2,1)S(1)} %copy-done.5, ...), custom_call_target="tpu_custom_call" | custom-call | tf_op jit(solution)/shard_map/down_project/pallas_call | solution.py:369
  429.1 14.7 %collective-permute-done.48 = bf16[2048,512]{1,0:T(8,128)(2,1)} collective-permute-done((bf16[2048,512]{1,0:T(8,128)(2,1)}, bf16[2048,512]{1,0:T(8,128)(2,1)}, u32[]{:S(2)}, u32[]{:S(2)}) %collective-permute-start.48) | collective-permute-done | bytes 2097184 | tf_op jit(solution)/shard_map/ppermute | solution.py:166
  457.6 8.4 %collective-permute-done.52 = bf16[64,2048]{1,0:T(8,128)(2,1)} collective-permute-done((bf16[64,2048]{1,0:T(8,128)(2,1)}, bf16[64,2048]{1,0:T(8,128)(2,1)}, u32[]{:S(2)}, u32[]{:S(2)}) %collective-permute-start.52) | collective-permute-done | bytes 262176 | tf_op jit(solution)/shard_map/ppermute | solution.py:182
  483.3 8.4 %attend_back.2.refs_0_ = bf16[1024,384]{1,0:T(8,128)(2,1)S(1)} custom-call(bf16[1024,2048]{1,0:T(8,128)(2,1)} %copy-done.27, bf16[2048,512]{1,0:T(8,128)(2,1)S(1)} %bitcast.136, f32[1024,128]{1,0:T(8,128)S(1)} %get-tuple-element.152.cosine_ref, f32[1024,128]{1,0:T(8,128)S(1)} %copy-done.1, s32[1024,1]{1,0:T(8,128)S(1)} %copy.46.column_ref, ...), custom_call_target="tpu_custom_call" | custom-call | flops 1 | bytes 1 | tf_op jit(solution)/shard_map/attend_back/pallas_call | solution.py:146
  491.7 9.4 %attend_back.3.refs_1_ = bf16[1024,384]{1,0:T(8,128)(2,1)S(1)} custom-call(bf16[1024,2048]{1,0:T(8,128)(2,1)} %copy-done.27, bf16[2048,512]{1,0:T(8,128)(2,1)} %bitcast.8.weight_ref.refs_3_, f32[1024,128]{1,0:T(8,128)S(1)} %get-tuple-element.152.cosine_ref, f32[1024,128]{1,0:T(8,128)S(1)} %copy-done.1, s32[1024,1]{1,0:T(8,128)S(1)} %copy.46.column_ref, ...), custom_call_target="tpu_custom_call" | custom-call | flops 1 | bytes 1 | tf_op jit(solution)/shard_map/attend_back/pallas_call | solution.py:146
  501.2 7.8 %qkv_back.1 = bf16[1024,2048]{1,0:T(8,128)(2,1)} custom-call(bf16[1024,384]{1,0:T(8,128)(2,1)S(1)} %attend_back.2.refs_0_, bf16[1024,384]{1,0:T(8,128)(2,1)S(1)} %attend_back.3.refs_1_, bf16[2048,512]{1,0:T(8,128)(2,1)S(1)} %bitcast.137, bf16[2048,512]{1,0:T(8,128)(2,1)} %bitcast.8.weight_ref.refs_3_), custom_call_target="tpu_custom_call" | custom-call | tf_op jit(solution)/shard_map/qkv_back/pallas_call | solution.py:390
  539.4 10.8 %all-to-all-done.5 = bf16[4,256,512]{2,1,0:T(8,128)(2,1)S(1)} async-done(((bf16[4,256,512]{2,1,0:T(8,128)(2,1)}), bf16[4,256,512]{2,1,0:T(8,128)(2,1)S(1)}, u32[]{:S(2)}, u32[]{:S(2)}) %all-to-all-start.5) | async-done | bytes 1048608 | tf_op jit(solution)/shard_map/all_to_all | solution.py:236
  561.5 32.9 %collective-permute-done.58 = bf16[64,2048]{1,0:T(8,128)(2,1)S(1)} collective-permute-done((bf16[64,2048]{1,0:T(8,128)(2,1)S(1)}, bf16[64,2048]{1,0:T(8,128)(2,1)S(1)}, u32[]{:S(2)}, u32[]{:S(2)}) %collective-permute-start.58) | collective-permute-done | bytes 262176 | tf_op jit(solution)/shard_map/ppermute | solution.py:179
  637.6 34.9 %all-to-all-done.7 = bf16[4,512,512]{1,2,0:T(8,128)(2,1)} async-done(((bf16[4,512,512]{1,2,0:T(8,128)(2,1)}), bf16[4,512,512]{1,2,0:T(8,128)(2,1)}, u32[]{:S(2)}, u32[]{:S(2)}) %all-to-all-start.7) | async-done | bytes 2097184 | tf_op jit(solution)/shard_map/all_to_all | solution.py:236
  697.9 19.5 %collective-permute-done.63.theirs_ref = bf16[2,512,512]{2,1,0:T(8,128)(2,1)} collective-permute-done((bf16[2,512,512]{2,1,0:T(8,128)(2,1)S(1)}, bf16[2,512,512]{2,1,0:T(8,128)(2,1)}, u32[]{:S(2)}, u32[]{:S(2)}) %collective-permute-start.63) | collective-permute-done | bytes 1048608 | tf_op jit(solution)/shard_map/ppermute | solution.py:166
  (378 shorter events, 341.8 us)
Async XLA Ops:
  36.3 65.3 %all-to-all-start.1 = ((bf16[4,512,512]{2,1,0:T(8,128)(2,1)}), bf16[4,512,512]{2,1,0:T(8,128)(2,1)S(1)}, u32[]{:S(2)}, u32[]{:S(2)}) async-start(bf16[4,512,512]{2,1,0:T(8,128)(2,1)} %get-tuple-element.53), calls=%async_computation.1 | async-start | bytes 4194304 | tf_op jit(solution)/shard_map/all_to_all | solution.py:236
  41.1 43.6 %collective-permute-start = (bf16[128,2048]{1,0:T(8,128)(2,1)}, bf16[128,2048]{1,0:T(8,128)(2,1)S(1)}, u32[]{:S(2)}, u32[]{:S(2)}) collective-permute-start(bf16[128,2048]{1,0:T(8,128)(2,1)} %fusion.6), channel_id=1, source_target_pairs={{0,4},{4,6},{6,2},{2,0},{1,5},{5,7},{7,3},{3,1},{8,12},{12,14},{14... | collective-permute-start | bytes 1572872 | tf_op jit(solution)/shard_map/ppermute | solution.py:179
  43.0 44.1 %collective-permute-start.2 = (bf16[128,2048]{1,0:T(8,128)(2,1)}, bf16[128,2048]{1,0:T(8,128)(2,1)}, u32[]{:S(2)}, u32[]{:S(2)}) collective-permute-start(bf16[128,2048]{1,0:T(8,128)(2,1)} %fusion.6), channel_id=1, source_target_pairs={{4,0},{6,4},{2,6},{0,2},{5,1},{7,5},{3,7},{1,3},{12,8},{14,12},{10... | collective-permute-start | bytes 1572872 | tf_op jit(solution)/shard_map/ppermute | solution.py:182
  101.6 48.1 %collective-permute-start.12 = (bf16[4,512,512]{2,1,0:T(8,128)(2,1)S(1)}, bf16[4,512,512]{2,1,0:T(8,128)(2,1)}, u32[]{:S(2)}, u32[]{:S(2)}) collective-permute-start(bf16[4,512,512]{2,1,0:T(8,128)(2,1)S(1)} %all-to-all-done.1), channel_id=1, source_target_pairs={{0,16},{16,0},{1,17},{17,1},{2,18},{18,2},{3,19},{19,3},{4,20},{20... | collective-permute-start | bytes 6291464 | tf_op jit(solution)/shard_map/ppermute | solution.py:166
  167.6 53.9 %all-to-all-start.2 = ((bf16[4,512,512]{2,1,0:T(8,128)(2,1)}), bf16[4,512,512]{2,1,0:T(8,128)(2,1)}, u32[]{:S(2)}, u32[]{:S(2)}) async-start(bf16[4,512,512]{2,1,0:T(8,128)(2,1)} %get-tuple-element.61), calls=%async_computation.2 | async-start | bytes 4194304 | tf_op jit(solution)/shard_map/all_to_all | solution.py:236
  175.4 37.3 %collective-permute-start.16 = (bf16[64,2048]{1,0:T(8,128)(2,1)S(1)}, bf16[64,2048]{1,0:T(8,128)(2,1)S(1)}, u32[]{:S(2)}, u32[]{:S(2)}) collective-permute-start(bf16[64,2048]{1,0:T(8,128)(2,1)S(1)} %get-tuple-element.140), channel_id=1, source_target_pairs={{0,4},{4,6},{6,2},{2,0},{1,5},{5,7},{7,3},{3,1},{8,12},{12,14},{14... | collective-permute-start | bytes 786440 | tf_op jit(solution)/shard_map/ppermute | solution.py:179
  177.4 35.3 %collective-permute-start.18 = (bf16[64,2048]{1,0:T(8,128)(2,1)S(1)}, bf16[64,2048]{1,0:T(8,128)(2,1)S(1)}, u32[]{:S(2)}, u32[]{:S(2)}) collective-permute-start(bf16[64,2048]{1,0:T(8,128)(2,1)S(1)} %get-tuple-element.141), channel_id=1, source_target_pairs={{4,0},{6,4},{2,6},{0,2},{5,1},{7,5},{3,7},{1,3},{12,8},{14,12},{10... | collective-permute-start | bytes 786440 | tf_op jit(solution)/shard_map/ppermute | solution.py:182
  221.6 44.9 %all-to-all-start.3 = ((bf16[4,256,512]{2,1,0:T(8,128)(2,1)}), bf16[4,256,512]{2,1,0:T(8,128)(2,1)}, u32[]{:S(2)}, u32[]{:S(2)}) async-start(bf16[4,256,512]{2,1,0:T(8,128)(2,1)} %get-tuple-element.64), calls=%async_computation.3 | async-start | bytes 2097152 | tf_op jit(solution)/shard_map/all_to_all | solution.py:236
  225.8 51.5 %collective-permute-start.24 = (bf16[4,512,512]{2,1,0:T(8,128)(2,1)}, bf16[4,512,512]{2,1,0:T(8,128)(2,1)}, u32[]{:S(2)}, u32[]{:S(2)}) collective-permute-start(bf16[4,512,512]{2,1,0:T(8,128)(2,1)} %all-to-all-done.2), channel_id=1, source_target_pairs={{0,16},{16,0},{1,17},{17,1},{2,18},{18,2},{3,19},{19,3},{4,20},{20... | collective-permute-start | bytes 6291464 | tf_op jit(solution)/shard_map/ppermute | solution.py:166
  398.9 44.9 %collective-permute-start.48 = (bf16[2048,512]{1,0:T(8,128)(2,1)}, bf16[2048,512]{1,0:T(8,128)(2,1)}, u32[]{:S(2)}, u32[]{:S(2)}) collective-permute-start(bf16[2048,512]{1,0:T(8,128)(2,1)} %slice.343), channel_id=1, source_target_pairs={{0,16},{16,0},{1,17},{17,1},{2,18},{18,2},{3,19},{19,3},{4,20},{20... | collective-permute-start | bytes 6291464 | tf_op jit(solution)/shard_map/ppermute | solution.py:166
  415.1 65.0 %collective-permute-start.55 = (bf16[128,2048]{1,0:T(8,128)(2,1)}, bf16[128,2048]{1,0:T(8,128)(2,1)}, u32[]{:S(2)}, u32[]{:S(2)}) collective-permute-start(bf16[128,2048]{1,0:T(8,128)(2,1)} %get-tuple-element.99), channel_id=1, source_target_pairs={{0,1},{1,0},{2,3},{3,2},{4,5},{5,4},{6,7},{7,6},{8,9},{9,8},{10,11... | collective-permute-start | bytes 1572872 | tf_op jit(solution)/shard_map/ppermute | solution.py:166
  419.0 54.1 %collective-permute-start.46 = (bf16[512,2048]{1,0:T(8,128)(2,1)}, bf16[512,2048]{1,0:T(8,128)(2,1)}, u32[]{:S(2)}, u32[]{:S(2)}) collective-permute-start(bf16[512,2048]{1,0:T(8,128)(2,1)} %convolution_convert_fusion.1), channel_id=1, source_target_pairs={{0,1},{1,0},{2,3},{3,2},{4,5},{5,4},{6,7},{7,6},{8,9},{9,8},{10,11... | collective-permute-start | bytes 6291464 | tf_op jit(solution)/shard_map/ppermute | solution.py:166
  452.3 83.4 %collective-permute-start.45 = (bf16[4,128,2048]{2,1,0:T(8,128)(2,1)}, bf16[4,128,2048]{2,1,0:T(8,128)(2,1)}, u32[]{:S(2)}, u32[]{:S(2)}) collective-permute-start(bf16[4,128,2048]{2,1,0:T(8,128)(2,1)} %slice_bitcast_fusion), channel_id=1, source_target_pairs={{0,2},{2,0},{1,3},{3,1},{4,6},{6,4},{5,7},{7,5},{8,10},{10,8},{9,1... | collective-permute-start | bytes 6291464 | tf_op jit(solution)/shard_map/ppermute | solution.py:166
  452.6 66.5 %all-to-all-start.4 = ((bf16[4,512,512]{2,1,0:T(8,128)(2,1)}), bf16[4,512,512]{2,1,0:T(8,128)(2,1)}, u32[]{:S(2)}, u32[]{:S(2)}) async-start(bf16[4,512,512]{2,1,0:T(8,128)(2,1)} %bitcast.151), calls=%async_computation.4 | async-start | bytes 4194304 | tf_op jit(solution)/shard_map/all_to_all | solution.py:236
  478.6 38.8 %collective-permute-start.47 = (bf16[256,2048]{1,0:T(8,128)(2,1)}, bf16[256,2048]{1,0:T(8,128)(2,1)}, u32[]{:S(2)}, u32[]{:S(2)}) collective-permute-start(bf16[256,2048]{1,0:T(8,128)(2,1)} %slice.341), channel_id=1, source_target_pairs={{0,16},{16,0},{1,17},{17,1},{2,18},{18,2},{3,19},{19,3},{4,20},{20... | collective-permute-start | bytes 3145736 | tf_op jit(solution)/shard_map/ppermute | solution.py:166
  512.2 42.6 %collective-permute-start.57 = (bf16[512,2048]{1,0:T(8,128)(2,1)}, bf16[512,2048]{1,0:T(8,128)(2,1)}, u32[]{:S(2)}, u32[]{:S(2)}) collective-permute-start(bf16[512,2048]{1,0:T(8,128)(2,1)} %slice.345), channel_id=1, source_target_pairs={{0,1},{1,0},{2,3},{3,2},{4,5},{5,4},{6,7},{7,6},{8,9},{9,8},{10,11... | collective-permute-start | bytes 6291464 | tf_op jit(solution)/shard_map/ppermute | solution.py:166
  529.7 69.0 %collective-permute-start.62 = (bf16[2048,512]{0,1:T(8,128)(2,1)}, bf16[2048,512]{0,1:T(8,128)(2,1)}, u32[]{:S(2)}, u32[]{:S(2)}) collective-permute-start(bf16[2048,512]{0,1:T(8,128)(2,1)} %pad_maximum_fusion), channel_id=1, source_target_pairs={{0,16},{16,0},{1,17},{17,1},{2,18},{18,2},{3,19},{19,3},{4,20},{20... | collective-permute-start | bytes 6291464 | tf_op jit(solution)/shard_map/ppermute | solution.py:166
  550.3 65.6 %all-to-all-start.6 = ((bf16[4,128,2048]{2,1,0:T(8,128)(2,1)}), bf16[4,128,2048]{2,1,0:T(8,128)(2,1)}, u32[]{:S(2)}, u32[]{:S(2)}) async-start(bf16[4,128,2048]{2,1,0:T(8,128)(2,1)} %fusion), calls=%async_computation.6 | async-start | bytes 4194304 | tf_op jit(solution)/shard_map/all_to_all | solution.py:236
  558.1 36.3 %collective-permute-start.58 = (bf16[64,2048]{1,0:T(8,128)(2,1)S(1)}, bf16[64,2048]{1,0:T(8,128)(2,1)S(1)}, u32[]{:S(2)}, u32[]{:S(2)}) collective-permute-start(bf16[64,2048]{1,0:T(8,128)(2,1)S(1)} %get-tuple-element.135), channel_id=1, source_target_pairs={{0,4},{4,6},{6,2},{2,0},{1,5},{5,7},{7,3},{3,1},{8,12},{12,14},{14... | collective-permute-start | bytes 786440 | tf_op jit(solution)/shard_map/ppermute | solution.py:179
  560.1 34.3 %collective-permute-start.59 = (bf16[64,2048]{1,0:T(8,128)(2,1)S(1)}, bf16[64,2048]{1,0:T(8,128)(2,1)S(1)}, u32[]{:S(2)}, u32[]{:S(2)}) collective-permute-start(bf16[64,2048]{1,0:T(8,128)(2,1)S(1)} %get-tuple-element.133), channel_id=1, source_target_pairs={{4,0},{6,4},{2,6},{0,2},{5,1},{7,5},{3,7},{1,3},{12,8},{14,12},{10... | collective-permute-start | bytes 786440 | tf_op jit(solution)/shard_map/ppermute | solution.py:182
  560.9 66.0 %collective-permute-start.64 = (bf16[4,512,512]{2,1,0:T(8,128)(2,1)}, bf16[4,512,512]{2,1,0:T(8,128)(2,1)}, u32[]{:S(2)}, u32[]{:S(2)}) collective-permute-start(bf16[4,512,512]{2,1,0:T(8,128)(2,1)} %all-to-all-done.4), channel_id=1, source_target_pairs={{0,16},{16,0},{1,17},{17,1},{2,18},{18,2},{3,19},{19,3},{4,20},{20... | collective-permute-start | bytes 6291464 | tf_op jit(solution)/shard_map/ppermute | solution.py:166
  619.3 53.2 %all-to-all-start.7 = ((bf16[4,512,512]{1,2,0:T(8,128)(2,1)}), bf16[4,512,512]{1,2,0:T(8,128)(2,1)}, u32[]{:S(2)}, u32[]{:S(2)}) async-start(bf16[4,512,512]{1,2,0:T(8,128)(2,1)} %copy.51), calls=%async_computation.7 | async-start | bytes 4194304 | tf_op jit(solution)/shard_map/all_to_all | solution.py:236
  626.4 67.1 %collective-permute-start.65 = (bf16[4,256,512]{2,1,0:T(8,128)(2,1)}, bf16[4,256,512]{2,1,0:T(8,128)(2,1)}, u32[]{:S(2)}, u32[]{:S(2)}) collective-permute-start(bf16[4,256,512]{2,1,0:T(8,128)(2,1)} %copy-done.42), channel_id=1, source_target_pairs={{0,16},{16,0},{1,17},{17,1},{2,18},{18,2},{3,19},{19,3},{4,20},{20... | collective-permute-start | bytes 3145736 | tf_op jit(solution)/shard_map/ppermute | solution.py:166
  674.8 46.4 %all-to-all-start.8 = ((bf16[4,256,512]{2,1,0:T(8,128)(2,1)}), bf16[4,256,512]{2,1,0:T(8,128)(2,1)}, u32[]{:S(2)}, u32[]{:S(2)}) async-start(bf16[4,256,512]{2,1,0:T(8,128)(2,1)} %bitcast.130), calls=%async_computation.8 | async-start | bytes 2097152 | tf_op jit(solution)/shard_map/all_to_all | solution.py:236
  (105 other events, 1475.8 us)

commit v4 on v3

v4 whole, which is shorter than its diff:
```python
import functools

import jax
import jax.numpy as jnp
from jax import lax
from jax.experimental import pallas as pl
from jax.experimental.pallas import tpu as pltpu
from jax.sharding import Mesh
from jax.sharding import PartitionSpec as P

HEAD_DIM = 128
BLOCK = 512
HALF = 2

epsilon = 1e-05
rope_base = 10000.0
masked_score = -1e30
low = jnp.bfloat16
CHEAP = pl.CostEstimate(flops=1, transcendentals=0, bytes_accessed=1)
wide = jnp.float32


def rope_tables(places, head_depth):
    halfway = head_depth // 2
    position = places.astype(jnp.float32)[:, None]
    frequency = rope_base ** (-(2.0 * jnp.arange(halfway).astype(jnp.float32)) / head_depth)
    angles = position * frequency[None, :]
    cosine = jnp.concatenate([jnp.cos(angles), jnp.cos(angles)], axis=1)
    sine_table = jnp.concatenate([jnp.sin(angles), jnp.sin(angles)], axis=1)
    return (cosine, sine_table)


def dot(left, right):
    return jnp.dot(left, right, preferred_element_type=wide)


def layer_norm(stream):
    average = jnp.mean(stream, axis=1, keepdims=True)
    centered = stream - average
    inverse = lax.rsqrt(jnp.mean(centered * centered, axis=1, keepdims=True) + epsilon)
    return centered * inverse, inverse


def norm_backward(normed, inverse, gradient):
    average = jnp.mean(gradient, axis=1, keepdims=True)
    crossed = jnp.mean(gradient * normed, axis=1, keepdims=True)
    return inverse * (gradient - average - normed * crossed)


def turn(array):
    return pltpu.roll(array, array.shape[1] // 2, 1)


def rope_sign(depth):
    return jnp.where(lax.broadcasted_iota(jnp.int32, (1, depth), 1) < depth // 2, -1.0, 1.0)


def attend_kernel(rows_ref, weight_ref, cosine_ref, sine_ref, column_ref, line_ref, qkv_ref, heads_ref, logsum_ref):
    depth = heads_ref.shape[1]
    qkv = dot(rows_ref[...], weight_ref[:, : 3 * depth])
    cosine, sine = cosine_ref[...], sine_ref[...] * rope_sign(depth)
    rope = lambda w: (w * cosine + turn(w) * sine).astype(low)
    queries, key_rows = rope(qkv[:, :depth]), rope(qkv[:, depth : 2 * depth])
    values = qkv[:, 2 * depth :].astype(low)
    qkv_ref[...] = jnp.concatenate([queries, key_rows, values], axis=1)
    for at in range(0, queries.shape[0], BLOCK):
        part = slice(at, at + BLOCK)
        scores = dot_last(queries[part], key_rows) * depth**-0.5
        scores = jnp.where(column_ref[part] >= line_ref[...], scores, masked_score)
        highest = jnp.max(scores, axis=1, keepdims=True)
        shifted = jnp.exp(scores - highest)
        totals = jnp.sum(shifted, axis=1, keepdims=True)
        logsum_ref[part] = highest + jnp.log(totals)
        weights = (shifted * (1.0 / totals)).astype(low)
        heads_ref[part] = dot(weights, values).astype(low)


def attend_back_kernel(
    middle_ref, weight_ref, cosine_ref, sine_ref, column_ref, line_ref, qkv_ref, logsum_ref, slope_ref
):
    depth = cosine_ref.shape[1]
    scaling = depth**-0.5
    queries, key_rows, values = (qkv_ref[:, i * depth : (i + 1) * depth] for i in range(3))
    head_grad = dot(middle_ref[...], weight_ref[:, 3 * depth :]).astype(low)
    query_parts = []
    key_grad = value_grad = None
    for at in range(0, queries.shape[0], BLOCK):
        part = slice(at, at + BLOCK)
        scores = dot_last(queries[part], key_rows) * scaling
        scores = jnp.where(column_ref[part] >= line_ref[...], scores, masked_score)
        probable = jnp.exp(scores - logsum_ref[part])
        product = dot_last(head_grad[part], values)
        slopes = probable * (product - jnp.sum(probable * product, axis=1, keepdims=True))
        slopes = slopes.astype(low)
        query_parts.append(dot(slopes, key_rows) * scaling)
        key_part = dot_first(slopes, queries[part]) * scaling
        value_part = dot_first(probable.astype(low), head_grad[part])
        key_grad = key_part if at == 0 else key_grad + key_part
        value_grad = value_part if at == 0 else value_grad + value_part
    cosine, sine = cosine_ref[...], sine_ref[...]
    undo = lambda g: (g * cosine - turn(g * sine) * rope_sign(depth)).astype(low)
    slope_ref[:, :depth] = undo(jnp.concatenate(query_parts, axis=0))
    slope_ref[:, depth : 2 * depth] = undo(key_grad)
    slope_ref[:, 2 * depth :] = value_grad.astype(low)


def project_kernel(columns, *refs):
    lefts, weights = refs[: len(refs) // 2 - 1], refs[len(refs) // 2 - 1 : -2]
    part = sum(dot_last(left[...], weight[:, columns]) for left, weight in zip(lefts, weights)).astype(low)
    first = 2 * pl.program_id(0) < pl.num_programs(0)

    @pl.when(first)
    def _():
        refs[-2][...] = part

    @pl.when(jnp.logical_not(first))
    def _():
        refs[-1][...] = part


def project(name, columns, lefts, weights, tile=256):
    count, width = lefts[0].shape[0], weights[0].shape[0]
    last = count // tile // HALF - 1
    whole = lambda array: pl.BlockSpec(array.shape, lambda i: (0, 0), pipeline_mode=pl.Buffered(buffer_count=1))
    return pl.pallas_call(
        functools.partial(project_kernel, columns),
        grid=(count // tile,),
        in_specs=[pl.BlockSpec((tile, left.shape[1]), lambda i: (i, 0)) for left in lefts]
        + [whole(weight) for weight in weights],
        out_specs=[
            pl.BlockSpec((tile, width), lambda i: (jnp.minimum(i, last), 0)),
            pl.BlockSpec((tile, width), lambda i: (jnp.maximum(i - last - 1, 0), 0)),
        ],
        out_shape=[jax.ShapeDtypeStruct((count // HALF, width), low)] * HALF,
        compiler_params=pltpu.CompilerParams(vmem_limit_bytes=48 * 1024 * 1024),
        cost_estimate=CHEAP,
        name=name,
    )(*lefts, *weights)


def head_sum_kernel(rows_ref, middle_ref, slope_ref, attended_ref, out_ref):
    parts = [dot_first(rows_ref[...], slope_ref[...]), dot_first(middle_ref[...], attended_ref[...])]
    out_ref[0] = jnp.concatenate(parts, axis=1).astype(low)


def gu_sum_kernel(blocks, rows_ref, slope_ref, *out_refs):
    rows = rows_ref[...]
    for block, out_ref in zip(blocks, out_refs):
        size = out_ref.shape[2]
        out_ref[0] = dot_first(rows, slope_ref[:, block * size : (block + 1) * size]).astype(low)


def down_sum_kernel(blocks, slope_ref, hidden_ref, *out_refs):
    slope = slope_ref[...]
    for block, out_ref in zip(blocks, out_refs):
        units = out_ref.shape[1]
        out_ref[0] = dot_first(hidden_ref[:, block * units : (block + 1) * units], slope).astype(low)


def call_blocks(kernel, name, cut, held, shapes):
    count, (length, width) = shapes[0][0], cut[0].shape
    return pl.pallas_call(
        kernel,
        grid=(count,),
        in_specs=[pl.BlockSpec((length, width // count), lambda i: (0, i))] * len(cut)
        + [pl.BlockSpec(array.shape, lambda i: (0, 0)) for array in held],
        out_specs=[pl.BlockSpec((1,) + shape[1:], lambda i: (i, 0, 0)) for shape in shapes],
        out_shape=[jax.ShapeDtypeStruct(shape, low) for shape in shapes],
        compiler_params=pltpu.CompilerParams(vmem_limit_bytes=48 * 1024 * 1024),
        cost_estimate=CHEAP,
        name=name,
    )(*cut, *held)


def assemble_kernel(x_ref, mine_ref, theirs_ref, query_ref, key_ref, value_ref, out_ref):
    line, block, depth = mine_ref.shape[0], mine_ref.shape[1], HEAD_DIM
    for i in range(line):
        for source, turned in ((mine_ref, x_ref[0]), (theirs_ref, 1 - x_ref[0])):
            place = pl.ds(pl.multiple_of((HALF * i + turned) * depth, depth), depth)
            for n, target in enumerate((query_ref, key_ref, value_ref)):
                target[:, place] = source[i, :, n * depth : (n + 1) * depth].astype(wide)
            out_ref[place, :] = source[i, :, 3 * depth :].astype(wide).T


def assemble(mine, theirs):
    line, block, _ = mine.shape
    shape = jax.ShapeDtypeStruct((block, block), wide)
    whole = pl.BlockSpec(memory_space=pltpu.VMEM)
    return pl.pallas_call(
        assemble_kernel,
        in_specs=[pl.BlockSpec(memory_space=pltpu.SMEM), whole, whole],
        out_specs=[whole] * 4,
        out_shape=[shape] * 4,
        cost_estimate=CHEAP,
        name="assemble",
    )(lax.axis_index("x")[None].astype(jnp.int32), mine, theirs)


def assemble_units_kernel(x_ref, gu_mine, down_mine, gu_theirs, down_theirs, gate_ref, up_ref, down_ref):
    units = down_mine.shape[1]
    mine, theirs = gu_mine[0].astype(wide), gu_theirs[0].astype(wide)
    first = jnp.where(x_ref[0] == 0, mine, theirs)
    second = jnp.where(x_ref[0] == 0, theirs, mine)
    gate_ref[...] = jnp.concatenate([first[:, :units], second[:, :units]], axis=1)
    up_ref[...] = jnp.concatenate([first[:, units:], second[:, units:]], axis=1)
    mine, theirs = down_mine[0].astype(wide), down_theirs[0].astype(wide)
    down_ref[:units] = jnp.where(x_ref[0] == 0, mine, theirs)
    down_ref[units:] = jnp.where(x_ref[0] == 0, theirs, mine)


def assemble_units(*arrays):
    rows, units, size = arrays[1].shape
    share = HALF * units
    arrived = [pl.BlockSpec((1,) + array.shape[1:], lambda i, x: (i, 0, 0)) for array in arrays]
    columns = pl.BlockSpec((size, share), lambda i, x: (0, i))
    wide_shape = jax.ShapeDtypeStruct((size, rows * share), wide)
    return pl.pallas_call(
        assemble_units_kernel,
        grid_spec=pltpu.PrefetchScalarGridSpec(
            num_scalar_prefetch=1,
            grid=(rows,),
            in_specs=arrived,
            out_specs=[columns, columns, pl.BlockSpec((share, size), lambda i, x: (i, 0))],
        ),
        out_shape=[wide_shape, wide_shape, jax.ShapeDtypeStruct((rows * share, size), wide)],
        compiler_params=pltpu.CompilerParams(vmem_limit_bytes=48 * 1024 * 1024),
        cost_estimate=CHEAP,
        name="assemble_units",
    )(lax.axis_index("x")[None].astype(jnp.int32), *arrays)


def call_whole(kernel, name, shapes, *arrays):
    whole = pl.BlockSpec(memory_space=pltpu.VMEM)
    return pl.pallas_call(
        kernel,
        in_specs=[whole] * len(arrays),
        out_specs=[whole] * len(shapes),
        out_shape=shapes,
        compiler_params=pltpu.CompilerParams(vmem_limit_bytes=48 * 1024 * 1024),
        cost_estimate=CHEAP,
        name=name,
    )(*arrays)


def dot_last(left, right):
    return lax.dot_general(left, right, (((1,), (1,)), ((), ())), preferred_element_type=wide)


def dot_first(left, right):
    return lax.dot_general(left, right, (((0,), (0,)), ((), ())), preferred_element_type=wide)


def swap(array, axis):
    return lax.ppermute(array, axis, [(0, 1), (1, 0)])


class Ring:
    def __init__(self, axes, line):
        self.axes = axes
        self.size = 2 * line
        self.half = line
        flat = [2 * n if n < line else 2 * (2 * line - 1 - n) + 1 for n in range(self.size)]
        self.upward = [(flat[i], flat[(i + 1) % self.size]) for i in range(self.size)]
        self.downward = [(b, a) for a, b in self.upward]

    def up(self, array):
        return lax.ppermute(array, self.axes, self.upward)

    def down(self, array):
        return lax.ppermute(array, self.axes, self.downward)

    def place(self):
        level, side = lax.axis_index(self.axes[:-1]), lax.axis_index(self.axes[-1])
        return jnp.where(side == 0, level, self.size - 1 - level)

    def slot(self, place, other, level):
        side = place // self.half
        spot = jnp.where((side == 0) != other, level, self.size - 1 - level)
        return (spot - place + self.half + self.size) % self.size

    def gather(self, shard, waits={}):
        half, cut = self.half, shard.shape[0] // 2
        slots = [None] * self.size
        slots[half] = rising = falling = shard
        for step in range(1, half + 1):
            rising, falling = after((rising, falling), waits.get(step))
            if step == half:
                break
            slots[half - step] = rising = self.up(rising)
            slots[half + step] = falling = self.down(falling)
        slots[0] = jnp.concatenate([self.up(rising[:cut]), self.down(falling[cut:])], axis=0)
        return slots

    def scatter_start(self, parts):
        cut = parts[0].shape[0] // 2
        return self.up(parts[0][:cut]), self.down(parts[0][cut:])

    def scatter_step(self, parts, step, moving):
        rising, falling = moving
        cut = rising.shape[0]
        over, under = parts[self.size - step], parts[step]
        if step == 1:
            over = jnp.concatenate([add_low(over[:cut], rising), over[cut:]], axis=0)
            under = jnp.concatenate([under[:cut], add_low(under[cut:], falling)], axis=0)
        else:
            over, under = add_low(over, rising), add_low(under, falling)
        return self.up(over), self.down(under)

    def scatter_end(self, parts, moving):
        return sum(part.astype(wide) for part in (parts[self.half],) + moving)

    def scatter(self, parts):
        moving = self.scatter_start(parts)
        for step in range(1, self.half):
            moving = self.scatter_step(parts, step, moving)
        return self.scatter_end(parts, moving)


def add_low(left, right):
    return (left.astype(wide) + right.astype(wide)).astype(low)


def split_rows(array, count):
    rows = array.shape[0] // count
    return [array[i * rows : (i + 1) * rows] for i in range(count)]


def gather_group(ring, slots):
    return jnp.concatenate(slots + [swap(slot, "core") for slot in slots], axis=0)


def scatter_group(ring, own, other, awaited=None):
    total = after(add_low(own, swap(other, "core")), awaited)
    return ring.scatter(split_rows(total, ring.size))


def exchange_rows(array):
    return lax.all_to_all(array, ROW, 0, 0, tiled=True)


ROW = ("zhi", "zlo")


def to_shard(blocks):
    return jnp.transpose(blocks, (1, 0, 2)).reshape(blocks.shape[1], -1)


def from_shards(arrays, seqs):
    rows, count = lax.axis_size(ROW), len(arrays)
    tokens, width = arrays[0].shape[0], arrays[0].shape[1] // rows
    stacked = jnp.concatenate(arrays, axis=0).reshape(count * tokens, rows, width)
    got = exchange_rows(jnp.transpose(stacked, (1, 0, 2)))
    return [
        got[:, i * tokens : (i + 1) * tokens].reshape(seqs, rows * tokens // seqs, width)
        for i in range(count)
    ]


def together(*arrays):
    return lax.optimization_barrier(arrays)


def after(arrays, others):
    if others is None:
        return arrays
    return lax.optimization_barrier((arrays, others))[0]


def sum_pairs(array):
    return lax.psum(array, "pair") if lax.axis_size("pair") > 1 else array


def pack_kernel(x_ref, query, key, value, out, gate, up, down, head, hidden):
    head[0] = jnp.concatenate([query[...], key[...], value[...], out[...].T], axis=1)
    hidden[0] = jnp.concatenate([jnp.concatenate([gate[...], up[...]], axis=1), down[...]], axis=0)


def pack(query, key, value, out, gate, up, down, rows, line):
    depth, block = HEAD_DIM, query.shape[0]
    units = gate.shape[1] // rows // HALF
    head_at = lambda r, x: HALF * (r % line) + x[0]
    head_in = pl.BlockSpec((block, depth), lambda r, x: (0, head_at(r, x)))
    out_in = pl.BlockSpec((depth, block), lambda r, x: (head_at(r, x), 0))
    unit_in = pl.BlockSpec((block, units), lambda r, x: (0, HALF * r + x[0]))
    down_in = pl.BlockSpec((units, block), lambda r, x: (HALF * r + x[0], 0))
    shapes = [(block, 4 * depth), (block + units, block)]
    return pl.pallas_call(
        pack_kernel,
        grid_spec=pltpu.PrefetchScalarGridSpec(
            num_scalar_prefetch=1,
            grid=(rows,),
            in_specs=[head_in, head_in, head_in, out_in, unit_in, unit_in, down_in],
            out_specs=[pl.BlockSpec((1,) + shape, lambda r, x: (r, 0, 0)) for shape in shapes],
        ),
        out_shape=[jax.ShapeDtypeStruct((rows,) + shape, low) for shape in shapes],
        name="pack_weights",
    )(lax.axis_index("x")[None].astype(jnp.int32), query, key, value, out, gate, up, down)


def mlp_kernel(place_ref, *refs):
    tiles, weights = refs[:4], refs[4:-5]
    hidden_ref, gu_slope_ref, grad_ref, rows_ref, slope_ref = refs[-5:]
    parts, height, span = weights[0].shape
    units = height - span
    rows_ref[...] = jnp.concatenate([tiles[0][...], tiles[2][...]], axis=0)
    slope_ref[...] = jnp.concatenate([tiles[1][...], tiles[3][...]], axis=0)
    cuts = [slice(k * span, (k + 1) * span) for k in range(parts)]
    totals = [None] * parts
    for i, weight in enumerate(weights):
        gate_up = sum(dot(rows_ref[:, cut], weight[k, :span]) for k, cut in enumerate(cuts))
        gate, up = gate_up[:, :units], gate_up[:, units:]
        sigmoid = 1.0 / (1.0 + jnp.exp(-gate))
        activated = gate * sigmoid
        hidden_ref[:, i * units : (i + 1) * units] = (activated * up).astype(low)
        hidden_grad = sum(dot_last(slope_ref[:, cut], weight[k, span:]) for k, cut in enumerate(cuts))
        gate_slope = hidden_grad * up * sigmoid * (1.0 + gate * (1.0 - sigmoid))
        gu_slope = jnp.concatenate([gate_slope, hidden_grad * activated], axis=1).astype(low)
        gu_slope_ref[:, 2 * i * units : 2 * (i + 1) * units] = gu_slope
        for k in range(parts):
            part = dot_last(gu_slope, weight[k, :span])
            totals[k] = part if i == 0 else totals[k] + part
    for k, cut in enumerate(cuts):
        grad_ref[:, cut] = totals[k].astype(low)


def feed_forward(ring, both, weights):
    count, width = both.shape[0] // HALF, both.shape[1]
    parts, height, span = weights[0].shape
    blocks, units, tile = len(weights), height - span, count // ring.size
    pair = lambda size: pl.BlockSpec((HALF * tile, size), lambda i, place: (i, 0))
    single = lambda n: pl.BlockSpec((tile, width), lambda i, place: (4 * i + n, 0))
    whole = lambda array: pl.BlockSpec(
        array.shape, lambda i, place: (0, 0, 0), pipeline_mode=pl.Buffered(buffer_count=1)
    )
    sizes = (blocks * units, 2 * blocks * units, width, width, width)
    return pl.pallas_call(
        mlp_kernel,
        grid_spec=pltpu.PrefetchScalarGridSpec(
            num_scalar_prefetch=1,
            grid=(ring.half,),
            in_specs=[single(n) for n in range(4)] + [whole(weight) for weight in weights],
            out_specs=[pair(size) for size in sizes],
        ),
        out_shape=[jax.ShapeDtypeStruct((count, size), low) for size in sizes],
        compiler_params=pltpu.CompilerParams(vmem_limit_bytes=48 * 1024 * 1024),
        cost_estimate=CHEAP,
        name="feed_forward",
    )(ring.place()[None].astype(jnp.int32), *[both] * 4, *weights)


def down_kernel(place_ref, hidden_ref, *refs):
    weights, out_ref = refs[:-1], refs[-1]
    parts, height, span = weights[0].shape
    units = height - span
    for k in range(parts):
        out_ref[:, k * span : (k + 1) * span] = sum(
            dot(hidden_ref[:, i * units : (i + 1) * units], weight[k, span:]) for i, weight in enumerate(weights)
        ).astype(low)


def down_project(ring, hidden, downs, width, other):
    tile = hidden.shape[0] // ring.size
    whole = lambda array: pl.BlockSpec(
        array.shape, lambda i, place: (0, 0, 0), pipeline_mode=pl.Buffered(buffer_count=1)
    )
    return pl.pallas_call(
        down_kernel,
        grid_spec=pltpu.PrefetchScalarGridSpec(
            num_scalar_prefetch=1,
            grid=(ring.half,),
            in_specs=[pl.BlockSpec((tile, hidden.shape[1]), lambda i, place: (ring.slot(place[0], other, i), 0))]
            + [whole(down) for down in downs],
            out_specs=pl.BlockSpec((tile, width), lambda i, place: (i, 0)),
        ),
        out_shape=jax.ShapeDtypeStruct((hidden.shape[0] // HALF, width), low),
        compiler_params=pltpu.CompilerParams(vmem_limit_bytes=48 * 1024 * 1024),
        cost_estimate=CHEAP,
        name="down_project",
    )(ring.place()[None].astype(jnp.int32), hidden, *downs)


def on_device(
    tokens,
    query_weight,
    key_weight,
    value_weight,
    out_weight,
    gate_weight,
    up_weight,
    down_weight,
    cotangent,
):
    depth = HEAD_DIM
    rows, line = lax.axis_size(ROW), lax.axis_size("zlo")
    small_ring = Ring(("zlo", "y"), line)
    large_ring = Ring(("zhi", "zlo", "y"), rows)
    seqs, width = tokens.shape[0], tokens.shape[2] * rows
    block = width // rows
    units = gate_weight.shape[1] // rows // HALF

    shard = seqs * tokens.shape[1] // rows
    pieces = [array.reshape(rows, shard, block) for array in (tokens, cotangent)]
    weights = (query_weight, key_weight, value_weight, out_weight, gate_weight, up_weight, down_weight)
    head_pieces, hidden_pieces = pack(*weights, rows, line)
    got = exchange_rows(jnp.concatenate(pieces, axis=1))
    got, head_pieces, hidden_pieces = together(got, head_pieces, hidden_pieces)
    stream = to_shard(got[:, :shard]).astype(wide)
    slope_low = to_shard(got[:, shard:])

    head_mine = exchange_rows(head_pieces)

    place = jnp.arange(2 * small_ring.size)
    core = (lax.axis_index("core") + place // small_ring.size) % 2
    spot = (small_ring.place() + place % small_ring.size + small_ring.half) % small_ring.size
    slot_side = spot // line
    slot_level = jnp.where(slot_side == 0, spot, small_ring.size - 1 - spot)
    first = ((2 * slot_side + core) * line + slot_level) * shard
    places = (first[:, None] + jnp.arange(shard)[None, :]).reshape(-1)
    cosine, sine_table = rope_tables(places, depth)

    normed_one, inverse_one = layer_norm(stream)
    rows_one = gather_group(small_ring, small_ring.gather(normed_one.astype(low)))
    rows_one, head_mine, hidden_pieces = together(rows_one, head_mine, hidden_pieces)
    heads_weight = [head_mine.reshape(width, 4 * depth)]
    heads_weight.append(swap(heads_weight[0], "x"))

    hidden_mine = exchange_rows(hidden_pieces)
    hidden_theirs = swap(hidden_mine, "x")
    length = rows_one.shape[0]
    seen = (cosine, sine_table, places[:, None], places[None, :])
    qkv_shape = jax.ShapeDtypeStruct((length, 3 * depth), low)
    kept = []
    for weight in heads_weight:
        shapes = [qkv_shape, jax.ShapeDtypeStruct((length, depth), low), jax.ShapeDtypeStruct((length, 1), wide)]
        kept.append(call_whole(attend_kernel, "attend", shapes, rows_one, weight, *seen))
    heads = [part[1] for part in kept]
    out_parts = project("out_project", slice(3 * depth, 4 * depth), heads, heads_weight)
    middle = stream + scatter_group(small_ring, *out_parts, hidden_mine)
    normed_two, inverse_two = layer_norm(middle)
    both = jnp.concatenate([normed_two.astype(low), slope_low], axis=0)
    both = jnp.concatenate(large_ring.gather(both, {4: hidden_theirs}), axis=0)
    hidden_weight = [hidden_mine, hidden_theirs, swap(hidden_mine, "core"), swap(hidden_theirs, "core")]
    hidden_low, gu_slope, grad_part, rows_two, slope_all = feed_forward(large_ring, both, hidden_weight)

    def gu_sums(i, left):
        kernel = functools.partial(gu_sum_kernel, (i, i + 2))
        return call_blocks(kernel, "gu_sum", [left], [gu_slope], [(rows, block, 2 * units)] * 2)

    def down_sums(i, left):
        kernel = functools.partial(down_sum_kernel, (i, i + 2))
        return call_blocks(kernel, "down_sum", [left], [hidden_low], [(rows, units, block)] * 2)

    parts = split_rows(grad_part, large_ring.size)
    moving = large_ring.scatter_start(parts)
    gu_own, gu_other = gu_sums(1, rows_two)
    moving, gu_own, gu_other, rows_two, slope_all, parts = together(
        moving, gu_own, gu_other, rows_two, slope_all, parts
    )
    moving = large_ring.scatter_step(parts, 1, moving)
    gu_other = swap(gu_other, "core")
    gu_mine, gu_mine_other = gu_sums(0, rows_two)
    moving, gu_own, gu_other, gu_mine, gu_mine_other, slope_all = together(
        moving, gu_own, gu_other, gu_mine, gu_mine_other, slope_all
    )

    def chunk(own, other, k, n):
        return swap(add_low(own[k : k + n], other[k : k + n]), "x")

    chunks = [chunk(gu_own, gu_other, 0, 1)]
    moving = large_ring.scatter_step(parts, 2, moving)
    down_own, down_other = down_sums(1, slope_all)
    moving, chunks, gu_own, gu_other, gu_mine_other, down_own, down_other, slope_all = together(
        moving, chunks, gu_own, gu_other, gu_mine_other, down_own, down_other, slope_all
    )
    chunks.append(chunk(gu_own, gu_other, 1, 1))
    moving = large_ring.scatter_step(parts, 3, moving)
    gu_mine_other = swap(gu_mine_other, "core")
    down_other = swap(down_other, "core")
    down_mine, down_mine_other = down_sums(0, slope_all)
    moving, chunks, gu_own, gu_other, gu_mine_other, down_other, down_mine, down_mine_other, hidden_low = together(
        moving, chunks, gu_own, gu_other, gu_mine_other, down_other, down_mine, down_mine_other, hidden_low
    )
    grad_two = large_ring.scatter_end(parts, moving)
    middle_grad = slope_low.astype(wide) + norm_backward(normed_two, inverse_two, grad_two)

    chunks.append(chunk(gu_own, gu_other, 2, 1))
    middle_low = middle_grad.astype(low)
    slots = [None, small_ring.up(middle_low), middle_low, small_ring.down(middle_low)]
    branch_other = down_project(large_ring, hidden_low, hidden_weight, width, True)
    slots[1:], chunks, gu_own, gu_other, down_mine_other, branch_other, gu_mine = together(
        slots[1:], chunks, gu_own, gu_other, down_mine_other, branch_other, gu_mine
    )
    chunks.append(chunk(gu_own, gu_other, 3, 1))
    cut = shard // 2
    slots[0] = jnp.concatenate([small_ring.up(slots[1][:cut]), small_ring.down(slots[3][cut:])], axis=0)
    down_mine_other = swap(down_mine_other, "core")
    gu_mine = add_low(gu_mine, gu_mine_other)
    slots, chunks, down_mine_other, down_own, down_other, gu_mine = together(
        slots, chunks, down_mine_other, down_own, down_other, gu_mine
    )
    down_chunks = [chunk(down_own, down_other, 0, rows // 2)]
    middle_all = gather_group(small_ring, slots)
    gu_total = sum_pairs(add_low(gu_mine, jnp.concatenate(chunks, axis=0)))
    gu_got = exchange_rows(gu_total)
    middle_all, down_chunks, down_own, down_other, branch_other = together(
        middle_all, down_chunks, down_own, down_other, branch_other
    )

    def head_back(head):
        qkv, attended, logsums = kept[head]
        arrays = (middle_all, heads_weight[head], *seen, qkv, logsums)
        (slope,) = call_whole(attend_back_kernel, "attend_back", [qkv_shape], *arrays)
        shape = (rows, block, 4 * depth)
        return slope, call_blocks(head_sum_kernel, "head_sum", [rows_one, middle_all], [slope, attended], [shape])[0]

    down_chunks.append(chunk(down_own, down_other, rows // 2, rows // 2))
    branch_other = split_rows(branch_other, HALF)
    branch_other[0] = swap(branch_other[0], "y")
    theirs_slope, theirs_sum = head_back(1)
    middle_all, theirs_slope, theirs_sum, down_chunks, branch_other, hidden_low = together(
        middle_all, theirs_slope, theirs_sum, down_chunks, branch_other, hidden_low
    )
    branch_other[1] = swap(branch_other[1], "y")
    head_first = swap(theirs_sum[: rows // 2], "x")
    mine_slope, mine_sum = head_back(0)
    back_parts = project("qkv_back", slice(0, 3 * depth), [mine_slope, theirs_slope], heads_weight)
    down_total = add_low(add_low(down_mine, down_mine_other), jnp.concatenate(down_chunks, axis=0))
    back_parts, mine_sum, head_first, theirs_sum, branch_other, gu_got, down_total, hidden_low = together(
        back_parts, mine_sum, head_first, theirs_sum, branch_other, gu_got, down_total, hidden_low
    )
    down_got = exchange_rows(sum_pairs(down_total))
    head_second = swap(theirs_sum[rows // 2 :], "x")
    back_total = add_low(back_parts[0], swap(back_parts[1], "core"))
    back_slots = split_rows(back_total, small_ring.size)
    moving = small_ring.scatter_start(back_slots)
    branch_own = down_project(large_ring, hidden_low, hidden_weight, width, False)
    branch_half = add_low(branch_own, jnp.concatenate(branch_other, axis=0)).reshape(rows, shard, width)
    moving, back_slots, down_got, branch_half, head_second, gu_got = together(
        moving, back_slots, down_got, branch_half, head_second, gu_got
    )
    branch_got = exchange_rows(branch_half)
    gu_theirs = swap(gu_got, "x")
    moving = small_ring.scatter_step(back_slots, 1, moving)
    head_total = sum_pairs(add_low(mine_sum, jnp.concatenate([head_first, head_second], axis=0)))
    moving, head_total, branch_got, gu_theirs, down_got = together(moving, head_total, branch_got, gu_theirs, down_got)
    head_got = exchange_rows(head_total)
    down_theirs = swap(down_got, "x")
    grad_one = small_ring.scatter_end(back_slots, moving)
    input_low = (middle_grad + norm_backward(normed_one, inverse_one, grad_one)).astype(low)
    output_low = (middle + jnp.sum(branch_got.astype(wide), axis=0)).astype(low)
    head_got, down_theirs, input_low, output_low, gu_got, down_got, gu_theirs = together(
        head_got, down_theirs, input_low, output_low, gu_got, down_got, gu_theirs
    )
    head_got = head_got.reshape(rows // line, line, block, 4 * depth)
    head_mine = jnp.sum(head_got.astype(wide), axis=0).astype(low)
    head_theirs = swap(head_mine, "x")
    layer_out, input_grad = from_shards((output_low, input_low), seqs)
    gate_grad, up_grad, down_grad = assemble_units(gu_got, down_got, gu_theirs, down_theirs)
    layer_out, input_grad, head_mine, head_theirs = together(layer_out, input_grad, head_mine, head_theirs)
    input_grad = input_grad.astype(wide)
    query_grad, key_grad, value_grad, out_grad = assemble(head_mine, head_theirs)

    return (
        layer_out,
        input_grad,
        query_grad,
        key_grad,
        value_grad,
        out_grad,
        gate_grad,
        up_grad,
        down_grad,
    )


def solution(mesh):
    dp, rows, cols = (mesh.shape[name] for name in ("dp", "row", "col"))
    sizes = (dp // HALF, HALF, HALF, rows // HALF, cols // HALF, HALF)
    fine = Mesh(mesh.devices.reshape(sizes), ("pair", "x", "zhi", "zlo", "y", "core"))
    across, inner, tall = ("pair", "x"), ("y", "core"), ROW
    split = P(across, inner, tall)
    inward = P(tall, inner)
    outward = P(inner, tall)
    return jax.shard_map(
        on_device,
        mesh=fine,
        in_specs=(split, inward, inward, inward, outward, inward, inward, outward, split),
        out_specs=(split, split, inward, inward, inward, outward, inward, inward, outward),
        check_vma=False,
    )
```

time: 735 us -> 701 us (0.954)
  Pallas kernels: 96.6 us -> 149 us
  matrix products: 35.2 us -> 0 us
  local copies, waits for them, and re-layouts: 77.5 us -> 55.4 us
  other arithmetic: 75.7 us -> 59.7 us
  starting transfers between devices: 98.4 us -> 87.3 us
    ppermute x20 -> x16, waiting for transfers between devices: 198 us -> 32.5 us  [up(): return lax.ppermute(array, self.axes, self.upward)]
    ppermute x20 -> x16, waiting for transfers between devices: 29.9 us -> 139 us  [down(): return lax.ppermute(array, self.axes, self.downward)]
    ppermute x26 -> x31, waiting for transfers between devices: 40.3 us -> 104 us  [swap(): return lax.ppermute(array, axis, [(0, 1), (1, 0)])]
    pallas_call x3 -> x10, Pallas kernels: 45 us -> 91.8 us  [the longest x6 38.3 us: call_blocks(): pl.pallas_call(kernel, grid=(count,), in_specs=[pl.BlockSpec((length, wid...]
    dot_general x8 -> x0, matrix products: 35.2 us -> none  [dot_tn(): return jnp.einsum('km,kn->mn', left, right, preferred_element_type=wide)]
    convert_element_type x7 -> x4, other arithmetic: 17.9 us -> 3.86 us  [the longest x1 1.58 us: on_device(): middle_low = middle_grad.astype(low)]
    convert_element_type x11 -> x22, other arithmetic: 20.9 us -> 34.2 us  [add_low(): return (left.astype(wide) + right.astype(wide)).astype(low)]
    ppermute x20 -> x16, starting transfers between devices: 22.5 us -> 14.1 us  [up(): return lax.ppermute(array, self.axes, self.upward)]
  transfers between devices with their start and end apart: 75 -> 71, of which waited for: 37 -> 43; matrix products, arithmetic and copies ran while one was open for 22% -> 12% of each run, Pallas kernels for 8% -> 16%
where the time goes in v4:
time: 701 us; the launch traced here: 696 us
  waiting for transfers between devices  343 us (49%)
  Pallas kernels  149 us (21%)
  starting transfers between devices  87.3 us (12%)
  other arithmetic  59.7 us (9%)
  local copies, waits for them, and re-layouts  55.4 us (8%)
    ppermute x16, waiting for transfers between devices, down(): return lax.ppermute(array, self.axes, self.downward)  139 us
    ppermute x31, waiting for transfers between devices, swap(): return lax.ppermute(array, axis, [(0, 1), (1, 0)])  104 us
    all_to_all x8, waiting for transfers between devices, exchange_rows(): return lax.all_to_all(array, ROW, 0, 0, tiled=True)  67.9 us
    unnamed x164, local copies, waits for them, and re-layouts  38.9 us
    pallas_call x6, Pallas kernels, call_blocks(): pl.pallas_call(kernel, grid=(count,), in_specs=[pl.BlockSpec((length, wid...  38.3 us
    all_to_all x8, starting transfers between devices, exchange_rows(): return lax.all_to_all(array, ROW, 0, 0, tiled=True)  37.1 us
    convert_element_type x22, other arithmetic, add_low(): return (left.astype(wide) + right.astype(wide)).astype(low)  34.2 us
    pallas_call x1, Pallas kernels, feed_forward(): pl.pallas_call(mlp_kernel, grid_spec=pltpu.PrefetchScalarGridSpec(num_sca...  32.8 us
  transfers between devices with their start and end apart: 71, of which 43 were waited for; matrix products, arithmetic and copies ran while one was open for 12% of the time, Pallas kernels for 16%

profile of v4, /device:TPU:0, one launch (start us, length us, event | category | flops | bytes accessed | tf_op | source)
XLA Modules:
  0.0 696.2 jit_solution(12015404505728932843)
XLA Ops:
  14.6 20.3 %all-to-all-done = bf16[4,256,512]{2,1,0:T(8,128)(2,1)S(1)} async-done(((bf16[4,256,512]{2,1,0:T(8,128)(2,1)}), bf16[4,256,512]{2,1,0:T(8,128)(2,1)S(1)}, u32[]{:S(2)}, u32[]{:S(2)}) %all-to-all-start) | async-done | bytes 1048608 | tf_op jit(solution)/shard_map/all_to_all | solution.py:338
  43.3 20.8 %collective-permute-done.2 = bf16[128,2048]{1,0:T(8,128)(2,1)} collective-permute-done((bf16[128,2048]{1,0:T(8,128)(2,1)}, bf16[128,2048]{1,0:T(8,128)(2,1)}, u32[]{:S(2)}, u32[]{:S(2)}) %collective-permute-start.2) | collective-permute-done | bytes 524320 | tf_op jit(solution)/shard_map/ppermute | solution.py:270
  68.6 16.6 %collective-permute-done.3 = bf16[64,2048]{1,0:T(8,128)(2,1)S(1)} collective-permute-done((bf16[64,2048]{1,0:T(8,128)(2,1)S(1)}, bf16[64,2048]{1,0:T(8,128)(2,1)S(1)}, u32[]{:S(2)}, u32[]{:S(2)}) %collective-permute-start.3) | collective-permute-done | bytes 262176 | tf_op jit(solution)/shard_map/ppermute | solution.py:270
  117.1 30.1 %collective-permute-done.8.weight_ref.refs_3_ = bf16[2048,512]{1,0:T(8,128)(2,1)} collective-permute-done((bf16[2048,512]{1,0:T(8,128)(2,1)S(1)}, bf16[2048,512]{1,0:T(8,128)(2,1)}, u32[]{:S(2)}, u32[]{:S(2)}) %collective-permute-start.8) | collective-permute-done | bytes 2097184 | tf_op jit(solution)/shard_map/ppermute | solution.py:254
  147.2 7.7 %attend.3 = (bf16[1024,384]{1,0:T(8,128)(2,1)S(1)}, bf16[1024,128]{1,0:T(8,128)(2,1)S(1)}, f32[1024,1]{1,0:T(8,128)S(1)}) custom-call(bf16[1024,2048]{1,0:T(8,128)(2,1)} %constant_dynamic-update-slice_fusion.rows_ref, bf16[2048,512]{1,0:T(8,128)(2,1)} %collective-permute-done.8.weight_ref.refs_3_, f32[1024,128]{1,0:T(8,128)S(1)} %get-tuple-element.353.cosine_ref, ...), custom_call_target="tpu_custom_call" | custom-call | flops 1 | bytes 1 | tf_op jit(solution)/shard_map/attend/pallas_call | solution.py:234
  169.1 7.7 %all-to-all-done.2.refs_4_.refs_0_ = bf16[4,768,512]{2,1,0:T(8,128)(2,1)} async-done(((bf16[4,768,512]{2,1,0:T(8,128)(2,1)}), bf16[4,768,512]{2,1,0:T(8,128)(2,1)}, u32[]{:S(2)}, u32[]{:S(2)}) %all-to-all-start.2) | async-done | bytes 3145760 | tf_op jit(solution)/shard_map/all_to_all | solution.py:338
  189.2 10.7 %collective-permute-done.13 = bf16[128,2048]{1,0:T(8,128)(2,1)S(1)} collective-permute-done((bf16[128,2048]{1,0:T(8,128)(2,1)S(1)}, bf16[128,2048]{1,0:T(8,128)(2,1)S(1)}, u32[]{:S(2)}, u32[]{:S(2)}) %collective-permute-start.13) | collective-permute-done | bytes 524320 | tf_op jit(solution)/shard_map/ppermute | solution.py:270
  206.1 20.7 %collective-permute-done.17 = bf16[256,2048]{1,0:T(8,128)(2,1)S(1)} collective-permute-done((bf16[256,2048]{1,0:T(8,128)(2,1)S(1)}, bf16[256,2048]{1,0:T(8,128)(2,1)S(1)}, u32[]{:S(2)}, u32[]{:S(2)}) %collective-permute-start.17) | collective-permute-done | bytes 1048608 | tf_op jit(solution)/shard_map/ppermute | solution.py:270
  229.0 21.0 %collective-permute-done.18 = bf16[256,2048]{1,0:T(8,128)(2,1)S(1)} collective-permute-done((bf16[256,2048]{1,0:T(8,128)(2,1)S(1)}, bf16[256,2048]{1,0:T(8,128)(2,1)S(1)}, u32[]{:S(2)}, u32[]{:S(2)}) %collective-permute-start.18) | collective-permute-done | bytes 1048608 | tf_op jit(solution)/shard_map/ppermute | solution.py:270
  252.2 20.5 %collective-permute-done.20.refs_5_.refs_1_ = bf16[4,768,512]{2,1,0:T(8,128)(2,1)} collective-permute-done((bf16[4,768,512]{2,1,0:T(8,128)(2,1)}, bf16[4,768,512]{2,1,0:T(8,128)(2,1)}, u32[]{:S(2)}, u32[]{:S(2)}) %collective-permute-start.20) | collective-permute-done | bytes 3145760 | tf_op jit(solution)/shard_map/ppermute | solution.py:254
  277.9 7.3 %collective-permute-done.21 = bf16[128,2048]{1,0:T(8,128)(2,1)} collective-permute-done((bf16[128,2048]{1,0:T(8,128)(2,1)}, bf16[128,2048]{1,0:T(8,128)(2,1)}, u32[]{:S(2)}, u32[]{:S(2)}) %collective-permute-start.21) | collective-permute-done | bytes 524320 | tf_op jit(solution)/shard_map/ppermute | solution.py:267
  298.2 32.8 %feed_forward.1 = (bf16[1024,1024]{1,0:T(8,128)(2,1)S(1)}, bf16[1024,2048]{1,0:T(8,128)(2,1)}, bf16[1024,2048]{1,0:T(8,128)(2,1)}, bf16[1024,2048]{1,0:T(8,128)(2,1)}, bf16[1024,2048]{1,0:T(8,128)(2,1)}) custom-call(s32[1]{0:T(128)} %bitcast.9.place_ref, bf16[2048,2048]{1,0:T(8,128)(2,1)} %copy-done.28, bf16[2048,2048]{1,0:T(8,128)(2,1)} %copy-done.28, ...), custom_call_target="tpu_custom_call" | custom-call | flops 1 | bytes 1 | tf_op jit(solution)/shard_map/feed_forward/pallas_call | solution.py:436
  336.7 7.7 %gu_sum.2 = (bf16[4,512,512]{2,1,0:T(8,128)(2,1)S(1)}, bf16[4,512,512]{2,1,0:T(8,128)(2,1)S(1)}) custom-call(bf16[1024,2048]{1,0:T(8,128)(2,1)} %get-tuple-element.192.rows_ref, bf16[1024,2048]{1,0:T(8,128)(2,1)} %get-tuple-element.179.slope_ref), custom_call_target="tpu_custom_call" | custom-call | flops 1 | bytes 1 | tf_op jit(solution)/shard_map/gu_sum/pallas_call | solution.py:162
  348.4 7.8 %gu_sum.3 = (bf16[4,512,512]{2,1,0:T(8,128)(2,1)S(1)}, bf16[4,512,512]{2,1,0:T(8,128)(2,1)S(1)}) custom-call(bf16[1024,2048]{1,0:T(8,128)(2,1)} %get-tuple-element.192.rows_ref, bf16[1024,2048]{1,0:T(8,128)(2,1)} %get-tuple-element.179.slope_ref), custom_call_target="tpu_custom_call" | custom-call | flops 1 | bytes 1 | tf_op jit(solution)/shard_map/gu_sum/pallas_call | solution.py:162
  407.4 7.7 %down_project.2 = bf16[512,2048]{1,0:T(8,128)(2,1)S(1)} custom-call(s32[1]{0:T(128)} %bitcast.9.place_ref, bf16[1024,1024]{1,0:T(8,128)(2,1)S(1)} %get-tuple-element.275.hidden_ref, bf16[4,768,512]{2,1,0:T(8,128)(2,1)} %all-to-all-done.2.refs_4_.refs_0_, bf16[4,768,512]{2,1,0:T(8,128)(2,1)} %collective-permute-done.20.refs_5_.refs_1_, ...), custom_call_target="tpu_custom_call" | custom-call | flops 1 | bytes 1 | tf_op jit(solution)/shard_map/down_project/pallas_call | solution.py:466
  465.4 8.9 %attend_back.2.slope_ref.refs_1_ = bf16[1024,384]{1,0:T(8,128)(2,1)S(1)} custom-call(bf16[1024,2048]{1,0:T(8,128)(2,1)} %constant_dynamic-update-slice_fusion.19.middle_ref, bf16[2048,512]{1,0:T(8,128)(2,1)} %collective-permute-done.8.weight_ref.refs_3_, f32[1024,128]{1,0:T(8,128)S(1)} %get-tuple-element.353.cosine_ref, f32[1024,128]{1,0:T(8,128)S(1)} %copy-done.3, ...), custom_call_target="tpu_custom_call" | custom-call | flops 1 | bytes 1 | tf_op jit(solution)/shard_map/attend_back/pallas_call | solution.py:234
  490.1 8.2 %attend_back.3.refs_0_.slope_ref = bf16[1024,384]{1,0:T(8,128)(2,1)S(1)} custom-call(bf16[1024,2048]{1,0:T(8,128)(2,1)} %constant_dynamic-update-slice_fusion.19.middle_ref, bf16[2048,512]{1,0:T(8,128)(2,1)S(1)} %bitcast.32, f32[1024,128]{1,0:T(8,128)S(1)} %get-tuple-element.353.cosine_ref, f32[1024,128]{1,0:T(8,128)S(1)} %copy-done.3, ...), custom_call_target="tpu_custom_call" | custom-call | flops 1 | bytes 1 | tf_op jit(solution)/shard_map/attend_back/pallas_call | solution.py:234
  506.1 7.9 %qkv_back.1 = (bf16[512,2048]{1,0:T(8,128)(2,1)S(1)}, bf16[512,2048]{1,0:T(8,128)(2,1)S(1)}) custom-call(bf16[1024,384]{1,0:T(8,128)(2,1)S(1)} %attend_back.3.refs_0_.slope_ref, bf16[1024,384]{1,0:T(8,128)(2,1)S(1)} %attend_back.2.slope_ref.refs_1_, bf16[2048,512]{1,0:T(8,128)(2,1)} %bitcast.31, bf16[2048,512]{1,0:T(8,128)(2,1)} %collective-permute-done.8.weight_ref.refs_3_), custom_call_target="tpu_custom_call" | custom-call | flops 1 | bytes 1 | tf_op jit(solution)/shard_map/qkv_back/pallas_call | solution.py:125
  525.3 7.7 %down_project.3 = bf16[512,2048]{1,0:T(8,128)(2,1)S(1)} custom-call(s32[1]{0:T(128)} %bitcast.9.place_ref, bf16[1024,1024]{1,0:T(8,128)(2,1)S(1)} %get-tuple-element.275.hidden_ref, bf16[4,768,512]{2,1,0:T(8,128)(2,1)} %all-to-all-done.2.refs_4_.refs_0_, bf16[4,768,512]{2,1,0:T(8,128)(2,1)} %collective-permute-done.20.refs_5_.refs_1_, ...), custom_call_target="tpu_custom_call" | custom-call | flops 1 | bytes 1 | tf_op jit(solution)/shard_map/down_project/pallas_call | solution.py:466
  565.4 29.7 %collective-permute-done.59 = bf16[128,2048]{1,0:T(8,128)(2,1)} collective-permute-done((bf16[128,2048]{1,0:T(8,128)(2,1)S(1)}, bf16[128,2048]{1,0:T(8,128)(2,1)}, u32[]{:S(2)}, u32[]{:S(2)}) %collective-permute-start.59) | collective-permute-done | bytes 524320 | tf_op jit(solution)/shard_map/ppermute | solution.py:270
  595.1 7.7 %collective-permute-done.58 = bf16[128,2048]{1,0:T(8,128)(2,1)} collective-permute-done((bf16[128,2048]{1,0:T(8,128)(2,1)S(1)}, bf16[128,2048]{1,0:T(8,128)(2,1)}, u32[]{:S(2)}, u32[]{:S(2)}) %collective-permute-start.58) | collective-permute-done | bytes 524320 | tf_op jit(solution)/shard_map/ppermute | solution.py:267
  618.3 16.4 %collective-permute-done.61.down_theirs = bf16[4,256,512]{2,1,0:T(8,128)(2,1)S(1)} collective-permute-done((bf16[4,256,512]{2,1,0:T(8,128)(2,1)S(1)}, bf16[4,256,512]{2,1,0:T(8,128)(2,1)S(1)}, u32[]{:S(2)}, u32[]{:S(2)}) %collective-permute-start.61) | collective-permute-done | bytes 1048608 | tf_op jit(solution)/shard_map/ppermute | solution.py:254
  634.7 23.5 %all-to-all-done.6 = bf16[4,512,512]{2,1,0:T(8,128)(2,1)} async-done(((bf16[4,512,512]{2,1,0:T(8,128)(2,1)}), bf16[4,512,512]{2,1,0:T(8,128)(2,1)}, u32[]{:S(2)}, u32[]{:S(2)}) %all-to-all-start.6) | async-done | bytes 2097184 | tf_op jit(solution)/shard_map/all_to_all | solution.py:338
  673.4 15.5 %all-to-all-done.7 = bf16[4,256,512]{2,1,0:T(8,128)(2,1)} async-done(((bf16[4,256,512]{2,1,0:T(8,128)(2,1)}), bf16[4,256,512]{2,1,0:T(8,128)(2,1)}, u32[]{:S(2)}, u32[]{:S(2)}) %all-to-all-start.7) | async-done | bytes 1048608 | tf_op jit(solution)/shard_map/all_to_all | solution.py:338
  (389 shorter events, 329.1 us)
Async XLA Ops:
  2.9 32.0 %all-to-all-start = ((bf16[4,256,512]{2,1,0:T(8,128)(2,1)}), bf16[4,256,512]{2,1,0:T(8,128)(2,1)S(1)}, u32[]{:S(2)}, u32[]{:S(2)}) async-start(bf16[4,256,512]{2,1,0:T(8,128)(2,1)} %pad_maximum_fusion), calls=%async_computation | async-start | bytes 2097152 | tf_op jit(solution)/shard_map/all_to_all | solution.py:338
  37.6 26.4 %collective-permute-start.2 = (bf16[128,2048]{1,0:T(8,128)(2,1)}, bf16[128,2048]{1,0:T(8,128)(2,1)}, u32[]{:S(2)}, u32[]{:S(2)}) collective-permute-start(bf16[128,2048]{1,0:T(8,128)(2,1)} %fusion.3), channel_id=1, source_target_pairs={{4,0},{6,4},{2,6},{0,2},{5,1},{7,5},{3,7},{1,3},{12,8},{14,12},{10... | collective-permute-start | bytes 1572872 | tf_op jit(solution)/shard_map/ppermute | solution.py:270
  39.2 25.9 %collective-permute-start = (bf16[128,2048]{1,0:T(8,128)(2,1)}, bf16[128,2048]{1,0:T(8,128)(2,1)}, u32[]{:S(2)}, u32[]{:S(2)}) collective-permute-start(bf16[128,2048]{1,0:T(8,128)(2,1)} %fusion.3), channel_id=1, source_target_pairs={{0,4},{4,6},{6,2},{2,0},{1,5},{5,7},{7,3},{3,1},{8,12},{12,14},{14... | collective-permute-start | bytes 1572872 | tf_op jit(solution)/shard_map/ppermute | solution.py:267
  39.7 59.4 %all-to-all-start.1 = ((bf16[4,512,512]{2,1,0:T(8,128)(2,1)}), bf16[4,512,512]{2,1,0:T(8,128)(2,1)S(1)}, u32[]{:S(2)}, u32[]{:S(2)}) async-start(bf16[4,512,512]{2,1,0:T(8,128)(2,1)} %get-tuple-element.165), calls=%async_computation.1 | async-start | bytes 4194304 | tf_op jit(solution)/shard_map/all_to_all | solution.py:338
  68.1 29.2 %collective-permute-start.6 = (bf16[128,2048]{1,0:T(8,128)(2,1)}, bf16[128,2048]{1,0:T(8,128)(2,1)S(1)}, u32[]{:S(2)}, u32[]{:S(2)}) collective-permute-start(bf16[128,2048]{1,0:T(8,128)(2,1)} %fusion.3), channel_id=1, source_target_pairs={{0,1},{1,0},{2,3},{3,2},{4,5},{5,4},{6,7},{7,6},{8,9},{9,8},{10,11... | collective-permute-start | bytes 1572872 | tf_op jit(solution)/shard_map/ppermute | solution.py:254
  68.1 30.1 %collective-permute-start.7 = (bf16[128,2048]{1,0:T(8,128)(2,1)}, bf16[128,2048]{1,0:T(8,128)(2,1)S(1)}, u32[]{:S(2)}, u32[]{:S(2)}) collective-permute-start(bf16[128,2048]{1,0:T(8,128)(2,1)} %collective-permute-done.2), channel_id=1, source_target_pairs={{0,1},{1,0},{2,3},{3,2},{4,5},{5,4},{6,7},{7,6},{8,9},{9,8},{10,11... | collective-permute-start | bytes 1572872 | tf_op jit(solution)/shard_map/ppermute | solution.py:254
  68.6 27.9 %collective-permute-start.5 = (bf16[128,2048]{1,0:T(8,128)(2,1)}, bf16[128,2048]{1,0:T(8,128)(2,1)S(1)}, u32[]{:S(2)}, u32[]{:S(2)}) collective-permute-start(bf16[128,2048]{1,0:T(8,128)(2,1)} %collective-permute-done), channel_id=1, source_target_pairs={{0,1},{1,0},{2,3},{3,2},{4,5},{5,4},{6,7},{7,6},{8,9},{9,8},{10,11... | collective-permute-start | bytes 1572872 | tf_op jit(solution)/shard_map/ppermute | solution.py:254
  99.0 48.1 %collective-permute-start.8 = (bf16[2048,512]{1,0:T(8,128)(2,1)S(1)}, bf16[2048,512]{1,0:T(8,128)(2,1)}, u32[]{:S(2)}, u32[]{:S(2)}) collective-permute-start(bf16[2048,512]{1,0:T(8,128)(2,1)S(1)} %bitcast.28), channel_id=1, source_target_pairs={{0,16},{16,0},{1,17},{17,1},{2,18},{18,2},{3,19},{19,3},{4,20},{20... | collective-permute-start | bytes 6291464 | tf_op jit(solution)/shard_map/ppermute | solution.py:254
  100.5 76.2 %all-to-all-start.2 = ((bf16[4,768,512]{2,1,0:T(8,128)(2,1)}), bf16[4,768,512]{2,1,0:T(8,128)(2,1)}, u32[]{:S(2)}, u32[]{:S(2)}) async-start(bf16[4,768,512]{2,1,0:T(8,128)(2,1)} %get-tuple-element.173), calls=%async_computation.2 | async-start | bytes 6291456 | tf_op jit(solution)/shard_map/all_to_all | solution.py:338
  204.9 67.8 %collective-permute-start.20 = (bf16[4,768,512]{2,1,0:T(8,128)(2,1)}, bf16[4,768,512]{2,1,0:T(8,128)(2,1)}, u32[]{:S(2)}, u32[]{:S(2)}) collective-permute-start(bf16[4,768,512]{2,1,0:T(8,128)(2,1)} %all-to-all-done.2.refs_4_.refs_0_), channel_id=1, source_target_pairs={{0,16},{16,0},{1,17},{17,1},{2,18},{18,2},{3,19},{19,3},{4,20},{20... | collective-permute-start | bytes 9437192 | tf_op jit(solution)/shard_map/ppermute | solution.py:254
  441.7 76.2 %all-to-all-start.3 = ((bf16[4,512,512]{2,1,0:T(8,128)(2,1)}), bf16[4,512,512]{2,1,0:T(8,128)(2,1)}, u32[]{:S(2)}, u32[]{:S(2)}) async-start(bf16[4,512,512]{2,1,0:T(8,128)(2,1)} %add_convert_fusion.3), calls=%async_computation.3 | async-start | bytes 4194304 | tf_op jit(solution)/shard_map/all_to_all | solution.py:338
  462.3 25.0 %collective-permute-start.51 = (bf16[256,2048]{1,0:T(8,128)(2,1)S(1)}, bf16[256,2048]{1,0:T(8,128)(2,1)S(1)}, u32[]{:S(2)}, u32[]{:S(2)}) collective-permute-start(bf16[256,2048]{1,0:T(8,128)(2,1)S(1)} %get-tuple-element.338), channel_id=1, source_target_pairs={{0,2},{2,0},{1,3},{3,1},{4,6},{6,4},{5,7},{7,5},{8,10},{10,8},{9,1... | collective-permute-start | bytes 3145736 | tf_op jit(solution)/shard_map/ppermute | solution.py:254
  488.4 28.7 %collective-permute-start.52 = (bf16[2,512,512]{2,1,0:T(8,128)(2,1)S(1)}, bf16[2,512,512]{2,1,0:T(8,128)(2,1)S(1)}, u32[]{:S(2)}, u32[]{:S(2)}) collective-permute-start(bf16[2,512,512]{2,1,0:T(8,128)(2,1)S(1)} %slice.222), channel_id=1, source_target_pairs={{0,16},{16,0},{1,17},{17,1},{2,18},{18,2},{3,19},{19,3},{4,20},{20... | collective-permute-start | bytes 3145736 | tf_op jit(solution)/shard_map/ppermute | solution.py:254
  489.1 28.9 %collective-permute-start.53 = (bf16[256,2048]{1,0:T(8,128)(2,1)S(1)}, bf16[256,2048]{1,0:T(8,128)(2,1)}, u32[]{:S(2)}, u32[]{:S(2)}) collective-permute-start(bf16[256,2048]{1,0:T(8,128)(2,1)S(1)} %get-tuple-element.261), channel_id=1, source_target_pairs={{0,2},{2,0},{1,3},{3,1},{4,6},{6,4},{5,7},{7,5},{8,10},{10,8},{9,1... | collective-permute-start | bytes 3145736 | tf_op jit(solution)/shard_map/ppermute | solution.py:254
  518.0 31.2 %all-to-all-start.4 = ((bf16[4,256,512]{2,1,0:T(8,128)(2,1)}), bf16[4,256,512]{2,1,0:T(8,128)(2,1)S(1)}, u32[]{:S(2)}, u32[]{:S(2)}) async-start(bf16[4,256,512]{2,1,0:T(8,128)(2,1)} %add_convert_fusion.6), calls=%async_computation.4 | async-start | bytes 2097152 | tf_op jit(solution)/shard_map/all_to_all | solution.py:338
  523.8 25.4 %collective-permute-start.57 = (bf16[2,512,512]{2,1,0:T(8,128)(2,1)S(1)}, bf16[2,512,512]{2,1,0:T(8,128)(2,1)}, u32[]{:S(2)}, u32[]{:S(2)}) collective-permute-start(bf16[2,512,512]{2,1,0:T(8,128)(2,1)S(1)} %slice.228), channel_id=1, source_target_pairs={{0,16},{16,0},{1,17},{17,1},{2,18},{18,2},{3,19},{19,3},{4,20},{20... | collective-permute-start | bytes 3145736 | tf_op jit(solution)/shard_map/ppermute | solution.py:254
  552.7 53.3 %all-to-all-start.5 = ((bf16[4,128,2048]{2,1,0:T(8,128)(2,1)}), bf16[4,128,2048]{2,1,0:T(8,128)(2,1)}, u32[]{:S(2)}, u32[]{:S(2)}) async-start(bf16[4,128,2048]{2,1,0:T(8,128)(2,1)} %bitcast.43), calls=%async_computation.5 | async-start | bytes 4194304 | tf_op jit(solution)/shard_map/all_to_all | solution.py:338
  557.5 47.6 %collective-permute-start.60 = (bf16[4,512,512]{2,1,0:T(8,128)(2,1)}, bf16[4,512,512]{2,1,0:T(8,128)(2,1)}, u32[]{:S(2)}, u32[]{:S(2)}) collective-permute-start(bf16[4,512,512]{2,1,0:T(8,128)(2,1)} %all-to-all-done.3.gu_mine), channel_id=1, source_target_pairs={{0,16},{16,0},{1,17},{17,1},{2,18},{18,2},{3,19},{19,3},{4,20},{20... | collective-permute-start | bytes 6291464 | tf_op jit(solution)/shard_map/ppermute | solution.py:254
  559.7 35.4 %collective-permute-start.59 = (bf16[128,2048]{1,0:T(8,128)(2,1)S(1)}, bf16[128,2048]{1,0:T(8,128)(2,1)}, u32[]{:S(2)}, u32[]{:S(2)}) collective-permute-start(bf16[128,2048]{1,0:T(8,128)(2,1)S(1)} %pad_maximum_fusion.12), channel_id=1, source_target_pairs={{4,0},{6,4},{2,6},{0,2},{5,1},{7,5},{3,7},{1,3},{12,8},{14,12},{10... | collective-permute-start | bytes 1572872 | tf_op jit(solution)/shard_map/ppermute | solution.py:270
  561.4 41.4 %collective-permute-start.58 = (bf16[128,2048]{1,0:T(8,128)(2,1)S(1)}, bf16[128,2048]{1,0:T(8,128)(2,1)}, u32[]{:S(2)}, u32[]{:S(2)}) collective-permute-start(bf16[128,2048]{1,0:T(8,128)(2,1)S(1)} %pad_maximum_fusion.11), channel_id=1, source_target_pairs={{0,4},{4,6},{6,2},{2,0},{1,5},{5,7},{7,3},{3,1},{8,12},{12,14},{14... | collective-permute-start | bytes 1572872 | tf_op jit(solution)/shard_map/ppermute | solution.py:267
  606.0 52.2 %all-to-all-start.6 = ((bf16[4,512,512]{2,1,0:T(8,128)(2,1)}), bf16[4,512,512]{2,1,0:T(8,128)(2,1)}, u32[]{:S(2)}, u32[]{:S(2)}) async-start(bf16[4,512,512]{2,1,0:T(8,128)(2,1)} %add_convert_fusion), calls=%async_computation.6 | async-start | bytes 4194304 | tf_op jit(solution)/shard_map/all_to_all | solution.py:338
  610.5 24.2 %collective-permute-start.61 = (bf16[4,256,512]{2,1,0:T(8,128)(2,1)S(1)}, bf16[4,256,512]{2,1,0:T(8,128)(2,1)S(1)}, u32[]{:S(2)}, u32[]{:S(2)}) collective-permute-start(bf16[4,256,512]{2,1,0:T(8,128)(2,1)S(1)} %copy-done.10), channel_id=1, source_target_pairs={{0,16},{16,0},{1,17},{17,1},{2,18},{18,2},{3,19},{19,3},{4,20},{20... | collective-permute-start | bytes 3145736 | tf_op jit(solution)/shard_map/ppermute | solution.py:254
  659.3 29.5 %all-to-all-start.7 = ((bf16[4,256,512]{2,1,0:T(8,128)(2,1)}), bf16[4,256,512]{2,1,0:T(8,128)(2,1)}, u32[]{:S(2)}, u32[]{:S(2)}) async-start(bf16[4,256,512]{2,1,0:T(8,128)(2,1)} %bitcast.27), calls=%async_computation.7 | async-start | bytes 2097152 | tf_op jit(solution)/shard_map/all_to_all | solution.py:338
  665.9 25.0 %collective-permute-start.62 = (bf16[2,512,512]{2,1,0:T(8,128)(2,1)S(1)}, bf16[2,512,512]{2,1,0:T(8,128)(2,1)}, u32[]{:S(2)}, u32[]{:S(2)}) collective-permute-start(bf16[2,512,512]{2,1,0:T(8,128)(2,1)S(1)} %reduce_sum.102.mine_ref), channel_id=1, source_target_pairs={{0,16},{16,0},{1,17},{17,1},{2,18},{18,2},{3,19},{19,3},{4,20},{20... | collective-permute-start | bytes 3145736 | tf_op jit(solution)/shard_map/ppermute | solution.py:254
  (118 other events, 1661.5 us)

commit v5 on v4

--- a/solution.py
+++ b/solution.py
@@ -55,9 +55,10 @@
     return jnp.where(lax.broadcasted_iota(jnp.int32, (1, depth), 1) < depth // 2, -1.0, 1.0)
 
 
-def attend_kernel(rows_ref, weight_ref, cosine_ref, sine_ref, column_ref, line_ref, qkv_ref, heads_ref, logsum_ref):
+def attend_kernel(own_ref, other_ref, weight_ref, cosine_ref, sine_ref, column_ref, line_ref, qkv_ref, heads_ref, logsum_ref):
     depth = heads_ref.shape[1]
-    qkv = dot(rows_ref[...], weight_ref[:, : 3 * depth])
+    weight = weight_ref[:, : 3 * depth]
+    qkv = jnp.concatenate([dot(own_ref[...], weight), dot(other_ref[...], weight)], axis=0)
     cosine, sine = cosine_ref[...], sine_ref[...] * rope_sign(depth)
     rope = lambda w: (w * cosine + turn(w) * sine).astype(low)
     queries, key_rows = rope(qkv[:, :depth]), rope(qkv[:, depth : 2 * depth])
@@ -76,12 +77,13 @@
 
 
 def attend_back_kernel(
-    middle_ref, weight_ref, cosine_ref, sine_ref, column_ref, line_ref, qkv_ref, logsum_ref, slope_ref
+    own_ref, other_ref, weight_ref, cosine_ref, sine_ref, column_ref, line_ref, qkv_ref, logsum_ref, slope_ref
 ):
     depth = cosine_ref.shape[1]
     scaling = depth**-0.5
     queries, key_rows, values = (qkv_ref[:, i * depth : (i + 1) * depth] for i in range(3))
-    head_grad = dot(middle_ref[...], weight_ref[:, 3 * depth :]).astype(low)
+    weight = weight_ref[:, 3 * depth :]
+    head_grad = jnp.concatenate([dot(own_ref[...], weight), dot(other_ref[...], weight)], axis=0).astype(low)
     query_parts = []
     key_grad = value_grad = None
     for at in range(0, queries.shape[0], BLOCK):
@@ -138,31 +140,38 @@
     )(*lefts, *weights)
 
 
-def head_sum_kernel(rows_ref, middle_ref, slope_ref, attended_ref, out_ref):
-    parts = [dot_first(rows_ref[...], slope_ref[...]), dot_first(middle_ref[...], attended_ref[...])]
+def head_sum_kernel(rows_own, rows_other, middle_own, middle_other, slope_ref, attended_ref, out_ref):
+    half = rows_own.shape[0]
+
+    def product(own, other, right):
+        return dot_first(own[...], right[:half]) + dot_first(other[...], right[half:])
+
+    parts = [product(rows_own, rows_other, slope_ref), product(middle_own, middle_other, attended_ref)]
     out_ref[0] = jnp.concatenate(parts, axis=1).astype(low)
 
 
-def gu_sum_kernel(blocks, rows_ref, slope_ref, *out_refs):
-    rows = rows_ref[...]
+def gu_sum_kernel(blocks, first_rows, second_rows, first_slope, second_slope, *out_refs):
+    first, second = first_rows[...], second_rows[...]
     for block, out_ref in zip(blocks, out_refs):
         size = out_ref.shape[2]
-        out_ref[0] = dot_first(rows, slope_ref[:, block * size : (block + 1) * size]).astype(low)
-
-
-def down_sum_kernel(blocks, slope_ref, hidden_ref, *out_refs):
-    slope = slope_ref[...]
+        cut = slice(block * size, (block + 1) * size)
+        out_ref[0] = (dot_first(first, first_slope[:, cut]) + dot_first(second, second_slope[:, cut])).astype(low)
+
+
+def down_sum_kernel(blocks, first_slope, second_slope, first_hidden, second_hidden, *out_refs):
+    first, second = first_slope[...], second_slope[...]
     for block, out_ref in zip(blocks, out_refs):
         units = out_ref.shape[1]
-        out_ref[0] = dot_first(hidden_ref[:, block * units : (block + 1) * units], slope).astype(low)
+        cut = slice(block * units, (block + 1) * units)
+        out_ref[0] = (dot_first(first_hidden[:, cut], first) + dot_first(second_hidden[:, cut], second)).astype(low)
 
 
 def call_blocks(kernel, name, cut, held, shapes):
-    count, (length, width) = shapes[0][0], cut[0].shape
+    count = shapes[0][0]
     return pl.pallas_call(
         kernel,
         grid=(count,),
-        in_specs=[pl.BlockSpec((length, width // count), lambda i: (0, i))] * len(cut)
+        in_specs=[pl.BlockSpec((array.shape[0], array.shape[1] // count), lambda i: (0, i)) for array in cut]
         + [pl.BlockSpec(array.shape, lambda i: (0, 0)) for array in held],
         out_specs=[pl.BlockSpec((1,) + shape[1:], lambda i: (i, 0, 0)) for shape in shapes],
         out_shape=[jax.ShapeDtypeStruct(shape, low) for shape in shapes],
@@ -196,22 +205,20 @@
     )(lax.axis_index("x")[None].astype(jnp.int32), mine, theirs)
 
 
-def assemble_units_kernel(x_ref, gu_mine, down_mine, gu_theirs, down_theirs, gate_ref, up_ref, down_ref):
-    units = down_mine.shape[1]
-    mine, theirs = gu_mine[0].astype(wide), gu_theirs[0].astype(wide)
+def assemble_units_kernel(x_ref, mine_ref, theirs_ref, gate_ref, up_ref, down_ref):
+    size, units = gate_ref.shape[0], down_ref.shape[0] // HALF
+    mine, theirs = mine_ref[0].astype(wide), theirs_ref[0].astype(wide)
     first = jnp.where(x_ref[0] == 0, mine, theirs)
     second = jnp.where(x_ref[0] == 0, theirs, mine)
-    gate_ref[...] = jnp.concatenate([first[:, :units], second[:, :units]], axis=1)
-    up_ref[...] = jnp.concatenate([first[:, units:], second[:, units:]], axis=1)
-    mine, theirs = down_mine[0].astype(wide), down_theirs[0].astype(wide)
-    down_ref[:units] = jnp.where(x_ref[0] == 0, mine, theirs)
-    down_ref[units:] = jnp.where(x_ref[0] == 0, theirs, mine)
-
-
-def assemble_units(*arrays):
-    rows, units, size = arrays[1].shape
-    share = HALF * units
-    arrived = [pl.BlockSpec((1,) + array.shape[1:], lambda i, x: (i, 0, 0)) for array in arrays]
+    gate_ref[...] = jnp.concatenate([first[:size, :units], second[:size, :units]], axis=1)
+    up_ref[...] = jnp.concatenate([first[:size, units:], second[:size, units:]], axis=1)
+    down_ref[...] = jnp.concatenate([first[size:], second[size:]], axis=0)
+
+
+def assemble_units(mine, theirs):
+    rows, height, size = mine.shape
+    share = HALF * (height - size)
+    arrived = pl.BlockSpec((1, height, size), lambda i, x: (i, 0, 0))
     columns = pl.BlockSpec((size, share), lambda i, x: (0, i))
     wide_shape = jax.ShapeDtypeStruct((size, rows * share), wide)
     return pl.pallas_call(
@@ -219,14 +226,14 @@
         grid_spec=pltpu.PrefetchScalarGridSpec(
             num_scalar_prefetch=1,
             grid=(rows,),
-            in_specs=arrived,
+            in_specs=[arrived, arrived],
             out_specs=[columns, columns, pl.BlockSpec((share, size), lambda i, x: (i, 0))],
         ),
         out_shape=[wide_shape, wide_shape, jax.ShapeDtypeStruct((rows * share, size), wide)],
         compiler_params=pltpu.CompilerParams(vmem_limit_bytes=48 * 1024 * 1024),
         cost_estimate=CHEAP,
         name="assemble_units",
-    )(lax.axis_index("x")[None].astype(jnp.int32), *arrays)
+    )(lax.axis_index("x")[None].astype(jnp.int32), mine, theirs)
 
 
 def call_whole(kernel, name, shapes, *arrays):
@@ -272,11 +279,6 @@
     def place(self):
         level, side = lax.axis_index(self.axes[:-1]), lax.axis_index(self.axes[-1])
         return jnp.where(side == 0, level, self.size - 1 - level)
-
-    def slot(self, place, other, level):
-        side = place // self.half
-        spot = jnp.where((side == 0) != other, level, self.size - 1 - level)
-        return (spot - place + self.half + self.size) % self.size
 
     def gather(self, shard, waits={}):
         half, cut = self.half, shard.shape[0] // 2
@@ -325,8 +327,9 @@
     return [array[i * rows : (i + 1) * rows] for i in range(count)]
 
 
-def gather_group(ring, slots):
-    return jnp.concatenate(slots + [swap(slot, "core") for slot in slots], axis=0)
+def gather_group(slots):
+    own = jnp.concatenate(slots, axis=0)
+    return [own, swap(own, "core")]
 
 
 def scatter_group(ring, own, other, awaited=None):
@@ -397,86 +400,57 @@
     )(lax.axis_index("x")[None].astype(jnp.int32), query, key, value, out, gate, up, down)
 
 
-def mlp_kernel(place_ref, *refs):
+def mlp_kernel(*refs):
     tiles, weights = refs[:4], refs[4:-5]
-    hidden_ref, gu_slope_ref, grad_ref, rows_ref, slope_ref = refs[-5:]
+    hidden_ref, gu_slope_ref, both_ref, rows_ref, slope_ref = refs[-5:]
     parts, height, span = weights[0].shape
     units = height - span
     rows_ref[...] = jnp.concatenate([tiles[0][...], tiles[2][...]], axis=0)
     slope_ref[...] = jnp.concatenate([tiles[1][...], tiles[3][...]], axis=0)
     cuts = [slice(k * span, (k + 1) * span) for k in range(parts)]
-    totals = [None] * parts
+    totals, branches = [None] * parts, [None] * parts
     for i, weight in enumerate(weights):
         gate_up = sum(dot(rows_ref[:, cut], weight[k, :span]) for k, cut in enumerate(cuts))
         gate, up = gate_up[:, :units], gate_up[:, units:]
         sigmoid = 1.0 / (1.0 + jnp.exp(-gate))
         activated = gate * sigmoid
-        hidden_ref[:, i * units : (i + 1) * units] = (activated * up).astype(low)
+        hidden = (activated * up).astype(low)
+        hidden_ref[:, i * units : (i + 1) * units] = hidden
         hidden_grad = sum(dot_last(slope_ref[:, cut], weight[k, span:]) for k, cut in enumerate(cuts))
         gate_slope = hidden_grad * up * sigmoid * (1.0 + gate * (1.0 - sigmoid))
         gu_slope = jnp.concatenate([gate_slope, hidden_grad * activated], axis=1).astype(low)
         gu_slope_ref[:, 2 * i * units : 2 * (i + 1) * units] = gu_slope
         for k in range(parts):
-            part = dot_last(gu_slope, weight[k, :span])
+            part, branch = dot_last(gu_slope, weight[k, :span]), dot(hidden, weight[k, span:])
             totals[k] = part if i == 0 else totals[k] + part
+            branches[k] = branch if i == 0 else branches[k] + branch
+    tile = tiles[0].shape[0]
     for k, cut in enumerate(cuts):
-        grad_ref[:, cut] = totals[k].astype(low)
-
-
-def feed_forward(ring, both, weights):
+        for n in range(HALF):
+            tokens = slice(n * tile, (n + 1) * tile)
+            both_ref[2 * n * tile : (2 * n + 1) * tile, cut] = totals[k][tokens].astype(low)
+            both_ref[(2 * n + 1) * tile : 2 * (n + 1) * tile, cut] = branches[k][tokens].astype(low)
+
+
+def feed_forward(both, weights, tile):
     count, width = both.shape[0] // HALF, both.shape[1]
     parts, height, span = weights[0].shape
-    blocks, units, tile = len(weights), height - span, count // ring.size
-    pair = lambda size: pl.BlockSpec((HALF * tile, size), lambda i, place: (i, 0))
-    single = lambda n: pl.BlockSpec((tile, width), lambda i, place: (4 * i + n, 0))
-    whole = lambda array: pl.BlockSpec(
-        array.shape, lambda i, place: (0, 0, 0), pipeline_mode=pl.Buffered(buffer_count=1)
-    )
-    sizes = (blocks * units, 2 * blocks * units, width, width, width)
+    blocks, units = len(weights), height - span
+    steps = count // (HALF * tile)
+    single = lambda n: pl.BlockSpec((tile, width), lambda i: (4 * i + n, 0))
+    whole = lambda array: pl.BlockSpec(array.shape, lambda i: (0, 0, 0), pipeline_mode=pl.Buffered(buffer_count=1))
+    shapes = [(count, size) for size in (blocks * units, 2 * blocks * units, width, width, width)]
+    shapes[2] = both.shape
     return pl.pallas_call(
         mlp_kernel,
-        grid_spec=pltpu.PrefetchScalarGridSpec(
-            num_scalar_prefetch=1,
-            grid=(ring.half,),
-            in_specs=[single(n) for n in range(4)] + [whole(weight) for weight in weights],
-            out_specs=[pair(size) for size in sizes],
-        ),
-        out_shape=[jax.ShapeDtypeStruct((count, size), low) for size in sizes],
+        grid=(steps,),
+        in_specs=[single(n) for n in range(4)] + [whole(weight) for weight in weights],
+        out_specs=[pl.BlockSpec((shape[0] // steps, shape[1]), lambda i: (i, 0)) for shape in shapes],
+        out_shape=[jax.ShapeDtypeStruct(shape, low) for shape in shapes],
         compiler_params=pltpu.CompilerParams(vmem_limit_bytes=48 * 1024 * 1024),
         cost_estimate=CHEAP,
         name="feed_forward",
-    )(ring.place()[None].astype(jnp.int32), *[both] * 4, *weights)
-
-
-def down_kernel(place_ref, hidden_ref, *refs):
-    weights, out_ref = refs[:-1], refs[-1]
-    parts, height, span = weights[0].shape
-    units = height - span
-    for k in range(parts):
-        out_ref[:, k * span : (k + 1) * span] = sum(
-            dot(hidden_ref[:, i * units : (i + 1) * units], weight[k, span:]) for i, weight in enumerate(weights)
-        ).astype(low)
-
-
-def down_project(ring, hidden, downs, width, other):
-    tile = hidden.shape[0] // ring.size
-    whole = lambda array: pl.BlockSpec(
-        array.shape, lambda i, place: (0, 0, 0), pipeline_mode=pl.Buffered(buffer_count=1)
-    )
-    return pl.pallas_call(
-        down_kernel,
-        grid_spec=pltpu.PrefetchScalarGridSpec(
-            num_scalar_prefetch=1,
-            grid=(ring.half,),
-            in_specs=[pl.BlockSpec((tile, hidden.shape[1]), lambda i, place: (ring.slot(place[0], other, i), 0))]
-            + [whole(down) for down in downs],
-            out_specs=pl.BlockSpec((tile, width), lambda i, place: (i, 0)),
-        ),
-        out_shape=jax.ShapeDtypeStruct((hidden.shape[0] // HALF, width), low),
-        compiler_params=pltpu.CompilerParams(vmem_limit_bytes=48 * 1024 * 1024),
-        cost_estimate=CHEAP,
-        name="down_project",
-    )(ring.place()[None].astype(jnp.int32), hidden, *downs)
+    )(*[both] * 4, *weights)
 
 
 def on_device(
@@ -519,143 +493,134 @@
     cosine, sine_table = rope_tables(places, depth)
 
     normed_one, inverse_one = layer_norm(stream)
-    rows_one = gather_group(small_ring, small_ring.gather(normed_one.astype(low)))
+    rows_one = gather_group(small_ring.gather(normed_one.astype(low)))
     rows_one, head_mine, hidden_pieces = together(rows_one, head_mine, hidden_pieces)
     heads_weight = [head_mine.reshape(width, 4 * depth)]
     heads_weight.append(swap(heads_weight[0], "x"))
 
     hidden_mine = exchange_rows(hidden_pieces)
     hidden_theirs = swap(hidden_mine, "x")
-    length = rows_one.shape[0]
+    length = HALF * rows_one[0].shape[0]
     seen = (cosine, sine_table, places[:, None], places[None, :])
     qkv_shape = jax.ShapeDtypeStruct((length, 3 * depth), low)
     kept = []
     for weight in heads_weight:
         shapes = [qkv_shape, jax.ShapeDtypeStruct((length, depth), low), jax.ShapeDtypeStruct((length, 1), wide)]
-        kept.append(call_whole(attend_kernel, "attend", shapes, rows_one, weight, *seen))
+        kept.append(call_whole(attend_kernel, "attend", shapes, *rows_one, weight, *seen))
     heads = [part[1] for part in kept]
     out_parts = project("out_project", slice(3 * depth, 4 * depth), heads, heads_weight)
     middle = stream + scatter_group(small_ring, *out_parts, hidden_mine)
     normed_two, inverse_two = layer_norm(middle)
     both = jnp.concatenate([normed_two.astype(low), slope_low], axis=0)
-    both = jnp.concatenate(large_ring.gather(both, {4: hidden_theirs}), axis=0)
-    hidden_weight = [hidden_mine, hidden_theirs, swap(hidden_mine, "core"), swap(hidden_theirs, "core")]
-    hidden_low, gu_slope, grad_part, rows_two, slope_all = feed_forward(large_ring, both, hidden_weight)
+    slots, size = [None] * large_ring.size, large_ring.half
+    slots[size] = rising = falling = both
+    for step in range(1, size):
+        if step == size - 1:
+            rising, falling, hidden_theirs = together(rising, falling, hidden_theirs)
+            hidden_weight = [hidden_mine, hidden_theirs, swap(hidden_mine, "core"), swap(hidden_theirs, "core")]
+            inner = jnp.concatenate(slots[2:6], axis=0)
+            inner_parts = feed_forward(inner, hidden_weight, shard)
+        slots[size - step] = rising = large_ring.up(rising)
+        slots[size + step] = falling = large_ring.down(falling)
+    rising, falling, inner_parts, hidden_weight = together(rising, falling, inner_parts, hidden_weight)
+    slots[size - step], slots[size + step] = rising, falling
+    slots[0] = jnp.concatenate([large_ring.up(rising[:shard]), large_ring.down(falling[shard:])], axis=0)
+    outer = jnp.concatenate([*slots[6:], *slots[:2]], axis=0)
+    outer_parts = feed_forward(outer, hidden_weight, shard)
+    hidden_low, gu_slope, both_parts, rows_two, slope_all = map(list, zip(inner_parts, outer_parts))
 
     def gu_sums(i, left):
         kernel = functools.partial(gu_sum_kernel, (i, i + 2))
-        return call_blocks(kernel, "gu_sum", [left], [gu_slope], [(rows, block, 2 * units)] * 2)
+        return call_blocks(kernel, "gu_sum", left, gu_slope, [(rows, block, 2 * units)] * 2)
 
     def down_sums(i, left):
         kernel = functools.partial(down_sum_kernel, (i, i + 2))
-        return call_blocks(kernel, "down_sum", [left], [hidden_low], [(rows, units, block)] * 2)
-
-    parts = split_rows(grad_part, large_ring.size)
-    moving = large_ring.scatter_start(parts)
+        return call_blocks(kernel, "down_sum", left, hidden_low, [(rows, units, block)] * 2)
+
+    def slot_parts(inner, outer):
+        inner, outer = split_rows(inner, 4), split_rows(outer, 4)
+        return outer[2:] + inner + outer[:2]
+
+    moving = large_ring.scatter_start(slot_parts(*both_parts))
     gu_own, gu_other = gu_sums(1, rows_two)
-    moving, gu_own, gu_other, rows_two, slope_all, parts = together(
-        moving, gu_own, gu_other, rows_two, slope_all, parts
-    )
+    moving, gu_own, gu_other, rows_two, slope_all, both_parts = together(
+        moving, gu_own, gu_other, rows_two, slope_all, both_parts
+    )
+    parts = slot_parts(*both_parts)
     moving = large_ring.scatter_step(parts, 1, moving)
     gu_other = swap(gu_other, "core")
     gu_mine, gu_mine_other = gu_sums(0, rows_two)
-    moving, gu_own, gu_other, gu_mine, gu_mine_other, slope_all = together(
-        moving, gu_own, gu_other, gu_mine, gu_mine_other, slope_all
+    down_own, down_other = down_sums(1, slope_all)
+    moving, gu_own, gu_other, gu_mine, gu_mine_other, slope_all, down_own, down_other = together(
+        moving, gu_own, gu_other, gu_mine, gu_mine_other, slope_all, down_own, down_other
     )
 
     def chunk(own, other, k, n):
         return swap(add_low(own[k : k + n], other[k : k + n]), "x")
 
-    chunks = [chunk(gu_own, gu_other, 0, 1)]
+    chunks = [chunk(gu_own, gu_other, 0, rows // 2)]
     moving = large_ring.scatter_step(parts, 2, moving)
-    down_own, down_other = down_sums(1, slope_all)
-    moving, chunks, gu_own, gu_other, gu_mine_other, down_own, down_other, slope_all = together(
-        moving, chunks, gu_own, gu_other, gu_mine_other, down_own, down_other, slope_all
-    )
-    chunks.append(chunk(gu_own, gu_other, 1, 1))
+    down_other, gu_mine_other = swap(down_other, "core"), swap(gu_mine_other, "core")
+    down_mine, down_mine_other = down_sums(0, slope_all)
+    moving, chunks, gu_own, gu_other, gu_mine, gu_mine_other, down_own, down_other, down_mine_other = together(
+        moving, chunks, gu_own, gu_other, gu_mine, gu_mine_other, down_own, down_other, down_mine_other
+    )
+    chunks.append(chunk(gu_own, gu_other, rows // 2, rows // 2))
     moving = large_ring.scatter_step(parts, 3, moving)
-    gu_mine_other = swap(gu_mine_other, "core")
-    down_other = swap(down_other, "core")
-    down_mine, down_mine_other = down_sums(0, slope_all)
-    moving, chunks, gu_own, gu_other, gu_mine_other, down_other, down_mine, down_mine_other, hidden_low = together(
-        moving, chunks, gu_own, gu_other, gu_mine_other, down_other, down_mine, down_mine_other, hidden_low
-    )
-    grad_two = large_ring.scatter_end(parts, moving)
+    down_mine_other = swap(down_mine_other, "core")
+    gu_mine = add_low(gu_mine, gu_mine_other)
+    moving, chunks, gu_mine, down_mine, down_mine_other, down_own, down_other = together(
+        moving, chunks, gu_mine, down_mine, down_mine_other, down_own, down_other
+    )
+    grad_two, branch = split_rows(large_ring.scatter_end(parts, moving), HALF)
     middle_grad = slope_low.astype(wide) + norm_backward(normed_two, inverse_two, grad_two)
-
-    chunks.append(chunk(gu_own, gu_other, 2, 1))
+    output_low = (middle + branch).astype(low)
+
+    down_chunks = [chunk(down_own, down_other, 0, rows // 2)]
     middle_low = middle_grad.astype(low)
     slots = [None, small_ring.up(middle_low), middle_low, small_ring.down(middle_low)]
-    branch_other = down_project(large_ring, hidden_low, hidden_weight, width, True)
-    slots[1:], chunks, gu_own, gu_other, down_mine_other, branch_other, gu_mine = together(
-        slots[1:], chunks, gu_own, gu_other, down_mine_other, branch_other, gu_mine
-    )
-    chunks.append(chunk(gu_own, gu_other, 3, 1))
+    down_mine = add_low(down_mine, down_mine_other)
+    slots[1:], down_chunks, down_own, down_other, down_mine, chunks, gu_mine = together(
+        slots[1:], down_chunks, down_own, down_other, down_mine, chunks, gu_mine
+    )
+    down_chunks.append(chunk(down_own, down_other, rows // 2, rows // 2))
     cut = shard // 2
     slots[0] = jnp.concatenate([small_ring.up(slots[1][:cut]), small_ring.down(slots[3][cut:])], axis=0)
-    down_mine_other = swap(down_mine_other, "core")
-    gu_mine = add_low(gu_mine, gu_mine_other)
-    slots, chunks, down_mine_other, down_own, down_other, gu_mine = together(
-        slots, chunks, down_mine_other, down_own, down_other, gu_mine
-    )
-    down_chunks = [chunk(down_own, down_other, 0, rows // 2)]
-    middle_all = gather_group(small_ring, slots)
-    gu_total = sum_pairs(add_low(gu_mine, jnp.concatenate(chunks, axis=0)))
-    gu_got = exchange_rows(gu_total)
-    middle_all, down_chunks, down_own, down_other, branch_other = together(
-        middle_all, down_chunks, down_own, down_other, branch_other
-    )
+    gu_total = add_low(gu_mine, jnp.concatenate(chunks, axis=0))
+    slots, down_chunks, gu_total = together(slots, down_chunks, gu_total)
+    down_total = add_low(down_mine, jnp.concatenate(down_chunks, axis=0))
+    unit_got = exchange_rows(sum_pairs(jnp.concatenate([gu_total, down_total], axis=1)))
+    middle_all = gather_group(slots)
 
     def head_back(head):
         qkv, attended, logsums = kept[head]
-        arrays = (middle_all, heads_weight[head], *seen, qkv, logsums)
+        arrays = (*middle_all, heads_weight[head], *seen, qkv, logsums)
         (slope,) = call_whole(attend_back_kernel, "attend_back", [qkv_shape], *arrays)
         shape = (rows, block, 4 * depth)
-        return slope, call_blocks(head_sum_kernel, "head_sum", [rows_one, middle_all], [slope, attended], [shape])[0]
-
-    down_chunks.append(chunk(down_own, down_other, rows // 2, rows // 2))
-    branch_other = split_rows(branch_other, HALF)
-    branch_other[0] = swap(branch_other[0], "y")
+        return slope, call_blocks(head_sum_kernel, "head_sum", rows_one + middle_all, [slope, attended], [shape])[0]
+
     theirs_slope, theirs_sum = head_back(1)
-    middle_all, theirs_slope, theirs_sum, down_chunks, branch_other, hidden_low = together(
-        middle_all, theirs_slope, theirs_sum, down_chunks, branch_other, hidden_low
-    )
-    branch_other[1] = swap(branch_other[1], "y")
-    head_first = swap(theirs_sum[: rows // 2], "x")
+    middle_all, theirs_slope, theirs_sum = together(middle_all, theirs_slope, theirs_sum)
+    head_chunks = [swap(theirs_sum[: rows // 2], "x")]
     mine_slope, mine_sum = head_back(0)
     back_parts = project("qkv_back", slice(0, 3 * depth), [mine_slope, theirs_slope], heads_weight)
-    down_total = add_low(add_low(down_mine, down_mine_other), jnp.concatenate(down_chunks, axis=0))
-    back_parts, mine_sum, head_first, theirs_sum, branch_other, gu_got, down_total, hidden_low = together(
-        back_parts, mine_sum, head_first, theirs_sum, branch_other, gu_got, down_total, hidden_low
-    )
-    down_got = exchange_rows(sum_pairs(down_total))
-    head_second = swap(theirs_sum[rows // 2 :], "x")
+    back_parts, mine_sum, head_chunks, theirs_sum = together(back_parts, mine_sum, head_chunks, theirs_sum)
+    head_chunks.append(swap(theirs_sum[rows // 2 :], "x"))
     back_total = add_low(back_parts[0], swap(back_parts[1], "core"))
-    back_slots = split_rows(back_total, small_ring.size)
-    moving = small_ring.scatter_start(back_slots)
-    branch_own = down_project(large_ring, hidden_low, hidden_weight, width, False)
-    branch_half = add_low(branch_own, jnp.concatenate(branch_other, axis=0)).reshape(rows, shard, width)
-    moving, back_slots, down_got, branch_half, head_second, gu_got = together(
-        moving, back_slots, down_got, branch_half, head_second, gu_got
-    )
-    branch_got = exchange_rows(branch_half)
-    gu_theirs = swap(gu_got, "x")
-    moving = small_ring.scatter_step(back_slots, 1, moving)
-    head_total = sum_pairs(add_low(mine_sum, jnp.concatenate([head_first, head_second], axis=0)))
-    moving, head_total, branch_got, gu_theirs, down_got = together(moving, head_total, branch_got, gu_theirs, down_got)
-    head_got = exchange_rows(head_total)
-    down_theirs = swap(down_got, "x")
-    grad_one = small_ring.scatter_end(back_slots, moving)
+    back_total, mine_sum, head_chunks, unit_got = together(back_total, mine_sum, head_chunks, unit_got)
+
+    head_got = exchange_rows(sum_pairs(add_low(mine_sum, jnp.concatenate(head_chunks, axis=0))))
+    unit_theirs = swap(unit_got, "x")
+    grad_one = small_ring.scatter(split_rows(back_total, small_ring.size))
     input_low = (middle_grad + norm_backward(normed_one, inverse_one, grad_one)).astype(low)
-    output_low = (middle + jnp.sum(branch_got.astype(wide), axis=0)).astype(low)
-    head_got, down_theirs, input_low, output_low, gu_got, down_got, gu_theirs = together(
-        head_got, down_theirs, input_low, output_low, gu_got, down_got, gu_theirs
+    head_got, unit_theirs, input_low, output_low, unit_got = together(
+        head_got, unit_theirs, input_low, output_low, unit_got
     )
     head_got = head_got.reshape(rows // line, line, block, 4 * depth)
     head_mine = jnp.sum(head_got.astype(wide), axis=0).astype(low)
     head_theirs = swap(head_mine, "x")
     layer_out, input_grad = from_shards((output_low, input_low), seqs)
-    gate_grad, up_grad, down_grad = assemble_units(gu_got, down_got, gu_theirs, down_theirs)
+    gate_grad, up_grad, down_grad = assemble_units(unit_got, unit_theirs)
     layer_out, input_grad, head_mine, head_theirs = together(layer_out, input_grad, head_mine, head_theirs)
     input_grad = input_grad.astype(wide)
     query_grad, key_grad, value_grad, out_grad = assemble(head_mine, head_theirs)

time: 701 us -> 668 us (0.953)
  local copies, waits for them, and re-layouts: 55.4 us -> 22.2 us
  waiting for transfers between devices: 343 us -> 376 us
  other arithmetic: 59.7 us -> 46.6 us
  starting transfers between devices: 87.3 us -> 74.2 us
    ppermute x16, waiting for transfers between devices: 139 us -> 47.4 us  [down(): return lax.ppermute(array, self.axes, self.downward)]
    ppermute x16, waiting for transfers between devices: 32.5 us -> 119 us  [up(): return lax.ppermute(array, self.axes, self.upward)]
    unnamed x164 -> x95, local copies, waits for them, and re-layouts: 38.9 us -> 17.1 us
    ppermute x31 -> x20, waiting for transfers between devices: 104 us -> 124 us  [swap(): return lax.ppermute(array, axis, [(0, 1), (1, 0)])]
    all_to_all x8 -> x6, waiting for transfers between devices: 67.9 us -> 85.4 us  [exchange_rows(): return lax.all_to_all(array, ROW, 0, 0, tiled=True)]
    convert_element_type x22 -> x17, other arithmetic: 34.2 us -> 24.4 us  [add_low(): return (left.astype(wide) + right.astype(wide)).astype(low)]
    all_to_all x8 -> x6, starting transfers between devices: 37.1 us -> 29.8 us  [exchange_rows(): return lax.all_to_all(array, ROW, 0, 0, tiled=True)]
    ppermute x31 -> x20, starting transfers between devices: 16.8 us -> 10.8 us  [swap(): return lax.ppermute(array, axis, [(0, 1), (1, 0)])]
  transfers between devices with their start and end apart: 71 -> 58, of which waited for: 43 -> 44; matrix products, arithmetic and copies ran while one was open for 12% -> 5% of each run, Pallas kernels for 16% -> 17%
where the time goes in v5:
time: 668 us; the launch traced here: 663 us
  waiting for transfers between devices  376 us (56%)
  Pallas kernels  142 us (21%)
  starting transfers between devices  74.2 us (11%)
  other arithmetic  46.6 us (7%)
  local copies, waits for them, and re-layouts  22.2 us (3%)
    ppermute x20, waiting for transfers between devices, swap(): return lax.ppermute(array, axis, [(0, 1), (1, 0)])  124 us
    ppermute x16, waiting for transfers between devices, up(): return lax.ppermute(array, self.axes, self.upward)  119 us
    all_to_all x6, waiting for transfers between devices, exchange_rows(): return lax.all_to_all(array, ROW, 0, 0, tiled=True)  85.4 us
    ppermute x16, waiting for transfers between devices, down(): return lax.ppermute(array, self.axes, self.downward)  47.4 us
    pallas_call x2, Pallas kernels, feed_forward(): pl.pallas_call(mlp_kernel, grid=(steps,), in_specs=[single(n) for n in ra...  44.4 us
    pallas_call x6, Pallas kernels, call_blocks(): pl.pallas_call(kernel, grid=(count,), in_specs=[pl.BlockSpec((array.shape...  37.6 us
    all_to_all x6, starting transfers between devices, exchange_rows(): return lax.all_to_all(array, ROW, 0, 0, tiled=True)  29.8 us
    pallas_call x4, Pallas kernels, call_whole(): pl.pallas_call(kernel, in_specs=[whole] * len(arrays), out_specs=[whole]...  29.2 us
  transfers between devices with their start and end apart: 58, of which 44 were waited for; matrix products, arithmetic and copies ran while one was open for 5% of the time, Pallas kernels for 17%

profile of v5, /device:TPU:0, one launch (start us, length us, event | category | flops | bytes accessed | tf_op | source)
XLA Modules:
  0.0 663.5 jit_solution(17499126218709963173)
XLA Ops:
  14.6 20.3 %all-to-all-done = bf16[4,256,512]{2,1,0:T(8,128)(2,1)S(1)} async-done(((bf16[4,256,512]{2,1,0:T(8,128)(2,1)}), bf16[4,256,512]{2,1,0:T(8,128)(2,1)S(1)}, u32[]{:S(2)}, u32[]{:S(2)}) %all-to-all-start) | async-done | bytes 1048608 | tf_op jit(solution)/shard_map/all_to_all | solution.py:341
  38.7 10.9 %collective-permute-done = bf16[128,2048]{1,0:T(8,128)(2,1)S(1)} collective-permute-done((bf16[128,2048]{1,0:T(8,128)(2,1)S(1)}, bf16[128,2048]{1,0:T(8,128)(2,1)S(1)}, u32[]{:S(2)}, u32[]{:S(2)}) %collective-permute-start) | collective-permute-done | bytes 524320 | tf_op jit(solution)/shard_map/ppermute | solution.py:274
  64.8 39.1 %all-to-all-done.1 = bf16[4,512,512]{2,1,0:T(8,128)(2,1)} async-done(((bf16[4,512,512]{2,1,0:T(8,128)(2,1)}), bf16[4,512,512]{2,1,0:T(8,128)(2,1)}, u32[]{:S(2)}, u32[]{:S(2)}) %all-to-all-start.1) | async-done | bytes 2097184 | tf_op jit(solution)/shard_map/all_to_all | solution.py:341
  122.0 28.9 %collective-permute-done.5.weight_ref.refs_3_ = bf16[2048,512]{1,0:T(8,128)(2,1)} collective-permute-done((bf16[2048,512]{1,0:T(8,128)(2,1)}, bf16[2048,512]{1,0:T(8,128)(2,1)}, u32[]{:S(2)}, u32[]{:S(2)}) %collective-permute-start.5) | collective-permute-done | bytes 2097184 | tf_op jit(solution)/shard_map/ppermute | solution.py:261
  170.8 9.4 %all-to-all-done.2.refs_4_ = bf16[4,768,512]{2,1,0:T(8,128)(2,1)} async-done(((bf16[4,768,512]{2,1,0:T(8,128)(2,1)}), bf16[4,768,512]{2,1,0:T(8,128)(2,1)}, u32[]{:S(2)}, u32[]{:S(2)}) %all-to-all-start.2) | async-done | bytes 3145760 | tf_op jit(solution)/shard_map/all_to_all | solution.py:341
  190.8 9.2 %collective-permute-done.10 = bf16[128,2048]{1,0:T(8,128)(2,1)S(1)} collective-permute-done((bf16[128,2048]{1,0:T(8,128)(2,1)S(1)}, bf16[128,2048]{1,0:T(8,128)(2,1)S(1)}, u32[]{:S(2)}, u32[]{:S(2)}) %collective-permute-start.10) | collective-permute-done | bytes 524320 | tf_op jit(solution)/shard_map/ppermute | solution.py:277
  204.2 21.3 %collective-permute-done.13 = bf16[256,2048]{1,0:T(8,128)(2,1)S(1)} collective-permute-done((bf16[256,2048]{1,0:T(8,128)(2,1)S(1)}, bf16[256,2048]{1,0:T(8,128)(2,1)S(1)}, u32[]{:S(2)}, u32[]{:S(2)}) %collective-permute-start.13) | collective-permute-done | bytes 1048608 | tf_op jit(solution)/shard_map/ppermute | solution.py:274
  227.6 18.9 %collective-permute-done.14 = bf16[256,2048]{1,0:T(8,128)(2,1)S(1)} collective-permute-done((bf16[256,2048]{1,0:T(8,128)(2,1)S(1)}, bf16[256,2048]{1,0:T(8,128)(2,1)S(1)}, u32[]{:S(2)}, u32[]{:S(2)}) %collective-permute-start.14) | collective-permute-done | bytes 1048608 | tf_op jit(solution)/shard_map/ppermute | solution.py:274
  247.0 11.0 %collective-permute-done.15.refs_5_ = bf16[4,768,512]{2,1,0:T(8,128)(2,1)S(1)} collective-permute-done((bf16[4,768,512]{2,1,0:T(8,128)(2,1)}, bf16[4,768,512]{2,1,0:T(8,128)(2,1)S(1)}, u32[]{:S(2)}, u32[]{:S(2)}) %collective-permute-start.15) | collective-permute-done | bytes 3145760 | tf_op jit(solution)/shard_map/ppermute | solution.py:261
  263.8 22.1 %feed_forward.2 = (bf16[512,1024]{1,0:T(8,128)(2,1)S(1)}, bf16[512,2048]{1,0:T(8,128)(2,1)S(1)}, bf16[1024,2048]{1,0:T(8,128)(2,1)}, bf16[512,2048]{1,0:T(8,128)(2,1)S(1)}, bf16[512,2048]{1,0:T(8,128)(2,1)}) custom-call(bf16[1024,2048]{1,0:T(8,128)(2,1)} %copy-done.20, bf16[1024,2048]{1,0:T(8,128)(2,1)} %copy-done.20, bf16[1024,2048]{1,0:T(8,128)(2,1)} %copy-done.20, ...), custom_call_target="tpu_custom_call" | custom-call | flops 1 | bytes 1 | tf_op jit(solution)/shard_map/feed_forward/pallas_call | solution.py:444
  288.4 11.6 %collective-permute-done.20 = bf16[128,2048]{1,0:T(8,128)(2,1)S(1)} collective-permute-done((bf16[128,2048]{1,0:T(8,128)(2,1)S(1)}, bf16[128,2048]{1,0:T(8,128)(2,1)S(1)}, u32[]{:S(2)}, u32[]{:S(2)}) %collective-permute-start.20) | collective-permute-done | bytes 524320 | tf_op jit(solution)/shard_map/ppermute | solution.py:274
  303.5 22.3 %feed_forward.3 = (bf16[512,1024]{1,0:T(8,128)(2,1)S(1)}, bf16[512,2048]{1,0:T(8,128)(2,1)S(1)}, bf16[1024,2048]{1,0:T(8,128)(2,1)}, bf16[512,2048]{1,0:T(8,128)(2,1)S(1)}, bf16[512,2048]{1,0:T(8,128)(2,1)}) custom-call(bf16[1024,2048]{1,0:T(8,128)(2,1)} %copy-done.21, bf16[1024,2048]{1,0:T(8,128)(2,1)} %copy-done.21, bf16[1024,2048]{1,0:T(8,128)(2,1)} %copy-done.21, ...), custom_call_target="tpu_custom_call" | custom-call | flops 1 | bytes 1 | tf_op jit(solution)/shard_map/feed_forward/pallas_call | solution.py:444
  331.8 7.9 %gu_sum.2 = (bf16[4,512,512]{2,1,0:T(8,128)(2,1)S(1)}, bf16[4,512,512]{2,1,0:T(8,128)(2,1)S(1)}) custom-call(bf16[512,2048]{1,0:T(8,128)(2,1)} %copy-done.7, bf16[512,2048]{1,0:T(8,128)(2,1)} %copy-done.9, bf16[512,2048]{1,0:T(8,128)(2,1)} %copy-done.6, bf16[512,2048]{1,0:T(8,128)(2,1)} %copy-done.8), custom_call_target="tpu_custom_call" | custom-call | flops 1 | bytes 1 | tf_op jit(solution)/shard_map/gu_sum/pallas_call | solution.py:171
  347.5 7.8 %gu_sum.3 = (bf16[4,512,512]{2,1,0:T(8,128)(2,1)S(1)}, bf16[4,512,512]{2,1,0:T(8,128)(2,1)S(1)}) custom-call(bf16[512,2048]{1,0:T(8,128)(2,1)} %copy-done.7, bf16[512,2048]{1,0:T(8,128)(2,1)} %copy-done.9, bf16[512,2048]{1,0:T(8,128)(2,1)} %copy-done.6, bf16[512,2048]{1,0:T(8,128)(2,1)} %copy-done.8), custom_call_target="tpu_custom_call" | custom-call | flops 1 | bytes 1 | tf_op jit(solution)/shard_map/gu_sum/pallas_call | solution.py:171
  360.2 10.0 %collective-permute-done.24 = bf16[256,2048]{1,0:T(8,128)(2,1)S(1)} collective-permute-done((bf16[256,2048]{1,0:T(8,128)(2,1)}, bf16[256,2048]{1,0:T(8,128)(2,1)S(1)}, u32[]{:S(2)}, u32[]{:S(2)}) %collective-permute-start.24) | collective-permute-done | bytes 1048608 | tf_op jit(solution)/shard_map/ppermute | solution.py:274
  387.6 12.2 %collective-permute-done.29 = bf16[2,512,512]{2,1,0:T(8,128)(2,1)} collective-permute-done((bf16[2,512,512]{2,1,0:T(8,128)(2,1)}, bf16[2,512,512]{2,1,0:T(8,128)(2,1)}, u32[]{:S(2)}, u32[]{:S(2)}) %collective-permute-start.29) | collective-permute-done | bytes 1048608 | tf_op jit(solution)/shard_map/ppermute | solution.py:261
  417.1 15.9 %collective-permute-done.34 = bf16[2,512,512]{2,1,0:T(8,128)(2,1)S(1)} collective-permute-done((bf16[2,512,512]{2,1,0:T(8,128)(2,1)S(1)}, bf16[2,512,512]{2,1,0:T(8,128)(2,1)S(1)}, u32[]{:S(2)}, u32[]{:S(2)}) %collective-permute-start.34) | collective-permute-done | bytes 1048608 | tf_op jit(solution)/shard_map/ppermute | solution.py:261
  507.3 8.1 %qkv_back.1 = (bf16[512,2048]{1,0:T(8,128)(2,1)S(1)}, bf16[512,2048]{1,0:T(8,128)(2,1)S(1)}) custom-call(bf16[1024,384]{1,0:T(8,128)(2,1)S(1)} %attend_back.3.refs_0_.slope_ref, bf16[1024,384]{1,0:T(8,128)(2,1)S(1)} %attend_back.2.slope_ref.refs_1_, bf16[2048,512]{1,0:T(8,128)(2,1)} %bitcast.5.weight_ref.refs_2_, ...), custom_call_target="tpu_custom_call" | custom-call | flops 1 | bytes 1 | tf_op jit(solution)/shard_map/qkv_back/pallas_call | solution.py:127
  524.3 19.4 %collective-permute-done.45 = bf16[2,512,512]{2,1,0:T(8,128)(2,1)} collective-permute-done((bf16[2,512,512]{2,1,0:T(8,128)(2,1)S(1)}, bf16[2,512,512]{2,1,0:T(8,128)(2,1)}, u32[]{:S(2)}, u32[]{:S(2)}) %collective-permute-start.45) | collective-permute-done | bytes 1048608 | tf_op jit(solution)/shard_map/ppermute | solution.py:261
  558.4 36.4 %collective-permute-done.47 = bf16[64,2048]{1,0:T(8,128)(2,1)S(1)} collective-permute-done((bf16[64,2048]{1,0:T(8,128)(2,1)S(1)}, bf16[64,2048]{1,0:T(8,128)(2,1)S(1)}, u32[]{:S(2)}, u32[]{:S(2)}) %collective-permute-start.47) | collective-permute-done | bytes 262176 | tf_op jit(solution)/shard_map/ppermute | solution.py:274
  597.6 17.0 %collective-permute-done.50 = bf16[128,2048]{1,0:T(8,128)(2,1)S(1)} collective-permute-done((bf16[128,2048]{1,0:T(8,128)(2,1)S(1)}, bf16[128,2048]{1,0:T(8,128)(2,1)S(1)}, u32[]{:S(2)}, u32[]{:S(2)}) %collective-permute-start.50) | collective-permute-done | bytes 524320 | tf_op jit(solution)/shard_map/ppermute | solution.py:277
  616.5 8.7 %collective-permute-done.46.theirs_ref = bf16[4,768,512]{2,1,0:T(8,128)(2,1)} collective-permute-done((bf16[4,768,512]{2,1,0:T(8,128)(2,1)}, bf16[4,768,512]{2,1,0:T(8,128)(2,1)}, u32[]{:S(2)}, u32[]{:S(2)}) %collective-permute-start.46) | collective-permute-done | bytes 3145760 | tf_op jit(solution)/shard_map/ppermute | solution.py:261
  635.7 7.6 %assemble_units.1 = (f32[512,2048]{1,0:T(8,128)}, f32[512,2048]{1,0:T(8,128)}, f32[2048,512]{1,0:T(8,128)}) custom-call(s32[1]{0:T(128)} %bitcast.2.x_ref, bf16[4,768,512]{2,1,0:T(8,128)(2,1)} %all-to-all-done.3.mine_ref, bf16[4,768,512]{2,1,0:T(8,128)(2,1)} %collective-permute-done.46.theirs_ref), custom_call_target="tpu_custom_call" | custom-call | flops 1 | bytes 1 | tf_op jit(solution)/shard_map/assemble_units/pallas_call | solution.py:224
  643.3 13.3 %all-to-all-done.5 = bf16[4,256,512]{2,1,0:T(8,128)(2,1)S(1)} async-done(((bf16[4,256,512]{2,1,0:T(8,128)(2,1)}), bf16[4,256,512]{2,1,0:T(8,128)(2,1)S(1)}, u32[]{:S(2)}, u32[]{:S(2)}) %all-to-all-start.5) | async-done | bytes 1048608 | tf_op jit(solution)/shard_map/all_to_all | solution.py:341
  (282 shorter events, 272.0 us)
Async XLA Ops:
  2.9 32.0 %all-to-all-start = ((bf16[4,256,512]{2,1,0:T(8,128)(2,1)}), bf16[4,256,512]{2,1,0:T(8,128)(2,1)S(1)}, u32[]{:S(2)}, u32[]{:S(2)}) async-start(bf16[4,256,512]{2,1,0:T(8,128)(2,1)} %pad_maximum_fusion.1), calls=%async_computation | async-start | bytes 2097152 | tf_op jit(solution)/shard_map/all_to_all | solution.py:341
  53.2 50.7 %all-to-all-start.1 = ((bf16[4,512,512]{2,1,0:T(8,128)(2,1)}), bf16[4,512,512]{2,1,0:T(8,128)(2,1)}, u32[]{:S(2)}, u32[]{:S(2)}) async-start(bf16[4,512,512]{2,1,0:T(8,128)(2,1)} %get-tuple-element.150), calls=%async_computation.1 | async-start | bytes 4194304 | tf_op jit(solution)/shard_map/all_to_all | solution.py:341
  103.9 46.9 %collective-permute-start.5 = (bf16[2048,512]{1,0:T(8,128)(2,1)}, bf16[2048,512]{1,0:T(8,128)(2,1)}, u32[]{:S(2)}, u32[]{:S(2)}) collective-permute-start(bf16[2048,512]{1,0:T(8,128)(2,1)} %bitcast.5.weight_ref.refs_2_), channel_id=1, source_target_pairs={{0,16},{16,0},{1,17},{17,1},{2,18},{18,2},{3,19},{19,3},{4,20},{20... | collective-permute-start | bytes 6291464 | tf_op jit(solution)/shard_map/ppermute | solution.py:261
  105.4 74.8 %all-to-all-start.2 = ((bf16[4,768,512]{2,1,0:T(8,128)(2,1)}), bf16[4,768,512]{2,1,0:T(8,128)(2,1)}, u32[]{:S(2)}, u32[]{:S(2)}) async-start(bf16[4,768,512]{2,1,0:T(8,128)(2,1)} %get-tuple-element.159), calls=%async_computation.2 | async-start | bytes 6291456 | tf_op jit(solution)/shard_map/all_to_all | solution.py:341
  190.1 67.9 %collective-permute-start.15 = (bf16[4,768,512]{2,1,0:T(8,128)(2,1)}, bf16[4,768,512]{2,1,0:T(8,128)(2,1)S(1)}, u32[]{:S(2)}, u32[]{:S(2)}) collective-permute-start(bf16[4,768,512]{2,1,0:T(8,128)(2,1)} %all-to-all-done.2.refs_4_), channel_id=1, source_target_pairs={{0,16},{16,0},{1,17},{17,1},{2,18},{18,2},{3,19},{19,3},{4,20},{20... | collective-permute-start | bytes 9437192 | tf_op jit(solution)/shard_map/ppermute | solution.py:261
  227.6 33.1 %collective-permute-start.18 = (bf16[4,768,512]{2,1,0:T(8,128)(2,1)}, bf16[4,768,512]{2,1,0:T(8,128)(2,1)S(1)}, u32[]{:S(2)}, u32[]{:S(2)}) collective-permute-start(bf16[4,768,512]{2,1,0:T(8,128)(2,1)} %all-to-all-done.2.refs_4_), channel_id=1, source_target_pairs={{0,1},{1,0},{2,3},{3,2},{4,5},{5,4},{6,7},{7,6},{8,9},{9,8},{10,11... | collective-permute-start | bytes 9437192 | tf_op jit(solution)/shard_map/ppermute | solution.py:261
  258.1 27.8 %collective-permute-start.16 = (bf16[256,2048]{1,0:T(8,128)(2,1)S(1)}, bf16[256,2048]{1,0:T(8,128)(2,1)S(1)}, u32[]{:S(2)}, u32[]{:S(2)}) collective-permute-start(bf16[256,2048]{1,0:T(8,128)(2,1)S(1)} %collective-permute-done.14), channel_id=1, source_target_pairs={{0,4},{4,8},{8,12},{12,14},{14,10},{10,6},{6,2},{2,0},{1,5},{5,9},... | collective-permute-start | bytes 3145736 | tf_op jit(solution)/shard_map/ppermute | solution.py:274
  259.6 26.3 %collective-permute-start.17 = (bf16[256,2048]{1,0:T(8,128)(2,1)S(1)}, bf16[256,2048]{1,0:T(8,128)(2,1)S(1)}, u32[]{:S(2)}, u32[]{:S(2)}) collective-permute-start(bf16[256,2048]{1,0:T(8,128)(2,1)S(1)} %collective-permute-done.12), channel_id=1, source_target_pairs={{4,0},{8,4},{12,8},{14,12},{10,14},{6,10},{2,6},{0,2},{5,1},{9,5},... | collective-permute-start | bytes 3145736 | tf_op jit(solution)/shard_map/ppermute | solution.py:277
  342.8 29.7 %collective-permute-start.26 = (bf16[4,512,512]{2,1,0:T(8,128)(2,1)S(1)}, bf16[4,512,512]{2,1,0:T(8,128)(2,1)}, u32[]{:S(2)}, u32[]{:S(2)}) collective-permute-start(bf16[4,512,512]{2,1,0:T(8,128)(2,1)S(1)} %get-tuple-element.190), channel_id=1, source_target_pairs={{0,1},{1,0},{2,3},{3,2},{4,5},{5,4},{6,7},{7,6},{8,9},{9,8},{10,11... | collective-permute-start | bytes 6291464 | tf_op jit(solution)/shard_map/ppermute | solution.py:261
  344.4 25.8 %collective-permute-start.24 = (bf16[256,2048]{1,0:T(8,128)(2,1)}, bf16[256,2048]{1,0:T(8,128)(2,1)S(1)}, u32[]{:S(2)}, u32[]{:S(2)}) collective-permute-start(bf16[256,2048]{1,0:T(8,128)(2,1)} %pad_maximum_fusion.3), channel_id=1, source_target_pairs={{0,4},{4,8},{8,12},{12,14},{14,10},{10,6},{6,2},{2,0},{1,5},{5,9},... | collective-permute-start | bytes 3145736 | tf_op jit(solution)/shard_map/ppermute | solution.py:274
  347.0 25.5 %collective-permute-start.25 = (bf16[256,2048]{1,0:T(8,128)(2,1)}, bf16[256,2048]{1,0:T(8,128)(2,1)S(1)}, u32[]{:S(2)}, u32[]{:S(2)}) collective-permute-start(bf16[256,2048]{1,0:T(8,128)(2,1)} %pad_maximum_fusion.4), channel_id=1, source_target_pairs={{4,0},{8,4},{12,8},{14,12},{10,14},{6,10},{2,6},{0,2},{5,1},{9,5},... | collective-permute-start | bytes 3145736 | tf_op jit(solution)/shard_map/ppermute | solution.py:277
  375.0 24.8 %collective-permute-start.29 = (bf16[2,512,512]{2,1,0:T(8,128)(2,1)}, bf16[2,512,512]{2,1,0:T(8,128)(2,1)}, u32[]{:S(2)}, u32[]{:S(2)}) collective-permute-start(bf16[2,512,512]{2,1,0:T(8,128)(2,1)} %add_convert_fusion.10), channel_id=1, source_target_pairs={{0,16},{16,0},{1,17},{17,1},{2,18},{18,2},{3,19},{19,3},{4,20},{20... | collective-permute-start | bytes 3145736 | tf_op jit(solution)/shard_map/ppermute | solution.py:261
  375.5 31.4 %collective-permute-start.30 = (bf16[4,512,512]{2,1,0:T(8,128)(2,1)S(1)}, bf16[4,512,512]{2,1,0:T(8,128)(2,1)}, u32[]{:S(2)}, u32[]{:S(2)}) collective-permute-start(bf16[4,512,512]{2,1,0:T(8,128)(2,1)S(1)} %get-tuple-element.206), channel_id=1, source_target_pairs={{0,1},{1,0},{2,3},{3,2},{4,5},{5,4},{6,7},{7,6},{8,9},{9,8},{10,11... | collective-permute-start | bytes 6291464 | tf_op jit(solution)/shard_map/ppermute | solution.py:261
  380.7 25.8 %collective-permute-start.28 = (bf16[256,2048]{1,0:T(8,128)(2,1)}, bf16[256,2048]{1,0:T(8,128)(2,1)S(1)}, u32[]{:S(2)}, u32[]{:S(2)}) collective-permute-start(bf16[256,2048]{1,0:T(8,128)(2,1)} %add_convert_fusion.11), channel_id=1, source_target_pairs={{4,0},{8,4},{12,8},{14,12},{10,14},{6,10},{2,6},{0,2},{5,1},{9,5},... | collective-permute-start | bytes 3145736 | tf_op jit(solution)/shard_map/ppermute | solution.py:277
  381.3 25.6 %collective-permute-start.27 = (bf16[256,2048]{1,0:T(8,128)(2,1)}, bf16[256,2048]{1,0:T(8,128)(2,1)}, u32[]{:S(2)}, u32[]{:S(2)}) collective-permute-start(bf16[256,2048]{1,0:T(8,128)(2,1)} %add_convert_fusion.12), channel_id=1, source_target_pairs={{0,4},{4,8},{8,12},{12,14},{14,10},{10,6},{6,2},{2,0},{1,5},{5,9},... | collective-permute-start | bytes 3145736 | tf_op jit(solution)/shard_map/ppermute | solution.py:274
  408.4 24.6 %collective-permute-start.34 = (bf16[2,512,512]{2,1,0:T(8,128)(2,1)S(1)}, bf16[2,512,512]{2,1,0:T(8,128)(2,1)S(1)}, u32[]{:S(2)}, u32[]{:S(2)}) collective-permute-start(bf16[2,512,512]{2,1,0:T(8,128)(2,1)S(1)} %add_convert_fusion.7), channel_id=1, source_target_pairs={{0,16},{16,0},{1,17},{17,1},{2,18},{18,2},{3,19},{19,3},{4,20},{20... | collective-permute-start | bytes 3145736 | tf_op jit(solution)/shard_map/ppermute | solution.py:261
  470.5 76.5 %all-to-all-start.3 = ((bf16[4,768,512]{2,1,0:T(8,128)(2,1)}), bf16[4,768,512]{2,1,0:T(8,128)(2,1)}, u32[]{:S(2)}, u32[]{:S(2)}) async-start(bf16[4,768,512]{2,1,0:T(8,128)(2,1)} %pad_maximum_fusion), calls=%async_computation.3 | async-start | bytes 6291456 | tf_op jit(solution)/shard_map/all_to_all | solution.py:341
  492.4 25.6 %collective-permute-start.43 = (bf16[2,512,512]{2,1,0:T(8,128)(2,1)S(1)}, bf16[2,512,512]{2,1,0:T(8,128)(2,1)S(1)}, u32[]{:S(2)}, u32[]{:S(2)}) collective-permute-start(bf16[2,512,512]{2,1,0:T(8,128)(2,1)S(1)} %slice.203), channel_id=1, source_target_pairs={{0,16},{16,0},{1,17},{17,1},{2,18},{18,2},{3,19},{19,3},{4,20},{20... | collective-permute-start | bytes 3145736 | tf_op jit(solution)/shard_map/ppermute | solution.py:261
  518.0 25.7 %collective-permute-start.45 = (bf16[2,512,512]{2,1,0:T(8,128)(2,1)S(1)}, bf16[2,512,512]{2,1,0:T(8,128)(2,1)}, u32[]{:S(2)}, u32[]{:S(2)}) collective-permute-start(bf16[2,512,512]{2,1,0:T(8,128)(2,1)S(1)} %slice.204), channel_id=1, source_target_pairs={{0,16},{16,0},{1,17},{17,1},{2,18},{18,2},{3,19},{19,3},{4,20},{20... | collective-permute-start | bytes 3145736 | tf_op jit(solution)/shard_map/ppermute | solution.py:261
  550.5 66.0 %all-to-all-start.4 = ((bf16[4,512,512]{2,1,0:T(8,128)(2,1)}), bf16[4,512,512]{2,1,0:T(8,128)(2,1)}, u32[]{:S(2)}, u32[]{:S(2)}) async-start(bf16[4,512,512]{2,1,0:T(8,128)(2,1)} %add_convert_fusion), calls=%async_computation.4 | async-start | bytes 4194304 | tf_op jit(solution)/shard_map/all_to_all | solution.py:341
  555.2 70.0 %collective-permute-start.46 = (bf16[4,768,512]{2,1,0:T(8,128)(2,1)}, bf16[4,768,512]{2,1,0:T(8,128)(2,1)}, u32[]{:S(2)}, u32[]{:S(2)}) collective-permute-start(bf16[4,768,512]{2,1,0:T(8,128)(2,1)} %all-to-all-done.3.mine_ref), channel_id=1, source_target_pairs={{0,16},{16,0},{1,17},{17,1},{2,18},{18,2},{3,19},{19,3},{4,20},{20... | collective-permute-start | bytes 9437192 | tf_op jit(solution)/shard_map/ppermute | solution.py:261
  556.3 38.5 %collective-permute-start.47 = (bf16[64,2048]{1,0:T(8,128)(2,1)S(1)}, bf16[64,2048]{1,0:T(8,128)(2,1)S(1)}, u32[]{:S(2)}, u32[]{:S(2)}) collective-permute-start(bf16[64,2048]{1,0:T(8,128)(2,1)S(1)} %get-tuple-element.304), channel_id=1, source_target_pairs={{0,4},{4,6},{6,2},{2,0},{1,5},{5,7},{7,3},{3,1},{8,12},{12,14},{14... | collective-permute-start | bytes 786440 | tf_op jit(solution)/shard_map/ppermute | solution.py:274
  558.3 36.5 %collective-permute-start.49 = (bf16[64,2048]{1,0:T(8,128)(2,1)S(1)}, bf16[64,2048]{1,0:T(8,128)(2,1)S(1)}, u32[]{:S(2)}, u32[]{:S(2)}) collective-permute-start(bf16[64,2048]{1,0:T(8,128)(2,1)S(1)} %get-tuple-element.305), channel_id=1, source_target_pairs={{4,0},{6,4},{2,6},{0,2},{5,1},{7,5},{3,7},{1,3},{12,8},{14,12},{10... | collective-permute-start | bytes 786440 | tf_op jit(solution)/shard_map/ppermute | solution.py:277
  627.6 29.1 %all-to-all-start.5 = ((bf16[4,256,512]{2,1,0:T(8,128)(2,1)}), bf16[4,256,512]{2,1,0:T(8,128)(2,1)S(1)}, u32[]{:S(2)}, u32[]{:S(2)}) async-start(bf16[4,256,512]{2,1,0:T(8,128)(2,1)} %bitcast.25), calls=%async_computation.5 | async-start | bytes 2097152 | tf_op jit(solution)/shard_map/all_to_all | solution.py:341
  (75 other events, 961.6 us)

commit v6 on v5

--- a/solution.py
+++ b/solution.py
@@ -134,7 +134,7 @@
             pl.BlockSpec((tile, width), lambda i: (jnp.maximum(i - last - 1, 0), 0)),
         ],
         out_shape=[jax.ShapeDtypeStruct((count // HALF, width), low)] * HALF,
-        compiler_params=pltpu.CompilerParams(vmem_limit_bytes=48 * 1024 * 1024),
+        compiler_params=pltpu.CompilerParams(vmem_limit_bytes=12 * 1024 * 1024),
         cost_estimate=CHEAP,
         name=name,
     )(*lefts, *weights)
@@ -150,20 +150,22 @@
     out_ref[0] = jnp.concatenate(parts, axis=1).astype(low)
 
 
-def gu_sum_kernel(blocks, first_rows, second_rows, first_slope, second_slope, *out_refs):
-    first, second = first_rows[...], second_rows[...]
+def gu_sum_kernel(blocks, parts, *refs):
+    rows, slopes, out_refs = refs[:parts], refs[parts : 2 * parts], refs[2 * parts :]
+    rows = [part[...] for part in rows]
     for block, out_ref in zip(blocks, out_refs):
         size = out_ref.shape[2]
         cut = slice(block * size, (block + 1) * size)
-        out_ref[0] = (dot_first(first, first_slope[:, cut]) + dot_first(second, second_slope[:, cut])).astype(low)
-
-
-def down_sum_kernel(blocks, first_slope, second_slope, first_hidden, second_hidden, *out_refs):
-    first, second = first_slope[...], second_slope[...]
+        out_ref[0] = sum(dot_first(left, right[:, cut]) for left, right in zip(rows, slopes)).astype(low)
+
+
+def down_sum_kernel(blocks, parts, *refs):
+    slopes, hiddens, out_refs = refs[:parts], refs[parts : 2 * parts], refs[2 * parts :]
+    slopes = [part[...] for part in slopes]
     for block, out_ref in zip(blocks, out_refs):
         units = out_ref.shape[1]
         cut = slice(block * units, (block + 1) * units)
-        out_ref[0] = (dot_first(first_hidden[:, cut], first) + dot_first(second_hidden[:, cut], second)).astype(low)
+        out_ref[0] = sum(dot_first(left[:, cut], right) for left, right in zip(hiddens, slopes)).astype(low)
 
 
 def call_blocks(kernel, name, cut, held, shapes):
@@ -175,7 +177,7 @@
         + [pl.BlockSpec(array.shape, lambda i: (0, 0)) for array in held],
         out_specs=[pl.BlockSpec((1,) + shape[1:], lambda i: (i, 0, 0)) for shape in shapes],
         out_shape=[jax.ShapeDtypeStruct(shape, low) for shape in shapes],
-        compiler_params=pltpu.CompilerParams(vmem_limit_bytes=48 * 1024 * 1024),
+        compiler_params=pltpu.CompilerParams(vmem_limit_bytes=12 * 1024 * 1024),
         cost_estimate=CHEAP,
         name=name,
     )(*cut, *held)
@@ -230,7 +232,7 @@
             out_specs=[columns, columns, pl.BlockSpec((share, size), lambda i, x: (i, 0))],
         ),
         out_shape=[wide_shape, wide_shape, jax.ShapeDtypeStruct((rows * share, size), wide)],
-        compiler_params=pltpu.CompilerParams(vmem_limit_bytes=48 * 1024 * 1024),
+        compiler_params=pltpu.CompilerParams(vmem_limit_bytes=10 * 1024 * 1024),
         cost_estimate=CHEAP,
         name="assemble_units",
     )(lax.axis_index("x")[None].astype(jnp.int32), mine, theirs)
@@ -243,7 +245,7 @@
         in_specs=[whole] * len(arrays),
         out_specs=[whole] * len(shapes),
         out_shape=shapes,
-        compiler_params=pltpu.CompilerParams(vmem_limit_bytes=48 * 1024 * 1024),
+        compiler_params=pltpu.CompilerParams(vmem_limit_bytes=18 * 1024 * 1024),
         cost_estimate=CHEAP,
         name=name,
     )(*arrays)
@@ -373,12 +375,14 @@
     return lax.psum(array, "pair") if lax.axis_size("pair") > 1 else array
 
 
-def pack_kernel(x_ref, query, key, value, out, gate, up, down, head, hidden):
-    head[0] = jnp.concatenate([query[...], key[...], value[...], out[...].T], axis=1)
+def pack_kernel(x_ref, slope, query, key, value, out, gate, up, down, head, hidden):
+    weight = jnp.concatenate([query[...], key[...], value[...], out[...].T], axis=1)
+    head[0] = jnp.concatenate([weight, slope[0]], axis=0)
     hidden[0] = jnp.concatenate([jnp.concatenate([gate[...], up[...]], axis=1), down[...]], axis=0)
 
 
-def pack(query, key, value, out, gate, up, down, rows, line):
+def pack(slope, query, key, value, out, gate, up, down, line):
+    rows, shard, _ = slope.shape
     depth, block = HEAD_DIM, query.shape[0]
     units = gate.shape[1] // rows // HALF
     head_at = lambda r, x: HALF * (r % line) + x[0]
@@ -386,18 +390,19 @@
     out_in = pl.BlockSpec((depth, block), lambda r, x: (head_at(r, x), 0))
     unit_in = pl.BlockSpec((block, units), lambda r, x: (0, HALF * r + x[0]))
     down_in = pl.BlockSpec((units, block), lambda r, x: (HALF * r + x[0], 0))
-    shapes = [(block, 4 * depth), (block + units, block)]
+    slope_in = pl.BlockSpec((1, shard, block), lambda r, x: (r, 0, 0))
+    shapes = [(block + shard, 4 * depth), (block + units, block)]
     return pl.pallas_call(
         pack_kernel,
         grid_spec=pltpu.PrefetchScalarGridSpec(
             num_scalar_prefetch=1,
             grid=(rows,),
-            in_specs=[head_in, head_in, head_in, out_in, unit_in, unit_in, down_in],
+            in_specs=[slope_in, head_in, head_in, head_in, out_in, unit_in, unit_in, down_in],
             out_specs=[pl.BlockSpec((1,) + shape, lambda r, x: (r, 0, 0)) for shape in shapes],
         ),
         out_shape=[jax.ShapeDtypeStruct((rows,) + shape, low) for shape in shapes],
         name="pack_weights",
-    )(lax.axis_index("x")[None].astype(jnp.int32), query, key, value, out, gate, up, down)
+    )(lax.axis_index("x")[None].astype(jnp.int32), slope, query, key, value, out, gate, up, down)
 
 
 def mlp_kernel(*refs):
@@ -447,7 +452,7 @@
         in_specs=[single(n) for n in range(4)] + [whole(weight) for weight in weights],
         out_specs=[pl.BlockSpec((shape[0] // steps, shape[1]), lambda i: (i, 0)) for shape in shapes],
         out_shape=[jax.ShapeDtypeStruct(shape, low) for shape in shapes],
-        compiler_params=pltpu.CompilerParams(vmem_limit_bytes=48 * 1024 * 1024),
+        compiler_params=pltpu.CompilerParams(vmem_limit_bytes=30 * 1024 * 1024),
         cost_estimate=CHEAP,
         name="feed_forward",
     )(*[both] * 4, *weights)
@@ -475,13 +480,11 @@
     shard = seqs * tokens.shape[1] // rows
     pieces = [array.reshape(rows, shard, block) for array in (tokens, cotangent)]
     weights = (query_weight, key_weight, value_weight, out_weight, gate_weight, up_weight, down_weight)
-    head_pieces, hidden_pieces = pack(*weights, rows, line)
-    got = exchange_rows(jnp.concatenate(pieces, axis=1))
+    head_pieces, hidden_pieces = pack(pieces[1], *weights, line)
+    got = exchange_rows(pieces[0])
     got, head_pieces, hidden_pieces = together(got, head_pieces, hidden_pieces)
-    stream = to_shard(got[:, :shard]).astype(wide)
-    slope_low = to_shard(got[:, shard:])
-
-    head_mine = exchange_rows(head_pieces)
+    stream = to_shard(got).astype(wide)
+    head_got = exchange_rows(head_pieces)
 
     place = jnp.arange(2 * small_ring.size)
     core = (lax.axis_index("core") + place // small_ring.size) % 2
@@ -493,10 +496,12 @@
     cosine, sine_table = rope_tables(places, depth)
 
     normed_one, inverse_one = layer_norm(stream)
-    rows_one = gather_group(small_ring.gather(normed_one.astype(low)))
-    rows_one, head_mine, hidden_pieces = together(rows_one, head_mine, hidden_pieces)
-    heads_weight = [head_mine.reshape(width, 4 * depth)]
+    rows_slots = small_ring.gather(normed_one.astype(low))
+    rows_slots, head_got, hidden_pieces = together(rows_slots, head_got, hidden_pieces)
+    rows_one = gather_group(rows_slots)
+    heads_weight = [head_got[:, :block].reshape(width, 4 * depth)]
     heads_weight.append(swap(heads_weight[0], "x"))
+    slope_low = to_shard(head_got[:, block:])
 
     hidden_mine = exchange_rows(hidden_pieces)
     hidden_theirs = swap(hidden_mine, "x")
@@ -518,28 +523,31 @@
         if step == size - 1:
             rising, falling, hidden_theirs = together(rising, falling, hidden_theirs)
             hidden_weight = [hidden_mine, hidden_theirs, swap(hidden_mine, "core"), swap(hidden_theirs, "core")]
-            inner = jnp.concatenate(slots[2:6], axis=0)
-            inner_parts = feed_forward(inner, hidden_weight, shard)
+            token_parts = [feed_forward(jnp.concatenate(slots[2:4], axis=0), hidden_weight, shard)]
         slots[size - step] = rising = large_ring.up(rising)
         slots[size + step] = falling = large_ring.down(falling)
-    rising, falling, inner_parts, hidden_weight = together(rising, falling, inner_parts, hidden_weight)
+    rising, falling, token_parts, hidden_weight, slots[4:6] = together(
+        rising, falling, token_parts, hidden_weight, slots[4:6]
+    )
     slots[size - step], slots[size + step] = rising, falling
-    slots[0] = jnp.concatenate([large_ring.up(rising[:shard]), large_ring.down(falling[shard:])], axis=0)
-    outer = jnp.concatenate([*slots[6:], *slots[:2]], axis=0)
-    outer_parts = feed_forward(outer, hidden_weight, shard)
-    hidden_low, gu_slope, both_parts, rows_two, slope_all = map(list, zip(inner_parts, outer_parts))
+    last = large_ring.up(rising[:shard]), large_ring.down(falling[shard:])
+    token_parts.append(feed_forward(jnp.concatenate(slots[4:6], axis=0), hidden_weight, shard))
+    last, token_parts, hidden_weight = together(last, token_parts, hidden_weight)
+    slots[0] = jnp.concatenate(last, axis=0)
+    token_parts.append(feed_forward(jnp.concatenate([*slots[6:], *slots[:2]], axis=0), hidden_weight, shard))
+    hidden_low, gu_slope, both_parts, rows_two, slope_all = map(list, zip(*token_parts))
 
     def gu_sums(i, left):
-        kernel = functools.partial(gu_sum_kernel, (i, i + 2))
+        kernel = functools.partial(gu_sum_kernel, (i, i + 2), len(left))
         return call_blocks(kernel, "gu_sum", left, gu_slope, [(rows, block, 2 * units)] * 2)
 
     def down_sums(i, left):
-        kernel = functools.partial(down_sum_kernel, (i, i + 2))
+        kernel = functools.partial(down_sum_kernel, (i, i + 2), len(left))
         return call_blocks(kernel, "down_sum", left, hidden_low, [(rows, units, block)] * 2)
 
-    def slot_parts(inner, outer):
-        inner, outer = split_rows(inner, 4), split_rows(outer, 4)
-        return outer[2:] + inner + outer[:2]
+    def slot_parts(first, second, third):
+        third = split_rows(third, 4)
+        return third[2:] + split_rows(first, 2) + split_rows(second, 2) + third[:2]
 
     moving = large_ring.scatter_start(slot_parts(*both_parts))
     gu_own, gu_other = gu_sums(1, rows_two)
@@ -551,39 +559,40 @@
     gu_other = swap(gu_other, "core")
     gu_mine, gu_mine_other = gu_sums(0, rows_two)
     down_own, down_other = down_sums(1, slope_all)
-    moving, gu_own, gu_other, gu_mine, gu_mine_other, slope_all, down_own, down_other = together(
-        moving, gu_own, gu_other, gu_mine, gu_mine_other, slope_all, down_own, down_other
-    )
-
-    def chunk(own, other, k, n):
-        return swap(add_low(own[k : k + n], other[k : k + n]), "x")
-
-    chunks = [chunk(gu_own, gu_other, 0, rows // 2)]
+    gu_theirs = [add_low(own, other) for own, other in zip(split_rows(gu_own, HALF), split_rows(gu_other, HALF))]
+    moving, gu_theirs, gu_mine, gu_mine_other, slope_all, down_own, down_other = together(
+        moving, gu_theirs, gu_mine, gu_mine_other, slope_all, down_own, down_other
+    )
+
+    chunks = [swap(gu_theirs[0], "x")]
     moving = large_ring.scatter_step(parts, 2, moving)
     down_other, gu_mine_other = swap(down_other, "core"), swap(gu_mine_other, "core")
     down_mine, down_mine_other = down_sums(0, slope_all)
-    moving, chunks, gu_own, gu_other, gu_mine, gu_mine_other, down_own, down_other, down_mine_other = together(
-        moving, chunks, gu_own, gu_other, gu_mine, gu_mine_other, down_own, down_other, down_mine_other
-    )
-    chunks.append(chunk(gu_own, gu_other, rows // 2, rows // 2))
+    down_theirs = [
+        add_low(own, other) for own, other in zip(split_rows(down_own, HALF), split_rows(down_other, HALF))
+    ]
+    moving, chunks, gu_theirs, gu_mine, gu_mine_other, down_theirs, down_mine_other = together(
+        moving, chunks, gu_theirs, gu_mine, gu_mine_other, down_theirs, down_mine_other
+    )
+    chunks.append(swap(gu_theirs[1], "x"))
     moving = large_ring.scatter_step(parts, 3, moving)
     down_mine_other = swap(down_mine_other, "core")
     gu_mine = add_low(gu_mine, gu_mine_other)
-    moving, chunks, gu_mine, down_mine, down_mine_other, down_own, down_other = together(
-        moving, chunks, gu_mine, down_mine, down_mine_other, down_own, down_other
+    moving, chunks, gu_mine, down_mine, down_mine_other, down_theirs = together(
+        moving, chunks, gu_mine, down_mine, down_mine_other, down_theirs
     )
     grad_two, branch = split_rows(large_ring.scatter_end(parts, moving), HALF)
     middle_grad = slope_low.astype(wide) + norm_backward(normed_two, inverse_two, grad_two)
     output_low = (middle + branch).astype(low)
 
-    down_chunks = [chunk(down_own, down_other, 0, rows // 2)]
+    down_chunks = [swap(down_theirs[0], "x")]
     middle_low = middle_grad.astype(low)
     slots = [None, small_ring.up(middle_low), middle_low, small_ring.down(middle_low)]
     down_mine = add_low(down_mine, down_mine_other)
-    slots[1:], down_chunks, down_own, down_other, down_mine, chunks, gu_mine = together(
-        slots[1:], down_chunks, down_own, down_other, down_mine, chunks, gu_mine
-    )
-    down_chunks.append(chunk(down_own, down_other, rows // 2, rows // 2))
+    slots[1:], down_chunks, down_theirs, down_mine, chunks, gu_mine = together(
+        slots[1:], down_chunks, down_theirs, down_mine, chunks, gu_mine
+    )
+    down_chunks.append(swap(down_theirs[1], "x"))
     cut = shard // 2
     slots[0] = jnp.concatenate([small_ring.up(slots[1][:cut]), small_ring.down(slots[3][cut:])], axis=0)
     gu_total = add_low(gu_mine, jnp.concatenate(chunks, axis=0))

time: 668 us -> 643 us (0.963)
  other arithmetic: 46.6 us -> 29.1 us
  Pallas kernels: 142 us -> 127 us
  waiting for transfers between devices: 376 us -> 364 us
  local copies, waits for them, and re-layouts: 22.2 us -> 34.1 us
  starting transfers between devices: 74.2 us -> 83.3 us
    ppermute x16, waiting for transfers between devices: 47.4 us -> 109 us  [down(): return lax.ppermute(array, self.axes, self.downward)]
    all_to_all x6, waiting for transfers between devices: 85.4 us -> 34.4 us  [exchange_rows(): return lax.all_to_all(array, ROW, 0, 0, tiled=True)]
    ppermute x20, waiting for transfers between devices: 124 us -> 85.9 us  [swap(): return lax.ppermute(array, axis, [(0, 1), (1, 0)])]
    ppermute x16, starting transfers between devices: 17.5 us -> 33.7 us  [down(): return lax.ppermute(array, self.axes, self.downward)]
    ppermute x16, waiting for transfers between devices: 119 us -> 134 us  [up(): return lax.ppermute(array, self.axes, self.upward)]
    convert_element_type x17 -> x16, other arithmetic: 24.4 us -> 12.4 us  [add_low(): return (left.astype(wide) + right.astype(wide)).astype(low)]
    pallas_call x2 -> x3, Pallas kernels: 44.4 us -> 36.9 us  [feed_forward(): pl.pallas_call(mlp_kernel, grid=(steps,), in_specs=[single(n) for n in ra...]
    pallas_call x6, Pallas kernels: 37.6 us -> 30.6 us  [call_blocks(): pl.pallas_call(kernel, grid=(count,), in_specs=[pl.BlockSpec((array.shape...]
  transfers between devices with their start and end apart: 58 -> 58, of which waited for: 44 -> 44; matrix products, arithmetic and copies ran while one was open for 5% -> 5% of each run, Pallas kernels for 17% -> 16%
where the time goes in v6:
time: 643 us; the launch traced here: 639 us
  waiting for transfers between devices  364 us (57%)
  Pallas kernels  127 us (20%)
  starting transfers between devices  83.3 us (13%)
  local copies, waits for them, and re-layouts  34.1 us (5%)
  other arithmetic  29.1 us (5%)
    ppermute x16, waiting for transfers between devices, up(): return lax.ppermute(array, self.axes, self.upward)  134 us
    ppermute x16, waiting for transfers between devices, down(): return lax.ppermute(array, self.axes, self.downward)  109 us
    ppermute x20, waiting for transfers between devices, swap(): return lax.ppermute(array, axis, [(0, 1), (1, 0)])  85.9 us
    pallas_call x3, Pallas kernels, feed_forward(): pl.pallas_call(mlp_kernel, grid=(steps,), in_specs=[single(n) for n in ra...  36.9 us
    all_to_all x6, waiting for transfers between devices, exchange_rows(): return lax.all_to_all(array, ROW, 0, 0, tiled=True)  34.4 us
    ppermute x16, starting transfers between devices, down(): return lax.ppermute(array, self.axes, self.downward)  33.7 us
    pallas_call x6, Pallas kernels, call_blocks(): pl.pallas_call(kernel, grid=(count,), in_specs=[pl.BlockSpec((array.shape...  30.6 us
    pallas_call x4, Pallas kernels, call_whole(): pl.pallas_call(kernel, in_specs=[whole] * len(arrays), out_specs=[whole]...  30.1 us
  transfers between devices with their start and end apart: 58, of which 44 were waited for; matrix products, arithmetic and copies ran while one was open for 5% of the time, Pallas kernels for 16%

profile of v6, /device:TPU:0, one launch (start us, length us, event | category | flops | bytes accessed | tf_op | source)
XLA Modules:
  0.0 639.1 jit_solution(14065305845657269067)
XLA Ops:
  12.6 8.8 %all-to-all-done = bf16[4,128,512]{2,1,0:T(8,128)(2,1)S(1)} async-done(((bf16[4,128,512]{2,1,0:T(8,128)(2,1)}), bf16[4,128,512]{2,1,0:T(8,128)(2,1)S(1)}, u32[]{:S(2)}, u32[]{:S(2)}) %all-to-all-start) | async-done | bytes 524320 | tf_op jit(solution)/shard_map/all_to_all | solution.py:343
  28.6 38.7 %collective-permute-done.2 = bf16[128,2048]{1,0:T(8,128)(2,1)S(1)} collective-permute-done((bf16[128,2048]{1,0:T(8,128)(2,1)S(1)}, bf16[128,2048]{1,0:T(8,128)(2,1)S(1)}, u32[]{:S(2)}, u32[]{:S(2)}) %collective-permute-start.2) | collective-permute-done | bytes 524320 | tf_op jit(solution)/shard_map/ppermute | solution.py:279
  67.4 12.4 %collective-permute-start.3 = (bf16[64,2048]{1,0:T(8,128)(2,1)S(1)}, bf16[64,2048]{1,0:T(8,128)(2,1)S(1)}, u32[]{:S(2)}, u32[]{:S(2)}) collective-permute-start(bf16[64,2048]{1,0:T(8,128)(2,1)S(1)} %slice.216), channel_id=1, source_target_pairs={{4,0},{6,4},{2,6},{0,2},{5,1},{7,5},{3,7},{1,3},{12,8},{14,12},{10... | collective-permute-start | bytes 786440 | tf_op jit(solution)/shard_map/ppermute | solution.py:279
  112.6 29.4 %collective-permute-done.5.weight_ref.refs_3_ = bf16[2048,512]{1,0:T(8,128)(2,1)} collective-permute-done((bf16[2048,512]{1,0:T(8,128)(2,1)S(1)}, bf16[2048,512]{1,0:T(8,128)(2,1)}, u32[]{:S(2)}, u32[]{:S(2)}) %collective-permute-start.5) | collective-permute-done | bytes 2097184 | tf_op jit(solution)/shard_map/ppermute | solution.py:263
  142.0 7.7 %attend.3 = (bf16[1024,384]{1,0:T(8,128)(2,1)S(1)}, bf16[1024,128]{1,0:T(8,128)(2,1)S(1)}, f32[1024,1]{1,0:T(8,128)S(1)}) custom-call(bf16[512,2048]{1,0:T(8,128)(2,1)} %constant_dynamic-update-slice_fusion.own_ref.rows_own, bf16[512,2048]{1,0:T(8,128)(2,1)} %collective-permute-done.4.other_ref.rows_other, ...), custom_call_target="tpu_custom_call" | custom-call | flops 1 | bytes 1 | tf_op jit(solution)/shard_map/attend/pallas_call | solution.py:243
  162.6 9.5 %all-to-all-done.2.refs_4_ = bf16[4,768,512]{2,1,0:T(8,128)(2,1)} async-done(((bf16[4,768,512]{2,1,0:T(8,128)(2,1)}), bf16[4,768,512]{2,1,0:T(8,128)(2,1)}, u32[]{:S(2)}, u32[]{:S(2)}) %all-to-all-start.2) | async-done | bytes 3145760 | tf_op jit(solution)/shard_map/all_to_all | solution.py:343
  187.3 8.7 %collective-permute-done.10 = bf16[128,2048]{1,0:T(8,128)(2,1)S(1)} collective-permute-done((bf16[128,2048]{1,0:T(8,128)(2,1)S(1)}, bf16[128,2048]{1,0:T(8,128)(2,1)S(1)}, u32[]{:S(2)}, u32[]{:S(2)}) %collective-permute-start.10) | collective-permute-done | bytes 524320 | tf_op jit(solution)/shard_map/ppermute | solution.py:279
  200.7 21.3 %collective-permute-done.13 = bf16[256,2048]{1,0:T(8,128)(2,1)S(1)} collective-permute-done((bf16[256,2048]{1,0:T(8,128)(2,1)S(1)}, bf16[256,2048]{1,0:T(8,128)(2,1)S(1)}, u32[]{:S(2)}, u32[]{:S(2)}) %collective-permute-start.13) | collective-permute-done | bytes 1048608 | tf_op jit(solution)/shard_map/ppermute | solution.py:276
  224.1 19.5 %collective-permute-done.14 = bf16[256,2048]{1,0:T(8,128)(2,1)S(1)} collective-permute-done((bf16[256,2048]{1,0:T(8,128)(2,1)S(1)}, bf16[256,2048]{1,0:T(8,128)(2,1)S(1)}, u32[]{:S(2)}, u32[]{:S(2)}) %collective-permute-start.14) | collective-permute-done | bytes 1048608 | tf_op jit(solution)/shard_map/ppermute | solution.py:276
  244.1 11.1 %collective-permute-done.15.refs_5_ = bf16[4,768,512]{2,1,0:T(8,128)(2,1)S(1)} collective-permute-done((bf16[4,768,512]{2,1,0:T(8,128)(2,1)}, bf16[4,768,512]{2,1,0:T(8,128)(2,1)S(1)}, u32[]{:S(2)}, u32[]{:S(2)}) %collective-permute-start.15) | collective-permute-done | bytes 3145760 | tf_op jit(solution)/shard_map/ppermute | solution.py:263
  260.9 9.4 %feed_forward.3 = (bf16[256,1024]{1,0:T(8,128)(2,1)S(1)}, bf16[256,2048]{1,0:T(8,128)(2,1)S(1)}, bf16[512,2048]{1,0:T(8,128)(2,1)S(1)}, bf16[256,2048]{1,0:T(8,128)(2,1)S(1)}, bf16[256,2048]{1,0:T(8,128)(2,1)S(1)}) custom-call(bf16[512,2048]{1,0:T(8,128)(2,1)S(1)} %pad_maximum_fusion.1.refs_0_.refs_1_.refs_2_.refs_3_, ...), custom_call_target="tpu_custom_call" | custom-call | flops 1 | bytes 1 | tf_op jit(solution)/shard_map/feed_forward/pallas_call | solution.py:449
  270.3 10.5 %collective-permute-done.16 = bf16[256,2048]{1,0:T(8,128)(2,1)S(1)} collective-permute-done((bf16[256,2048]{1,0:T(8,128)(2,1)S(1)}, bf16[256,2048]{1,0:T(8,128)(2,1)S(1)}, u32[]{:S(2)}, u32[]{:S(2)}) %collective-permute-start.16) | collective-permute-done | bytes 1048608 | tf_op jit(solution)/shard_map/ppermute | solution.py:276
  284.3 9.5 %feed_forward.4 = (bf16[256,1024]{1,0:T(8,128)(2,1)S(1)}, bf16[256,2048]{1,0:T(8,128)(2,1)S(1)}, bf16[512,2048]{1,0:T(8,128)(2,1)S(1)}, bf16[256,2048]{1,0:T(8,128)(2,1)S(1)}, bf16[256,2048]{1,0:T(8,128)(2,1)S(1)}) custom-call(bf16[512,2048]{1,0:T(8,128)(2,1)S(1)} %pad_maximum_fusion.2.refs_0_.refs_1_.refs_2_.refs_3_, ...), custom_call_target="tpu_custom_call" | custom-call | flops 1 | bytes 1 | tf_op jit(solution)/shard_map/feed_forward/pallas_call | solution.py:449
  298.4 18.0 %feed_forward.5 = (bf16[512,1024]{1,0:T(8,128)(2,1)S(1)}, bf16[512,2048]{1,0:T(8,128)(2,1)S(1)}, bf16[1024,2048]{1,0:T(8,128)(2,1)S(1)}, bf16[512,2048]{1,0:T(8,128)(2,1)S(1)}, bf16[512,2048]{1,0:T(8,128)(2,1)S(1)}) custom-call(bf16[1024,2048]{1,0:T(8,128)(2,1)} %constant_dynamic-update-slice_fusion.4.refs_0_.refs_1_.refs_2_.refs_3_, ...), custom_call_target="tpu_custom_call" | custom-call | flops 1 | bytes 1 | tf_op jit(solution)/shard_map/feed_forward/pallas_call | solution.py:449
  342.2 13.8 %collective-permute-done.24 = bf16[256,2048]{1,0:T(8,128)(2,1)S(1)} collective-permute-done((bf16[256,2048]{1,0:T(8,128)(2,1)S(1)}, bf16[256,2048]{1,0:T(8,128)(2,1)S(1)}, u32[]{:S(2)}, u32[]{:S(2)}) %collective-permute-start.24) | collective-permute-done | bytes 1048608 | tf_op jit(solution)/shard_map/ppermute | solution.py:276
  364.3 18.4 %collective-permute-done.28 = bf16[256,2048]{1,0:T(8,128)(2,1)S(1)} collective-permute-done((bf16[256,2048]{1,0:T(8,128)(2,1)S(1)}, bf16[256,2048]{1,0:T(8,128)(2,1)S(1)}, u32[]{:S(2)}, u32[]{:S(2)}) %collective-permute-start.28) | collective-permute-done | bytes 1048608 | tf_op jit(solution)/shard_map/ppermute | solution.py:279
  388.9 21.0 %collective-permute-done.32 = bf16[256,2048]{1,0:T(8,128)(2,1)S(1)} collective-permute-done((bf16[256,2048]{1,0:T(8,128)(2,1)S(1)}, bf16[256,2048]{1,0:T(8,128)(2,1)S(1)}, u32[]{:S(2)}, u32[]{:S(2)}) %collective-permute-start.32) | collective-permute-done | bytes 1048608 | tf_op jit(solution)/shard_map/ppermute | solution.py:276
  418.2 8.6 %collective-permute-done.37 = bf16[128,2048]{1,0:T(8,128)(2,1)S(1)} collective-permute-done((bf16[128,2048]{1,0:T(8,128)(2,1)S(1)}, bf16[128,2048]{1,0:T(8,128)(2,1)S(1)}, u32[]{:S(2)}, u32[]{:S(2)}) %collective-permute-start.37) | collective-permute-done | bytes 524320 | tf_op jit(solution)/shard_map/ppermute | solution.py:279
  453.5 7.9 %attend_back.2.slope_ref.refs_1_ = bf16[1024,384]{1,0:T(8,128)(2,1)S(1)} custom-call(bf16[512,2048]{1,0:T(8,128)(2,1)} %constant_dynamic-update-slice_fusion.9.own_ref.middle_own, bf16[512,2048]{1,0:T(8,128)(2,1)} %collective-permute-done.42.other_ref.middle_other, bf16[2048,512]{1,0:T(8,128)(2,1)} %collective-permute-done.5.weight_ref.refs_3_, ...), custom_call_target="tpu_custom_call" | custom-call | flops 1 | bytes 1 | tf_op jit(solution)/shard_map/attend_back/pallas_call | solution.py:243
  500.7 19.6 %collective-permute-done.45 = bf16[2,512,512]{2,1,0:T(8,128)(2,1)} collective-permute-done((bf16[2,512,512]{2,1,0:T(8,128)(2,1)S(1)}, bf16[2,512,512]{2,1,0:T(8,128)(2,1)}, u32[]{:S(2)}, u32[]{:S(2)}) %collective-permute-start.45) | collective-permute-done | bytes 1048608 | tf_op jit(solution)/shard_map/ppermute | solution.py:263
  533.6 35.6 %collective-permute-done.47 = bf16[64,2048]{1,0:T(8,128)(2,1)S(1)} collective-permute-done((bf16[64,2048]{1,0:T(8,128)(2,1)S(1)}, bf16[64,2048]{1,0:T(8,128)(2,1)S(1)}, u32[]{:S(2)}, u32[]{:S(2)}) %collective-permute-start.47) | collective-permute-done | bytes 262176 | tf_op jit(solution)/shard_map/ppermute | solution.py:276
  572.1 17.0 %collective-permute-done.50 = bf16[128,2048]{1,0:T(8,128)(2,1)S(1)} collective-permute-done((bf16[128,2048]{1,0:T(8,128)(2,1)S(1)}, bf16[128,2048]{1,0:T(8,128)(2,1)S(1)}, u32[]{:S(2)}, u32[]{:S(2)}) %collective-permute-start.50) | collective-permute-done | bytes 524320 | tf_op jit(solution)/shard_map/ppermute | solution.py:279
  591.0 8.6 %collective-permute-done.46.theirs_ref = bf16[4,768,512]{2,1,0:T(8,128)(2,1)S(1)} collective-permute-done((bf16[4,768,512]{2,1,0:T(8,128)(2,1)}, bf16[4,768,512]{2,1,0:T(8,128)(2,1)S(1)}, u32[]{:S(2)}, u32[]{:S(2)}) %collective-permute-start.46) | collective-permute-done | bytes 3145760 | tf_op jit(solution)/shard_map/ppermute | solution.py:263
  616.8 14.4 %all-to-all-done.5 = bf16[4,256,512]{2,1,0:T(8,128)(2,1)} async-done(((bf16[4,256,512]{2,1,0:T(8,128)(2,1)}), bf16[4,256,512]{2,1,0:T(8,128)(2,1)}, u32[]{:S(2)}, u32[]{:S(2)}) %all-to-all-start.5) | async-done | bytes 1048608 | tf_op jit(solution)/shard_map/all_to_all | solution.py:343
  (276 shorter events, 257.4 us)
Async XLA Ops:
  21.5 65.5 %all-to-all-start.1 = ((bf16[4,640,512]{2,1,0:T(8,128)(2,1)}), bf16[4,640,512]{2,1,0:T(8,128)(2,1)S(1)}, u32[]{:S(2)}, u32[]{:S(2)}) async-start(bf16[4,640,512]{2,1,0:T(8,128)(2,1)} %get-tuple-element.177), calls=%async_computation.1 | async-start | bytes 5242880 | tf_op jit(solution)/shard_map/all_to_all | solution.py:343
  26.5 40.8 %collective-permute-start.2 = (bf16[128,2048]{1,0:T(8,128)(2,1)S(1)}, bf16[128,2048]{1,0:T(8,128)(2,1)S(1)}, u32[]{:S(2)}, u32[]{:S(2)}) collective-permute-start(bf16[128,2048]{1,0:T(8,128)(2,1)S(1)} %fusion.4), channel_id=1, source_target_pairs={{4,0},{6,4},{2,6},{0,2},{5,1},{7,5},{3,7},{1,3},{12,8},{14,12},{10... | collective-permute-start | bytes 1572872 | tf_op jit(solution)/shard_map/ppermute | solution.py:279
  28.1 51.7 %collective-permute-start = (bf16[128,2048]{1,0:T(8,128)(2,1)S(1)}, bf16[128,2048]{1,0:T(8,128)(2,1)S(1)}, u32[]{:S(2)}, u32[]{:S(2)}) collective-permute-start(bf16[128,2048]{1,0:T(8,128)(2,1)S(1)} %fusion.4), channel_id=1, source_target_pairs={{0,4},{4,6},{6,2},{2,0},{1,5},{5,7},{7,3},{3,1},{8,12},{12,14},{14... | collective-permute-start | bytes 1572872 | tf_op jit(solution)/shard_map/ppermute | solution.py:276
  93.7 48.2 %collective-permute-start.5 = (bf16[2048,512]{1,0:T(8,128)(2,1)S(1)}, bf16[2048,512]{1,0:T(8,128)(2,1)}, u32[]{:S(2)}, u32[]{:S(2)}) collective-permute-start(bf16[2048,512]{1,0:T(8,128)(2,1)S(1)} %bitcast.26), channel_id=1, source_target_pairs={{0,16},{16,0},{1,17},{17,1},{2,18},{18,2},{3,19},{19,3},{4,20},{20... | collective-permute-start | bytes 6291464 | tf_op jit(solution)/shard_map/ppermute | solution.py:263
  95.3 76.8 %all-to-all-start.2 = ((bf16[4,768,512]{2,1,0:T(8,128)(2,1)}), bf16[4,768,512]{2,1,0:T(8,128)(2,1)}, u32[]{:S(2)}, u32[]{:S(2)}) async-start(bf16[4,768,512]{2,1,0:T(8,128)(2,1)} %get-tuple-element.188), calls=%async_computation.2 | async-start | bytes 6291456 | tf_op jit(solution)/shard_map/all_to_all | solution.py:343
  186.7 68.5 %collective-permute-start.15 = (bf16[4,768,512]{2,1,0:T(8,128)(2,1)}, bf16[4,768,512]{2,1,0:T(8,128)(2,1)S(1)}, u32[]{:S(2)}, u32[]{:S(2)}) collective-permute-start(bf16[4,768,512]{2,1,0:T(8,128)(2,1)} %all-to-all-done.2.refs_4_), channel_id=1, source_target_pairs={{0,16},{16,0},{1,17},{17,1},{2,18},{18,2},{3,19},{19,3},{4,20},{20... | collective-permute-start | bytes 9437192 | tf_op jit(solution)/shard_map/ppermute | solution.py:263
  224.1 34.5 %collective-permute-start.18 = (bf16[4,768,512]{2,1,0:T(8,128)(2,1)}, bf16[4,768,512]{2,1,0:T(8,128)(2,1)S(1)}, u32[]{:S(2)}, u32[]{:S(2)}) collective-permute-start(bf16[4,768,512]{2,1,0:T(8,128)(2,1)} %all-to-all-done.2.refs_4_), channel_id=1, source_target_pairs={{0,1},{1,0},{2,3},{3,2},{4,5},{5,4},{6,7},{7,6},{8,9},{9,8},{10,11... | collective-permute-start | bytes 9437192 | tf_op jit(solution)/shard_map/ppermute | solution.py:263
  255.2 25.6 %collective-permute-start.16 = (bf16[256,2048]{1,0:T(8,128)(2,1)S(1)}, bf16[256,2048]{1,0:T(8,128)(2,1)S(1)}, u32[]{:S(2)}, u32[]{:S(2)}) collective-permute-start(bf16[256,2048]{1,0:T(8,128)(2,1)S(1)} %collective-permute-done.14), channel_id=1, source_target_pairs={{0,4},{4,8},{8,12},{12,14},{14,10},{10,6},{6,2},{2,0},{1,5},{5,9},... | collective-permute-start | bytes 3145736 | tf_op jit(solution)/shard_map/ppermute | solution.py:276
  256.6 25.3 %collective-permute-start.17 = (bf16[256,2048]{1,0:T(8,128)(2,1)S(1)}, bf16[256,2048]{1,0:T(8,128)(2,1)S(1)}, u32[]{:S(2)}, u32[]{:S(2)}) collective-permute-start(bf16[256,2048]{1,0:T(8,128)(2,1)S(1)} %collective-permute-done.12), channel_id=1, source_target_pairs={{4,0},{8,4},{12,8},{14,12},{10,14},{6,10},{2,6},{0,2},{5,1},{9,5},... | collective-permute-start | bytes 3145736 | tf_op jit(solution)/shard_map/ppermute | solution.py:279
  330.4 25.6 %collective-permute-start.24 = (bf16[256,2048]{1,0:T(8,128)(2,1)S(1)}, bf16[256,2048]{1,0:T(8,128)(2,1)S(1)}, u32[]{:S(2)}, u32[]{:S(2)}) collective-permute-start(bf16[256,2048]{1,0:T(8,128)(2,1)S(1)} %pad_maximum_fusion.4), channel_id=1, source_target_pairs={{0,4},{4,8},{8,12},{12,14},{14,10},{10,6},{6,2},{2,0},{1,5},{5,9},... | collective-permute-start | bytes 3145736 | tf_op jit(solution)/shard_map/ppermute | solution.py:276
  331.3 25.3 %collective-permute-start.25 = (bf16[256,2048]{1,0:T(8,128)(2,1)S(1)}, bf16[256,2048]{1,0:T(8,128)(2,1)S(1)}, u32[]{:S(2)}, u32[]{:S(2)}) collective-permute-start(bf16[256,2048]{1,0:T(8,128)(2,1)S(1)} %pad_maximum_fusion.5), channel_id=1, source_target_pairs={{4,0},{8,4},{12,8},{14,12},{10,14},{6,10},{2,6},{0,2},{5,1},{9,5},... | collective-permute-start | bytes 3145736 | tf_op jit(solution)/shard_map/ppermute | solution.py:279
  356.6 28.2 %collective-permute-start.30 = (bf16[4,512,512]{2,1,0:T(8,128)(2,1)S(1)}, bf16[4,512,512]{2,1,0:T(8,128)(2,1)S(1)}, u32[]{:S(2)}, u32[]{:S(2)}) collective-permute-start(bf16[4,512,512]{2,1,0:T(8,128)(2,1)S(1)} %get-tuple-element.261), channel_id=1, source_target_pairs={{0,1},{1,0},{2,3},{3,2},{4,5},{5,4},{6,7},{7,6},{8,9},{9,8},{10,11... | collective-permute-start | bytes 6291464 | tf_op jit(solution)/shard_map/ppermute | solution.py:263
  357.1 25.6 %collective-permute-start.28 = (bf16[256,2048]{1,0:T(8,128)(2,1)S(1)}, bf16[256,2048]{1,0:T(8,128)(2,1)S(1)}, u32[]{:S(2)}, u32[]{:S(2)}) collective-permute-start(bf16[256,2048]{1,0:T(8,128)(2,1)S(1)} %add_convert_fusion.9), channel_id=1, source_target_pairs={{4,0},{8,4},{12,8},{14,12},{10,14},{6,10},{2,6},{0,2},{5,1},{9,5},... | collective-permute-start | bytes 3145736 | tf_op jit(solution)/shard_map/ppermute | solution.py:279
  359.1 25.4 %collective-permute-start.27 = (bf16[256,2048]{1,0:T(8,128)(2,1)S(1)}, bf16[256,2048]{1,0:T(8,128)(2,1)S(1)}, u32[]{:S(2)}, u32[]{:S(2)}) collective-permute-start(bf16[256,2048]{1,0:T(8,128)(2,1)S(1)} %add_convert_fusion.10), channel_id=1, source_target_pairs={{0,4},{4,8},{8,12},{12,14},{14,10},{10,6},{6,2},{2,0},{1,5},{5,9},... | collective-permute-start | bytes 3145736 | tf_op jit(solution)/shard_map/ppermute | solution.py:276
  359.8 25.1 %collective-permute-start.29 = (bf16[2,512,512]{2,1,0:T(8,128)(2,1)S(1)}, bf16[2,512,512]{2,1,0:T(8,128)(2,1)S(1)}, u32[]{:S(2)}, u32[]{:S(2)}) collective-permute-start(bf16[2,512,512]{2,1,0:T(8,128)(2,1)S(1)} %get-tuple-element.258), channel_id=1, source_target_pairs={{0,16},{16,0},{1,17},{17,1},{2,18},{18,2},{3,19},{19,3},{4,20},{20... | collective-permute-start | bytes 3145736 | tf_op jit(solution)/shard_map/ppermute | solution.py:263
  385.7 24.3 %collective-permute-start.32 = (bf16[256,2048]{1,0:T(8,128)(2,1)S(1)}, bf16[256,2048]{1,0:T(8,128)(2,1)S(1)}, u32[]{:S(2)}, u32[]{:S(2)}) collective-permute-start(bf16[256,2048]{1,0:T(8,128)(2,1)S(1)} %add_convert_fusion.8), channel_id=1, source_target_pairs={{0,4},{4,8},{8,12},{12,14},{14,10},{10,6},{6,2},{2,0},{1,5},{5,9},... | collective-permute-start | bytes 3145736 | tf_op jit(solution)/shard_map/ppermute | solution.py:276
  445.4 76.6 %all-to-all-start.3 = ((bf16[4,768,512]{2,1,0:T(8,128)(2,1)}), bf16[4,768,512]{2,1,0:T(8,128)(2,1)}, u32[]{:S(2)}, u32[]{:S(2)}) async-start(bf16[4,768,512]{2,1,0:T(8,128)(2,1)} %pad_maximum_fusion), calls=%async_computation.3 | async-start | bytes 6291456 | tf_op jit(solution)/shard_map/all_to_all | solution.py:343
  467.9 25.6 %collective-permute-start.43 = (bf16[2,512,512]{2,1,0:T(8,128)(2,1)S(1)}, bf16[2,512,512]{2,1,0:T(8,128)(2,1)S(1)}, u32[]{:S(2)}, u32[]{:S(2)}) collective-permute-start(bf16[2,512,512]{2,1,0:T(8,128)(2,1)S(1)} %slice.203), channel_id=1, source_target_pairs={{0,16},{16,0},{1,17},{17,1},{2,18},{18,2},{3,19},{19,3},{4,20},{20... | collective-permute-start | bytes 3145736 | tf_op jit(solution)/shard_map/ppermute | solution.py:263
  494.6 25.7 %collective-permute-start.45 = (bf16[2,512,512]{2,1,0:T(8,128)(2,1)S(1)}, bf16[2,512,512]{2,1,0:T(8,128)(2,1)}, u32[]{:S(2)}, u32[]{:S(2)}) collective-permute-start(bf16[2,512,512]{2,1,0:T(8,128)(2,1)S(1)} %slice.204), channel_id=1, source_target_pairs={{0,16},{16,0},{1,17},{17,1},{2,18},{18,2},{3,19},{19,3},{4,20},{20... | collective-permute-start | bytes 3145736 | tf_op jit(solution)/shard_map/ppermute | solution.py:263
  525.1 65.9 %all-to-all-start.4 = ((bf16[4,512,512]{2,1,0:T(8,128)(2,1)}), bf16[4,512,512]{2,1,0:T(8,128)(2,1)}, u32[]{:S(2)}, u32[]{:S(2)}) async-start(bf16[4,512,512]{2,1,0:T(8,128)(2,1)} %add_convert_fusion), calls=%async_computation.4 | async-start | bytes 4194304 | tf_op jit(solution)/shard_map/all_to_all | solution.py:343
  529.6 70.0 %collective-permute-start.46 = (bf16[4,768,512]{2,1,0:T(8,128)(2,1)}, bf16[4,768,512]{2,1,0:T(8,128)(2,1)S(1)}, u32[]{:S(2)}, u32[]{:S(2)}) collective-permute-start(bf16[4,768,512]{2,1,0:T(8,128)(2,1)} %all-to-all-done.3.mine_ref), channel_id=1, source_target_pairs={{0,16},{16,0},{1,17},{17,1},{2,18},{18,2},{3,19},{19,3},{4,20},{20... | collective-permute-start | bytes 9437192 | tf_op jit(solution)/shard_map/ppermute | solution.py:263
  531.5 37.7 %collective-permute-start.47 = (bf16[64,2048]{1,0:T(8,128)(2,1)S(1)}, bf16[64,2048]{1,0:T(8,128)(2,1)S(1)}, u32[]{:S(2)}, u32[]{:S(2)}) collective-permute-start(bf16[64,2048]{1,0:T(8,128)(2,1)S(1)} %get-tuple-element.358), channel_id=1, source_target_pairs={{0,4},{4,6},{6,2},{2,0},{1,5},{5,7},{7,3},{3,1},{8,12},{12,14},{14... | collective-permute-start | bytes 786440 | tf_op jit(solution)/shard_map/ppermute | solution.py:276
  533.6 35.7 %collective-permute-start.49 = (bf16[64,2048]{1,0:T(8,128)(2,1)S(1)}, bf16[64,2048]{1,0:T(8,128)(2,1)S(1)}, u32[]{:S(2)}, u32[]{:S(2)}) collective-permute-start(bf16[64,2048]{1,0:T(8,128)(2,1)S(1)} %get-tuple-element.359), channel_id=1, source_target_pairs={{4,0},{6,4},{2,6},{0,2},{5,1},{7,5},{3,7},{1,3},{12,8},{14,12},{10... | collective-permute-start | bytes 786440 | tf_op jit(solution)/shard_map/ppermute | solution.py:279
  602.0 29.3 %all-to-all-start.5 = ((bf16[4,256,512]{2,1,0:T(8,128)(2,1)}), bf16[4,256,512]{2,1,0:T(8,128)(2,1)}, u32[]{:S(2)}, u32[]{:S(2)}) async-start(bf16[4,256,512]{2,1,0:T(8,128)(2,1)} %bitcast.42), calls=%async_computation.5 | async-start | bytes 2097152 | tf_op jit(solution)/shard_map/all_to_all | solution.py:343
  (73 other events, 915.2 us)

commit v7 on v6

--- a/solution.py
+++ b/solution.py
@@ -150,22 +150,24 @@
     out_ref[0] = jnp.concatenate(parts, axis=1).astype(low)
 
 
-def gu_sum_kernel(blocks, parts, *refs):
+def gu_sum_kernel(blocks, *refs):
+    parts = len(blocks)
     rows, slopes, out_refs = refs[:parts], refs[parts : 2 * parts], refs[2 * parts :]
     rows = [part[...] for part in rows]
-    for block, out_ref in zip(blocks, out_refs):
+    for n, out_ref in enumerate(out_refs):
         size = out_ref.shape[2]
-        cut = slice(block * size, (block + 1) * size)
-        out_ref[0] = sum(dot_first(left, right[:, cut]) for left, right in zip(rows, slopes)).astype(low)
-
-
-def down_sum_kernel(blocks, parts, *refs):
+        cuts = [slice(own[n] * size, (own[n] + 1) * size) for own in blocks]
+        out_ref[0] = sum(dot_first(left, right[:, cut]) for left, right, cut in zip(rows, slopes, cuts)).astype(low)
+
+
+def down_sum_kernel(blocks, *refs):
+    parts = len(blocks)
     slopes, hiddens, out_refs = refs[:parts], refs[parts : 2 * parts], refs[2 * parts :]
     slopes = [part[...] for part in slopes]
-    for block, out_ref in zip(blocks, out_refs):
+    for n, out_ref in enumerate(out_refs):
         units = out_ref.shape[1]
-        cut = slice(block * units, (block + 1) * units)
-        out_ref[0] = sum(dot_first(left[:, cut], right) for left, right in zip(hiddens, slopes)).astype(low)
+        cuts = [slice(own[n] * units, (own[n] + 1) * units) for own in blocks]
+        out_ref[0] = sum(dot_first(left[:, cut], right) for left, right, cut in zip(hiddens, slopes, cuts)).astype(low)
 
 
 def call_blocks(kernel, name, cut, held, shapes):
@@ -405,9 +407,10 @@
     )(lax.axis_index("x")[None].astype(jnp.int32), slope, query, key, value, out, gate, up, down)
 
 
-def mlp_kernel(*refs):
-    tiles, weights = refs[:4], refs[4:-5]
-    hidden_ref, gu_slope_ref, both_ref, rows_ref, slope_ref = refs[-5:]
+def mlp_kernel(blocks, *refs):
+    tiles, weights, rest = refs[:4], refs[4 : 4 + blocks], refs[4 + blocks :]
+    earlier = rest[0] if len(rest) > 5 else None
+    hidden_ref, gu_slope_ref, both_ref, rows_ref, slope_ref = rest[-5:]
     parts, height, span = weights[0].shape
     units = height - span
     rows_ref[...] = jnp.concatenate([tiles[0][...], tiles[2][...]], axis=0)
@@ -431,13 +434,15 @@
             branches[k] = branch if i == 0 else branches[k] + branch
     tile = tiles[0].shape[0]
     for k, cut in enumerate(cuts):
-        for n in range(HALF):
-            tokens = slice(n * tile, (n + 1) * tile)
-            both_ref[2 * n * tile : (2 * n + 1) * tile, cut] = totals[k][tokens].astype(low)
-            both_ref[(2 * n + 1) * tile : 2 * (n + 1) * tile, cut] = branches[k][tokens].astype(low)
-
-
-def feed_forward(both, weights, tile):
+        for n in range(2 * HALF):
+            place = slice(n * tile, (n + 1) * tile)
+            total = (branches if n % 2 else totals)[k][n // 2 * tile : (n // 2 + 1) * tile]
+            if earlier is not None:
+                total = total + earlier[place, cut].astype(wide)
+            both_ref[place, cut] = total.astype(low)
+
+
+def feed_forward(both, weights, tile, earlier=()):
     count, width = both.shape[0] // HALF, both.shape[1]
     parts, height, span = weights[0].shape
     blocks, units = len(weights), height - span
@@ -447,15 +452,17 @@
     shapes = [(count, size) for size in (blocks * units, 2 * blocks * units, width, width, width)]
     shapes[2] = both.shape
     return pl.pallas_call(
-        mlp_kernel,
+        functools.partial(mlp_kernel, blocks),
         grid=(steps,),
-        in_specs=[single(n) for n in range(4)] + [whole(weight) for weight in weights],
+        in_specs=[single(n) for n in range(4)]
+        + [whole(weight) for weight in weights]
+        + [pl.BlockSpec((array.shape[0] // steps, width), lambda i: (i, 0)) for array in earlier],
         out_specs=[pl.BlockSpec((shape[0] // steps, shape[1]), lambda i: (i, 0)) for shape in shapes],
         out_shape=[jax.ShapeDtypeStruct(shape, low) for shape in shapes],
         compiler_params=pltpu.CompilerParams(vmem_limit_bytes=30 * 1024 * 1024),
         cost_estimate=CHEAP,
         name="feed_forward",
-    )(*[both] * 4, *weights)
+    )(*[both] * 4, *weights, *earlier)
 
 
 def on_device(
@@ -519,86 +526,76 @@
     both = jnp.concatenate([normed_two.astype(low), slope_low], axis=0)
     slots, size = [None] * large_ring.size, large_ring.half
     slots[size] = rising = falling = both
+    hidden_mine = [hidden_mine, swap(hidden_mine, "core")]
     for step in range(1, size):
-        if step == size - 1:
-            rising, falling, hidden_theirs = together(rising, falling, hidden_theirs)
-            hidden_weight = [hidden_mine, hidden_theirs, swap(hidden_mine, "core"), swap(hidden_theirs, "core")]
-            token_parts = [feed_forward(jnp.concatenate(slots[2:4], axis=0), hidden_weight, shard)]
         slots[size - step] = rising = large_ring.up(rising)
         slots[size + step] = falling = large_ring.down(falling)
-    rising, falling, token_parts, hidden_weight, slots[4:6] = together(
-        rising, falling, token_parts, hidden_weight, slots[4:6]
-    )
+        if step < size - 1:
+            rising, falling, hidden_mine = together(rising, falling, hidden_mine)
+            slots[size - step], slots[size + step] = rising, falling
+    inner = jnp.concatenate(slots[2:6], axis=0)
+    inner_mine = feed_forward(inner, hidden_mine, shard)
+    rising, falling, inner_mine, inner, hidden_theirs = together(rising, falling, inner_mine, inner, hidden_theirs)
     slots[size - step], slots[size + step] = rising, falling
     last = large_ring.up(rising[:shard]), large_ring.down(falling[shard:])
-    token_parts.append(feed_forward(jnp.concatenate(slots[4:6], axis=0), hidden_weight, shard))
-    last, token_parts, hidden_weight = together(last, token_parts, hidden_weight)
+    hidden_theirs = [hidden_theirs, swap(hidden_theirs, "core")]
+    inner_theirs = feed_forward(inner, hidden_theirs, shard, inner_mine[2:3])
+    last, inner_theirs, hidden_mine, hidden_theirs = together(last, inner_theirs, hidden_mine, hidden_theirs)
     slots[0] = jnp.concatenate(last, axis=0)
-    token_parts.append(feed_forward(jnp.concatenate([*slots[6:], *slots[:2]], axis=0), hidden_weight, shard))
-    hidden_low, gu_slope, both_parts, rows_two, slope_all = map(list, zip(*token_parts))
-
-    def gu_sums(i, left):
-        kernel = functools.partial(gu_sum_kernel, (i, i + 2), len(left))
-        return call_blocks(kernel, "gu_sum", left, gu_slope, [(rows, block, 2 * units)] * 2)
-
-    def down_sums(i, left):
-        kernel = functools.partial(down_sum_kernel, (i, i + 2), len(left))
-        return call_blocks(kernel, "down_sum", left, hidden_low, [(rows, units, block)] * 2)
-
-    def slot_parts(first, second, third):
-        third = split_rows(third, 4)
-        return third[2:] + split_rows(first, 2) + split_rows(second, 2) + third[:2]
+    outer = feed_forward(jnp.concatenate([*slots[6:], *slots[:2]], axis=0), hidden_mine + hidden_theirs, shard)
+    both_parts, rows_two, slope_all = [inner_theirs[2], outer[2]], [inner_mine[3], outer[3]], [inner_mine[4], outer[4]]
+
+    def gu_sums(inner_part, outer_at, left):
+        kernel = functools.partial(gu_sum_kernel, ((0, 1), (outer_at, outer_at + 1)))
+        return call_blocks(kernel, "gu_sum", left, [inner_part[1], outer[1]], [(rows, block, 2 * units)] * 2)
+
+    def down_sums(inner_part, outer_at, left):
+        kernel = functools.partial(down_sum_kernel, ((0, 1), (outer_at, outer_at + 1)))
+        return call_blocks(kernel, "down_sum", left, [inner_part[0], outer[0]], [(rows, units, block)] * 2)
+
+    def slot_parts(inner, outer):
+        outer = split_rows(outer, 4)
+        return outer[2:] + split_rows(inner, 4) + outer[:2]
 
     moving = large_ring.scatter_start(slot_parts(*both_parts))
-    gu_own, gu_other = gu_sums(1, rows_two)
+    gu_own, gu_other = gu_sums(inner_theirs, HALF, rows_two)
     moving, gu_own, gu_other, rows_two, slope_all, both_parts = together(
         moving, gu_own, gu_other, rows_two, slope_all, both_parts
     )
     parts = slot_parts(*both_parts)
+    gu_other = swap(gu_other, "core")
+    gu_theirs = [add_low(own, other) for own, other in zip(split_rows(gu_own, HALF), split_rows(gu_other, HALF))]
+    moving, gu_theirs, rows_two, slope_all = together(moving, gu_theirs, rows_two, slope_all)
+
+    chunks = [swap(gu_theirs[0], "x")]
     moving = large_ring.scatter_step(parts, 1, moving)
-    gu_other = swap(gu_other, "core")
-    gu_mine, gu_mine_other = gu_sums(0, rows_two)
-    down_own, down_other = down_sums(1, slope_all)
-    gu_theirs = [add_low(own, other) for own, other in zip(split_rows(gu_own, HALF), split_rows(gu_other, HALF))]
-    moving, gu_theirs, gu_mine, gu_mine_other, slope_all, down_own, down_other = together(
-        moving, gu_theirs, gu_mine, gu_mine_other, slope_all, down_own, down_other
-    )
-
-    chunks = [swap(gu_theirs[0], "x")]
-    moving = large_ring.scatter_step(parts, 2, moving)
-    down_other, gu_mine_other = swap(down_other, "core"), swap(gu_mine_other, "core")
-    down_mine, down_mine_other = down_sums(0, slope_all)
-    down_theirs = [
-        add_low(own, other) for own, other in zip(split_rows(down_own, HALF), split_rows(down_other, HALF))
-    ]
-    moving, chunks, gu_theirs, gu_mine, gu_mine_other, down_theirs, down_mine_other = together(
-        moving, chunks, gu_theirs, gu_mine, gu_mine_other, down_theirs, down_mine_other
+    gu_mine, gu_mine_other = gu_sums(inner_mine, 0, rows_two)
+    down_own, down_other = down_sums(inner_theirs, HALF, slope_all)
+    moving, chunks, gu_theirs, gu_mine, gu_mine_other, slope_all, down_own, down_other = together(
+        moving, chunks, gu_theirs, gu_mine, gu_mine_other, slope_all, down_own, down_other
     )
     chunks.append(swap(gu_theirs[1], "x"))
+    moving = large_ring.scatter_step(parts, 2, moving)
+    down_other = swap(down_other, "core")
+    down_mine, down_mine_other = down_sums(inner_mine, 0, slope_all)
+    down_theirs = add_low(down_own, down_other)
+    gu_mine_other = swap(gu_mine_other, "core")
+    moving, chunks, gu_mine, gu_mine_other, down_theirs, down_mine, down_mine_other = together(
+        moving, chunks, gu_mine, gu_mine_other, down_theirs, down_mine, down_mine_other
+    )
+    down_theirs = swap(down_theirs, "x")
     moving = large_ring.scatter_step(parts, 3, moving)
-    down_mine_other = swap(down_mine_other, "core")
-    gu_mine = add_low(gu_mine, gu_mine_other)
-    moving, chunks, gu_mine, down_mine, down_mine_other, down_theirs = together(
-        moving, chunks, gu_mine, down_mine, down_mine_other, down_theirs
-    )
+    down_mine = add_low(down_mine, swap(down_mine_other, "core"))
+    gu_total = add_low(add_low(gu_mine, gu_mine_other), jnp.concatenate(chunks, axis=0))
+    moving, gu_total, down_mine, down_theirs = together(moving, gu_total, down_mine, down_theirs)
     grad_two, branch = split_rows(large_ring.scatter_end(parts, moving), HALF)
     middle_grad = slope_low.astype(wide) + norm_backward(normed_two, inverse_two, grad_two)
     output_low = (middle + branch).astype(low)
 
-    down_chunks = [swap(down_theirs[0], "x")]
-    middle_low = middle_grad.astype(low)
-    slots = [None, small_ring.up(middle_low), middle_low, small_ring.down(middle_low)]
-    down_mine = add_low(down_mine, down_mine_other)
-    slots[1:], down_chunks, down_theirs, down_mine, chunks, gu_mine = together(
-        slots[1:], down_chunks, down_theirs, down_mine, chunks, gu_mine
-    )
-    down_chunks.append(swap(down_theirs[1], "x"))
-    cut = shard // 2
-    slots[0] = jnp.concatenate([small_ring.up(slots[1][:cut]), small_ring.down(slots[3][cut:])], axis=0)
-    gu_total = add_low(gu_mine, jnp.concatenate(chunks, axis=0))
-    slots, down_chunks, gu_total = together(slots, down_chunks, gu_total)
-    down_total = add_low(down_mine, jnp.concatenate(down_chunks, axis=0))
-    unit_got = exchange_rows(sum_pairs(jnp.concatenate([gu_total, down_total], axis=1)))
+    slots = small_ring.gather(middle_grad.astype(low))
+    unit_total = jnp.concatenate([gu_total, add_low(down_mine, down_theirs)], axis=1)
+    slots, unit_total = together(slots, unit_total)
+    unit_got = exchange_rows(sum_pairs(unit_total))
     middle_all = gather_group(slots)
 
     def head_back(head):

time: 643 us -> 623 us (0.969)
  starting transfers between devices: 83.3 us -> 70.8 us
  waiting for transfers between devices: 364 us -> 354 us
    ppermute x16, waiting for transfers between devices: 134 us -> 200 us  [up(): return lax.ppermute(array, self.axes, self.upward)]
    ppermute x16, waiting for transfers between devices: 109 us -> 49.5 us  [down(): return lax.ppermute(array, self.axes, self.downward)]
    ppermute x16, starting transfers between devices: 33.7 us -> 16.6 us  [down(): return lax.ppermute(array, self.axes, self.downward)]
    ppermute x20 -> x19, waiting for transfers between devices: 85.9 us -> 71.6 us  [swap(): return lax.ppermute(array, axis, [(0, 1), (1, 0)])]
    unnamed x89 -> x96, local copies, waits for them, and re-layouts: 22.9 us -> 24.7 us
  transfers between devices with their start and end apart: 58 -> 57, of which waited for: 44 -> 42; matrix products, arithmetic and copies ran while one was open for 5% -> 5% of each run, Pallas kernels for 16% -> 17%
where the time goes in v7:
time: 623 us; the launch traced here: 619 us
  waiting for transfers between devices  354 us (57%)
  Pallas kernels  127 us (20%)
  starting transfers between devices  70.8 us (11%)
  local copies, waits for them, and re-layouts  36.3 us (6%)
  other arithmetic  28.8 us (5%)
    ppermute x16, waiting for transfers between devices, up(): return lax.ppermute(array, self.axes, self.upward)  200 us
    ppermute x19, waiting for transfers between devices, swap(): return lax.ppermute(array, axis, [(0, 1), (1, 0)])  71.6 us
    ppermute x16, waiting for transfers between devices, down(): return lax.ppermute(array, self.axes, self.downward)  49.5 us
    pallas_call x3, Pallas kernels, feed_forward(): pl.pallas_call(functools.partial(mlp_kernel, blocks), grid=(steps,), in_s...  35.5 us
    all_to_all x6, waiting for transfers between devices, exchange_rows(): return lax.all_to_all(array, ROW, 0, 0, tiled=True)  33.5 us
    pallas_call x6, Pallas kernels, call_blocks(): pl.pallas_call(kernel, grid=(count,), in_specs=[pl.BlockSpec((array.shape...  30.9 us
    pallas_call x4, Pallas kernels, call_whole(): pl.pallas_call(kernel, in_specs=[whole] * len(arrays), out_specs=[whole]...  30.3 us
    all_to_all x6, starting transfers between devices, exchange_rows(): return lax.all_to_all(array, ROW, 0, 0, tiled=True)  29.4 us
  transfers between devices with their start and end apart: 57, of which 42 were waited for; matrix products, arithmetic and copies ran while one was open for 5% of the time, Pallas kernels for 17%

profile of v7, /device:TPU:0, one launch (start us, length us, event | category | flops | bytes accessed | tf_op | source)
XLA Modules:
  0.0 618.8 jit_solution(10284870579357889007)
XLA Ops:
  12.6 8.8 %all-to-all-done = bf16[4,128,512]{2,1,0:T(8,128)(2,1)S(1)} async-done(((bf16[4,128,512]{2,1,0:T(8,128)(2,1)}), bf16[4,128,512]{2,1,0:T(8,128)(2,1)S(1)}, u32[]{:S(2)}, u32[]{:S(2)}) %all-to-all-start) | async-done | bytes 524320 | tf_op jit(solution)/shard_map/all_to_all | solution.py:345
  29.0 50.1 %collective-permute-done = bf16[128,2048]{1,0:T(8,128)(2,1)S(1)} collective-permute-done((bf16[128,2048]{1,0:T(8,128)(2,1)S(1)}, bf16[128,2048]{1,0:T(8,128)(2,1)S(1)}, u32[]{:S(2)}, u32[]{:S(2)}) %collective-permute-start) | collective-permute-done | bytes 524320 | tf_op jit(solution)/shard_map/ppermute | solution.py:278
  104.7 7.3 %attend.2 = (bf16[1024,384]{1,0:T(8,128)(2,1)S(1)}, bf16[1024,128]{1,0:T(8,128)(2,1)S(1)}, f32[1024,1]{1,0:T(8,128)S(1)}) custom-call(bf16[512,2048]{1,0:T(8,128)(2,1)} %constant_dynamic-update-slice_fusion.own_ref.rows_own, bf16[512,2048]{1,0:T(8,128)(2,1)} %collective-permute-done.4.other_ref.rows_other, bf16[2048,512]{1,0:T(8,128)(2,1)S(1)} %bitcast.27, ...), custom_call_target="tpu_custom_call" | custom-call | flops 1 | bytes 1 | tf_op jit(solution)/shard_map/attend/pallas_call | solution.py:245
  113.7 30.2 %collective-permute-done.5.weight_ref.refs_3_ = bf16[2048,512]{1,0:T(8,128)(2,1)} collective-permute-done((bf16[2048,512]{1,0:T(8,128)(2,1)S(1)}, bf16[2048,512]{1,0:T(8,128)(2,1)}, u32[]{:S(2)}, u32[]{:S(2)}) %collective-permute-start.5) | collective-permute-done | bytes 2097184 | tf_op jit(solution)/shard_map/ppermute | solution.py:265
  143.9 7.8 %attend.3 = (bf16[1024,384]{1,0:T(8,128)(2,1)S(1)}, bf16[1024,128]{1,0:T(8,128)(2,1)S(1)}, f32[1024,1]{1,0:T(8,128)S(1)}) custom-call(bf16[512,2048]{1,0:T(8,128)(2,1)} %constant_dynamic-update-slice_fusion.own_ref.rows_own, bf16[512,2048]{1,0:T(8,128)(2,1)} %collective-permute-done.4.other_ref.rows_other, ...), custom_call_target="tpu_custom_call" | custom-call | flops 1 | bytes 1 | tf_op jit(solution)/shard_map/attend/pallas_call | solution.py:245
  164.4 9.1 %all-to-all-done.2.refs_4_ = bf16[4,768,512]{2,1,0:T(8,128)(2,1)} async-done(((bf16[4,768,512]{2,1,0:T(8,128)(2,1)}), bf16[4,768,512]{2,1,0:T(8,128)(2,1)}, u32[]{:S(2)}, u32[]{:S(2)}) %all-to-all-start.2) | async-done | bytes 3145760 | tf_op jit(solution)/shard_map/all_to_all | solution.py:345
  186.2 9.1 %collective-permute-done.8 = bf16[128,2048]{1,0:T(8,128)(2,1)S(1)} collective-permute-done((bf16[128,2048]{1,0:T(8,128)(2,1)S(1)}, bf16[128,2048]{1,0:T(8,128)(2,1)S(1)}, u32[]{:S(2)}, u32[]{:S(2)}) %collective-permute-start.8) | collective-permute-done | bytes 524320 | tf_op jit(solution)/shard_map/ppermute | solution.py:278
  199.2 20.5 %collective-permute-done.11 = bf16[256,2048]{1,0:T(8,128)(2,1)S(1)} collective-permute-done((bf16[256,2048]{1,0:T(8,128)(2,1)S(1)}, bf16[256,2048]{1,0:T(8,128)(2,1)S(1)}, u32[]{:S(2)}, u32[]{:S(2)}) %collective-permute-start.11) | collective-permute-done | bytes 1048608 | tf_op jit(solution)/shard_map/ppermute | solution.py:278
  223.1 19.9 %collective-permute-done.14 = bf16[256,2048]{1,0:T(8,128)(2,1)S(1)} collective-permute-done((bf16[256,2048]{1,0:T(8,128)(2,1)S(1)}, bf16[256,2048]{1,0:T(8,128)(2,1)S(1)}, u32[]{:S(2)}, u32[]{:S(2)}) %collective-permute-start.14) | collective-permute-done | bytes 1048608 | tf_op jit(solution)/shard_map/ppermute | solution.py:278
  246.9 9.3 %feed_forward.3 = (bf16[512,512]{1,0:T(8,128)(2,1)S(1)}, bf16[512,1024]{1,0:T(8,128)(2,1)S(1)}, bf16[1024,2048]{1,0:T(8,128)(2,1)S(1)}, bf16[512,2048]{1,0:T(8,128)(2,1)S(1)}, bf16[512,2048]{1,0:T(8,128)(2,1)S(1)}) custom-call(bf16[1024,2048]{1,0:T(8,128)(2,1)S(1)} %constant_dynamic-update-slice_fusion.4.refs_0_.refs_1_.refs_2_.refs_3_, ...), custom_call_target="tpu_custom_call" | custom-call | flops 1 | bytes 1 | tf_op jit(solution)/shard_map/feed_forward/pallas_call | solution.py:454
  271.8 7.8 %feed_forward.4 = (bf16[512,512]{1,0:T(8,128)(2,1)S(1)}, bf16[512,1024]{1,0:T(8,128)(2,1)S(1)}, bf16[1024,2048]{1,0:T(8,128)(2,1)S(1)}, bf16[512,2048]{1,0:T(8,128)(2,1)}, bf16[512,2048]{1,0:T(8,128)(2,1)}) custom-call(bf16[1024,2048]{1,0:T(8,128)(2,1)S(1)} %constant_dynamic-update-slice_fusion.4.refs_0_.refs_1_.refs_2_.refs_3_, ...), custom_call_target="tpu_custom_call" | custom-call | flops 1 | bytes 1 | tf_op jit(solution)/shard_map/feed_forward/pallas_call | solution.py:454
  285.7 18.4 %feed_forward.5 = (bf16[512,1024]{1,0:T(8,128)(2,1)S(1)}, bf16[512,2048]{1,0:T(8,128)(2,1)S(1)}, bf16[1024,2048]{1,0:T(8,128)(2,1)S(1)}, bf16[512,2048]{1,0:T(8,128)(2,1)S(1)}, bf16[512,2048]{1,0:T(8,128)(2,1)S(1)}) custom-call(bf16[1024,2048]{1,0:T(8,128)(2,1)} %constant_dynamic-update-slice_fusion.9.refs_0_.refs_1_.refs_2_.refs_3_, ...), custom_call_target="tpu_custom_call" | custom-call | flops 1 | bytes 1 | tf_op jit(solution)/shard_map/feed_forward/pallas_call | solution.py:454
  335.1 13.3 %collective-permute-done.26 = bf16[256,2048]{1,0:T(8,128)(2,1)S(1)} collective-permute-done((bf16[256,2048]{1,0:T(8,128)(2,1)S(1)}, bf16[256,2048]{1,0:T(8,128)(2,1)S(1)}, u32[]{:S(2)}, u32[]{:S(2)}) %collective-permute-start.26) | collective-permute-done | bytes 1048608 | tf_op jit(solution)/shard_map/ppermute | solution.py:281
  357.7 18.3 %collective-permute-done.29 = bf16[256,2048]{1,0:T(8,128)(2,1)S(1)} collective-permute-done((bf16[256,2048]{1,0:T(8,128)(2,1)S(1)}, bf16[256,2048]{1,0:T(8,128)(2,1)S(1)}, u32[]{:S(2)}, u32[]{:S(2)}) %collective-permute-start.29) | collective-permute-done | bytes 1048608 | tf_op jit(solution)/shard_map/ppermute | solution.py:281
  382.7 21.7 %collective-permute-done.33 = bf16[256,2048]{1,0:T(8,128)(2,1)S(1)} collective-permute-done((bf16[256,2048]{1,0:T(8,128)(2,1)S(1)}, bf16[256,2048]{1,0:T(8,128)(2,1)S(1)}, u32[]{:S(2)}, u32[]{:S(2)}) %collective-permute-start.33) | collective-permute-done | bytes 1048608 | tf_op jit(solution)/shard_map/ppermute | solution.py:278
  410.5 10.9 %collective-permute-done.37 = bf16[128,2048]{1,0:T(8,128)(2,1)S(1)} collective-permute-done((bf16[128,2048]{1,0:T(8,128)(2,1)S(1)}, bf16[128,2048]{1,0:T(8,128)(2,1)S(1)}, u32[]{:S(2)}, u32[]{:S(2)}) %collective-permute-start.37) | collective-permute-done | bytes 524320 | tf_op jit(solution)/shard_map/ppermute | solution.py:278
  440.2 7.9 %attend_back.2.slope_ref.refs_1_ = bf16[1024,384]{1,0:T(8,128)(2,1)S(1)} custom-call(bf16[512,2048]{1,0:T(8,128)(2,1)} %constant_dynamic-update-slice_fusion.14.own_ref.middle_own, bf16[512,2048]{1,0:T(8,128)(2,1)} %collective-permute-done.41.other_ref.middle_other, bf16[2048,512]{1,0:T(8,128)(2,1)} %collective-permute-done.5.weight_ref.refs_3_, ...), custom_call_target="tpu_custom_call" | custom-call | flops 1 | bytes 1 | tf_op jit(solution)/shard_map/attend_back/pallas_call | solution.py:245
  455.9 7.3 %attend_back.3.refs_0_.slope_ref = bf16[1024,384]{1,0:T(8,128)(2,1)S(1)} custom-call(bf16[512,2048]{1,0:T(8,128)(2,1)} %constant_dynamic-update-slice_fusion.14.own_ref.middle_own, bf16[512,2048]{1,0:T(8,128)(2,1)} %collective-permute-done.41.other_ref.middle_other, bf16[2048,512]{1,0:T(8,128)(2,1)S(1)} %bitcast.29, ...), custom_call_target="tpu_custom_call" | custom-call | flops 1 | bytes 1 | tf_op jit(solution)/shard_map/attend_back/pallas_call | solution.py:245
  470.9 7.4 %qkv_back.1 = (bf16[512,2048]{1,0:T(8,128)(2,1)S(1)}, bf16[512,2048]{1,0:T(8,128)(2,1)S(1)}) custom-call(bf16[1024,384]{1,0:T(8,128)(2,1)S(1)} %attend_back.3.refs_0_.slope_ref, bf16[1024,384]{1,0:T(8,128)(2,1)S(1)} %attend_back.2.slope_ref.refs_1_, bf16[2048,512]{1,0:T(8,128)(2,1)S(1)} %bitcast.30, bf16[2048,512]{1,0:T(8,128)(2,1)} %collective-permute-done.5.weight_ref.refs_3_), custom_call_target="tpu_custom_call" | custom-call | flops 1 | bytes 1 | tf_op jit(solution)/shard_map/qkv_back/pallas_call | solution.py:127
  487.5 19.5 %collective-permute-done.44 = bf16[2,512,512]{2,1,0:T(8,128)(2,1)} collective-permute-done((bf16[2,512,512]{2,1,0:T(8,128)(2,1)S(1)}, bf16[2,512,512]{2,1,0:T(8,128)(2,1)}, u32[]{:S(2)}, u32[]{:S(2)}) %collective-permute-start.44) | collective-permute-done | bytes 1048608 | tf_op jit(solution)/shard_map/ppermute | solution.py:265
  519.4 37.2 %collective-permute-done.46 = bf16[64,2048]{1,0:T(8,128)(2,1)S(1)} collective-permute-done((bf16[64,2048]{1,0:T(8,128)(2,1)S(1)}, bf16[64,2048]{1,0:T(8,128)(2,1)S(1)}, u32[]{:S(2)}, u32[]{:S(2)}) %collective-permute-start.46) | collective-permute-done | bytes 262176 | tf_op jit(solution)/shard_map/ppermute | solution.py:278
  559.4 10.2 %collective-permute-done.47 = bf16[128,2048]{1,0:T(8,128)(2,1)S(1)} collective-permute-done((bf16[128,2048]{1,0:T(8,128)(2,1)S(1)}, bf16[128,2048]{1,0:T(8,128)(2,1)S(1)}, u32[]{:S(2)}, u32[]{:S(2)}) %collective-permute-start.47) | collective-permute-done | bytes 524320 | tf_op jit(solution)/shard_map/ppermute | solution.py:278
  589.6 7.6 %assemble_units.1 = (f32[512,2048]{1,0:T(8,128)}, f32[512,2048]{1,0:T(8,128)}, f32[2048,512]{1,0:T(8,128)}) custom-call(s32[1]{0:T(128)} %bitcast.1.x_ref, bf16[4,768,512]{2,1,0:T(8,128)(2,1)} %all-to-all-done.3.mine_ref, bf16[4,768,512]{2,1,0:T(8,128)(2,1)} %collective-permute-done.45.theirs_ref), custom_call_target="tpu_custom_call" | custom-call | flops 1 | bytes 1 | tf_op jit(solution)/shard_map/assemble_units/pallas_call | solution.py:228
  597.3 14.0 %all-to-all-done.5 = bf16[4,256,512]{2,1,0:T(8,128)(2,1)} async-done(((bf16[4,256,512]{2,1,0:T(8,128)(2,1)}), bf16[4,256,512]{2,1,0:T(8,128)(2,1)}, u32[]{:S(2)}, u32[]{:S(2)}) %all-to-all-start.5) | async-done | bytes 1048608 | tf_op jit(solution)/shard_map/all_to_all | solution.py:345
  (279 shorter events, 243.4 us)
Async XLA Ops:
  21.5 69.1 %all-to-all-start.1 = ((bf16[4,640,512]{2,1,0:T(8,128)(2,1)}), bf16[4,640,512]{2,1,0:T(8,128)(2,1)}, u32[]{:S(2)}, u32[]{:S(2)}) async-start(bf16[4,640,512]{2,1,0:T(8,128)(2,1)} %get-tuple-element.158), calls=%async_computation.1 | async-start | bytes 5242880 | tf_op jit(solution)/shard_map/all_to_all | solution.py:345
  26.9 52.2 %collective-permute-start = (bf16[128,2048]{1,0:T(8,128)(2,1)S(1)}, bf16[128,2048]{1,0:T(8,128)(2,1)S(1)}, u32[]{:S(2)}, u32[]{:S(2)}) collective-permute-start(bf16[128,2048]{1,0:T(8,128)(2,1)S(1)} %fusion.4), channel_id=1, source_target_pairs={{0,4},{4,6},{6,2},{2,0},{1,5},{5,7},{7,3},{3,1},{8,12},{12,14},{14... | collective-permute-start | bytes 1572872 | tf_op jit(solution)/shard_map/ppermute | solution.py:278
  28.9 52.7 %collective-permute-start.2 = (bf16[128,2048]{1,0:T(8,128)(2,1)S(1)}, bf16[128,2048]{1,0:T(8,128)(2,1)S(1)}, u32[]{:S(2)}, u32[]{:S(2)}) collective-permute-start(bf16[128,2048]{1,0:T(8,128)(2,1)S(1)} %fusion.4), channel_id=1, source_target_pairs={{4,0},{6,4},{2,6},{0,2},{5,1},{7,5},{3,7},{1,3},{12,8},{14,12},{10... | collective-permute-start | bytes 1572872 | tf_op jit(solution)/shard_map/ppermute | solution.py:281
  95.7 48.2 %collective-permute-start.5 = (bf16[2048,512]{1,0:T(8,128)(2,1)S(1)}, bf16[2048,512]{1,0:T(8,128)(2,1)}, u32[]{:S(2)}, u32[]{:S(2)}) collective-permute-start(bf16[2048,512]{1,0:T(8,128)(2,1)S(1)} %bitcast.26), channel_id=1, source_target_pairs={{0,16},{16,0},{1,17},{17,1},{2,18},{18,2},{3,19},{19,3},{4,20},{20... | collective-permute-start | bytes 6291464 | tf_op jit(solution)/shard_map/ppermute | solution.py:265
  97.3 76.2 %all-to-all-start.2 = ((bf16[4,768,512]{2,1,0:T(8,128)(2,1)}), bf16[4,768,512]{2,1,0:T(8,128)(2,1)}, u32[]{:S(2)}, u32[]{:S(2)}) async-start(bf16[4,768,512]{2,1,0:T(8,128)(2,1)} %get-tuple-element.169), calls=%async_computation.2 | async-start | bytes 6291456 | tf_op jit(solution)/shard_map/all_to_all | solution.py:345
  185.1 36.0 %collective-permute-start.13 = (bf16[4,768,512]{2,1,0:T(8,128)(2,1)}, bf16[4,768,512]{2,1,0:T(8,128)(2,1)S(1)}, u32[]{:S(2)}, u32[]{:S(2)}) collective-permute-start(bf16[4,768,512]{2,1,0:T(8,128)(2,1)} %all-to-all-done.2.refs_4_), channel_id=1, source_target_pairs={{0,1},{1,0},{2,3},{3,2},{4,5},{5,4},{6,7},{7,6},{8,9},{9,8},{10,11... | collective-permute-start | bytes 9437192 | tf_op jit(solution)/shard_map/ppermute | solution.py:265
  198.6 67.2 %collective-permute-start.18 = (bf16[4,768,512]{2,1,0:T(8,128)(2,1)}, bf16[4,768,512]{2,1,0:T(8,128)(2,1)S(1)}, u32[]{:S(2)}, u32[]{:S(2)}) collective-permute-start(bf16[4,768,512]{2,1,0:T(8,128)(2,1)} %all-to-all-done.2.refs_4_), channel_id=1, source_target_pairs={{0,16},{16,0},{1,17},{17,1},{2,18},{18,2},{3,19},{19,3},{4,20},{20... | collective-permute-start | bytes 9437192 | tf_op jit(solution)/shard_map/ppermute | solution.py:265
  323.1 25.3 %collective-permute-start.26 = (bf16[256,2048]{1,0:T(8,128)(2,1)S(1)}, bf16[256,2048]{1,0:T(8,128)(2,1)S(1)}, u32[]{:S(2)}, u32[]{:S(2)}) collective-permute-start(bf16[256,2048]{1,0:T(8,128)(2,1)S(1)} %pad_maximum_fusion.3), channel_id=1, source_target_pairs={{4,0},{8,4},{12,8},{14,12},{10,14},{6,10},{2,6},{0,2},{5,1},{9,5},... | collective-permute-start | bytes 3145736 | tf_op jit(solution)/shard_map/ppermute | solution.py:281
  324.7 25.0 %collective-permute-start.25 = (bf16[256,2048]{1,0:T(8,128)(2,1)S(1)}, bf16[256,2048]{1,0:T(8,128)(2,1)S(1)}, u32[]{:S(2)}, u32[]{:S(2)}) collective-permute-start(bf16[256,2048]{1,0:T(8,128)(2,1)S(1)} %pad_maximum_fusion.2), channel_id=1, source_target_pairs={{0,4},{4,8},{8,12},{12,14},{14,10},{10,6},{6,2},{2,0},{1,5},{5,9},... | collective-permute-start | bytes 3145736 | tf_op jit(solution)/shard_map/ppermute | solution.py:278
  350.0 28.0 %collective-permute-start.31 = (bf16[4,512,512]{2,1,0:T(8,128)(2,1)S(1)}, bf16[4,512,512]{2,1,0:T(8,128)(2,1)S(1)}, u32[]{:S(2)}, u32[]{:S(2)}) collective-permute-start(bf16[4,512,512]{2,1,0:T(8,128)(2,1)S(1)} %get-tuple-element.238), channel_id=1, source_target_pairs={{0,1},{1,0},{2,3},{3,2},{4,5},{5,4},{6,7},{7,6},{8,9},{9,8},{10,11... | collective-permute-start | bytes 6291464 | tf_op jit(solution)/shard_map/ppermute | solution.py:265
  350.9 25.1 %collective-permute-start.29 = (bf16[256,2048]{1,0:T(8,128)(2,1)S(1)}, bf16[256,2048]{1,0:T(8,128)(2,1)S(1)}, u32[]{:S(2)}, u32[]{:S(2)}) collective-permute-start(bf16[256,2048]{1,0:T(8,128)(2,1)S(1)} %add_convert_fusion.10), channel_id=1, source_target_pairs={{4,0},{8,4},{12,8},{14,12},{10,14},{6,10},{2,6},{0,2},{5,1},{9,5},... | collective-permute-start | bytes 3145736 | tf_op jit(solution)/shard_map/ppermute | solution.py:281
  352.8 24.8 %collective-permute-start.28 = (bf16[256,2048]{1,0:T(8,128)(2,1)S(1)}, bf16[256,2048]{1,0:T(8,128)(2,1)S(1)}, u32[]{:S(2)}, u32[]{:S(2)}) collective-permute-start(bf16[256,2048]{1,0:T(8,128)(2,1)S(1)} %add_convert_fusion.11), channel_id=1, source_target_pairs={{0,4},{4,8},{8,12},{12,14},{14,10},{10,6},{6,2},{2,0},{1,5},{5,9},... | collective-permute-start | bytes 3145736 | tf_op jit(solution)/shard_map/ppermute | solution.py:278
  378.8 25.6 %collective-permute-start.33 = (bf16[256,2048]{1,0:T(8,128)(2,1)S(1)}, bf16[256,2048]{1,0:T(8,128)(2,1)S(1)}, u32[]{:S(2)}, u32[]{:S(2)}) collective-permute-start(bf16[256,2048]{1,0:T(8,128)(2,1)S(1)} %get-tuple-element.310), channel_id=1, source_target_pairs={{0,4},{4,8},{8,12},{12,14},{14,10},{10,6},{6,2},{2,0},{1,5},{5,9},... | collective-permute-start | bytes 3145736 | tf_op jit(solution)/shard_map/ppermute | solution.py:278
  379.7 25.3 %collective-permute-start.34 = (bf16[256,2048]{1,0:T(8,128)(2,1)S(1)}, bf16[256,2048]{1,0:T(8,128)(2,1)S(1)}, u32[]{:S(2)}, u32[]{:S(2)}) collective-permute-start(bf16[256,2048]{1,0:T(8,128)(2,1)S(1)} %get-tuple-element.309), channel_id=1, source_target_pairs={{4,0},{8,4},{12,8},{14,12},{10,14},{6,10},{2,6},{0,2},{5,1},{9,5},... | collective-permute-start | bytes 3145736 | tf_op jit(solution)/shard_map/ppermute | solution.py:281
  380.9 25.0 %collective-permute-start.36 = (bf16[4,256,512]{2,1,0:T(8,128)(2,1)S(1)}, bf16[4,256,512]{2,1,0:T(8,128)(2,1)S(1)}, u32[]{:S(2)}, u32[]{:S(2)}) collective-permute-start(bf16[4,256,512]{2,1,0:T(8,128)(2,1)S(1)} %add_convert_fusion.9), channel_id=1, source_target_pairs={{0,16},{16,0},{1,17},{17,1},{2,18},{18,2},{3,19},{19,3},{4,20},{20... | collective-permute-start | bytes 3145736 | tf_op jit(solution)/shard_map/ppermute | solution.py:265
  432.1 76.5 %all-to-all-start.3 = ((bf16[4,768,512]{2,1,0:T(8,128)(2,1)}), bf16[4,768,512]{2,1,0:T(8,128)(2,1)}, u32[]{:S(2)}, u32[]{:S(2)}) async-start(bf16[4,768,512]{2,1,0:T(8,128)(2,1)} %pad_maximum_fusion), calls=%async_computation.3 | async-start | bytes 6291456 | tf_op jit(solution)/shard_map/all_to_all | solution.py:345
  454.6 25.6 %collective-permute-start.42 = (bf16[2,512,512]{2,1,0:T(8,128)(2,1)S(1)}, bf16[2,512,512]{2,1,0:T(8,128)(2,1)S(1)}, u32[]{:S(2)}, u32[]{:S(2)}) collective-permute-start(bf16[2,512,512]{2,1,0:T(8,128)(2,1)S(1)} %slice.187), channel_id=1, source_target_pairs={{0,16},{16,0},{1,17},{17,1},{2,18},{18,2},{3,19},{19,3},{4,20},{20... | collective-permute-start | bytes 3145736 | tf_op jit(solution)/shard_map/ppermute | solution.py:265
  481.3 25.7 %collective-permute-start.44 = (bf16[2,512,512]{2,1,0:T(8,128)(2,1)S(1)}, bf16[2,512,512]{2,1,0:T(8,128)(2,1)}, u32[]{:S(2)}, u32[]{:S(2)}) collective-permute-start(bf16[2,512,512]{2,1,0:T(8,128)(2,1)S(1)} %slice.188), channel_id=1, source_target_pairs={{0,16},{16,0},{1,17},{17,1},{2,18},{18,2},{3,19},{19,3},{4,20},{20... | collective-permute-start | bytes 3145736 | tf_op jit(solution)/shard_map/ppermute | solution.py:265
  508.6 70.0 %collective-permute-start.45 = (bf16[4,768,512]{2,1,0:T(8,128)(2,1)}, bf16[4,768,512]{2,1,0:T(8,128)(2,1)}, u32[]{:S(2)}, u32[]{:S(2)}) collective-permute-start(bf16[4,768,512]{2,1,0:T(8,128)(2,1)} %all-to-all-done.3.mine_ref), channel_id=1, source_target_pairs={{0,16},{16,0},{1,17},{17,1},{2,18},{18,2},{3,19},{19,3},{4,20},{20... | collective-permute-start | bytes 9437192 | tf_op jit(solution)/shard_map/ppermute | solution.py:265
  512.5 66.2 %all-to-all-start.4 = ((bf16[4,512,512]{2,1,0:T(8,128)(2,1)}), bf16[4,512,512]{2,1,0:T(8,128)(2,1)}, u32[]{:S(2)}, u32[]{:S(2)}) async-start(bf16[4,512,512]{2,1,0:T(8,128)(2,1)} %add_convert_fusion), calls=%async_computation.4 | async-start | bytes 4194304 | tf_op jit(solution)/shard_map/all_to_all | solution.py:345
  517.3 39.3 %collective-permute-start.46 = (bf16[64,2048]{1,0:T(8,128)(2,1)S(1)}, bf16[64,2048]{1,0:T(8,128)(2,1)S(1)}, u32[]{:S(2)}, u32[]{:S(2)}) collective-permute-start(bf16[64,2048]{1,0:T(8,128)(2,1)S(1)} %get-tuple-element.322), channel_id=1, source_target_pairs={{0,4},{4,6},{6,2},{2,0},{1,5},{5,7},{7,3},{3,1},{8,12},{12,14},{14... | collective-permute-start | bytes 786440 | tf_op jit(solution)/shard_map/ppermute | solution.py:278
  519.3 37.2 %collective-permute-start.48 = (bf16[64,2048]{1,0:T(8,128)(2,1)S(1)}, bf16[64,2048]{1,0:T(8,128)(2,1)S(1)}, u32[]{:S(2)}, u32[]{:S(2)}) collective-permute-start(bf16[64,2048]{1,0:T(8,128)(2,1)S(1)} %get-tuple-element.323), channel_id=1, source_target_pairs={{4,0},{6,4},{2,6},{0,2},{5,1},{7,5},{3,7},{1,3},{12,8},{14,12},{10... | collective-permute-start | bytes 786440 | tf_op jit(solution)/shard_map/ppermute | solution.py:281
  581.0 30.2 %all-to-all-start.5 = ((bf16[4,256,512]{2,1,0:T(8,128)(2,1)}), bf16[4,256,512]{2,1,0:T(8,128)(2,1)}, u32[]{:S(2)}, u32[]{:S(2)}) async-start(bf16[4,256,512]{2,1,0:T(8,128)(2,1)} %bitcast.25), calls=%async_computation.5 | async-start | bytes 2097152 | tf_op jit(solution)/shard_map/all_to_all | solution.py:345
  588.5 25.1 %collective-permute-start.50 = (bf16[2,512,512]{2,1,0:T(8,128)(2,1)}, bf16[2,512,512]{2,1,0:T(8,128)(2,1)}, u32[]{:S(2)}, u32[]{:S(2)}) collective-permute-start(bf16[2,512,512]{2,1,0:T(8,128)(2,1)} %reduce_sum.92.mine_ref), channel_id=1, source_target_pairs={{0,16},{16,0},{1,17},{17,1},{2,18},{18,2},{3,19},{19,3},{4,20},{20... | collective-permute-start | bytes 3145736 | tf_op jit(solution)/shard_map/ppermute | solution.py:265
  (74 other events, 806.3 us)

commit v8 on v7

--- a/solution.py
+++ b/solution.py
@@ -134,7 +134,7 @@
             pl.BlockSpec((tile, width), lambda i: (jnp.maximum(i - last - 1, 0), 0)),
         ],
         out_shape=[jax.ShapeDtypeStruct((count // HALF, width), low)] * HALF,
-        compiler_params=pltpu.CompilerParams(vmem_limit_bytes=12 * 1024 * 1024),
+        compiler_params=pltpu.CompilerParams(vmem_limit_bytes=9 * 1024 * 1024),
         cost_estimate=CHEAP,
         name=name,
     )(*lefts, *weights)
@@ -179,7 +179,7 @@
         + [pl.BlockSpec(array.shape, lambda i: (0, 0)) for array in held],
         out_specs=[pl.BlockSpec((1,) + shape[1:], lambda i: (i, 0, 0)) for shape in shapes],
         out_shape=[jax.ShapeDtypeStruct(shape, low) for shape in shapes],
-        compiler_params=pltpu.CompilerParams(vmem_limit_bytes=12 * 1024 * 1024),
+        compiler_params=pltpu.CompilerParams(vmem_limit_bytes=10 * 1024 * 1024),
         cost_estimate=CHEAP,
         name=name,
     )(*cut, *held)
@@ -247,7 +247,7 @@
         in_specs=[whole] * len(arrays),
         out_specs=[whole] * len(shapes),
         out_shape=shapes,
-        compiler_params=pltpu.CompilerParams(vmem_limit_bytes=18 * 1024 * 1024),
+        compiler_params=pltpu.CompilerParams(vmem_limit_bytes=15 * 1024 * 1024),
         cost_estimate=CHEAP,
         name=name,
     )(*arrays)
@@ -459,7 +459,7 @@
         + [pl.BlockSpec((array.shape[0] // steps, width), lambda i: (i, 0)) for array in earlier],
         out_specs=[pl.BlockSpec((shape[0] // steps, shape[1]), lambda i: (i, 0)) for shape in shapes],
         out_shape=[jax.ShapeDtypeStruct(shape, low) for shape in shapes],
-        compiler_params=pltpu.CompilerParams(vmem_limit_bytes=30 * 1024 * 1024),
+        compiler_params=pltpu.CompilerParams(vmem_limit_bytes=22 * 1024 * 1024),
         cost_estimate=CHEAP,
         name="feed_forward",
     )(*[both] * 4, *weights, *earlier)

time: 623 us -> 618 us (level)
  waiting for transfers between devices: 354 us -> 365 us
  local copies, waits for them, and re-layouts: 36.3 us -> 28.4 us
    ppermute x19, waiting for transfers between devices: 71.6 us -> 79.9 us  [swap(): return lax.ppermute(array, axis, [(0, 1), (1, 0)])]
    unnamed x96 -> x90, local copies, waits for them, and re-layouts: 24.7 us -> 18.9 us
  transfers between devices with their start and end apart: 57 -> 57, of which waited for: 42 -> 44; matrix products, arithmetic and copies ran while one was open for 5% -> 4% of each run, Pallas kernels for 17% -> 17%
where the time goes in v8:
time: 618 us; the launch traced here: 614 us
  waiting for transfers between devices  365 us (59%)
  Pallas kernels  125 us (20%)
  starting transfers between devices  68.7 us (11%)
  local copies, waits for them, and re-layouts  28.4 us (5%)
  other arithmetic  25.7 us (4%)
    ppermute x16, waiting for transfers between devices, up(): return lax.ppermute(array, self.axes, self.upward)  200 us
    ppermute x19, waiting for transfers between devices, swap(): return lax.ppermute(array, axis, [(0, 1), (1, 0)])  79.9 us
    ppermute x16, waiting for transfers between devices, down(): return lax.ppermute(array, self.axes, self.downward)  50.2 us
    all_to_all x6, waiting for transfers between devices, exchange_rows(): return lax.all_to_all(array, ROW, 0, 0, tiled=True)  34.9 us
    pallas_call x3, Pallas kernels, feed_forward(): pl.pallas_call(functools.partial(mlp_kernel, blocks), grid=(steps,), in_s...  33.7 us
    pallas_call x6, Pallas kernels, call_blocks(): pl.pallas_call(kernel, grid=(count,), in_specs=[pl.BlockSpec((array.shape...  30.5 us
    pallas_call x4, Pallas kernels, call_whole(): pl.pallas_call(kernel, in_specs=[whole] * len(arrays), out_specs=[whole]...  30.1 us
    all_to_all x6, starting transfers between devices, exchange_rows(): return lax.all_to_all(array, ROW, 0, 0, tiled=True)  27.8 us
  transfers between devices with their start and end apart: 57, of which 44 were waited for; matrix products, arithmetic and copies ran while one was open for 4% of the time, Pallas kernels for 17%

profile of v8, /device:TPU:0, one launch (start us, length us, event | category | flops | bytes accessed | tf_op | source)
XLA Modules:
  0.0 614.4 jit_solution(2182091707041945124)
XLA Ops:
  12.6 8.8 %all-to-all-done = bf16[4,128,512]{2,1,0:T(8,128)(2,1)S(1)} async-done(((bf16[4,128,512]{2,1,0:T(8,128)(2,1)}), bf16[4,128,512]{2,1,0:T(8,128)(2,1)S(1)}, u32[]{:S(2)}, u32[]{:S(2)}) %all-to-all-start) | async-done | bytes 524320 | tf_op jit(solution)/shard_map/all_to_all | solution.py:345
  28.6 49.6 %collective-permute-done = bf16[128,2048]{1,0:T(8,128)(2,1)S(1)} collective-permute-done((bf16[128,2048]{1,0:T(8,128)(2,1)S(1)}, bf16[128,2048]{1,0:T(8,128)(2,1)S(1)}, u32[]{:S(2)}, u32[]{:S(2)}) %collective-permute-start) | collective-permute-done | bytes 524320 | tf_op jit(solution)/shard_map/ppermute | solution.py:278
  105.4 7.3 %attend.2 = (bf16[1024,384]{1,0:T(8,128)(2,1)S(1)}, bf16[1024,128]{1,0:T(8,128)(2,1)S(1)}, f32[1024,1]{1,0:T(8,128)S(1)}) custom-call(bf16[512,2048]{1,0:T(8,128)(2,1)} %constant_dynamic-update-slice_fusion.own_ref.rows_own, bf16[512,2048]{1,0:T(8,128)(2,1)} %collective-permute-done.4.other_ref.rows_other, bf16[2048,512]{1,0:T(8,128)(2,1)S(1)} %bitcast.27, ...), custom_call_target="tpu_custom_call" | custom-call | flops 1 | bytes 1 | tf_op jit(solution)/shard_map/attend/pallas_call | solution.py:245
  113.6 31.1 %collective-permute-done.5.weight_ref.refs_3_ = bf16[2048,512]{1,0:T(8,128)(2,1)} collective-permute-done((bf16[2048,512]{1,0:T(8,128)(2,1)S(1)}, bf16[2048,512]{1,0:T(8,128)(2,1)}, u32[]{:S(2)}, u32[]{:S(2)}) %collective-permute-start.5) | collective-permute-done | bytes 2097184 | tf_op jit(solution)/shard_map/ppermute | solution.py:265
  144.7 7.7 %attend.3 = (bf16[1024,384]{1,0:T(8,128)(2,1)S(1)}, bf16[1024,128]{1,0:T(8,128)(2,1)S(1)}, f32[1024,1]{1,0:T(8,128)S(1)}) custom-call(bf16[512,2048]{1,0:T(8,128)(2,1)} %constant_dynamic-update-slice_fusion.own_ref.rows_own, bf16[512,2048]{1,0:T(8,128)(2,1)} %collective-permute-done.4.other_ref.rows_other, ...), custom_call_target="tpu_custom_call" | custom-call | flops 1 | bytes 1 | tf_op jit(solution)/shard_map/attend/pallas_call | solution.py:245
  164.5 9.7 %all-to-all-done.2.refs_4_ = bf16[4,768,512]{2,1,0:T(8,128)(2,1)} async-done(((bf16[4,768,512]{2,1,0:T(8,128)(2,1)}), bf16[4,768,512]{2,1,0:T(8,128)(2,1)}, u32[]{:S(2)}, u32[]{:S(2)}) %all-to-all-start.2) | async-done | bytes 3145760 | tf_op jit(solution)/shard_map/all_to_all | solution.py:345
  186.9 9.0 %collective-permute-done.8 = bf16[128,2048]{1,0:T(8,128)(2,1)S(1)} collective-permute-done((bf16[128,2048]{1,0:T(8,128)(2,1)S(1)}, bf16[128,2048]{1,0:T(8,128)(2,1)S(1)}, u32[]{:S(2)}, u32[]{:S(2)}) %collective-permute-start.8) | collective-permute-done | bytes 524320 | tf_op jit(solution)/shard_map/ppermute | solution.py:278
  199.9 20.5 %collective-permute-done.11 = bf16[256,2048]{1,0:T(8,128)(2,1)S(1)} collective-permute-done((bf16[256,2048]{1,0:T(8,128)(2,1)S(1)}, bf16[256,2048]{1,0:T(8,128)(2,1)S(1)}, u32[]{:S(2)}, u32[]{:S(2)}) %collective-permute-start.11) | collective-permute-done | bytes 1048608 | tf_op jit(solution)/shard_map/ppermute | solution.py:278
  223.8 19.9 %collective-permute-done.14 = bf16[256,2048]{1,0:T(8,128)(2,1)S(1)} collective-permute-done((bf16[256,2048]{1,0:T(8,128)(2,1)S(1)}, bf16[256,2048]{1,0:T(8,128)(2,1)S(1)}, u32[]{:S(2)}, u32[]{:S(2)}) %collective-permute-start.14) | collective-permute-done | bytes 1048608 | tf_op jit(solution)/shard_map/ppermute | solution.py:278
  247.7 9.1 %feed_forward.3 = (bf16[512,512]{1,0:T(8,128)(2,1)S(1)}, bf16[512,1024]{1,0:T(8,128)(2,1)S(1)}, bf16[1024,2048]{1,0:T(8,128)(2,1)S(1)}, bf16[512,2048]{1,0:T(8,128)(2,1)S(1)}, bf16[512,2048]{1,0:T(8,128)(2,1)S(1)}) custom-call(bf16[1024,2048]{1,0:T(8,128)(2,1)S(1)} %constant_dynamic-update-slice_fusion.4.refs_0_.refs_1_.refs_2_.refs_3_, ...), custom_call_target="tpu_custom_call" | custom-call | flops 1 | bytes 1 | tf_op jit(solution)/shard_map/feed_forward/pallas_call | solution.py:454
  256.8 9.8 %collective-permute-done.18.refs_4_.refs_6_ = bf16[4,768,512]{2,1,0:T(8,128)(2,1)S(1)} collective-permute-done((bf16[4,768,512]{2,1,0:T(8,128)(2,1)}, bf16[4,768,512]{2,1,0:T(8,128)(2,1)S(1)}, u32[]{:S(2)}, u32[]{:S(2)}) %collective-permute-start.18) | collective-permute-done | bytes 3145760 | tf_op jit(solution)/shard_map/ppermute | solution.py:265
  272.3 7.6 %feed_forward.4 = (bf16[512,512]{1,0:T(8,128)(2,1)S(1)}, bf16[512,1024]{1,0:T(8,128)(2,1)S(1)}, bf16[1024,2048]{1,0:T(8,128)(2,1)S(1)}, bf16[512,2048]{1,0:T(8,128)(2,1)}, bf16[512,2048]{1,0:T(8,128)(2,1)}) custom-call(bf16[1024,2048]{1,0:T(8,128)(2,1)S(1)} %constant_dynamic-update-slice_fusion.4.refs_0_.refs_1_.refs_2_.refs_3_, ...), custom_call_target="tpu_custom_call" | custom-call | flops 1 | bytes 1 | tf_op jit(solution)/shard_map/feed_forward/pallas_call | solution.py:454
  286.1 17.0 %feed_forward.5 = (bf16[512,1024]{1,0:T(8,128)(2,1)S(1)}, bf16[512,2048]{1,0:T(8,128)(2,1)S(1)}, bf16[1024,2048]{1,0:T(8,128)(2,1)S(1)}, bf16[512,2048]{1,0:T(8,128)(2,1)S(1)}, bf16[512,2048]{1,0:T(8,128)(2,1)S(1)}) custom-call(bf16[1024,2048]{1,0:T(8,128)(2,1)S(1)} %constant_dynamic-update-slice_fusion.9.refs_0_.refs_1_.refs_2_.refs_3_, ...), custom_call_target="tpu_custom_call" | custom-call | flops 1 | bytes 1 | tf_op jit(solution)/shard_map/feed_forward/pallas_call | solution.py:454
  333.9 13.5 %collective-permute-done.26 = bf16[256,2048]{1,0:T(8,128)(2,1)S(1)} collective-permute-done((bf16[256,2048]{1,0:T(8,128)(2,1)S(1)}, bf16[256,2048]{1,0:T(8,128)(2,1)S(1)}, u32[]{:S(2)}, u32[]{:S(2)}) %collective-permute-start.26) | collective-permute-done | bytes 1048608 | tf_op jit(solution)/shard_map/ppermute | solution.py:281
  356.6 18.4 %collective-permute-done.29 = bf16[256,2048]{1,0:T(8,128)(2,1)S(1)} collective-permute-done((bf16[256,2048]{1,0:T(8,128)(2,1)S(1)}, bf16[256,2048]{1,0:T(8,128)(2,1)S(1)}, u32[]{:S(2)}, u32[]{:S(2)}) %collective-permute-start.29) | collective-permute-done | bytes 1048608 | tf_op jit(solution)/shard_map/ppermute | solution.py:281
  381.6 21.8 %collective-permute-done.33 = bf16[256,2048]{1,0:T(8,128)(2,1)S(1)} collective-permute-done((bf16[256,2048]{1,0:T(8,128)(2,1)S(1)}, bf16[256,2048]{1,0:T(8,128)(2,1)S(1)}, u32[]{:S(2)}, u32[]{:S(2)}) %collective-permute-start.33) | collective-permute-done | bytes 1048608 | tf_op jit(solution)/shard_map/ppermute | solution.py:278
  409.4 10.9 %collective-permute-done.37 = bf16[128,2048]{1,0:T(8,128)(2,1)S(1)} collective-permute-done((bf16[128,2048]{1,0:T(8,128)(2,1)S(1)}, bf16[128,2048]{1,0:T(8,128)(2,1)S(1)}, u32[]{:S(2)}, u32[]{:S(2)}) %collective-permute-start.37) | collective-permute-done | bytes 524320 | tf_op jit(solution)/shard_map/ppermute | solution.py:278
  439.2 7.9 %attend_back.2.slope_ref.refs_1_ = bf16[1024,384]{1,0:T(8,128)(2,1)S(1)} custom-call(bf16[512,2048]{1,0:T(8,128)(2,1)} %constant_dynamic-update-slice_fusion.14.own_ref.middle_own, bf16[512,2048]{1,0:T(8,128)(2,1)} %collective-permute-done.41.other_ref.middle_other, bf16[2048,512]{1,0:T(8,128)(2,1)} %collective-permute-done.5.weight_ref.refs_3_, ...), custom_call_target="tpu_custom_call" | custom-call | flops 1 | bytes 1 | tf_op jit(solution)/shard_map/attend_back/pallas_call | solution.py:245
  468.4 7.9 %qkv_back.1 = (bf16[512,2048]{1,0:T(8,128)(2,1)S(1)}, bf16[512,2048]{1,0:T(8,128)(2,1)S(1)}) custom-call(bf16[1024,384]{1,0:T(8,128)(2,1)S(1)} %attend_back.3.refs_0_.slope_ref, bf16[1024,384]{1,0:T(8,128)(2,1)S(1)} %attend_back.2.slope_ref.refs_1_, bf16[2048,512]{1,0:T(8,128)(2,1)S(1)} %bitcast.30, bf16[2048,512]{1,0:T(8,128)(2,1)} %collective-permute-done.5.weight_ref.refs_3_), custom_call_target="tpu_custom_call" | custom-call | flops 1 | bytes 1 | tf_op jit(solution)/shard_map/qkv_back/pallas_call | solution.py:127
  486.4 19.5 %collective-permute-done.44 = bf16[2,512,512]{2,1,0:T(8,128)(2,1)} collective-permute-done((bf16[2,512,512]{2,1,0:T(8,128)(2,1)S(1)}, bf16[2,512,512]{2,1,0:T(8,128)(2,1)}, u32[]{:S(2)}, u32[]{:S(2)}) %collective-permute-start.44) | collective-permute-done | bytes 1048608 | tf_op jit(solution)/shard_map/ppermute | solution.py:265
  518.1 37.2 %collective-permute-done.46 = bf16[64,2048]{1,0:T(8,128)(2,1)S(1)} collective-permute-done((bf16[64,2048]{1,0:T(8,128)(2,1)S(1)}, bf16[64,2048]{1,0:T(8,128)(2,1)S(1)}, u32[]{:S(2)}, u32[]{:S(2)}) %collective-permute-start.46) | collective-permute-done | bytes 262176 | tf_op jit(solution)/shard_map/ppermute | solution.py:278
  558.2 10.2 %collective-permute-done.47 = bf16[128,2048]{1,0:T(8,128)(2,1)S(1)} collective-permute-done((bf16[128,2048]{1,0:T(8,128)(2,1)S(1)}, bf16[128,2048]{1,0:T(8,128)(2,1)S(1)}, u32[]{:S(2)}, u32[]{:S(2)}) %collective-permute-start.47) | collective-permute-done | bytes 524320 | tf_op jit(solution)/shard_map/ppermute | solution.py:278
  585.3 7.6 %assemble_units.1 = (f32[512,2048]{1,0:T(8,128)}, f32[512,2048]{1,0:T(8,128)}, f32[2048,512]{1,0:T(8,128)}) custom-call(s32[1]{0:T(128)} %bitcast.1.x_ref, bf16[4,768,512]{2,1,0:T(8,128)(2,1)} %all-to-all-done.3.mine_ref, bf16[4,768,512]{2,1,0:T(8,128)(2,1)} %collective-permute-done.45.theirs_ref), custom_call_target="tpu_custom_call" | custom-call | flops 1 | bytes 1 | tf_op jit(solution)/shard_map/assemble_units/pallas_call | solution.py:228
  592.9 14.7 %all-to-all-done.5 = bf16[4,256,512]{2,1,0:T(8,128)(2,1)S(1)} async-done(((bf16[4,256,512]{2,1,0:T(8,128)(2,1)}), bf16[4,256,512]{2,1,0:T(8,128)(2,1)S(1)}, u32[]{:S(2)}, u32[]{:S(2)}) %all-to-all-start.5) | async-done | bytes 1048608 | tf_op jit(solution)/shard_map/all_to_all | solution.py:345
  (273 shorter events, 235.6 us)
Async XLA Ops:
  21.5 68.2 %all-to-all-start.1 = ((bf16[4,640,512]{2,1,0:T(8,128)(2,1)}), bf16[4,640,512]{2,1,0:T(8,128)(2,1)S(1)}, u32[]{:S(2)}, u32[]{:S(2)}) async-start(bf16[4,640,512]{2,1,0:T(8,128)(2,1)} %get-tuple-element.158), calls=%async_computation.1 | async-start | bytes 5242880 | tf_op jit(solution)/shard_map/all_to_all | solution.py:345
  26.5 51.7 %collective-permute-start = (bf16[128,2048]{1,0:T(8,128)(2,1)S(1)}, bf16[128,2048]{1,0:T(8,128)(2,1)S(1)}, u32[]{:S(2)}, u32[]{:S(2)}) collective-permute-start(bf16[128,2048]{1,0:T(8,128)(2,1)S(1)} %fusion.4), channel_id=1, source_target_pairs={{0,4},{4,6},{6,2},{2,0},{1,5},{5,7},{7,3},{3,1},{8,12},{12,14},{14... | collective-permute-start | bytes 1572872 | tf_op jit(solution)/shard_map/ppermute | solution.py:278
  28.5 52.2 %collective-permute-start.2 = (bf16[128,2048]{1,0:T(8,128)(2,1)S(1)}, bf16[128,2048]{1,0:T(8,128)(2,1)S(1)}, u32[]{:S(2)}, u32[]{:S(2)}) collective-permute-start(bf16[128,2048]{1,0:T(8,128)(2,1)S(1)} %fusion.4), channel_id=1, source_target_pairs={{4,0},{6,4},{2,6},{0,2},{5,1},{7,5},{3,7},{1,3},{12,8},{14,12},{10... | collective-permute-start | bytes 1572872 | tf_op jit(solution)/shard_map/ppermute | solution.py:281
  96.4 48.2 %collective-permute-start.5 = (bf16[2048,512]{1,0:T(8,128)(2,1)S(1)}, bf16[2048,512]{1,0:T(8,128)(2,1)}, u32[]{:S(2)}, u32[]{:S(2)}) collective-permute-start(bf16[2048,512]{1,0:T(8,128)(2,1)S(1)} %bitcast.26), channel_id=1, source_target_pairs={{0,16},{16,0},{1,17},{17,1},{2,18},{18,2},{3,19},{19,3},{4,20},{20... | collective-permute-start | bytes 6291464 | tf_op jit(solution)/shard_map/ppermute | solution.py:265
  98.0 76.2 %all-to-all-start.2 = ((bf16[4,768,512]{2,1,0:T(8,128)(2,1)}), bf16[4,768,512]{2,1,0:T(8,128)(2,1)}, u32[]{:S(2)}, u32[]{:S(2)}) async-start(bf16[4,768,512]{2,1,0:T(8,128)(2,1)} %get-tuple-element.169), calls=%async_computation.2 | async-start | bytes 6291456 | tf_op jit(solution)/shard_map/all_to_all | solution.py:345
  185.8 36.0 %collective-permute-start.13 = (bf16[4,768,512]{2,1,0:T(8,128)(2,1)}, bf16[4,768,512]{2,1,0:T(8,128)(2,1)S(1)}, u32[]{:S(2)}, u32[]{:S(2)}) collective-permute-start(bf16[4,768,512]{2,1,0:T(8,128)(2,1)} %all-to-all-done.2.refs_4_), channel_id=1, source_target_pairs={{0,1},{1,0},{2,3},{3,2},{4,5},{5,4},{6,7},{7,6},{8,9},{9,8},{10,11... | collective-permute-start | bytes 9437192 | tf_op jit(solution)/shard_map/ppermute | solution.py:265
  199.4 67.2 %collective-permute-start.18 = (bf16[4,768,512]{2,1,0:T(8,128)(2,1)}, bf16[4,768,512]{2,1,0:T(8,128)(2,1)S(1)}, u32[]{:S(2)}, u32[]{:S(2)}) collective-permute-start(bf16[4,768,512]{2,1,0:T(8,128)(2,1)} %all-to-all-done.2.refs_4_), channel_id=1, source_target_pairs={{0,16},{16,0},{1,17},{17,1},{2,18},{18,2},{3,19},{19,3},{4,20},{20... | collective-permute-start | bytes 9437192 | tf_op jit(solution)/shard_map/ppermute | solution.py:265
  322.1 25.3 %collective-permute-start.26 = (bf16[256,2048]{1,0:T(8,128)(2,1)S(1)}, bf16[256,2048]{1,0:T(8,128)(2,1)S(1)}, u32[]{:S(2)}, u32[]{:S(2)}) collective-permute-start(bf16[256,2048]{1,0:T(8,128)(2,1)S(1)} %pad_maximum_fusion.3), channel_id=1, source_target_pairs={{4,0},{8,4},{12,8},{14,12},{10,14},{6,10},{2,6},{0,2},{5,1},{9,5},... | collective-permute-start | bytes 3145736 | tf_op jit(solution)/shard_map/ppermute | solution.py:281
  323.7 25.0 %collective-permute-start.25 = (bf16[256,2048]{1,0:T(8,128)(2,1)S(1)}, bf16[256,2048]{1,0:T(8,128)(2,1)S(1)}, u32[]{:S(2)}, u32[]{:S(2)}) collective-permute-start(bf16[256,2048]{1,0:T(8,128)(2,1)S(1)} %pad_maximum_fusion.2), channel_id=1, source_target_pairs={{0,4},{4,8},{8,12},{12,14},{14,10},{10,6},{6,2},{2,0},{1,5},{5,9},... | collective-permute-start | bytes 3145736 | tf_op jit(solution)/shard_map/ppermute | solution.py:278
  324.4 24.6 %collective-permute-start.27 = (bf16[2,512,512]{2,1,0:T(8,128)(2,1)S(1)}, bf16[2,512,512]{2,1,0:T(8,128)(2,1)S(1)}, u32[]{:S(2)}, u32[]{:S(2)}) collective-permute-start(bf16[2,512,512]{2,1,0:T(8,128)(2,1)S(1)} %get-tuple-element.220), channel_id=1, source_target_pairs={{0,16},{16,0},{1,17},{17,1},{2,18},{18,2},{3,19},{19,3},{4,20},{20... | collective-permute-start | bytes 3145736 | tf_op jit(solution)/shard_map/ppermute | solution.py:265
  349.0 27.9 %collective-permute-start.31 = (bf16[4,512,512]{2,1,0:T(8,128)(2,1)S(1)}, bf16[4,512,512]{2,1,0:T(8,128)(2,1)S(1)}, u32[]{:S(2)}, u32[]{:S(2)}) collective-permute-start(bf16[4,512,512]{2,1,0:T(8,128)(2,1)S(1)} %get-tuple-element.238), channel_id=1, source_target_pairs={{0,1},{1,0},{2,3},{3,2},{4,5},{5,4},{6,7},{7,6},{8,9},{9,8},{10,11... | collective-permute-start | bytes 6291464 | tf_op jit(solution)/shard_map/ppermute | solution.py:265
  349.9 25.1 %collective-permute-start.29 = (bf16[256,2048]{1,0:T(8,128)(2,1)S(1)}, bf16[256,2048]{1,0:T(8,128)(2,1)S(1)}, u32[]{:S(2)}, u32[]{:S(2)}) collective-permute-start(bf16[256,2048]{1,0:T(8,128)(2,1)S(1)} %add_convert_fusion.10), channel_id=1, source_target_pairs={{4,0},{8,4},{12,8},{14,12},{10,14},{6,10},{2,6},{0,2},{5,1},{9,5},... | collective-permute-start | bytes 3145736 | tf_op jit(solution)/shard_map/ppermute | solution.py:281
  351.8 24.8 %collective-permute-start.28 = (bf16[256,2048]{1,0:T(8,128)(2,1)S(1)}, bf16[256,2048]{1,0:T(8,128)(2,1)S(1)}, u32[]{:S(2)}, u32[]{:S(2)}) collective-permute-start(bf16[256,2048]{1,0:T(8,128)(2,1)S(1)} %add_convert_fusion.11), channel_id=1, source_target_pairs={{0,4},{4,8},{8,12},{12,14},{14,10},{10,6},{6,2},{2,0},{1,5},{5,9},... | collective-permute-start | bytes 3145736 | tf_op jit(solution)/shard_map/ppermute | solution.py:278
  377.8 25.6 %collective-permute-start.33 = (bf16[256,2048]{1,0:T(8,128)(2,1)S(1)}, bf16[256,2048]{1,0:T(8,128)(2,1)S(1)}, u32[]{:S(2)}, u32[]{:S(2)}) collective-permute-start(bf16[256,2048]{1,0:T(8,128)(2,1)S(1)} %get-tuple-element.310), channel_id=1, source_target_pairs={{0,4},{4,8},{8,12},{12,14},{14,10},{10,6},{6,2},{2,0},{1,5},{5,9},... | collective-permute-start | bytes 3145736 | tf_op jit(solution)/shard_map/ppermute | solution.py:278
  378.7 25.3 %collective-permute-start.34 = (bf16[256,2048]{1,0:T(8,128)(2,1)S(1)}, bf16[256,2048]{1,0:T(8,128)(2,1)S(1)}, u32[]{:S(2)}, u32[]{:S(2)}) collective-permute-start(bf16[256,2048]{1,0:T(8,128)(2,1)S(1)} %get-tuple-element.309), channel_id=1, source_target_pairs={{4,0},{8,4},{12,8},{14,12},{10,14},{6,10},{2,6},{0,2},{5,1},{9,5},... | collective-permute-start | bytes 3145736 | tf_op jit(solution)/shard_map/ppermute | solution.py:281
  379.8 25.0 %collective-permute-start.36 = (bf16[4,256,512]{2,1,0:T(8,128)(2,1)S(1)}, bf16[4,256,512]{2,1,0:T(8,128)(2,1)S(1)}, u32[]{:S(2)}, u32[]{:S(2)}) collective-permute-start(bf16[4,256,512]{2,1,0:T(8,128)(2,1)S(1)} %add_convert_fusion.9), channel_id=1, source_target_pairs={{0,16},{16,0},{1,17},{17,1},{2,18},{18,2},{3,19},{19,3},{4,20},{20... | collective-permute-start | bytes 3145736 | tf_op jit(solution)/shard_map/ppermute | solution.py:265
  431.1 76.5 %all-to-all-start.3 = ((bf16[4,768,512]{2,1,0:T(8,128)(2,1)}), bf16[4,768,512]{2,1,0:T(8,128)(2,1)}, u32[]{:S(2)}, u32[]{:S(2)}) async-start(bf16[4,768,512]{2,1,0:T(8,128)(2,1)} %pad_maximum_fusion), calls=%async_computation.3 | async-start | bytes 6291456 | tf_op jit(solution)/shard_map/all_to_all | solution.py:345
  453.5 25.6 %collective-permute-start.42 = (bf16[2,512,512]{2,1,0:T(8,128)(2,1)S(1)}, bf16[2,512,512]{2,1,0:T(8,128)(2,1)S(1)}, u32[]{:S(2)}, u32[]{:S(2)}) collective-permute-start(bf16[2,512,512]{2,1,0:T(8,128)(2,1)S(1)} %slice.187), channel_id=1, source_target_pairs={{0,16},{16,0},{1,17},{17,1},{2,18},{18,2},{3,19},{19,3},{4,20},{20... | collective-permute-start | bytes 3145736 | tf_op jit(solution)/shard_map/ppermute | solution.py:265
  480.2 25.7 %collective-permute-start.44 = (bf16[2,512,512]{2,1,0:T(8,128)(2,1)S(1)}, bf16[2,512,512]{2,1,0:T(8,128)(2,1)}, u32[]{:S(2)}, u32[]{:S(2)}) collective-permute-start(bf16[2,512,512]{2,1,0:T(8,128)(2,1)S(1)} %slice.188), channel_id=1, source_target_pairs={{0,16},{16,0},{1,17},{17,1},{2,18},{18,2},{3,19},{19,3},{4,20},{20... | collective-permute-start | bytes 3145736 | tf_op jit(solution)/shard_map/ppermute | solution.py:265
  507.6 70.0 %collective-permute-start.45 = (bf16[4,768,512]{2,1,0:T(8,128)(2,1)}, bf16[4,768,512]{2,1,0:T(8,128)(2,1)}, u32[]{:S(2)}, u32[]{:S(2)}) collective-permute-start(bf16[4,768,512]{2,1,0:T(8,128)(2,1)} %all-to-all-done.3.mine_ref), channel_id=1, source_target_pairs={{0,16},{16,0},{1,17},{17,1},{2,18},{18,2},{3,19},{19,3},{4,20},{20... | collective-permute-start | bytes 9437192 | tf_op jit(solution)/shard_map/ppermute | solution.py:265
  511.3 66.4 %all-to-all-start.4 = ((bf16[4,512,512]{2,1,0:T(8,128)(2,1)}), bf16[4,512,512]{2,1,0:T(8,128)(2,1)}, u32[]{:S(2)}, u32[]{:S(2)}) async-start(bf16[4,512,512]{2,1,0:T(8,128)(2,1)} %add_convert_fusion), calls=%async_computation.4 | async-start | bytes 4194304 | tf_op jit(solution)/shard_map/all_to_all | solution.py:345
  516.0 39.3 %collective-permute-start.46 = (bf16[64,2048]{1,0:T(8,128)(2,1)S(1)}, bf16[64,2048]{1,0:T(8,128)(2,1)S(1)}, u32[]{:S(2)}, u32[]{:S(2)}) collective-permute-start(bf16[64,2048]{1,0:T(8,128)(2,1)S(1)} %get-tuple-element.322), channel_id=1, source_target_pairs={{0,4},{4,6},{6,2},{2,0},{1,5},{5,7},{7,3},{3,1},{8,12},{12,14},{14... | collective-permute-start | bytes 786440 | tf_op jit(solution)/shard_map/ppermute | solution.py:278
  518.0 37.3 %collective-permute-start.48 = (bf16[64,2048]{1,0:T(8,128)(2,1)S(1)}, bf16[64,2048]{1,0:T(8,128)(2,1)S(1)}, u32[]{:S(2)}, u32[]{:S(2)}) collective-permute-start(bf16[64,2048]{1,0:T(8,128)(2,1)S(1)} %get-tuple-element.323), channel_id=1, source_target_pairs={{4,0},{6,4},{2,6},{0,2},{5,1},{7,5},{3,7},{1,3},{12,8},{14,12},{10... | collective-permute-start | bytes 786440 | tf_op jit(solution)/shard_map/ppermute | solution.py:281
  578.8 28.9 %all-to-all-start.5 = ((bf16[4,256,512]{2,1,0:T(8,128)(2,1)}), bf16[4,256,512]{2,1,0:T(8,128)(2,1)S(1)}, u32[]{:S(2)}, u32[]{:S(2)}) async-start(bf16[4,256,512]{2,1,0:T(8,128)(2,1)} %bitcast.25), calls=%async_computation.5 | async-start | bytes 2097152 | tf_op jit(solution)/shard_map/all_to_all | solution.py:345
  (71 other events, 910.3 us)

commit v9 on v8

--- a/solution.py
+++ b/solution.py
@@ -9,7 +9,7 @@
 from jax.sharding import PartitionSpec as P
 
 HEAD_DIM = 128
-BLOCK = 512
+BLOCK = 256
 HALF = 2
 
 epsilon = 1e-05
@@ -247,7 +247,7 @@
         in_specs=[whole] * len(arrays),
         out_specs=[whole] * len(shapes),
         out_shape=shapes,
-        compiler_params=pltpu.CompilerParams(vmem_limit_bytes=15 * 1024 * 1024),
+        compiler_params=pltpu.CompilerParams(vmem_limit_bytes=12 * 1024 * 1024),
         cost_estimate=CHEAP,
         name=name,
     )(*arrays)

time: 618 us -> 619 us (level)
  no operation moved by 1% of the time
where the time goes in v9:
time: 619 us; the launch traced here: 615 us
  waiting for transfers between devices  364 us (59%)
  Pallas kernels  125 us (20%)
  starting transfers between devices  69.3 us (11%)
  local copies, waits for them, and re-layouts  29.2 us (5%)
  other arithmetic  25.7 us (4%)
    ppermute x16, waiting for transfers between devices, up(): return lax.ppermute(array, self.axes, self.upward)  200 us
    ppermute x19, waiting for transfers between devices, swap(): return lax.ppermute(array, axis, [(0, 1), (1, 0)])  79.3 us
    ppermute x16, waiting for transfers between devices, down(): return lax.ppermute(array, self.axes, self.downward)  50.2 us
    all_to_all x6, waiting for transfers between devices, exchange_rows(): return lax.all_to_all(array, ROW, 0, 0, tiled=True)  33.9 us
    pallas_call x3, Pallas kernels, feed_forward(): pl.pallas_call(functools.partial(mlp_kernel, blocks), grid=(steps,), in_s...  33.3 us
    pallas_call x4, Pallas kernels, call_whole(): pl.pallas_call(kernel, in_specs=[whole] * len(arrays), out_specs=[whole]...  31.4 us
    pallas_call x6, Pallas kernels, call_blocks(): pl.pallas_call(kernel, grid=(count,), in_specs=[pl.BlockSpec((array.shape...  30.4 us
    all_to_all x6, starting transfers between devices, exchange_rows(): return lax.all_to_all(array, ROW, 0, 0, tiled=True)  27.9 us
  transfers between devices with their start and end apart: 57, of which 44 were waited for; matrix products, arithmetic and copies ran while one was open for 4% of the time, Pallas kernels for 17%

profile of v9, /device:TPU:0, one launch (start us, length us, event | category | flops | bytes accessed | tf_op | source)
XLA Modules:
  0.0 615.0 jit_solution(10833322831193166414)
XLA Ops:
  12.6 8.8 %all-to-all-done = bf16[4,128,512]{2,1,0:T(8,128)(2,1)S(1)} async-done(((bf16[4,128,512]{2,1,0:T(8,128)(2,1)}), bf16[4,128,512]{2,1,0:T(8,128)(2,1)S(1)}, u32[]{:S(2)}, u32[]{:S(2)}) %all-to-all-start) | async-done | bytes 524320 | tf_op jit(solution)/shard_map/all_to_all | solution.py:345
  28.6 49.6 %collective-permute-done = bf16[128,2048]{1,0:T(8,128)(2,1)S(1)} collective-permute-done((bf16[128,2048]{1,0:T(8,128)(2,1)S(1)}, bf16[128,2048]{1,0:T(8,128)(2,1)S(1)}, u32[]{:S(2)}, u32[]{:S(2)}) %collective-permute-start) | collective-permute-done | bytes 524320 | tf_op jit(solution)/shard_map/ppermute | solution.py:278
  105.4 7.5 %attend.2 = (bf16[1024,384]{1,0:T(8,128)(2,1)S(1)}, bf16[1024,128]{1,0:T(8,128)(2,1)S(1)}, f32[1024,1]{1,0:T(8,128)S(1)}) custom-call(bf16[512,2048]{1,0:T(8,128)(2,1)} %constant_dynamic-update-slice_fusion.own_ref.rows_own, bf16[512,2048]{1,0:T(8,128)(2,1)} %collective-permute-done.4.other_ref.rows_other, bf16[2048,512]{1,0:T(8,128)(2,1)S(1)} %bitcast.27, ...), custom_call_target="tpu_custom_call" | custom-call | flops 1 | bytes 1 | tf_op jit(solution)/shard_map/attend/pallas_call | solution.py:245
  113.8 30.8 %collective-permute-done.5.weight_ref.refs_3_ = bf16[2048,512]{1,0:T(8,128)(2,1)} collective-permute-done((bf16[2048,512]{1,0:T(8,128)(2,1)S(1)}, bf16[2048,512]{1,0:T(8,128)(2,1)}, u32[]{:S(2)}, u32[]{:S(2)}) %collective-permute-start.5) | collective-permute-done | bytes 2097184 | tf_op jit(solution)/shard_map/ppermute | solution.py:265
  144.7 7.9 %attend.3 = (bf16[1024,384]{1,0:T(8,128)(2,1)S(1)}, bf16[1024,128]{1,0:T(8,128)(2,1)S(1)}, f32[1024,1]{1,0:T(8,128)S(1)}) custom-call(bf16[512,2048]{1,0:T(8,128)(2,1)} %constant_dynamic-update-slice_fusion.own_ref.rows_own, bf16[512,2048]{1,0:T(8,128)(2,1)} %collective-permute-done.4.other_ref.rows_other, ...), custom_call_target="tpu_custom_call" | custom-call | flops 1 | bytes 1 | tf_op jit(solution)/shard_map/attend/pallas_call | solution.py:245
  165.1 9.1 %all-to-all-done.2.refs_4_ = bf16[4,768,512]{2,1,0:T(8,128)(2,1)} async-done(((bf16[4,768,512]{2,1,0:T(8,128)(2,1)}), bf16[4,768,512]{2,1,0:T(8,128)(2,1)}, u32[]{:S(2)}, u32[]{:S(2)}) %all-to-all-start.2) | async-done | bytes 3145760 | tf_op jit(solution)/shard_map/all_to_all | solution.py:345
  187.3 9.0 %collective-permute-done.8 = bf16[128,2048]{1,0:T(8,128)(2,1)S(1)} collective-permute-done((bf16[128,2048]{1,0:T(8,128)(2,1)S(1)}, bf16[128,2048]{1,0:T(8,128)(2,1)S(1)}, u32[]{:S(2)}, u32[]{:S(2)}) %collective-permute-start.8) | collective-permute-done | bytes 524320 | tf_op jit(solution)/shard_map/ppermute | solution.py:278
  200.3 20.5 %collective-permute-done.11 = bf16[256,2048]{1,0:T(8,128)(2,1)S(1)} collective-permute-done((bf16[256,2048]{1,0:T(8,128)(2,1)S(1)}, bf16[256,2048]{1,0:T(8,128)(2,1)S(1)}, u32[]{:S(2)}, u32[]{:S(2)}) %collective-permute-start.11) | collective-permute-done | bytes 1048608 | tf_op jit(solution)/shard_map/ppermute | solution.py:278
  224.2 19.9 %collective-permute-done.14 = bf16[256,2048]{1,0:T(8,128)(2,1)S(1)} collective-permute-done((bf16[256,2048]{1,0:T(8,128)(2,1)S(1)}, bf16[256,2048]{1,0:T(8,128)(2,1)S(1)}, u32[]{:S(2)}, u32[]{:S(2)}) %collective-permute-start.14) | collective-permute-done | bytes 1048608 | tf_op jit(solution)/shard_map/ppermute | solution.py:278
  248.1 9.1 %feed_forward.3 = (bf16[512,512]{1,0:T(8,128)(2,1)S(1)}, bf16[512,1024]{1,0:T(8,128)(2,1)S(1)}, bf16[1024,2048]{1,0:T(8,128)(2,1)S(1)}, bf16[512,2048]{1,0:T(8,128)(2,1)S(1)}, bf16[512,2048]{1,0:T(8,128)(2,1)S(1)}) custom-call(bf16[1024,2048]{1,0:T(8,128)(2,1)S(1)} %constant_dynamic-update-slice_fusion.4.refs_0_.refs_1_.refs_2_.refs_3_, ...), custom_call_target="tpu_custom_call" | custom-call | flops 1 | bytes 1 | tf_op jit(solution)/shard_map/feed_forward/pallas_call | solution.py:454
  257.2 9.8 %collective-permute-done.18.refs_4_.refs_6_ = bf16[4,768,512]{2,1,0:T(8,128)(2,1)S(1)} collective-permute-done((bf16[4,768,512]{2,1,0:T(8,128)(2,1)}, bf16[4,768,512]{2,1,0:T(8,128)(2,1)S(1)}, u32[]{:S(2)}, u32[]{:S(2)}) %collective-permute-start.18) | collective-permute-done | bytes 3145760 | tf_op jit(solution)/shard_map/ppermute | solution.py:265
  286.5 17.0 %feed_forward.5 = (bf16[512,1024]{1,0:T(8,128)(2,1)S(1)}, bf16[512,2048]{1,0:T(8,128)(2,1)S(1)}, bf16[1024,2048]{1,0:T(8,128)(2,1)S(1)}, bf16[512,2048]{1,0:T(8,128)(2,1)S(1)}, bf16[512,2048]{1,0:T(8,128)(2,1)S(1)}) custom-call(bf16[1024,2048]{1,0:T(8,128)(2,1)S(1)} %constant_dynamic-update-slice_fusion.9.refs_0_.refs_1_.refs_2_.refs_3_, ...), custom_call_target="tpu_custom_call" | custom-call | flops 1 | bytes 1 | tf_op jit(solution)/shard_map/feed_forward/pallas_call | solution.py:454
  334.3 13.5 %collective-permute-done.26 = bf16[256,2048]{1,0:T(8,128)(2,1)S(1)} collective-permute-done((bf16[256,2048]{1,0:T(8,128)(2,1)S(1)}, bf16[256,2048]{1,0:T(8,128)(2,1)S(1)}, u32[]{:S(2)}, u32[]{:S(2)}) %collective-permute-start.26) | collective-permute-done | bytes 1048608 | tf_op jit(solution)/shard_map/ppermute | solution.py:281
  357.2 18.4 %collective-permute-done.29 = bf16[256,2048]{1,0:T(8,128)(2,1)S(1)} collective-permute-done((bf16[256,2048]{1,0:T(8,128)(2,1)S(1)}, bf16[256,2048]{1,0:T(8,128)(2,1)S(1)}, u32[]{:S(2)}, u32[]{:S(2)}) %collective-permute-start.29) | collective-permute-done | bytes 1048608 | tf_op jit(solution)/shard_map/ppermute | solution.py:281
  382.2 21.8 %collective-permute-done.33 = bf16[256,2048]{1,0:T(8,128)(2,1)S(1)} collective-permute-done((bf16[256,2048]{1,0:T(8,128)(2,1)S(1)}, bf16[256,2048]{1,0:T(8,128)(2,1)S(1)}, u32[]{:S(2)}, u32[]{:S(2)}) %collective-permute-start.33) | collective-permute-done | bytes 1048608 | tf_op jit(solution)/shard_map/ppermute | solution.py:278
  410.0 10.9 %collective-permute-done.37 = bf16[128,2048]{1,0:T(8,128)(2,1)S(1)} collective-permute-done((bf16[128,2048]{1,0:T(8,128)(2,1)S(1)}, bf16[128,2048]{1,0:T(8,128)(2,1)S(1)}, u32[]{:S(2)}, u32[]{:S(2)}) %collective-permute-start.37) | collective-permute-done | bytes 524320 | tf_op jit(solution)/shard_map/ppermute | solution.py:278
  439.7 8.3 %attend_back.2.slope_ref.refs_1_ = bf16[1024,384]{1,0:T(8,128)(2,1)S(1)} custom-call(bf16[512,2048]{1,0:T(8,128)(2,1)} %constant_dynamic-update-slice_fusion.14.own_ref.middle_own, bf16[512,2048]{1,0:T(8,128)(2,1)} %collective-permute-done.41.other_ref.middle_other, bf16[2048,512]{1,0:T(8,128)(2,1)} %collective-permute-done.5.weight_ref.refs_3_, ...), custom_call_target="tpu_custom_call" | custom-call | flops 1 | bytes 1 | tf_op jit(solution)/shard_map/attend_back/pallas_call | solution.py:245
  455.9 7.6 %attend_back.3.refs_0_.slope_ref = bf16[1024,384]{1,0:T(8,128)(2,1)S(1)} custom-call(bf16[512,2048]{1,0:T(8,128)(2,1)} %constant_dynamic-update-slice_fusion.14.own_ref.middle_own, bf16[512,2048]{1,0:T(8,128)(2,1)} %collective-permute-done.41.other_ref.middle_other, bf16[2048,512]{1,0:T(8,128)(2,1)S(1)} %bitcast.29, ...), custom_call_target="tpu_custom_call" | custom-call | flops 1 | bytes 1 | tf_op jit(solution)/shard_map/attend_back/pallas_call | solution.py:245
  469.9 7.9 %qkv_back.1 = (bf16[512,2048]{1,0:T(8,128)(2,1)S(1)}, bf16[512,2048]{1,0:T(8,128)(2,1)S(1)}) custom-call(bf16[1024,384]{1,0:T(8,128)(2,1)S(1)} %attend_back.3.refs_0_.slope_ref, bf16[1024,384]{1,0:T(8,128)(2,1)S(1)} %attend_back.2.slope_ref.refs_1_, bf16[2048,512]{1,0:T(8,128)(2,1)S(1)} %bitcast.30, bf16[2048,512]{1,0:T(8,128)(2,1)} %collective-permute-done.5.weight_ref.refs_3_), custom_call_target="tpu_custom_call" | custom-call | flops 1 | bytes 1 | tf_op jit(solution)/shard_map/qkv_back/pallas_call | solution.py:127
  487.4 19.6 %collective-permute-done.44 = bf16[2,512,512]{2,1,0:T(8,128)(2,1)} collective-permute-done((bf16[2,512,512]{2,1,0:T(8,128)(2,1)S(1)}, bf16[2,512,512]{2,1,0:T(8,128)(2,1)}, u32[]{:S(2)}, u32[]{:S(2)}) %collective-permute-start.44) | collective-permute-done | bytes 1048608 | tf_op jit(solution)/shard_map/ppermute | solution.py:265
  518.7 37.2 %collective-permute-done.46 = bf16[64,2048]{1,0:T(8,128)(2,1)S(1)} collective-permute-done((bf16[64,2048]{1,0:T(8,128)(2,1)S(1)}, bf16[64,2048]{1,0:T(8,128)(2,1)S(1)}, u32[]{:S(2)}, u32[]{:S(2)}) %collective-permute-start.46) | collective-permute-done | bytes 262176 | tf_op jit(solution)/shard_map/ppermute | solution.py:278
  558.7 10.2 %collective-permute-done.47 = bf16[128,2048]{1,0:T(8,128)(2,1)S(1)} collective-permute-done((bf16[128,2048]{1,0:T(8,128)(2,1)S(1)}, bf16[128,2048]{1,0:T(8,128)(2,1)S(1)}, u32[]{:S(2)}, u32[]{:S(2)}) %collective-permute-start.47) | collective-permute-done | bytes 524320 | tf_op jit(solution)/shard_map/ppermute | solution.py:278
  585.9 7.6 %assemble_units.1 = (f32[512,2048]{1,0:T(8,128)}, f32[512,2048]{1,0:T(8,128)}, f32[2048,512]{1,0:T(8,128)}) custom-call(s32[1]{0:T(128)} %bitcast.1.x_ref, bf16[4,768,512]{2,1,0:T(8,128)(2,1)} %all-to-all-done.3.mine_ref, bf16[4,768,512]{2,1,0:T(8,128)(2,1)} %collective-permute-done.45.theirs_ref), custom_call_target="tpu_custom_call" | custom-call | flops 1 | bytes 1 | tf_op jit(solution)/shard_map/assemble_units/pallas_call | solution.py:228
  593.5 14.7 %all-to-all-done.5 = bf16[4,256,512]{2,1,0:T(8,128)(2,1)S(1)} async-done(((bf16[4,256,512]{2,1,0:T(8,128)(2,1)}), bf16[4,256,512]{2,1,0:T(8,128)(2,1)S(1)}, u32[]{:S(2)}, u32[]{:S(2)}) %all-to-all-start.5) | async-done | bytes 1048608 | tf_op jit(solution)/shard_map/all_to_all | solution.py:345
  (273 shorter events, 236.2 us)
Async XLA Ops:
  21.5 68.2 %all-to-all-start.1 = ((bf16[4,640,512]{2,1,0:T(8,128)(2,1)}), bf16[4,640,512]{2,1,0:T(8,128)(2,1)S(1)}, u32[]{:S(2)}, u32[]{:S(2)}) async-start(bf16[4,640,512]{2,1,0:T(8,128)(2,1)} %get-tuple-element.158), calls=%async_computation.1 | async-start | bytes 5242880 | tf_op jit(solution)/shard_map/all_to_all | solution.py:345
  26.5 51.7 %collective-permute-start = (bf16[128,2048]{1,0:T(8,128)(2,1)S(1)}, bf16[128,2048]{1,0:T(8,128)(2,1)S(1)}, u32[]{:S(2)}, u32[]{:S(2)}) collective-permute-start(bf16[128,2048]{1,0:T(8,128)(2,1)S(1)} %fusion.4), channel_id=1, source_target_pairs={{0,4},{4,6},{6,2},{2,0},{1,5},{5,7},{7,3},{3,1},{8,12},{12,14},{14... | collective-permute-start | bytes 1572872 | tf_op jit(solution)/shard_map/ppermute | solution.py:278
  28.5 52.2 %collective-permute-start.2 = (bf16[128,2048]{1,0:T(8,128)(2,1)S(1)}, bf16[128,2048]{1,0:T(8,128)(2,1)S(1)}, u32[]{:S(2)}, u32[]{:S(2)}) collective-permute-start(bf16[128,2048]{1,0:T(8,128)(2,1)S(1)} %fusion.4), channel_id=1, source_target_pairs={{4,0},{6,4},{2,6},{0,2},{5,1},{7,5},{3,7},{1,3},{12,8},{14,12},{10... | collective-permute-start | bytes 1572872 | tf_op jit(solution)/shard_map/ppermute | solution.py:281
  96.4 48.2 %collective-permute-start.5 = (bf16[2048,512]{1,0:T(8,128)(2,1)S(1)}, bf16[2048,512]{1,0:T(8,128)(2,1)}, u32[]{:S(2)}, u32[]{:S(2)}) collective-permute-start(bf16[2048,512]{1,0:T(8,128)(2,1)S(1)} %bitcast.26), channel_id=1, source_target_pairs={{0,16},{16,0},{1,17},{17,1},{2,18},{18,2},{3,19},{19,3},{4,20},{20... | collective-permute-start | bytes 6291464 | tf_op jit(solution)/shard_map/ppermute | solution.py:265
  98.0 76.2 %all-to-all-start.2 = ((bf16[4,768,512]{2,1,0:T(8,128)(2,1)}), bf16[4,768,512]{2,1,0:T(8,128)(2,1)}, u32[]{:S(2)}, u32[]{:S(2)}) async-start(bf16[4,768,512]{2,1,0:T(8,128)(2,1)} %get-tuple-element.169), calls=%async_computation.2 | async-start | bytes 6291456 | tf_op jit(solution)/shard_map/all_to_all | solution.py:345
  186.2 36.0 %collective-permute-start.13 = (bf16[4,768,512]{2,1,0:T(8,128)(2,1)}, bf16[4,768,512]{2,1,0:T(8,128)(2,1)S(1)}, u32[]{:S(2)}, u32[]{:S(2)}) collective-permute-start(bf16[4,768,512]{2,1,0:T(8,128)(2,1)} %all-to-all-done.2.refs_4_), channel_id=1, source_target_pairs={{0,1},{1,0},{2,3},{3,2},{4,5},{5,4},{6,7},{7,6},{8,9},{9,8},{10,11... | collective-permute-start | bytes 9437192 | tf_op jit(solution)/shard_map/ppermute | solution.py:265
  199.8 67.2 %collective-permute-start.18 = (bf16[4,768,512]{2,1,0:T(8,128)(2,1)}, bf16[4,768,512]{2,1,0:T(8,128)(2,1)S(1)}, u32[]{:S(2)}, u32[]{:S(2)}) collective-permute-start(bf16[4,768,512]{2,1,0:T(8,128)(2,1)} %all-to-all-done.2.refs_4_), channel_id=1, source_target_pairs={{0,16},{16,0},{1,17},{17,1},{2,18},{18,2},{3,19},{19,3},{4,20},{20... | collective-permute-start | bytes 9437192 | tf_op jit(solution)/shard_map/ppermute | solution.py:265
  322.5 25.3 %collective-permute-start.26 = (bf16[256,2048]{1,0:T(8,128)(2,1)S(1)}, bf16[256,2048]{1,0:T(8,128)(2,1)S(1)}, u32[]{:S(2)}, u32[]{:S(2)}) collective-permute-start(bf16[256,2048]{1,0:T(8,128)(2,1)S(1)} %pad_maximum_fusion.3), channel_id=1, source_target_pairs={{4,0},{8,4},{12,8},{14,12},{10,14},{6,10},{2,6},{0,2},{5,1},{9,5},... | collective-permute-start | bytes 3145736 | tf_op jit(solution)/shard_map/ppermute | solution.py:281
  324.1 25.1 %collective-permute-start.25 = (bf16[256,2048]{1,0:T(8,128)(2,1)S(1)}, bf16[256,2048]{1,0:T(8,128)(2,1)S(1)}, u32[]{:S(2)}, u32[]{:S(2)}) collective-permute-start(bf16[256,2048]{1,0:T(8,128)(2,1)S(1)} %pad_maximum_fusion.2), channel_id=1, source_target_pairs={{0,4},{4,8},{8,12},{12,14},{14,10},{10,6},{6,2},{2,0},{1,5},{5,9},... | collective-permute-start | bytes 3145736 | tf_op jit(solution)/shard_map/ppermute | solution.py:278
  324.9 24.6 %collective-permute-start.27 = (bf16[2,512,512]{2,1,0:T(8,128)(2,1)S(1)}, bf16[2,512,512]{2,1,0:T(8,128)(2,1)S(1)}, u32[]{:S(2)}, u32[]{:S(2)}) collective-permute-start(bf16[2,512,512]{2,1,0:T(8,128)(2,1)S(1)} %get-tuple-element.220), channel_id=1, source_target_pairs={{0,16},{16,0},{1,17},{17,1},{2,18},{18,2},{3,19},{19,3},{4,20},{20... | collective-permute-start | bytes 3145736 | tf_op jit(solution)/shard_map/ppermute | solution.py:265
  349.6 27.9 %collective-permute-start.31 = (bf16[4,512,512]{2,1,0:T(8,128)(2,1)S(1)}, bf16[4,512,512]{2,1,0:T(8,128)(2,1)S(1)}, u32[]{:S(2)}, u32[]{:S(2)}) collective-permute-start(bf16[4,512,512]{2,1,0:T(8,128)(2,1)S(1)} %get-tuple-element.238), channel_id=1, source_target_pairs={{0,1},{1,0},{2,3},{3,2},{4,5},{5,4},{6,7},{7,6},{8,9},{9,8},{10,11... | collective-permute-start | bytes 6291464 | tf_op jit(solution)/shard_map/ppermute | solution.py:265
  350.5 25.1 %collective-permute-start.29 = (bf16[256,2048]{1,0:T(8,128)(2,1)S(1)}, bf16[256,2048]{1,0:T(8,128)(2,1)S(1)}, u32[]{:S(2)}, u32[]{:S(2)}) collective-permute-start(bf16[256,2048]{1,0:T(8,128)(2,1)S(1)} %add_convert_fusion.10), channel_id=1, source_target_pairs={{4,0},{8,4},{12,8},{14,12},{10,14},{6,10},{2,6},{0,2},{5,1},{9,5},... | collective-permute-start | bytes 3145736 | tf_op jit(solution)/shard_map/ppermute | solution.py:281
  352.4 24.8 %collective-permute-start.28 = (bf16[256,2048]{1,0:T(8,128)(2,1)S(1)}, bf16[256,2048]{1,0:T(8,128)(2,1)S(1)}, u32[]{:S(2)}, u32[]{:S(2)}) collective-permute-start(bf16[256,2048]{1,0:T(8,128)(2,1)S(1)} %add_convert_fusion.11), channel_id=1, source_target_pairs={{0,4},{4,8},{8,12},{12,14},{14,10},{10,6},{6,2},{2,0},{1,5},{5,9},... | collective-permute-start | bytes 3145736 | tf_op jit(solution)/shard_map/ppermute | solution.py:278
  378.4 25.6 %collective-permute-start.33 = (bf16[256,2048]{1,0:T(8,128)(2,1)S(1)}, bf16[256,2048]{1,0:T(8,128)(2,1)S(1)}, u32[]{:S(2)}, u32[]{:S(2)}) collective-permute-start(bf16[256,2048]{1,0:T(8,128)(2,1)S(1)} %get-tuple-element.310), channel_id=1, source_target_pairs={{0,4},{4,8},{8,12},{12,14},{14,10},{10,6},{6,2},{2,0},{1,5},{5,9},... | collective-permute-start | bytes 3145736 | tf_op jit(solution)/shard_map/ppermute | solution.py:278
  379.2 25.3 %collective-permute-start.34 = (bf16[256,2048]{1,0:T(8,128)(2,1)S(1)}, bf16[256,2048]{1,0:T(8,128)(2,1)S(1)}, u32[]{:S(2)}, u32[]{:S(2)}) collective-permute-start(bf16[256,2048]{1,0:T(8,128)(2,1)S(1)} %get-tuple-element.309), channel_id=1, source_target_pairs={{4,0},{8,4},{12,8},{14,12},{10,14},{6,10},{2,6},{0,2},{5,1},{9,5},... | collective-permute-start | bytes 3145736 | tf_op jit(solution)/shard_map/ppermute | solution.py:281
  380.4 25.0 %collective-permute-start.36 = (bf16[4,256,512]{2,1,0:T(8,128)(2,1)S(1)}, bf16[4,256,512]{2,1,0:T(8,128)(2,1)S(1)}, u32[]{:S(2)}, u32[]{:S(2)}) collective-permute-start(bf16[4,256,512]{2,1,0:T(8,128)(2,1)S(1)} %add_convert_fusion.9), channel_id=1, source_target_pairs={{0,16},{16,0},{1,17},{17,1},{2,18},{18,2},{3,19},{19,3},{4,20},{20... | collective-permute-start | bytes 3145736 | tf_op jit(solution)/shard_map/ppermute | solution.py:265
  431.6 76.5 %all-to-all-start.3 = ((bf16[4,768,512]{2,1,0:T(8,128)(2,1)}), bf16[4,768,512]{2,1,0:T(8,128)(2,1)}, u32[]{:S(2)}, u32[]{:S(2)}) async-start(bf16[4,768,512]{2,1,0:T(8,128)(2,1)} %pad_maximum_fusion), calls=%async_computation.3 | async-start | bytes 6291456 | tf_op jit(solution)/shard_map/all_to_all | solution.py:345
  454.5 25.6 %collective-permute-start.42 = (bf16[2,512,512]{2,1,0:T(8,128)(2,1)S(1)}, bf16[2,512,512]{2,1,0:T(8,128)(2,1)S(1)}, u32[]{:S(2)}, u32[]{:S(2)}) collective-permute-start(bf16[2,512,512]{2,1,0:T(8,128)(2,1)S(1)} %slice.187), channel_id=1, source_target_pairs={{0,16},{16,0},{1,17},{17,1},{2,18},{18,2},{3,19},{19,3},{4,20},{20... | collective-permute-start | bytes 3145736 | tf_op jit(solution)/shard_map/ppermute | solution.py:265
  481.2 25.7 %collective-permute-start.44 = (bf16[2,512,512]{2,1,0:T(8,128)(2,1)S(1)}, bf16[2,512,512]{2,1,0:T(8,128)(2,1)}, u32[]{:S(2)}, u32[]{:S(2)}) collective-permute-start(bf16[2,512,512]{2,1,0:T(8,128)(2,1)S(1)} %slice.188), channel_id=1, source_target_pairs={{0,16},{16,0},{1,17},{17,1},{2,18},{18,2},{3,19},{19,3},{4,20},{20... | collective-permute-start | bytes 3145736 | tf_op jit(solution)/shard_map/ppermute | solution.py:265
  508.2 70.0 %collective-permute-start.45 = (bf16[4,768,512]{2,1,0:T(8,128)(2,1)}, bf16[4,768,512]{2,1,0:T(8,128)(2,1)}, u32[]{:S(2)}, u32[]{:S(2)}) collective-permute-start(bf16[4,768,512]{2,1,0:T(8,128)(2,1)} %all-to-all-done.3.mine_ref), channel_id=1, source_target_pairs={{0,16},{16,0},{1,17},{17,1},{2,18},{18,2},{3,19},{19,3},{4,20},{20... | collective-permute-start | bytes 9437192 | tf_op jit(solution)/shard_map/ppermute | solution.py:265
  511.9 66.4 %all-to-all-start.4 = ((bf16[4,512,512]{2,1,0:T(8,128)(2,1)}), bf16[4,512,512]{2,1,0:T(8,128)(2,1)}, u32[]{:S(2)}, u32[]{:S(2)}) async-start(bf16[4,512,512]{2,1,0:T(8,128)(2,1)} %add_convert_fusion), calls=%async_computation.4 | async-start | bytes 4194304 | tf_op jit(solution)/shard_map/all_to_all | solution.py:345
  516.6 39.3 %collective-permute-start.46 = (bf16[64,2048]{1,0:T(8,128)(2,1)S(1)}, bf16[64,2048]{1,0:T(8,128)(2,1)S(1)}, u32[]{:S(2)}, u32[]{:S(2)}) collective-permute-start(bf16[64,2048]{1,0:T(8,128)(2,1)S(1)} %get-tuple-element.322), channel_id=1, source_target_pairs={{0,4},{4,6},{6,2},{2,0},{1,5},{5,7},{7,3},{3,1},{8,12},{12,14},{14... | collective-permute-start | bytes 786440 | tf_op jit(solution)/shard_map/ppermute | solution.py:278
  518.6 37.3 %collective-permute-start.48 = (bf16[64,2048]{1,0:T(8,128)(2,1)S(1)}, bf16[64,2048]{1,0:T(8,128)(2,1)S(1)}, u32[]{:S(2)}, u32[]{:S(2)}) collective-permute-start(bf16[64,2048]{1,0:T(8,128)(2,1)S(1)} %get-tuple-element.323), channel_id=1, source_target_pairs={{4,0},{6,4},{2,6},{0,2},{5,1},{7,5},{3,7},{1,3},{12,8},{14,12},{10... | collective-permute-start | bytes 786440 | tf_op jit(solution)/shard_map/ppermute | solution.py:281
  579.4 28.9 %all-to-all-start.5 = ((bf16[4,256,512]{2,1,0:T(8,128)(2,1)}), bf16[4,256,512]{2,1,0:T(8,128)(2,1)S(1)}, u32[]{:S(2)}, u32[]{:S(2)}) async-start(bf16[4,256,512]{2,1,0:T(8,128)(2,1)} %bitcast.25), calls=%async_computation.5 | async-start | bytes 2097152 | tf_op jit(solution)/shard_map/all_to_all | solution.py:345
  (71 other events, 905.1 us)
